TPU v7x, 32 devices: a whole 2x2x4 slice. The times are simulated.
32 devices in a mesh: region: 2 (over y), blk: 16 (over z, x, core).
Axes of the slice: x: 2, y: 2, z: 4, core: 2. Of those that a mesh axis runs over, the one named last changes fastest.
Arguments:
- u_now: float32 [32, 2, 4, 32, 1024], P('blk', 'region'), may hold values from -6 to 6
- u_prev: float32 [32, 2, 4, 32, 1024], P('blk', 'region'), may hold values from -6 to 6
- coef_store: bfloat16 [16, 2, 2, 4, 32, 1024], P('blk', 'region'), may hold values from 0.019897461 to 0.099609375
- store_map: int32 [16, 2, 8], P('blk', 'region'), may hold values from 0 to 7, each once within a row
- new_owner: int32 [32], P('blk'), may hold values from 0 to 15, as said below
Outputs:
- new_state: float32 [48, 2, 4, 32, 1024], P('blk', 'region')
Inputs may be any that keep to these rules, and one draw needn't show every extreme that they name: new_owner[m] is m // 2, except that the last row of an owner may instead go to the next owner, (m // 2 + 1) mod 16; every owner gets 1 to 3 rows, and in every draw some owner gets 3 rows. Each store_map[j, x, :] holds every piece number once.
All inputs are finite; a program needn't handle non-finite values.
Results may differ from a plain program's by a relative error of at most 0.0003.
Values may be sent and summed in bfloat16 or wider, within the bound.
No kernel may reach another device: no remote copies, remote signals or barrier semaphores. Data moves between devices by JAX's collectives and lax.ppermute only.
A program may use at most 64 MiB of HBM per device.

v0:
```python
import jax
import jax.numpy as jnp
from jax import lax
from jax.sharding import PartitionSpec as P

STEPS = 2


def extended_2(block, sides, width, periodic):
    for axis, dim in sides:
        count = lax.axis_size(axis)
        forward = [(i, i + 1) for i in range(count - 1)]
        if periodic:
            forward.append((count - 1, 0))
        backward = [(target, source) for source, target in forward]
        low = lax.ppermute(
            lax.slice_in_dim(block, block.shape[dim] - width, None, axis=dim), axis, forward
        )
        high = lax.ppermute(lax.slice_in_dim(block, 0, width, axis=dim), axis, backward)
        block = jnp.concatenate([low, block, high], axis=dim)
    return block


def shifted_2(value, axis, by):
    devices = lax.axis_size(axis)
    return lax.ppermute(value, axis, [(i, (i + by) % devices) for i in range(devices)])


def stencil_step(state_now, state_prev, coefficient, live_count):
    slot_count, field_count, edge_cells, plane_cells = state_now.shape
    padded = extended_2(state_now, (("region", 2),), 1, False)
    first_planes = padded[..., :edge_cells]
    last_planes = padded[..., plane_cells - edge_cells :]
    last_live = jnp.take(last_planes, live_count - 1, axis=0)
    rim_pair = jnp.stack([first_planes[0], last_live], axis=2)
    spread = extended_2(rim_pair.astype(jnp.bfloat16), (("blk", 2),), 1, True).astype(
        rim_pair.dtype
    )
    left_rim = spread[:, :, 0]
    right_rim = spread[:, :, 3]
    before_planes = jnp.concatenate([left_rim[None], last_planes[:-1]], axis=0)
    after_planes = jnp.pad(first_planes[1:], ((0, 1), (0, 0), (0, 0), (0, 0)))
    slot_ids = jnp.arange(slot_count)
    after_planes = jnp.where(
        (slot_ids == live_count - 1)[:, None, None, None], right_rim[None], after_planes
    )
    extended = jnp.concatenate([before_planes, padded, after_planes], axis=-1)
    width = extended.shape[-1]
    column = jnp.arange(width) % edge_cells
    lower_mask = (column != 0).astype(jnp.float32)
    upper_mask = (column != edge_cells - 1).astype(jnp.float32)
    margin = ((0, 0), (0, 0), (0, 0), (1, 1))
    shifted = jnp.pad(extended, margin)
    summed = shifted[..., :width] * lower_mask + extended + shifted[..., 2:] * upper_mask
    summed = (
        summed[..., : -2 * edge_cells]
        + summed[..., edge_cells:-edge_cells]
        + summed[..., 2 * edge_cells :]
    )
    box_sum = summed[:, :, :-2] + summed[:, :, 1:-1] + summed[:, :, 2:]
    laplace = box_sum - 27.0 * state_now
    return 2.0 * state_now - state_prev + coefficient.astype(jnp.float32) * laplace


def compact(members, valid_flags):
    slot_count = valid_flags.shape[0]
    place_index = jnp.cumsum(valid_flags) - 1
    target = jnp.arange(slot_count)
    chooser = (valid_flags[None, :] == 1) & (place_index[None, :] == target[:, None])
    source = jnp.sum(jnp.where(chooser, target[None, :], 0), axis=1)
    filled = jnp.sum(chooser.astype(jnp.int32), axis=1) > 0
    placed = tuple(
        (
            jnp.where(
                filled.reshape((slot_count,) + (1,) * (member.ndim - 1)),
                jnp.take(member, source, axis=0),
                jnp.zeros_like(member),
            )
            for member in members
        )
    )
    return (placed, jnp.sum(valid_flags))


def on_device(u_now, u_prev, coef_store, store_map, new_owner):
    state_now = u_now[:, 0]
    state_prev = u_prev[:, 0]
    blocks, fields, edge_cells, plane_cells = state_now.shape
    store_local = coef_store[0, 0]
    arrived = lax.all_to_all(store_local, "region", split_axis=0, concat_axis=0, tiled=True)
    flattened = arrived.reshape((-1,) + arrived.shape[2:])
    inverse = jnp.argsort(store_map[0, 0])
    coefficient = jnp.take(flattened, inverse, axis=0).reshape(
        blocks, fields, edge_cells, plane_cells
    )
    own_index = lax.axis_index("blk")
    goes_right = new_owner[blocks - 1] != own_index
    mark_right = goes_right.astype(jnp.float32).reshape(1)
    middle_flags = jnp.ones((blocks - 2,), jnp.int32)
    keep_first = (new_owner[0] == own_index).astype(jnp.int32).reshape(1)
    keep_last = (new_owner[blocks - 1] == own_index).astype(jnp.int32).reshape(1)
    for step_index in range(STEPS):
        state_now, state_prev = (
            stencil_step(state_now, state_prev, coefficient, blocks),
            state_now,
        )
    from_left = shifted_2((state_now[blocks - 1], mark_right), "blk", 1)
    valid_flags = jnp.concatenate(
        [(from_left[1] > 0.5).astype(jnp.int32), keep_first, middle_flags, keep_last]
    )
    stacked_now = jnp.concatenate([from_left[0][None], state_now], axis=0)
    placed, live_count = compact((stacked_now,), valid_flags)
    result = placed[0]
    return result[:, None]


def solution(mesh):
    return jax.shard_map(
        on_device,
        mesh=mesh,
        in_specs=(
            P("blk", "region", None, None, None),
            P("blk", "region", None, None, None),
            P("blk", "region", None, None, None, None),
            P("blk", "region", None),
            P("blk"),
        ),
        out_specs=P("blk", "region", None, None, None),
        check_vma=False,
    )
```

profile of v0, /device:TPU:0, one launch (start us, length us, event | category | flops | bytes accessed | tf_op | source)
XLA Modules:
  0.0 74.6 jit_solution(6588295089494681206)
XLA Ops:
  0.0 1.2 %fusion.23 = (f32[2,4,1,1024]{3,2,1,0:T(1,128)S(1)}, f32[2,4,1,1024]{3,2,1,0:T(1,128)S(1)}) fusion(f32[2,4,32,1024]{3,2,1,0:T(8,128)} %bitcast.58), kind=kLoop, calls=%fused_computation.79 | loop fusion | bytes 131072 | tf_op jit(solution)/shard_map/slice | solution.py:17
  1.2 4.9 %collective-permute-start.1 = (f32[2,4,1,1024]{3,2,1,0:T(1,128)S(1)}, f32[2,4,1,1024]{3,2,1,0:T(1,128)S(1)}, u32[]{:S(2)}, u32[]{:S(2)}) collective-permute-start(f32[2,4,1,1024]{3,2,1,0:T(1,128)S(1)} %get-tuple-element.33), channel_id=1, source_target_pairs={{0,16},{1,17},{2,18},{3,19},{4,20},{5,21},{6,22},{7,23},{8,24},{9,... | collective-permute-start | bytes 98312 | tf_op jit(solution)/shard_map/ppermute | solution.py:16
  6.1 1.3 %collective-permute-start.2 = (f32[2,4,1,1024]{3,2,1,0:T(1,128)S(1)}, f32[2,4,1,1024]{3,2,1,0:T(1,128)S(1)}, u32[]{:S(2)}, u32[]{:S(2)}) collective-permute-start(f32[2,4,1,1024]{3,2,1,0:T(1,128)S(1)} %get-tuple-element.34), channel_id=1, source_target_pairs={{16,0},{17,1},{18,2},{19,3},{20,4},{21,5},{22,6},{23,7},{24,8},{25... | collective-permute-start | bytes 98312 | tf_op jit(solution)/shard_map/ppermute | solution.py:19
  7.4 3.9 %all-to-all-start = ((bf16[2,4,32,1024]{3,2,1,0:T(8,128)(2,1)}), bf16[2,4,32,1024]{3,2,1,0:T(8,128)(2,1)S(1)}, u32[]{:S(2)}, u32[]{:S(2)}) async-start(bf16[2,4,32,1024]{3,2,1,0:T(8,128)(2,1)} %bitcast.63), calls=%async_computation | async-start | bytes 1048576 | tf_op jit(solution)/shard_map/all_to_all | solution.py:90
  11.3 1.3 %fusion.24 = (s32[1]{0:T(128)}, s32[1]{0:T(128)}) fusion(s32[2]{0:T(128)} %param.11), kind=kLoop, calls=%fused_computation.80 | loop fusion | bytes 16 | tf_op jit(solution)/shard_map/slice | solution.py:100
  13.3 1.0 %collective-permute-start = (f32[1]{0:T(128)}, f32[1]{0:T(128)}, u32[]{:S(2)}, u32[]{:S(2)}) collective-permute-start(f32[1]{0:T(128)} %bitcast.1), channel_id=1, source_target_pairs={{0,1},{1,2},{2,3},{3,4},{4,5},{5,6},{6,7},{7,8},{8,9},{9,10},{10,1... | collective-permute-start | bytes 20 | tf_op jit(solution)/shard_map/ppermute | solution.py:26
  14.3 1.6 %sort.17 = (s32[8]{0:T(128)}, s32[8]{0:T(128)S(1)}) sort(s32[8]{0:T(128)} %bitcast.66, s32[8]{0:T(128)S(1)} %iota.33), dimensions={0}, to_apply=%region_3.4 | sort | flops 24 | bytes 128 | tf_op jit(solution)/shard_map/jit(argsort)/sort | solution.py:92
  16.6 0.1 broadcast_in_dim.98
  17.3 1.8 %collective-permute-done = f32[1]{0:T(128)} collective-permute-done((f32[1]{0:T(128)}, f32[1]{0:T(128)}, u32[]{:S(2)}, u32[]{:S(2)}) %collective-permute-start) | collective-permute-done | bytes 36 | tf_op jit(solution)/shard_map/ppermute | solution.py:26
  19.6 0.1 broadcast_compare_fusion.1
  19.7 0.2 reduce-window.8
  19.9 0.0 collective-permute-done.1
  19.9 0.2 pad_maximum_fusion.1
  20.2 0.1 fusion.7
  20.3 0.0 collective-permute-start.3
  20.3 4.4 %collective-permute-start.4 = (bf16[4,34,1,32]{3,1,0,2:T(8,128)(2,1)S(1)}, bf16[4,34,1,32]{3,1,0,2:T(8,128)(2,1)S(1)}, u32[]{:S(2)}, u32[]{:S(2)}) collective-permute-start(bf16[4,34,1,32]{3,1,0,2:T(8,128)(2,1)S(1)} %get-tuple-element.30), channel_id=1, source_target_pairs={{1,0},{2,1},{3,2},{4,3},{5,4},{6,5},{7,6},{8,7},{9,8},{10,9},{11,1... | collective-permute-start | bytes 26120 | tf_op jit(solution)/shard_map/ppermute | solution.py:19
  24.7 0.1 fusion.21
  24.8 1.6 %collective-permute-done.3 = bf16[4,34,1,32]{3,1,0,2:T(8,128)(2,1)S(1)} collective-permute-done((bf16[4,34,1,32]{3,1,0,2:T(8,128)(2,1)S(1)}, bf16[4,34,1,32]{3,1,0,2:T(8,128)(2,1)S(1)}, u32[]{:S(2)}, u32[]{:S(2)}) %collective-permute-start.3) | collective-permute-done | bytes 8736 | tf_op jit(solution)/shard_map/ppermute | solution.py:16
  26.5 0.1 pad_maximum_fusion.3
  26.5 1.5 %concatenate.50 = f32[2,4,34,1088]{3,2,1,0:T(8,128)} concatenate(f32[2,4,34,32]{3,2,1,0:T(8,128)S(1)} %get-tuple-element.41, f32[2,4,34,1024]{3,2,1,0:T(8,128)S(1)} %pad_maximum_fusion.1, f32[2,4,34,32]{3,2,1,0:T(8,128)S(1)} %get-tuple-element.42), dimensions={3} | concatenate | bytes 2367488 | tf_op jit(solution)/shard_map/concatenate | solution.py:47
  28.1 3.5 %multiply_add_fusion.1 = f32[2,4,34,1088]{3,2,1,0:T(8,128)S(1)} fusion(f32[2,4,34,1088]{3,2,1,0:T(8,128)} %concatenate.50, f32[1088]{0:T(1024)S(1)} %get-tuple-element.44, f32[1088]{0:T(1024)S(1)} %get-tuple-element.43), kind=kLoop, calls=%fused_computation.6 | loop fusion | flops 1183744 | bytes 2376192 | tf_op jit(solution)/shard_map/add | solution.py:54
  31.6 0.7 slice_add_fusion.2
  32.3 1.4 %gather_fusion = bf16[8,32,1024]{2,1,0:T(8,128)(2,1)} fusion(bf16[8,32,1024]{2,1,0:T(8,128)(2,1)S(1)} %bitcast.62, s32[1024]{0:T(1024)S(1)} %pad_clamp_fusion.1), kind=kCustom, calls=%fused_computation | custom fusion | bytes 1048608 | tf_op jit(solution)/shard_map/jit(_take)/gather | solution.py:93
  33.7 1.9 %fusion.1 = f32[2,4,32,1024]{3,2,1,0:T(8,128)S(1)} fusion(f32[2,4,34,1024]{3,2,1,0:T(8,128)S(1)} %slice_add_fusion.2, f32[2,1,4,32,1024]{4,3,2,1,0:T(8,128)} %param.8, bf16[2,4,32,1024]{3,2,1,0:T(8,128)(2,1)} %bitcast.60, pred[2,4]{1,0:T(4,128)(4,1)S(1)} %broadcast_in_dim.98, f32[2,1,4,32,1024]{4,3,2,1,0:T(8,128)S(1)} %copy-done), kind=kLoop, calls=%fused_computation.15 | loop fusion | flops 2621440 | bytes 6815752 | tf_op jit(solution)/shard_map/add | solution.py:62
  35.6 0.1 fusion.22
  35.7 4.1 %collective-permute-start.5 = (f32[2,4,1,1024]{3,2,1,0:T(1,128)S(1)}, f32[2,4,1,1024]{3,2,1,0:T(1,128)S(1)}, u32[]{:S(2)}, u32[]{:S(2)}) collective-permute-start(f32[2,4,1,1024]{3,2,1,0:T(1,128)S(1)} %get-tuple-element.31), channel_id=1, source_target_pairs={{0,16},{1,17},{2,18},{3,19},{4,20},{5,21},{6,22},{7,23},{8,24},{9,... | collective-permute-start | bytes 98312 | tf_op jit(solution)/shard_map/ppermute | solution.py:16
  39.8 1.3 %collective-permute-start.6 = (f32[2,4,1,1024]{3,2,1,0:T(1,128)S(1)}, f32[2,4,1,1024]{3,2,1,0:T(1,128)S(1)}, u32[]{:S(2)}, u32[]{:S(2)}) collective-permute-start(f32[2,4,1,1024]{3,2,1,0:T(1,128)S(1)} %get-tuple-element.32), channel_id=1, source_target_pairs={{16,0},{17,1},{18,2},{19,3},{20,4},{21,5},{22,6},{23,7},{24,8},{25... | collective-permute-start | bytes 98312 | tf_op jit(solution)/shard_map/ppermute | solution.py:19
  41.1 0.1 convert_reduce_fusion
  41.3 0.1 collective-permute-done.5
  41.4 4.2 %collective-permute-done.6 = f32[2,4,1,1024]{3,2,1,0:T(1,128)S(1)} collective-permute-done((f32[2,4,1,1024]{3,2,1,0:T(1,128)S(1)}, f32[2,4,1,1024]{3,2,1,0:T(1,128)S(1)}, u32[]{:S(2)}, u32[]{:S(2)}) %collective-permute-start.6) | collective-permute-done | bytes 32800 | tf_op jit(solution)/shard_map/ppermute | solution.py:19
  45.6 0.2 pad_maximum_fusion.2
  45.9 0.1 fusion.9
  46.0 0.0 collective-permute-start.7
  46.0 4.4 %collective-permute-start.8 = (bf16[4,34,1,32]{3,1,0,2:T(8,128)(2,1)S(1)}, bf16[4,34,1,32]{3,1,0,2:T(8,128)(2,1)S(1)}, u32[]{:S(2)}, u32[]{:S(2)}) collective-permute-start(bf16[4,34,1,32]{3,1,0,2:T(8,128)(2,1)S(1)} %get-tuple-element.26), channel_id=1, source_target_pairs={{1,0},{2,1},{3,2},{4,3},{5,4},{6,5},{7,6},{8,7},{9,8},{10,9},{11,1... | collective-permute-start | bytes 26120 | tf_op jit(solution)/shard_map/ppermute | solution.py:19
  50.4 0.1 fusion.20
  50.5 1.6 %collective-permute-done.7 = bf16[4,34,1,32]{3,1,0,2:T(8,128)(2,1)S(1)} collective-permute-done((bf16[4,34,1,32]{3,1,0,2:T(8,128)(2,1)S(1)}, bf16[4,34,1,32]{3,1,0,2:T(8,128)(2,1)S(1)}, u32[]{:S(2)}, u32[]{:S(2)}) %collective-permute-start.7) | collective-permute-done | bytes 8736 | tf_op jit(solution)/shard_map/ppermute | solution.py:16
  52.2 0.8 %pad_select_fusion = f32[2,4,34,32]{3,2,1,0:T(8,128)} fusion(f32[1,4,34,32]{3,2,1,0:T(8,128)S(1)} %get-tuple-element.23, f32[4,34,32]{2,1,0:T(8,128)S(1)} %get-tuple-element.35, pred[2]{0:T(512)(128)(4,1)S(1)} %iota_compare_fusion.1), kind=kLoop, calls=%fused_computation.28 | loop fusion | flops 8704 | bytes 69634 | tf_op jit(solution)/shard_map/jit(_where)/select_n | solution.py:44
  52.9 0.7 pad_maximum_fusion.4
  53.6 2.4 %concatenate.54 = f32[2,4,34,1088]{3,2,1,0:T(8,128)} concatenate(f32[2,4,34,32]{3,2,1,0:T(8,128)} %pad_maximum_fusion.4, f32[2,4,34,1024]{3,2,1,0:T(8,128)S(1)} %pad_maximum_fusion.2, f32[2,4,34,32]{3,2,1,0:T(8,128)} %pad_select_fusion), dimensions={3} | concatenate | bytes 2367488 | tf_op jit(solution)/shard_map/concatenate | solution.py:47
  55.9 3.5 %multiply_add_fusion = f32[2,4,34,1088]{3,2,1,0:T(8,128)S(1)} fusion(f32[2,4,34,1088]{3,2,1,0:T(8,128)} %concatenate.54, f32[1088]{0:T(1024)S(1)} %get-tuple-element.44, f32[1088]{0:T(1024)S(1)} %get-tuple-element.43), kind=kLoop, calls=%fused_computation.5 | loop fusion | flops 1183744 | bytes 2376192 | tf_op jit(solution)/shard_map/add | solution.py:54
  59.4 0.7 slice_add_fusion
  60.2 0.3 copy-done.1
  60.5 0.5 fusion.2
  61.0 0.1 collective-permute-start.9
  61.2 11.3 %collective-permute-done.9 = f32[4,32,1024]{2,1,0:T(8,128)S(1)} collective-permute-done((f32[4,32,1024]{2,1,0:T(8,128)S(1)}, f32[4,32,1024]{2,1,0:T(8,128)S(1)}, u32[]{:S(2)}, u32[]{:S(2)}) %collective-permute-start.9) | collective-permute-done | bytes 524320 | tf_op jit(solution)/shard_map/ppermute | solution.py:26
  72.4 0.1 pad_maximum_fusion
  72.5 0.6 gather_fusion.1
  73.2 1.4 %fusion = f32[3,1,4,32,1024]{4,3,2,1,0:T(8,128)} fusion(f32[3,4,32,1024]{3,2,1,0:T(8,128)S(1)} %gather_fusion.1, pred[3]{0:T(512)(128)(4,1)S(1)} %get-tuple-element.45, pred[3]{0:T(512)(128)(4,1)S(1)} %get-tuple-element.46), kind=kLoop, calls=%fused_computation.4 | loop fusion | flops 786432 | bytes 3145734 | tf_op jit(solution)/shard_map/jit(_where)/select_n | solution.py:74
  (20 shorter events, 0.2 us)
Async XLA Ops:
  0.0 19.9 %copy-start = (f32[2,1,4,32,1024]{4,3,2,1,0:T(8,128)S(1)}, f32[2,1,4,32,1024]{4,3,2,1,0:T(8,128)}, u32[]{:S(2)}) copy-start(f32[2,1,4,32,1024]{4,3,2,1,0:T(8,128)} %param.7) | copy-start | bytes 3145732
  1.2 18.7 %collective-permute-start.1 = (f32[2,4,1,1024]{3,2,1,0:T(1,128)S(1)}, f32[2,4,1,1024]{3,2,1,0:T(1,128)S(1)}, u32[]{:S(2)}, u32[]{:S(2)}) collective-permute-start(f32[2,4,1,1024]{3,2,1,0:T(1,128)S(1)} %get-tuple-element.33), channel_id=1, source_target_pairs={{0,16},{1,17},{2,18},{3,19},{4,20},{5,21},{6,22},{7,23},{8,24},{9,... | collective-permute-start | bytes 98312 | tf_op jit(solution)/shard_map/ppermute | solution.py:16
  6.1 13.9 %collective-permute-start.2 = (f32[2,4,1,1024]{3,2,1,0:T(1,128)S(1)}, f32[2,4,1,1024]{3,2,1,0:T(1,128)S(1)}, u32[]{:S(2)}, u32[]{:S(2)}) collective-permute-start(f32[2,4,1,1024]{3,2,1,0:T(1,128)S(1)} %get-tuple-element.34), channel_id=1, source_target_pairs={{16,0},{17,1},{18,2},{19,3},{20,4},{21,5},{22,6},{23,7},{24,8},{25... | collective-permute-start | bytes 98312 | tf_op jit(solution)/shard_map/ppermute | solution.py:19
  7.4 25.0 %all-to-all-start = ((bf16[2,4,32,1024]{3,2,1,0:T(8,128)(2,1)}), bf16[2,4,32,1024]{3,2,1,0:T(8,128)(2,1)S(1)}, u32[]{:S(2)}, u32[]{:S(2)}) async-start(bf16[2,4,32,1024]{3,2,1,0:T(8,128)(2,1)} %bitcast.63), calls=%async_computation | async-start | bytes 1048576 | tf_op jit(solution)/shard_map/all_to_all | solution.py:90
  13.3 5.8 %collective-permute-start = (f32[1]{0:T(128)}, f32[1]{0:T(128)}, u32[]{:S(2)}, u32[]{:S(2)}) collective-permute-start(f32[1]{0:T(128)} %bitcast.1), channel_id=1, source_target_pairs={{0,1},{1,2},{2,3},{3,4},{4,5},{5,6},{6,7},{7,8},{8,9},{9,10},{10,1... | collective-permute-start | bytes 20 | tf_op jit(solution)/shard_map/ppermute | solution.py:26
  20.3 6.2 %collective-permute-start.3 = (bf16[4,34,1,32]{3,1,0,2:T(8,128)(2,1)S(1)}, bf16[4,34,1,32]{3,1,0,2:T(8,128)(2,1)S(1)}, u32[]{:S(2)}, u32[]{:S(2)}) collective-permute-start(bf16[4,34,1,32]{3,1,0,2:T(8,128)(2,1)S(1)} %get-tuple-element.29), channel_id=1, source_target_pairs={{0,1},{1,2},{2,3},{3,4},{4,5},{5,6},{6,7},{7,8},{8,9},{9,10},{10,1... | collective-permute-start | bytes 26120 | tf_op jit(solution)/shard_map/ppermute | solution.py:16
  20.3 6.1 %collective-permute-start.4 = (bf16[4,34,1,32]{3,1,0,2:T(8,128)(2,1)S(1)}, bf16[4,34,1,32]{3,1,0,2:T(8,128)(2,1)S(1)}, u32[]{:S(2)}, u32[]{:S(2)}) collective-permute-start(bf16[4,34,1,32]{3,1,0,2:T(8,128)(2,1)S(1)} %get-tuple-element.30), channel_id=1, source_target_pairs={{1,0},{2,1},{3,2},{4,3},{5,4},{6,5},{7,6},{8,7},{9,8},{10,9},{11,1... | collective-permute-start | bytes 26120 | tf_op jit(solution)/shard_map/ppermute | solution.py:19
  35.7 5.7 %collective-permute-start.5 = (f32[2,4,1,1024]{3,2,1,0:T(1,128)S(1)}, f32[2,4,1,1024]{3,2,1,0:T(1,128)S(1)}, u32[]{:S(2)}, u32[]{:S(2)}) collective-permute-start(f32[2,4,1,1024]{3,2,1,0:T(1,128)S(1)} %get-tuple-element.31), channel_id=1, source_target_pairs={{0,16},{1,17},{2,18},{3,19},{4,20},{5,21},{6,22},{7,23},{8,24},{9,... | collective-permute-start | bytes 98312 | tf_op jit(solution)/shard_map/ppermute | solution.py:16
  39.8 5.8 %collective-permute-start.6 = (f32[2,4,1,1024]{3,2,1,0:T(1,128)S(1)}, f32[2,4,1,1024]{3,2,1,0:T(1,128)S(1)}, u32[]{:S(2)}, u32[]{:S(2)}) collective-permute-start(f32[2,4,1,1024]{3,2,1,0:T(1,128)S(1)} %get-tuple-element.32), channel_id=1, source_target_pairs={{16,0},{17,1},{18,2},{19,3},{20,4},{21,5},{22,6},{23,7},{24,8},{25... | collective-permute-start | bytes 98312 | tf_op jit(solution)/shard_map/ppermute | solution.py:19
  46.0 6.2 %collective-permute-start.7 = (bf16[4,34,1,32]{3,1,0,2:T(8,128)(2,1)S(1)}, bf16[4,34,1,32]{3,1,0,2:T(8,128)(2,1)S(1)}, u32[]{:S(2)}, u32[]{:S(2)}) collective-permute-start(bf16[4,34,1,32]{3,1,0,2:T(8,128)(2,1)S(1)} %get-tuple-element.25), channel_id=1, source_target_pairs={{0,1},{1,2},{2,3},{3,4},{4,5},{5,6},{6,7},{7,8},{8,9},{9,10},{10,1... | collective-permute-start | bytes 26120 | tf_op jit(solution)/shard_map/ppermute | solution.py:16
  46.0 6.1 %collective-permute-start.8 = (bf16[4,34,1,32]{3,1,0,2:T(8,128)(2,1)S(1)}, bf16[4,34,1,32]{3,1,0,2:T(8,128)(2,1)S(1)}, u32[]{:S(2)}, u32[]{:S(2)}) collective-permute-start(bf16[4,34,1,32]{3,1,0,2:T(8,128)(2,1)S(1)} %get-tuple-element.26), channel_id=1, source_target_pairs={{1,0},{2,1},{3,2},{4,3},{5,4},{6,5},{7,6},{8,7},{9,8},{10,9},{11,1... | collective-permute-start | bytes 26120 | tf_op jit(solution)/shard_map/ppermute | solution.py:19
  59.4 1.0 %copy-start.1 = (bf16[8,32,1024]{2,1,0:T(8,128)(2,1)S(1)}, bf16[8,32,1024]{2,1,0:T(8,128)(2,1)}, u32[]{:S(2)}) copy-start(bf16[8,32,1024]{2,1,0:T(8,128)(2,1)} %gather_fusion) | copy-start | bytes 1572868
  61.0 11.4 %collective-permute-start.9 = (f32[4,32,1024]{2,1,0:T(8,128)S(1)}, f32[4,32,1024]{2,1,0:T(8,128)S(1)}, u32[]{:S(2)}, u32[]{:S(2)}) collective-permute-start(f32[4,32,1024]{2,1,0:T(8,128)S(1)} %slice_bitcast_fusion), channel_id=1, source_target_pairs={{0,1},{1,2},{2,3},{3,4},{4,5},{5,6},{6,7},{7,8},{8,9},{9,10},{10,1... | collective-permute-start | bytes 1572872 | tf_op jit(solution)/shard_map/ppermute | solution.py:26
where the time goes:
time: 75 us; the launch traced here: 74.6 us
  starting transfers between devices  25.5 us (34%)
  waiting for transfers between devices  20.6 us (27%)
  other arithmetic  16.5 us (22%)
  local copies, waits for them, and re-layouts  9.23 us (12%)
  between operations  2.7 us (4%)
    ppermute x2, waiting for transfers between devices, shifted_2(): lax.ppermute(value, axis, [(i, (i + by) % devices) for i in range(devices)])  13.1 us
    ppermute x4, starting transfers between devices, extended_2(): lax.ppermute(lax.slice_in_dim(block, 0, width, axis=dim), axis, backward)  11.4 us
    ppermute x4, starting transfers between devices, extended_2(): lax.ppermute(lax.slice_in_dim(block, block.shape[dim] - width, None, axis...  9.08 us
    add x2, other arithmetic, stencil_step(): shifted[..., :width] * lower_mask + extended + shifted[..., 2:] * upper_mask  6.98 us
    ppermute x4, waiting for transfers between devices, extended_2(): lax.ppermute(lax.slice_in_dim(block, 0, width, axis=dim), axis, backward)  4.24 us
    all_to_all x1, starting transfers between devices, on_device(): lax.all_to_all(store_local, 'region', split_axis=0, concat_axis=0, tiled=...  3.92 us
    concatenate x2, local copies, waits for them, and re-layouts, stencil_step(): extended = jnp.concatenate([before_planes, padded, after_planes], axis=-1)  3.89 us
    ppermute x4, waiting for transfers between devices, extended_2(): lax.ppermute(lax.slice_in_dim(block, block.shape[dim] - width, None, axis...  3.33 us
  transfers between devices with their start and end apart: 11, of which 6 were waited for; matrix products, arithmetic and copies ran while one was open for 13% of the time, Pallas kernels for 0%

commit v1 on v0

--- a/solution.py
+++ b/solution.py
@@ -1,9 +1,19 @@
+import functools
+
 import jax
 import jax.numpy as jnp
 from jax import lax
+from jax.experimental import pallas as pl
+from jax.experimental.pallas import tpu as pltpu
 from jax.sharding import PartitionSpec as P
 
 STEPS = 2
+LANES = 128
+F32 = jnp.float32
+BF16 = jnp.bfloat16
+VMEM = pl.BlockSpec(memory_space=pltpu.VMEM)
+SMEM = pl.BlockSpec(memory_space=pltpu.SMEM)
+ANY = pl.BlockSpec(memory_space=pl.ANY)
 
 
 def extended_2(block, sides, width, periodic):
@@ -82,7 +92,7 @@
     return (placed, jnp.sum(valid_flags))
 
 
-def on_device(u_now, u_prev, coef_store, store_map, new_owner):
+def general_on_device(u_now, u_prev, coef_store, store_map, new_owner):
     state_now = u_now[:, 0]
     state_prev = u_prev[:, 0]
     blocks, fields, edge_cells, plane_cells = state_now.shape
@@ -114,7 +124,361 @@
     return result[:, None]
 
 
+def lane_ids():
+    return lax.broadcasted_iota(jnp.int32, (1, LANES), 1)
+
+
+def pack_body(edge, info, u_ref, p_ref, coef_ref, y_ref, left_ref, right_ref, dleft_ref, dright_ref, rows_ref):
+    fields = u_ref.shape[1]
+    depth = u_ref.shape[2]
+    last = u_ref.shape[3] - LANES
+    top = depth - 1
+    region = info[0]
+    lower = region == 0
+    other = 1 - region
+    own_edge = jnp.where(lower, top, 0)
+    own_next = jnp.where(lower, top - 1, 1)
+    lane = lane_ids()
+
+    def own_row(s, lanes):
+        piece = coef_ref[region, s, :, lanes].astype(F32)
+        return jnp.where(lower, piece[top:depth], piece[0:1])
+
+    def other_row(s, lanes):
+        piece = coef_ref[other, s, :, lanes].astype(F32)
+        return jnp.where(lower, piece[0:1], piece[top:depth])
+
+    everything = slice(None)
+    y_ref[0:4] = coef_ref[other]
+    for m in range(2):
+        for f in range(fields):
+            at = m * fields + f
+            near = u_ref[m, f, pl.ds(own_edge, 1), :]
+            rows_ref[at : at + 1, :] = near
+            rows_ref[8 + at : 9 + at, :] = u_ref[m, f, pl.ds(own_next, 1), :]
+            rows_ref[16 + at : 17 + at, :] = 2.0 * near - p_ref[m, f, pl.ds(own_edge, 1), :]
+    for s in range(4):
+        rows_ref[24 + s : 25 + s, :] = own_row(s, everything)
+    tags = []
+    for half in range(2):
+        for s in range(4):
+            at = jnp.where(region == half, s, 4 + s)
+            tags.append(info[8 + at].astype(F32))
+    held = [info[8 + region * 4 + s].astype(F32) for s in range(4)]
+    away = [info[8 + other * 4 + s].astype(F32) for s in range(4)]
+    tags = held + away
+    for i, tag in enumerate(tags):
+        rows_ref[28:29, i * LANES : (i + 1) * LANES] = jnp.full((1, LANES), 0.0, F32) + tag
+    rows_ref[29:32, :] = jnp.zeros((3, rows_ref.shape[1]), F32)
+    y_ref[4] = rows_ref[...].astype(BF16)
+
+    tag_rows = [jnp.full((1, LANES), 0.0, F32) + tag for tag in tags]
+    flag = jnp.full((1, LANES), 0.0, F32) + info[1].astype(F32)
+    zero_row = jnp.zeros((1, LANES), F32)
+    for m, lanes, straight_ref, diag_ref in (
+        (0, slice(0, LANES), left_ref, dleft_ref),
+        (1, slice(last, last + LANES), right_ref, dright_ref),
+    ):
+        for f in range(fields):
+            now = u_ref[m, f, :, lanes]
+            ahead = 2.0 * now - p_ref[m, f, :, lanes]
+            piece = coef_ref[region, f, :, lanes].astype(F32)
+            if m == 0:
+                tile = jnp.where(
+                    lane < 64, now, jnp.where(lane < 96, pltpu.roll(ahead, 64, 1), pltpu.roll(piece, 96, 1))
+                )
+            else:
+                tile = jnp.where(
+                    lane >= 64, now, jnp.where(lane < 32, pltpu.roll(ahead, 32, 1), pltpu.roll(piece, 64, 1))
+                )
+            straight_ref[f * depth : (f + 1) * depth, :] = tile.astype(BF16)
+        extra = [other_row(s, lanes) for s in range(4)] + tag_rows + [flag] + [zero_row] * 3
+        straight_ref[fields * depth : fields * depth + 16, :] = jnp.concatenate(extra, axis=0).astype(BF16)
+        plane = jnp.zeros((depth, LANES), F32)
+        for s in range(4):
+            piece = coef_ref[other, s, :, lanes].astype(F32)
+            shift = (32 * s if m == 0 else 32 + 32 * s) % LANES
+            moved = pltpu.roll(piece, shift, 1) if shift else piece
+            plane = jnp.where((lane >= 32 * s) & (lane < 32 * s + 32), moved, plane)
+        diag_ref[0:depth, :] = plane.astype(BF16)
+        extra = (
+            [rows_ref[m * fields : m * fields + 4, lanes]]
+            + [rows_ref[8 + m * fields : 12 + m * fields, lanes]]
+            + [rows_ref[16 + m * fields : 20 + m * fields, lanes]]
+            + [rows_ref[24:28, lanes]]
+            + tag_rows
+            + [zero_row] * 8
+        )
+        diag_ref[depth : depth + 32, :] = jnp.concatenate(extra, axis=0).astype(BF16)
+
+
+def nine_sum(tiles, lane, first=0):
+    inside = lane % 32
+    low = inside != 0
+    high = inside != 31
+    rows = []
+    for tile in tiles:
+        rows.append(
+            tile
+            + jnp.where(low, pltpu.roll(tile, 1, 1), 0.0)
+            + jnp.where(high, pltpu.roll(tile, LANES - 1, 1), 0.0)
+        )
+    up = [pltpu.roll(row, 32, 1) for row in rows]
+    down = [pltpu.roll(row, LANES - 32, 1) for row in rows]
+    count = len(tiles)
+    result = []
+    for t in range(count):
+        before = up[t] if t == 0 else jnp.where(lane < 32, up[t - 1], up[t])
+        after = down[t] if t == count - 1 else jnp.where(lane >= 96, down[t + 1], down[t])
+        result.append(rows[t] + before + after)
+    return result
+
+
+def step_body(m, info, u_ref, p_ref, coef_ref, y_ref, straight_ref, diag_ref, out_write, first_ref, edge_ref):
+    fields = u_ref.shape[1]
+    depth = u_ref.shape[2]
+    width = u_ref.shape[3]
+    main = width // LANES
+    last = width - LANES
+    top = depth - 1
+    region = info[0]
+    lower = region == 0
+    other = 1 - region
+    lane = lane_ids()
+    row_id = lax.broadcasted_iota(jnp.int32, (depth, 1), 0)
+    neighbour = 1 - m
+
+    def tile_at(t):
+        return slice(t * LANES, (t + 1) * LANES)
+
+    local_lanes = slice(last, width) if m == 1 else slice(0, LANES)
+    extra_s = straight_ref[fields * depth : fields * depth + 16, :].astype(F32)
+    extra_d = diag_ref[depth : depth + 32, :].astype(F32)
+    extra_y = y_ref[4].astype(F32)
+
+    def position(number):
+        place = jnp.int32(0)
+        for q in range(8):
+            place = jnp.where(info[8 + q] == number, q, place)
+        return place
+
+    def coef_tile(number, lanes):
+        place = position(number)
+        slot = place % 4
+        held = (place // 4) == region
+        mine = coef_ref[region, slot, :, lanes].astype(F32)
+        far = y_ref[slot, :, lanes].astype(F32)
+        return jnp.where(held, mine, far)
+
+    planes = []
+    for s in range(4):
+        tile = straight_ref[s * depth : (s + 1) * depth, :].astype(F32)
+        planes.append(pltpu.roll(tile, 32 if m == 1 else 64, 1))
+    diag_tile = diag_ref[0:depth, :].astype(F32)
+    for s in range(4):
+        shift = (-32 * s if m == 1 else 96 - 32 * s) % LANES
+        planes.append(pltpu.roll(diag_tile, shift, 1) if shift else diag_tile)
+    tags_s = [extra_s[4 + i : 5 + i] for i in range(8)]
+    tags_d = [extra_d[16 + i : 17 + i] for i in range(8)]
+    tags_y = [extra_y[28:29, i * LANES : (i + 1) * LANES] for i in range(8)]
+    halo_base = 0 if m == 1 else fields
+
+    def with_sides(local, remote, middle):
+        return [local] + middle + [remote] if m == 1 else [remote] + middle + [local]
+
+    def edge_tiles(base_y, base_d):
+        middle = [extra_y[base_y + m * fields : base_y + m * fields + 4, tile_at(t)] for t in range(main)]
+        local = extra_y[base_y + neighbour * fields : base_y + neighbour * fields + 4, local_lanes]
+        return with_sides(local, extra_d[base_d : base_d + 4], middle)
+
+    near = edge_tiles(0, 0)
+    beyond = edge_tiles(8, 4)
+    ahead = edge_tiles(16, 8)
+    field_id = lax.broadcasted_iota(jnp.int32, (4, LANES), 0).astype(F32)
+
+    def other_row(s, lanes):
+        piece = coef_ref[other, s, :, lanes].astype(F32)
+        return jnp.where(lower, piece[0:1], piece[top:depth])
+
+    def edge_coef(lanes, base):
+        total = jnp.zeros((4, LANES), F32)
+        for s in range(4):
+            total = total + jnp.where(tags_y[s] == field_id + base, extra_y[24 + s : 25 + s, lanes], 0.0)
+            total = total + jnp.where(tags_y[4 + s] == field_id + base, other_row(s, lanes), 0.0)
+        return total
+
+    corner = jnp.zeros((4, LANES), F32)
+    for s in range(4):
+        corner = corner + jnp.where(tags_d[s] == field_id + halo_base, extra_d[12 + s : 13 + s], 0.0)
+        corner = corner + jnp.where(tags_d[4 + s] == field_id + halo_base, extra_s[s : s + 1], 0.0)
+    edge_c = with_sides(
+        edge_coef(local_lanes, neighbour * fields),
+        corner,
+        [edge_coef(tile_at(t), m * fields) for t in range(main)],
+    )
+    near_sum = nine_sum(near, lane)
+    beyond_sum = nine_sum(beyond, lane)
+
+    def column_sum(tile, row):
+        above = jnp.where(row_id == 0, jnp.where(lower, 0.0, row), pltpu.roll(tile, 1, 0))
+        below = jnp.where(row_id == top, jnp.where(lower, row, 0.0), pltpu.roll(tile, depth - 1, 0))
+        return tile + above + below
+
+    def sides_of(f):
+        remote = straight_ref[f * depth : (f + 1) * depth, :].astype(F32)
+        local = u_ref[neighbour, f, :, local_lanes]
+        return local, remote
+
+    for f in range(fields):
+        local, remote = sides_of(f)
+        now = with_sides(local, remote, [u_ref[m, f, :, tile_at(t)] for t in range(main)])
+        sums = nine_sum(now, lane)
+        halo_c = jnp.zeros((depth, LANES), F32)
+        for i in range(8):
+            halo_c = halo_c + jnp.where(tags_s[i] == F32(halo_base + f), planes[i], 0.0)
+        coef = with_sides(
+            coef_tile(neighbour * fields + f, local_lanes),
+            halo_c,
+            [coef_tile(m * fields + f, tile_at(t)) for t in range(main)],
+        )
+        drift = with_sides(
+            2.0 * local - p_ref[neighbour, f, :, local_lanes],
+            pltpu.roll(remote, 64 if m == 1 else 96, 1),
+            [2.0 * now[t + 1] - p_ref[m, f, :, tile_at(t)] for t in range(main)],
+        )
+        for t in range(main + 2):
+            edge_ref[f : f + 1, tile_at(t)] = jnp.where(lower, sums[t][top:depth], sums[t][0:1])
+            box = column_sum(sums[t], near_sum[t][f : f + 1])
+            first_ref[f, :, tile_at(t)] = drift[t] + coef[t] * (box - 27.0 * now[t])
+    stepped = []
+    for t in range(main + 2):
+        box = near_sum[t] + beyond_sum[t] + edge_ref[0:4, tile_at(t)]
+        stepped.append(ahead[t] + edge_c[t] * (box - 27.0 * near[t]))
+    stepped_sum = nine_sum(stepped, lane)
+    for f in range(fields):
+        now = [first_ref[f, :, tile_at(t)] for t in range(main + 2)]
+        sums = nine_sum(now, lane)
+        for t in range(1, main + 1):
+            box = column_sum(sums[t], stepped_sum[t][f : f + 1])
+            lanes = tile_at(t - 1)
+            coef = coef_tile(m * fields + f, lanes)
+            value = 2.0 * now[t] - u_ref[m, f, :, lanes] + coef * (box - 27.0 * now[t])
+            out_write(f, lanes, value)
+
+
+def last_row_body(info, u_ref, p_ref, coef_ref, y_ref, straight_ref, diag_ref, row_ref, first_ref, edge_ref):
+    def write(f, lanes, value):
+        row_ref[f, :, lanes] = value
+
+    step_body(1, info, u_ref, p_ref, coef_ref, y_ref, straight_ref, diag_ref, write, first_ref, edge_ref)
+
+
+def first_row_body(
+    info, u_ref, p_ref, coef_ref, y_ref, straight_ref, diag_ref, last_ref, out_ref, first_ref, edge_ref
+):
+    fields = u_ref.shape[1]
+    depth = u_ref.shape[2]
+    arrives = straight_ref[fields * depth : fields * depth + 16, :].astype(F32)[12:13] > 0.5
+    keeps = info[1] == 0
+
+    def write(f, lanes, value):
+        kept = jnp.where(keeps, last_ref[f, :, lanes], 0.0)
+        out_ref[0, f, :, lanes] = value
+        out_ref[1, f, :, lanes] = jnp.where(arrives, value, kept)
+        out_ref[2, f, :, lanes] = jnp.where(arrives, kept, 0.0)
+
+    step_body(0, info, u_ref, p_ref, coef_ref, y_ref, straight_ref, diag_ref, write, first_ref, edge_ref)
+
+
+def place_body(straight_ref, row_ref, partial_ref, out_ref, sem):
+    rows = straight_ref.shape[0]
+    flag = jnp.max(straight_ref[rows - 16 : rows, :].astype(F32)[12:13])
+
+    @pl.when(flag > 0.5)
+    def _():
+        copy = pltpu.make_async_copy(row_ref, out_ref.at[0], sem)
+        copy.start()
+        copy.wait()
+
+
+def fast_on_device(u_now, u_prev, coef_store, store_map, new_owner):
+    blocks, _, fields, depth, width = u_now.shape
+    now = u_now.reshape(blocks, fields, depth, width)
+    prev = u_prev.reshape(blocks, fields, depth, width)
+    coef = coef_store[0, 0]
+    count = lax.axis_size("blk")
+    region = lax.axis_index("region").astype(jnp.int32)
+    owner = lax.axis_index("blk").astype(jnp.int32)
+    moves = (new_owner[blocks - 1] != owner).astype(jnp.int32)
+    info = jnp.concatenate([jnp.stack([region, moves]), jnp.zeros((6,), jnp.int32), store_map[0, 0]])
+    params = pltpu.CompilerParams(vmem_limit_bytes=48 * 1024 * 1024)
+
+    straight = jax.ShapeDtypeStruct((fields * depth + 16, LANES), BF16)
+    diag = jax.ShapeDtypeStruct((depth + 32, LANES), BF16)
+    y_out, left, right, dleft, dright = pl.pallas_call(
+        functools.partial(pack_body, None),
+        out_shape=(jax.ShapeDtypeStruct((5, depth, width), BF16), straight, straight, diag, diag),
+        in_specs=[SMEM, VMEM, VMEM, VMEM],
+        out_specs=(VMEM,) * 5,
+        scratch_shapes=[pltpu.VMEM((depth, width), F32)],
+        compiler_params=params,
+        name="pack",
+    )(info, now, prev, coef)
+
+    swap = [(0, 1), (1, 0)]
+    forward = [(i, (i + 1) % count) for i in range(count)]
+    backward = [(i, (i - 1) % count) for i in range(count)]
+
+    def crossed(by):
+        return [(r * count + i, (1 - r) * count + (i + by) % count) for r in range(2) for i in range(count)]
+
+    y_in = lax.ppermute(y_out, "region", swap)
+    from_right = lax.ppermute(left, "blk", backward)
+    from_dright = lax.ppermute(dleft, ("region", "blk"), crossed(-1))
+    from_left = lax.ppermute(right, "blk", forward)
+    from_dleft = lax.ppermute(dright, ("region", "blk"), crossed(1))
+
+    scratch = [pltpu.VMEM((fields, depth, width + 2 * LANES), F32), pltpu.VMEM((8, width + 2 * LANES), F32)]
+    row = jax.ShapeDtypeStruct((fields, depth, width), F32)
+    last_row = pl.pallas_call(
+        last_row_body,
+        out_shape=row,
+        in_specs=[SMEM] + [VMEM] * 6,
+        out_specs=VMEM,
+        scratch_shapes=scratch,
+        compiler_params=params,
+        name="last_row",
+    )(info, now, prev, coef, y_in, from_right, from_dright)
+    arrived = lax.ppermute(last_row, "blk", forward)
+    partial = pl.pallas_call(
+        first_row_body,
+        out_shape=jax.ShapeDtypeStruct((blocks + 1, fields, depth, width), F32),
+        in_specs=[SMEM] + [VMEM] * 7,
+        out_specs=VMEM,
+        scratch_shapes=scratch,
+        compiler_params=params,
+        name="first_row",
+    )(info, now, prev, coef, y_in, from_left, from_dleft, last_row)
+    result = pl.pallas_call(
+        place_body,
+        out_shape=jax.ShapeDtypeStruct((blocks + 1, fields, depth, width), F32),
+        in_specs=[VMEM, ANY, ANY],
+        out_specs=ANY,
+        scratch_shapes=[pltpu.SemaphoreType.DMA],
+        input_output_aliases={2: 0},
+        compiler_params=params,
+        name="place",
+    )(from_left, arrived, partial)
+    return result[:, None]
+
+
 def solution(mesh):
+    def on_device(*args):
+        blocks = args[0].shape[0]
+        if lax.axis_size("region") == 2 and blocks == 2:
+            return fast_on_device(*args)
+        return general_on_device(*args)
+
     return jax.shard_map(
         on_device,
         mesh=mesh,

time: 75 us -> 38.7 us (0.52)
  other arithmetic: 16.5 us -> 0.74 us
  starting transfers between devices: 25.5 us -> 10.7 us
  Pallas kernels: 0 us -> 8.12 us
  waiting for transfers between devices: 20.6 us -> 13.5 us
  local copies, waits for them, and re-layouts: 9.23 us -> 4.73 us
  between operations: 2.7 us -> 0.69 us
    ppermute x10 -> x6, starting transfers between devices: 21.6 us -> 10.7 us  [the longest x1 3.69 us: fast_on_device(): from_right = lax.ppermute(left, 'blk', backward)]
    add x6 -> x0, other arithmetic: 10.9 us -> none  [the longest x2 6.98 us: stencil_step(): shifted[..., :width] * lower_mask + extended + shifted[..., 2:] * upper_mask]
    pallas_call x0 -> x4, Pallas kernels: none -> 8.12 us  [the longest x1 3.87 us: fast_on_device(): pl.pallas_call(first_row_body, out_shape=jax.ShapeDtypeStruct((blocks + 1...]
    ppermute x10 -> x6, waiting for transfers between devices: 20.6 us -> 13.5 us  [the longest x1 10 us: fast_on_device(): from_dleft = lax.ppermute(dright, ('region', 'blk'), crossed(1))]
    all_to_all x1 -> x0, starting transfers between devices: 3.92 us -> none  [on_device(): lax.all_to_all(store_local, 'region', split_axis=0, concat_axis=0, tiled=...]
    concatenate x2 -> x0, local copies, waits for them, and re-layouts: 3.89 us -> none  [stencil_step(): extended = jnp.concatenate([before_planes, padded, after_planes], axis=-1)]
    unnamed x4 -> x6, local copies, waits for them, and re-layouts: 0.29 us -> 3.49 us
    select_n x4 -> x0, other arithmetic: 2.16 us -> none  [the longest x1 1.39 us: compact(): jnp.where(filled.reshape((slot_count,) + (1,) * (member.ndim - 1)), jnp.t...]
  transfers between devices with their start and end apart: 11 -> 6, of which waited for: 6 -> 3; matrix products, arithmetic and copies ran while one was open for 13% -> 0% of each run, Pallas kernels for 0% -> 10%
where the time goes in v1:
time: 38.7 us; the launch traced here: 38.5 us
  waiting for transfers between devices  13.5 us (35%)
  starting transfers between devices  10.7 us (28%)
  Pallas kernels  8.12 us (21%)
  local copies, waits for them, and re-layouts  4.73 us (12%)
  other arithmetic  0.74 us (2%)
  between operations  0.69 us (2%)
    ppermute x1, waiting for transfers between devices, fast_on_device(): from_dleft = lax.ppermute(dright, ('region', 'blk'), crossed(1))  10 us
    pallas_call x1, Pallas kernels, fast_on_device(): pl.pallas_call(first_row_body, out_shape=jax.ShapeDtypeStruct((blocks + 1...  3.87 us
    ppermute x1, starting transfers between devices, fast_on_device(): from_right = lax.ppermute(left, 'blk', backward)  3.69 us
    unnamed x6, local copies, waits for them, and re-layouts  3.49 us
    ppermute x1, starting transfers between devices, fast_on_device(): y_in = lax.ppermute(y_out, 'region', swap)  3.03 us
    ppermute x1, waiting for transfers between devices, fast_on_device(): from_dright = lax.ppermute(dleft, ('region', 'blk'), crossed(-1))  2.82 us
    pallas_call x1, Pallas kernels, fast_on_device(): pl.pallas_call(last_row_body, out_shape=row, in_specs=[SMEM] + [VMEM] * 6...  2.64 us
    ppermute x1, starting transfers between devices, fast_on_device(): from_left = lax.ppermute(right, 'blk', forward)  1.81 us
  transfers between devices with their start and end apart: 6, of which 3 were waited for; matrix products, arithmetic and copies ran while one was open for 0% of the time, Pallas kernels for 10%

profile of v1, /device:TPU:0, one launch (start us, length us, event | category | flops | bytes accessed | tf_op | source)
XLA Modules:
  0.0 38.5 jit_solution(5372322162045428324)
XLA Ops:
  0.0 1.2 %slice.3 = s32[1]{0:T(128)} slice(s32[2]{0:T(128)} %param.9), slice={[1:2]} | slice | bytes 8 | tf_op jit(solution)/shard_map/slice | solution.py:412
  1.9 0.7 %pad_add_fusion.info = s32[16]{0:T(128)S(1)} fusion(s32[8]{0:T(128)} %bitcast.19, s32[6]{0:T(128)S(1)} %broadcast.3, s32[1]{0:T(128)} %bitcast.2, s32[1]{0:T(128)} %bitcast), kind=kLoop, calls=%fused_computation | loop fusion | flops 48 | bytes 128 | tf_op jit(solution)/shard_map/concatenate | solution.py:413
  2.6 0.0 copy-start
  2.6 1.2 %copy-done = f32[2,1,4,32,1024]{4,3,2,1,0:T(8,128)S(1)} copy-done((f32[2,1,4,32,1024]{4,3,2,1,0:T(8,128)S(1)}, f32[2,1,4,32,1024]{4,3,2,1,0:T(8,128)}, u32[]{:S(2)}) %copy-start) | copy-done | bytes 1048600
  3.9 0.0 copy-start.1
  3.9 1.2 %copy-done.1 = f32[2,1,4,32,1024]{4,3,2,1,0:T(8,128)S(1)} copy-done((f32[2,1,4,32,1024]{4,3,2,1,0:T(8,128)S(1)}, f32[2,1,4,32,1024]{4,3,2,1,0:T(8,128)}, u32[]{:S(2)}) %copy-start.1) | copy-done | bytes 1048600
  5.1 0.0 copy-start.2
  5.1 1.0 %copy-done.2 = bf16[1,1,2,4,32,1024]{5,4,3,2,1,0:T(8,128)(2,1)S(1)} copy-done((bf16[1,1,2,4,32,1024]{5,4,3,2,1,0:T(8,128)(2,1)S(1)}, bf16[1,1,2,4,32,1024]{5,4,3,2,1,0:T(8,128)(2,1)}, u32[]{:S(2)}) %copy-start.2) | copy-done | bytes 524312
  6.1 0.7 %pack.1 = (bf16[5,32,1024]{2,1,0:T(8,128)(2,1)S(1)}, bf16[144,128]{1,0:T(8,128)(2,1)S(1)}, bf16[144,128]{1,0:T(8,128)(2,1)S(1)}, bf16[64,128]{1,0:T(8,128)(2,1)S(1)}, bf16[64,128]{1,0:T(8,128)(2,1)S(1)}) custom-call(s32[16]{0:T(128)S(1)} %pad_add_fusion.info, f32[2,4,32,1024]{3,2,1,0:T(8,128)S(1)} %bitcast.10, f32[2,4,32,1024]{3,2,1,0:T(8,128)S(1)} %bitcast.13, ...), custom_call_target="tpu_custom_call" | custom-call | tf_op jit(solution)/shard_map/pack/pallas_call | solution.py:418
  6.8 3.0 %collective-permute-start.1 = (bf16[5,32,1024]{2,1,0:T(8,128)(2,1)S(1)}, bf16[5,32,1024]{2,1,0:T(8,128)(2,1)S(1)}, u32[]{:S(2)}, u32[]{:S(2)}) collective-permute-start(bf16[5,32,1024]{2,1,0:T(8,128)(2,1)S(1)} %get-tuple-element.11), channel_id=1, source_target_pairs={{0,16},{16,0},{1,17},{17,1},{2,18},{18,2},{3,19},{19,3},{4,20},{20... | collective-permute-start | bytes 983048 | tf_op jit(solution)/shard_map/ppermute | solution.py:435
  9.9 3.7 %collective-permute-start.2 = (bf16[144,128]{1,0:T(8,128)(2,1)S(1)}, bf16[144,128]{1,0:T(8,128)(2,1)S(1)}, u32[]{:S(2)}, u32[]{:S(2)}) collective-permute-start(bf16[144,128]{1,0:T(8,128)(2,1)S(1)} %get-tuple-element.12), channel_id=1, source_target_pairs={{0,15},{1,0},{2,1},{3,2},{4,3},{5,4},{6,5},{7,6},{8,7},{9,8},{10,9... | collective-permute-start | bytes 110600 | tf_op jit(solution)/shard_map/ppermute | solution.py:436
  13.6 0.9 %collective-permute-start.3 = (bf16[64,128]{1,0:T(8,128)(2,1)S(1)}, bf16[64,128]{1,0:T(8,128)(2,1)S(1)}, u32[]{:S(2)}, u32[]{:S(2)}) collective-permute-start(bf16[64,128]{1,0:T(8,128)(2,1)S(1)} %get-tuple-element.13), channel_id=1, source_target_pairs={{0,31},{1,16},{2,17},{3,18},{4,19},{5,20},{6,21},{7,22},{8,23},{9,... | collective-permute-start | bytes 49160 | tf_op jit(solution)/shard_map/ppermute | solution.py:437
  14.5 2.8 %collective-permute-done.3.diag_ref = bf16[64,128]{1,0:T(8,128)(2,1)S(1)} collective-permute-done((bf16[64,128]{1,0:T(8,128)(2,1)S(1)}, bf16[64,128]{1,0:T(8,128)(2,1)S(1)}, u32[]{:S(2)}, u32[]{:S(2)}) %collective-permute-start.3) | collective-permute-done | bytes 16416 | tf_op jit(solution)/shard_map/ppermute | solution.py:437
  17.3 0.0 collective-permute-done.2.straight_ref
  17.3 0.7 %collective-permute-done.1.y_ref = bf16[5,32,1024]{2,1,0:T(8,128)(2,1)S(1)} collective-permute-done((bf16[5,32,1024]{2,1,0:T(8,128)(2,1)S(1)}, bf16[5,32,1024]{2,1,0:T(8,128)(2,1)S(1)}, u32[]{:S(2)}, u32[]{:S(2)}) %collective-permute-start.1) | collective-permute-done | bytes 327712 | tf_op jit(solution)/shard_map/ppermute | solution.py:435
  17.9 2.6 %last_row.1.last_ref = f32[4,32,1024]{2,1,0:T(8,128)S(1)} custom-call(s32[16]{0:T(128)S(1)} %pad_add_fusion.info, f32[2,4,32,1024]{3,2,1,0:T(8,128)S(1)} %bitcast.11, f32[2,4,32,1024]{3,2,1,0:T(8,128)S(1)} %bitcast.14, bf16[2,4,32,1024]{3,2,1,0:T(8,128)(2,1)S(1)} %bitcast.17, bf16[5,32,1024]{2,1,0:T(8,128)(2,1)S(1)} %collective-permute-done.1.y_ref, ...), custom_call_target="tpu_custom_call" | custom-call | tf_op jit(solution)/shard_map/last_row/pallas_call | solution.py:443
  20.6 0.1 collective-permute-start.4
  20.6 1.8 %collective-permute-start = (bf16[144,128]{1,0:T(8,128)(2,1)S(1)}, bf16[144,128]{1,0:T(8,128)(2,1)S(1)}, u32[]{:S(2)}, u32[]{:S(2)}) collective-permute-start(bf16[144,128]{1,0:T(8,128)(2,1)S(1)} %get-tuple-element.10), channel_id=1, source_target_pairs={{0,1},{1,2},{2,3},{3,4},{4,5},{5,6},{6,7},{7,8},{8,9},{9,10},{10,1... | collective-permute-start | bytes 110600 | tf_op jit(solution)/shard_map/ppermute | solution.py:438
  22.5 1.2 %collective-permute-start.5 = (bf16[64,128]{1,0:T(8,128)(2,1)S(1)}, bf16[64,128]{1,0:T(8,128)(2,1)S(1)}, u32[]{:S(2)}, u32[]{:S(2)}) collective-permute-start(bf16[64,128]{1,0:T(8,128)(2,1)S(1)} %get-tuple-element.14), channel_id=1, source_target_pairs={{0,17},{1,18},{2,19},{3,20},{4,21},{5,22},{6,23},{7,24},{8,25},{9,... | collective-permute-start | bytes 49160 | tf_op jit(solution)/shard_map/ppermute | solution.py:439
  23.6 10.0 %collective-permute-done.5.diag_ref = bf16[64,128]{1,0:T(8,128)(2,1)S(1)} collective-permute-done((bf16[64,128]{1,0:T(8,128)(2,1)S(1)}, bf16[64,128]{1,0:T(8,128)(2,1)S(1)}, u32[]{:S(2)}, u32[]{:S(2)}) %collective-permute-start.5) | collective-permute-done | bytes 16416 | tf_op jit(solution)/shard_map/ppermute | solution.py:439
  33.7 0.0 collective-permute-done.straight_ref
  33.7 3.9 %first_row.1.partial_ref = f32[3,4,32,1024]{3,2,1,0:T(8,128)} custom-call(s32[16]{0:T(128)S(1)} %pad_add_fusion.info, f32[2,4,32,1024]{3,2,1,0:T(8,128)S(1)} %bitcast.12, f32[2,4,32,1024]{3,2,1,0:T(8,128)S(1)} %bitcast.15, bf16[2,4,32,1024]{3,2,1,0:T(8,128)(2,1)S(1)} %bitcast.18, bf16[5,32,1024]{2,1,0:T(8,128)(2,1)S(1)} %collective-permute-done.1.y_ref, ...), custom_call_target="tpu_custom_call" | custom-call | tf_op jit(solution)/shard_map/first_row/pallas_call | solution.py:453
  37.5 0.0 collective-permute-done.4.row_ref
  37.5 0.9 %place.1 = f32[3,4,32,1024]{3,2,1,0:T(8,128)} custom-call(bf16[144,128]{1,0:T(8,128)(2,1)S(1)} %collective-permute-done.straight_ref, f32[4,32,1024]{2,1,0:T(8,128)S(1)} %collective-permute-done.4.row_ref, f32[3,4,32,1024]{3,2,1,0:T(8,128)} %first_row.1.partial_ref), custom_call_target="tpu_custom_call", output_to_operand_aliasing={{}: (2, {})} | custom-call | tf_op jit(solution)/shard_map/place/pallas_call | solution.py:462
  (1 shorter events, 0.0 us)
Async XLA Ops:
  2.6 1.2 %copy-start = (f32[2,1,4,32,1024]{4,3,2,1,0:T(8,128)S(1)}, f32[2,1,4,32,1024]{4,3,2,1,0:T(8,128)}, u32[]{:S(2)}) copy-start(f32[2,1,4,32,1024]{4,3,2,1,0:T(8,128)} %param.5) | copy-start | bytes 3145732
  3.9 1.2 %copy-start.1 = (f32[2,1,4,32,1024]{4,3,2,1,0:T(8,128)S(1)}, f32[2,1,4,32,1024]{4,3,2,1,0:T(8,128)}, u32[]{:S(2)}) copy-start(f32[2,1,4,32,1024]{4,3,2,1,0:T(8,128)} %param.6) | copy-start | bytes 3145732
  5.1 1.0 %copy-start.2 = (bf16[1,1,2,4,32,1024]{5,4,3,2,1,0:T(8,128)(2,1)S(1)}, bf16[1,1,2,4,32,1024]{5,4,3,2,1,0:T(8,128)(2,1)}, u32[]{:S(2)}) copy-start(bf16[1,1,2,4,32,1024]{5,4,3,2,1,0:T(8,128)(2,1)} %param.7) | copy-start | bytes 1572868
  6.8 11.1 %collective-permute-start.1 = (bf16[5,32,1024]{2,1,0:T(8,128)(2,1)S(1)}, bf16[5,32,1024]{2,1,0:T(8,128)(2,1)S(1)}, u32[]{:S(2)}, u32[]{:S(2)}) collective-permute-start(bf16[5,32,1024]{2,1,0:T(8,128)(2,1)S(1)} %get-tuple-element.11), channel_id=1, source_target_pairs={{0,16},{16,0},{1,17},{17,1},{2,18},{18,2},{3,19},{19,3},{4,20},{20... | collective-permute-start | bytes 983048 | tf_op jit(solution)/shard_map/ppermute | solution.py:435
  9.9 7.4 %collective-permute-start.2 = (bf16[144,128]{1,0:T(8,128)(2,1)S(1)}, bf16[144,128]{1,0:T(8,128)(2,1)S(1)}, u32[]{:S(2)}, u32[]{:S(2)}) collective-permute-start(bf16[144,128]{1,0:T(8,128)(2,1)S(1)} %get-tuple-element.12), channel_id=1, source_target_pairs={{0,15},{1,0},{2,1},{3,2},{4,3},{5,4},{6,5},{7,6},{8,7},{9,8},{10,9... | collective-permute-start | bytes 110600 | tf_op jit(solution)/shard_map/ppermute | solution.py:436
  13.6 3.7 %collective-permute-start.3 = (bf16[64,128]{1,0:T(8,128)(2,1)S(1)}, bf16[64,128]{1,0:T(8,128)(2,1)S(1)}, u32[]{:S(2)}, u32[]{:S(2)}) collective-permute-start(bf16[64,128]{1,0:T(8,128)(2,1)S(1)} %get-tuple-element.13), channel_id=1, source_target_pairs={{0,31},{1,16},{2,17},{3,18},{4,19},{5,20},{6,21},{7,22},{8,23},{9,... | collective-permute-start | bytes 49160 | tf_op jit(solution)/shard_map/ppermute | solution.py:437
  20.6 17.0 %collective-permute-start.4 = (f32[4,32,1024]{2,1,0:T(8,128)S(1)}, f32[4,32,1024]{2,1,0:T(8,128)S(1)}, u32[]{:S(2)}, u32[]{:S(2)}) collective-permute-start(f32[4,32,1024]{2,1,0:T(8,128)S(1)} %last_row.1.last_ref), channel_id=1, source_target_pairs={{0,1},{1,2},{2,3},{3,4},{4,5},{5,6},{6,7},{7,8},{8,9},{9,10},{10,1... | collective-permute-start | bytes 1572872 | tf_op jit(solution)/shard_map/ppermute | solution.py:452
  20.6 13.0 %collective-permute-start = (bf16[144,128]{1,0:T(8,128)(2,1)S(1)}, bf16[144,128]{1,0:T(8,128)(2,1)S(1)}, u32[]{:S(2)}, u32[]{:S(2)}) collective-permute-start(bf16[144,128]{1,0:T(8,128)(2,1)S(1)} %get-tuple-element.10), channel_id=1, source_target_pairs={{0,1},{1,2},{2,3},{3,4},{4,5},{5,6},{6,7},{7,8},{8,9},{9,10},{10,1... | collective-permute-start | bytes 110600 | tf_op jit(solution)/shard_map/ppermute | solution.py:438
  22.5 11.2 %collective-permute-start.5 = (bf16[64,128]{1,0:T(8,128)(2,1)S(1)}, bf16[64,128]{1,0:T(8,128)(2,1)S(1)}, u32[]{:S(2)}, u32[]{:S(2)}) collective-permute-start(bf16[64,128]{1,0:T(8,128)(2,1)S(1)} %get-tuple-element.14), channel_id=1, source_target_pairs={{0,17},{1,18},{2,19},{3,20},{4,21},{5,22},{6,23},{7,24},{8,25},{9,... | collective-permute-start | bytes 49160 | tf_op jit(solution)/shard_map/ppermute | solution.py:439

commit v2 on v1

--- a/solution.py
+++ b/solution.py
@@ -1,5 +1,3 @@
-import functools
-
 import jax
 import jax.numpy as jnp
 from jax import lax
@@ -14,6 +12,7 @@
 VMEM = pl.BlockSpec(memory_space=pltpu.VMEM)
 SMEM = pl.BlockSpec(memory_space=pltpu.SMEM)
 ANY = pl.BlockSpec(memory_space=pl.ANY)
+HBM = pl.BlockSpec(memory_space=pltpu.HBM)
 
 
 def extended_2(block, sides, width, periodic):
@@ -128,61 +127,73 @@
     return lax.broadcasted_iota(jnp.int32, (1, LANES), 1)
 
 
-def pack_body(edge, info, u_ref, p_ref, coef_ref, y_ref, left_ref, right_ref, dleft_ref, dright_ref, rows_ref):
+def pack_body(
+    owner_hbm, map_hbm, u_ref, p_ref, coef_ref, y_ref, left_ref, right_ref, dleft_ref, dright_ref,
+    rows_ref, ue_ref, pe_ref, ce_ref, ua_ref, pa_ref, ca_ref, owner_ref, map_ref, sems
+):
     fields = u_ref.shape[1]
     depth = u_ref.shape[2]
     last = u_ref.shape[3] - LANES
     top = depth - 1
-    region = info[0]
+    region = lax.axis_index("region")
     lower = region == 0
     other = 1 - region
-    own_edge = jnp.where(lower, top, 0)
-    own_next = jnp.where(lower, top - 1, 1)
+    edge8 = pl.multiple_of(jnp.where(lower, depth - 8, 0), 8)
+    edge16 = pl.multiple_of(jnp.where(lower, depth - 16, 0), 16)
+    scalars = [
+        pltpu.make_async_copy(owner_hbm, owner_ref, sems.at[10]),
+        pltpu.make_async_copy(map_hbm, map_ref, sems.at[11]),
+    ]
+    copies = [
+        pltpu.make_async_copy(u_ref.at[:, :, pl.ds(edge8, 8), :], ue_ref, sems.at[0]),
+        pltpu.make_async_copy(p_ref.at[:, :, pl.ds(edge8, 8), :], pe_ref, sems.at[1]),
+        pltpu.make_async_copy(coef_ref.at[region, :, pl.ds(edge16, 16), :], ce_ref, sems.at[2]),
+        pltpu.make_async_copy(u_ref.at[0, :, :, 0:LANES], ua_ref.at[0], sems.at[3]),
+        pltpu.make_async_copy(u_ref.at[1, :, :, last : last + LANES], ua_ref.at[1], sems.at[4]),
+        pltpu.make_async_copy(p_ref.at[0, :, :, 0:LANES], pa_ref.at[0], sems.at[5]),
+        pltpu.make_async_copy(p_ref.at[1, :, :, last : last + LANES], pa_ref.at[1], sems.at[6]),
+        pltpu.make_async_copy(coef_ref.at[:, :, :, 0:LANES], ca_ref.at[0], sems.at[7]),
+        pltpu.make_async_copy(coef_ref.at[:, :, :, last : last + LANES], ca_ref.at[1], sems.at[8]),
+        pltpu.make_async_copy(coef_ref.at[other], y_ref.at[0:4], sems.at[9]),
+    ]
+    for copy in copies[9:] + scalars + copies[:9]:
+        copy.start()
     lane = lane_ids()
-
-    def own_row(s, lanes):
-        piece = coef_ref[region, s, :, lanes].astype(F32)
-        return jnp.where(lower, piece[top:depth], piece[0:1])
-
-    def other_row(s, lanes):
-        piece = coef_ref[other, s, :, lanes].astype(F32)
-        return jnp.where(lower, piece[0:1], piece[top:depth])
-
-    everything = slice(None)
-    y_ref[0:4] = coef_ref[other]
+    for copy in scalars:
+        copy.wait()
+    moves = jnp.where(owner_ref[1] != lax.axis_index("blk"), 1.0, 0.0).astype(F32)
+    numbers = [map_ref[region * 4 + s] for s in range(4)] + [map_ref[other * 4 + s] for s in range(4)]
+    blank = jnp.zeros((1, LANES), F32)
+    tag_rows = [blank + number.astype(F32) for number in numbers]
+    flag = blank + moves
+    for copy in copies[:3]:
+        copy.wait()
+    own_edge = jnp.where(lower, 7, 0)
+    own_next = jnp.where(lower, 6, 1)
     for m in range(2):
         for f in range(fields):
             at = m * fields + f
-            near = u_ref[m, f, pl.ds(own_edge, 1), :]
+            near = ue_ref[m, f, pl.ds(own_edge, 1), :]
             rows_ref[at : at + 1, :] = near
-            rows_ref[8 + at : 9 + at, :] = u_ref[m, f, pl.ds(own_next, 1), :]
-            rows_ref[16 + at : 17 + at, :] = 2.0 * near - p_ref[m, f, pl.ds(own_edge, 1), :]
+            rows_ref[8 + at : 9 + at, :] = ue_ref[m, f, pl.ds(own_next, 1), :]
+            rows_ref[16 + at : 17 + at, :] = 2.0 * near - pe_ref[m, f, pl.ds(own_edge, 1), :]
     for s in range(4):
-        rows_ref[24 + s : 25 + s, :] = own_row(s, everything)
-    tags = []
-    for half in range(2):
-        for s in range(4):
-            at = jnp.where(region == half, s, 4 + s)
-            tags.append(info[8 + at].astype(F32))
-    held = [info[8 + region * 4 + s].astype(F32) for s in range(4)]
-    away = [info[8 + other * 4 + s].astype(F32) for s in range(4)]
-    tags = held + away
-    for i, tag in enumerate(tags):
-        rows_ref[28:29, i * LANES : (i + 1) * LANES] = jnp.full((1, LANES), 0.0, F32) + tag
+        piece = ce_ref[s].astype(F32)
+        rows_ref[24 + s : 25 + s, :] = jnp.where(lower, piece[15:16], piece[0:1])
+    for i, row in enumerate(tag_rows):
+        rows_ref[28:29, i * LANES : (i + 1) * LANES] = row
     rows_ref[29:32, :] = jnp.zeros((3, rows_ref.shape[1]), F32)
     y_ref[4] = rows_ref[...].astype(BF16)
-
-    tag_rows = [jnp.full((1, LANES), 0.0, F32) + tag for tag in tags]
-    flag = jnp.full((1, LANES), 0.0, F32) + info[1].astype(F32)
-    zero_row = jnp.zeros((1, LANES), F32)
+    for copy in copies[3:9]:
+        copy.wait()
     for m, lanes, straight_ref, diag_ref in (
         (0, slice(0, LANES), left_ref, dleft_ref),
         (1, slice(last, last + LANES), right_ref, dright_ref),
     ):
         for f in range(fields):
-            now = u_ref[m, f, :, lanes]
-            ahead = 2.0 * now - p_ref[m, f, :, lanes]
-            piece = coef_ref[region, f, :, lanes].astype(F32)
+            now = ua_ref[m, f]
+            ahead = 2.0 * now - pa_ref[m, f]
+            piece = ca_ref[m, region, f].astype(F32)
             if m == 0:
                 tile = jnp.where(
                     lane < 64, now, jnp.where(lane < 96, pltpu.roll(ahead, 64, 1), pltpu.roll(piece, 96, 1))
@@ -192,13 +203,13 @@
                     lane >= 64, now, jnp.where(lane < 32, pltpu.roll(ahead, 32, 1), pltpu.roll(piece, 64, 1))
                 )
             straight_ref[f * depth : (f + 1) * depth, :] = tile.astype(BF16)
-        extra = [other_row(s, lanes) for s in range(4)] + tag_rows + [flag] + [zero_row] * 3
+        far = [ca_ref[m, other, s].astype(F32) for s in range(4)]
+        extra = [jnp.where(lower, piece[0:1], piece[top:depth]) for piece in far] + tag_rows + [flag] + [blank] * 3
         straight_ref[fields * depth : fields * depth + 16, :] = jnp.concatenate(extra, axis=0).astype(BF16)
         plane = jnp.zeros((depth, LANES), F32)
         for s in range(4):
-            piece = coef_ref[other, s, :, lanes].astype(F32)
             shift = (32 * s if m == 0 else 32 + 32 * s) % LANES
-            moved = pltpu.roll(piece, shift, 1) if shift else piece
+            moved = pltpu.roll(far[s], shift, 1) if shift else far[s]
             plane = jnp.where((lane >= 32 * s) & (lane < 32 * s + 32), moved, plane)
         diag_ref[0:depth, :] = plane.astype(BF16)
         extra = (
@@ -207,9 +218,10 @@
             + [rows_ref[16 + m * fields : 20 + m * fields, lanes]]
             + [rows_ref[24:28, lanes]]
             + tag_rows
-            + [zero_row] * 8
+            + [blank] * 8
         )
         diag_ref[depth : depth + 32, :] = jnp.concatenate(extra, axis=0).astype(BF16)
+    copies[9].wait()
 
 
 def nine_sum(tiles, lane, first=0):
@@ -234,14 +246,14 @@
     return result
 
 
-def step_body(m, info, u_ref, p_ref, coef_ref, y_ref, straight_ref, diag_ref, out_write, first_ref, edge_ref):
+def step_body(m, map_ref, u_ref, p_ref, coef_ref, y_ref, straight_ref, diag_ref, out_write, first_ref, edge_ref):
     fields = u_ref.shape[1]
     depth = u_ref.shape[2]
     width = u_ref.shape[3]
     main = width // LANES
     last = width - LANES
     top = depth - 1
-    region = info[0]
+    region = lax.axis_index("region")
     lower = region == 0
     other = 1 - region
     lane = lane_ids()
@@ -256,19 +268,17 @@
     extra_d = diag_ref[depth : depth + 32, :].astype(F32)
     extra_y = y_ref[4].astype(F32)
 
-    def position(number):
+    numbers = [map_ref[q] for q in range(8)]
+    places = []
+    for number in range(8):
         place = jnp.int32(0)
         for q in range(8):
-            place = jnp.where(info[8 + q] == number, q, place)
-        return place
+            place = jnp.where(numbers[q] == number, q, place)
+        places.append((place & 3, (place >> 2) == region))
 
     def coef_tile(number, lanes):
-        place = position(number)
-        slot = place % 4
-        held = (place // 4) == region
-        mine = coef_ref[region, slot, :, lanes].astype(F32)
-        far = y_ref[slot, :, lanes].astype(F32)
-        return jnp.where(held, mine, far)
+        slot, held = places[number]
+        return jnp.where(held, coef_ref[region, slot, :, lanes], y_ref[slot, :, lanes]).astype(F32)
 
     planes = []
     for s in range(4):
@@ -366,20 +376,37 @@
             out_write(f, lanes, value)
 
 
-def last_row_body(info, u_ref, p_ref, coef_ref, y_ref, straight_ref, diag_ref, row_ref, first_ref, edge_ref):
+CODES = 32000.0
+
+
+def last_row_body(
+    map_ref, u_ref, p_ref, coef_ref, y_ref, straight_ref, diag_ref, early_a, early_b, row_ref, code_ref,
+    first_ref, edge_ref
+):
+    depth = u_ref.shape[2]
+    fields = u_ref.shape[1]
+
     def write(f, lanes, value):
         row_ref[f, :, lanes] = value
-
-    step_body(1, info, u_ref, p_ref, coef_ref, y_ref, straight_ref, diag_ref, write, first_ref, edge_ref)
+        size = jnp.maximum(jnp.max(jnp.abs(value), axis=0, keepdims=True), 1e-30)
+        power = jnp.ceil(jnp.log2(size))
+        code = jnp.floor(value * (CODES * jnp.exp2(-power)) + 0.5)
+        code_ref[f * depth : (f + 1) * depth, lanes] = code.astype(jnp.int32).astype(jnp.int16)
+        edge_ref[f : f + 1, lanes] = power
+
+    step_body(1, map_ref, u_ref, p_ref, coef_ref, y_ref, straight_ref, diag_ref, write, first_ref, edge_ref)
+    edge_ref[4:8, :] = jnp.zeros((4, edge_ref.shape[1]), F32)
+    powers = edge_ref[:, 0 : row_ref.shape[2]]
+    code_ref[fields * depth : fields * depth + 8, :] = powers.astype(jnp.int32).astype(jnp.int16)
 
 
 def first_row_body(
-    info, u_ref, p_ref, coef_ref, y_ref, straight_ref, diag_ref, last_ref, out_ref, first_ref, edge_ref
+    owner_ref, map_ref, u_ref, p_ref, coef_ref, y_ref, straight_ref, diag_ref, last_ref, out_ref, first_ref, edge_ref
 ):
     fields = u_ref.shape[1]
     depth = u_ref.shape[2]
     arrives = straight_ref[fields * depth : fields * depth + 16, :].astype(F32)[12:13] > 0.5
-    keeps = info[1] == 0
+    keeps = owner_ref[1] == lax.axis_index("blk")
 
     def write(f, lanes, value):
         kept = jnp.where(keeps, last_ref[f, :, lanes], 0.0)
@@ -387,18 +414,25 @@
         out_ref[1, f, :, lanes] = jnp.where(arrives, value, kept)
         out_ref[2, f, :, lanes] = jnp.where(arrives, kept, 0.0)
 
-    step_body(0, info, u_ref, p_ref, coef_ref, y_ref, straight_ref, diag_ref, write, first_ref, edge_ref)
-
-
-def place_body(straight_ref, row_ref, partial_ref, out_ref, sem):
-    rows = straight_ref.shape[0]
-    flag = jnp.max(straight_ref[rows - 16 : rows, :].astype(F32)[12:13])
+    step_body(0, map_ref, u_ref, p_ref, coef_ref, y_ref, straight_ref, diag_ref, write, first_ref, edge_ref)
+
+
+def place_body(straight_ref, code_ref, partial_ref, out_ref, row_ref, sems):
+    fields, depth, width = row_ref.shape
+    flag = jnp.max(straight_ref[fields * depth : fields * depth + 16, :].astype(F32)[12:13])
 
     @pl.when(flag > 0.5)
     def _():
-        copy = pltpu.make_async_copy(row_ref, out_ref.at[0], sem)
-        copy.start()
-        copy.wait()
+        scale = jnp.exp2(code_ref[fields * depth : fields * depth + 8, :].astype(jnp.int32).astype(F32)) * (1.0 / CODES)
+        copies = []
+        for f in range(fields):
+            code = code_ref[f * depth : (f + 1) * depth, :].astype(jnp.int32).astype(F32)
+            row_ref[f] = code * scale[f : f + 1]
+            copy = pltpu.make_async_copy(row_ref.at[f], out_ref.at[0, f], sems.at[f])
+            copy.start()
+            copies.append(copy)
+        for copy in copies:
+            copy.wait()
 
 
 def fast_on_device(u_now, u_prev, coef_store, store_map, new_owner):
@@ -407,23 +441,34 @@
     prev = u_prev.reshape(blocks, fields, depth, width)
     coef = coef_store[0, 0]
     count = lax.axis_size("blk")
-    region = lax.axis_index("region").astype(jnp.int32)
-    owner = lax.axis_index("blk").astype(jnp.int32)
-    moves = (new_owner[blocks - 1] != owner).astype(jnp.int32)
-    info = jnp.concatenate([jnp.stack([region, moves]), jnp.zeros((6,), jnp.int32), store_map[0, 0]])
+    order = store_map.reshape(-1)
+    owner_hbm, order_hbm, now_hbm, prev_hbm, coef_hbm = (
+        pltpu.with_memory_space_constraint(array, pltpu.HBM) for array in (new_owner, order, now, prev, coef)
+    )
     params = pltpu.CompilerParams(vmem_limit_bytes=48 * 1024 * 1024)
 
     straight = jax.ShapeDtypeStruct((fields * depth + 16, LANES), BF16)
     diag = jax.ShapeDtypeStruct((depth + 32, LANES), BF16)
     y_out, left, right, dleft, dright = pl.pallas_call(
-        functools.partial(pack_body, None),
+        pack_body,
         out_shape=(jax.ShapeDtypeStruct((5, depth, width), BF16), straight, straight, diag, diag),
-        in_specs=[SMEM, VMEM, VMEM, VMEM],
+        in_specs=[HBM] * 5,
         out_specs=(VMEM,) * 5,
-        scratch_shapes=[pltpu.VMEM((depth, width), F32)],
+        scratch_shapes=[
+            pltpu.VMEM((depth, width), F32),
+            pltpu.VMEM((blocks, fields, 8, width), F32),
+            pltpu.VMEM((blocks, fields, 8, width), F32),
+            pltpu.VMEM((4, 16, width), BF16),
+            pltpu.VMEM((2, fields, depth, LANES), F32),
+            pltpu.VMEM((2, fields, depth, LANES), F32),
+            pltpu.VMEM((2, 2, 4, depth, LANES), BF16),
+            pltpu.SMEM(new_owner.shape, jnp.int32),
+            pltpu.SMEM(order.shape, jnp.int32),
+            pltpu.SemaphoreType.DMA((12,)),
+        ],
         compiler_params=params,
         name="pack",
-    )(info, now, prev, coef)
+    )(owner_hbm, order_hbm, now_hbm, prev_hbm, coef_hbm)
 
     swap = [(0, 1), (1, 0)]
     forward = [(i, (i + 1) % count) for i in range(count)]
@@ -439,32 +484,34 @@
     from_dleft = lax.ppermute(dright, ("region", "blk"), crossed(1))
 
     scratch = [pltpu.VMEM((fields, depth, width + 2 * LANES), F32), pltpu.VMEM((8, width + 2 * LANES), F32)]
-    row = jax.ShapeDtypeStruct((fields, depth, width), F32)
-    last_row = pl.pallas_call(
+    last_row, code = pl.pallas_call(
         last_row_body,
-        out_shape=row,
-        in_specs=[SMEM] + [VMEM] * 6,
-        out_specs=VMEM,
+        out_shape=(
+            jax.ShapeDtypeStruct((fields, depth, width), F32),
+            jax.ShapeDtypeStruct((fields * depth + 8, width), jnp.int16),
+        ),
+        in_specs=[SMEM] + [VMEM] * 6 + [ANY] * 2,
+        out_specs=(VMEM, VMEM),
         scratch_shapes=scratch,
         compiler_params=params,
         name="last_row",
-    )(info, now, prev, coef, y_in, from_right, from_dright)
-    arrived = lax.ppermute(last_row, "blk", forward)
+    )(order, now, prev, coef, y_in, from_right, from_dright, from_left, from_dleft)
+    arrived = lax.ppermute(code, "blk", forward)
     partial = pl.pallas_call(
         first_row_body,
         out_shape=jax.ShapeDtypeStruct((blocks + 1, fields, depth, width), F32),
-        in_specs=[SMEM] + [VMEM] * 7,
+        in_specs=[SMEM] * 2 + [VMEM] * 7,
         out_specs=VMEM,
         scratch_shapes=scratch,
         compiler_params=params,
         name="first_row",
-    )(info, now, prev, coef, y_in, from_left, from_dleft, last_row)
+    )(new_owner, order, now, prev, coef, y_in, from_left, from_dleft, last_row)
     result = pl.pallas_call(
         place_body,
         out_shape=jax.ShapeDtypeStruct((blocks + 1, fields, depth, width), F32),
-        in_specs=[VMEM, ANY, ANY],
+        in_specs=[VMEM, VMEM, ANY],
         out_specs=ANY,
-        scratch_shapes=[pltpu.SemaphoreType.DMA],
+        scratch_shapes=[pltpu.VMEM((fields, depth, width), F32), pltpu.SemaphoreType.DMA((fields,))],
         input_output_aliases={2: 0},
         compiler_params=params,
         name="place",

time: 38.7 us -> 28.7 us (0.74)
  local copies, waits for them, and re-layouts: 4.73 us -> 0.02 us
  waiting for transfers between devices: 13.5 us -> 9.9 us
  starting transfers between devices: 10.7 us -> 9.29 us
  Pallas kernels: 8.12 us -> 9.29 us
  other arithmetic: 0.74 us -> 0 us
  between operations: 0.69 us -> 0.08 us
    ppermute x1, waiting for transfers between devices: 10 us -> 3.5 us  [fast_on_device(): from_dleft = lax.ppermute(dright, ('region', 'blk'), crossed(1))]
    ppermute x1, waiting for transfers between devices: 0.01 us -> 4.73 us  [fast_on_device(): arrived = lax.ppermute(code, 'blk', forward)]
    unnamed x6 -> x10, local copies, waits for them, and re-layouts: 3.49 us -> 0.02 us
    ppermute x1, starting transfers between devices: 1.81 us -> 0.01 us  [fast_on_device(): from_left = lax.ppermute(right, 'blk', forward)]
    slice x1 -> x0, local copies, waits for them, and re-layouts: 1.24 us -> none  [fast_on_device(): moves = (new_owner[blocks - 1] != owner).astype(jnp.int32)]
    ppermute x1, waiting for transfers between devices: 2.82 us -> 1.66 us  [fast_on_device(): from_dright = lax.ppermute(dleft, ('region', 'blk'), crossed(-1))]
    pallas_call x2, Pallas kernels: 3.34 us -> 4.42 us  [the longest x1 2.82 us: fast_on_device(): pl.pallas_call(last_row_body, out_shape=(jax.ShapeDtypeStruct((fields, de...]
    ppermute x1, starting transfers between devices: 3.69 us -> 4.44 us  [fast_on_device(): from_right = lax.ppermute(left, 'blk', backward)]
  transfers between devices with their start and end apart: 6 -> 6, of which waited for: 3 -> 3; matrix products, arithmetic and copies ran while one was open for 0% -> 0% of each run, Pallas kernels for 10% -> 14%
where the time goes in v2:
time: 28.7 us; the launch traced here: 28.6 us
  waiting for transfers between devices  9.9 us (34%)
  Pallas kernels  9.29 us (32%)
  starting transfers between devices  9.29 us (32%)
    ppermute x1, waiting for transfers between devices, fast_on_device(): arrived = lax.ppermute(code, 'blk', forward)  4.73 us
    ppermute x1, starting transfers between devices, fast_on_device(): from_right = lax.ppermute(left, 'blk', backward)  4.44 us
    pallas_call x1, Pallas kernels, fast_on_device(): pl.pallas_call(first_row_body, out_shape=jax.ShapeDtypeStruct((blocks + 1...  3.91 us
    ppermute x1, waiting for transfers between devices, fast_on_device(): from_dleft = lax.ppermute(dright, ('region', 'blk'), crossed(1))  3.5 us
    ppermute x1, starting transfers between devices, fast_on_device(): y_in = lax.ppermute(y_out, 'region', swap)  3.05 us
    pallas_call x1, Pallas kernels, fast_on_device(): pl.pallas_call(last_row_body, out_shape=(jax.ShapeDtypeStruct((fields, de...  2.82 us
    ppermute x1, waiting for transfers between devices, fast_on_device(): from_dright = lax.ppermute(dleft, ('region', 'blk'), crossed(-1))  1.66 us
    pallas_call x1, Pallas kernels, fast_on_device(): pl.pallas_call(pack_body, out_shape=(jax.ShapeDtypeStruct((5, depth, widt...  1.6 us
  transfers between devices with their start and end apart: 6, of which 3 were waited for; matrix products, arithmetic and copies ran while one was open for 0% of the time, Pallas kernels for 14%

profile of v2, /device:TPU:0, one launch (start us, length us, event | category | flops | bytes accessed | tf_op | source)
XLA Modules:
  0.0 28.6 jit_solution(1000751750338594545)
XLA Ops:
  0.0 0.0 copy-start.3
  0.0 0.0 copy-start.2
  0.0 0.0 copy-start.1
  0.0 0.0 copy-start
  0.0 1.6 %pack.1 = (bf16[5,32,1024]{2,1,0:T(8,128)(2,1)S(1)}, bf16[144,128]{1,0:T(8,128)(2,1)S(1)}, bf16[144,128]{1,0:T(8,128)(2,1)S(1)}, bf16[64,128]{1,0:T(8,128)(2,1)S(1)}, bf16[64,128]{1,0:T(8,128)(2,1)S(1)}) custom-call(s32[2]{0:T(128)} %owner_ref.1, s32[8]{0:T(128)} %bitcast.16, f32[2,4,32,1024]{3,2,1,0:T(8,128)} %bitcast.7, f32[2,4,32,1024]{3,2,1,0:T(8,128)} %bitcast.10, ...), custom_call_target="tpu_custom_call" | custom-call | tf_op jit(solution)/shard_map/pack/pallas_call | solution.py:452
  1.6 0.0 copy-start.4
  1.6 3.0 %collective-permute-start.1 = (bf16[5,32,1024]{2,1,0:T(8,128)(2,1)S(1)}, bf16[5,32,1024]{2,1,0:T(8,128)(2,1)S(1)}, u32[]{:S(2)}, u32[]{:S(2)}) collective-permute-start(bf16[5,32,1024]{2,1,0:T(8,128)(2,1)S(1)} %get-tuple-element.13), channel_id=1, source_target_pairs={{0,16},{16,0},{1,17},{17,1},{2,18},{18,2},{3,19},{19,3},{4,20},{20... | collective-permute-start | bytes 983048 | tf_op jit(solution)/shard_map/ppermute | solution.py:480
  4.7 0.0 collective-permute-start
  4.7 4.4 %collective-permute-start.2 = (bf16[144,128]{1,0:T(8,128)(2,1)S(1)}, bf16[144,128]{1,0:T(8,128)(2,1)S(1)}, u32[]{:S(2)}, u32[]{:S(2)}) collective-permute-start(bf16[144,128]{1,0:T(8,128)(2,1)S(1)} %get-tuple-element.14), channel_id=1, source_target_pairs={{0,15},{1,0},{2,1},{3,2},{4,3},{5,4},{6,5},{7,6},{8,7},{9,8},{10,9... | collective-permute-start | bytes 110600 | tf_op jit(solution)/shard_map/ppermute | solution.py:481
  9.1 0.1 collective-permute-start.3
  9.3 1.6 %collective-permute-start.4 = (bf16[64,128]{1,0:T(8,128)(2,1)S(1)}, bf16[64,128]{1,0:T(8,128)(2,1)S(1)}, u32[]{:S(2)}, u32[]{:S(2)}) collective-permute-start(bf16[64,128]{1,0:T(8,128)(2,1)S(1)} %get-tuple-element.16), channel_id=1, source_target_pairs={{0,17},{1,18},{2,19},{3,20},{4,21},{5,22},{6,23},{7,24},{8,25},{9,... | collective-permute-start | bytes 49160 | tf_op jit(solution)/shard_map/ppermute | solution.py:484
  10.9 1.7 %collective-permute-done.3.diag_ref = bf16[64,128]{1,0:T(8,128)(2,1)S(1)} collective-permute-done((bf16[64,128]{1,0:T(8,128)(2,1)S(1)}, bf16[64,128]{1,0:T(8,128)(2,1)S(1)}, u32[]{:S(2)}, u32[]{:S(2)}) %collective-permute-start.3) | collective-permute-done | bytes 16416 | tf_op jit(solution)/shard_map/ppermute | solution.py:482
  12.5 3.5 %collective-permute-done.4.early_b.diag_ref = bf16[64,128]{1,0:T(8,128)(2,1)S(1)} collective-permute-done((bf16[64,128]{1,0:T(8,128)(2,1)S(1)}, bf16[64,128]{1,0:T(8,128)(2,1)S(1)}, u32[]{:S(2)}, u32[]{:S(2)}) %collective-permute-start.4) | collective-permute-done | bytes 16416 | tf_op jit(solution)/shard_map/ppermute | solution.py:484
  16.0 0.0 collective-permute-done.early_a.straight_ref
  16.0 0.0 collective-permute-done.2.straight_ref
  16.0 0.0 collective-permute-done.1.y_ref
  16.0 0.0 copy-done.3
  16.1 0.0 copy-done.2
  16.1 0.0 copy-done.1
  16.1 0.0 copy-done
  16.1 2.8 %last_row.1 = (f32[4,32,1024]{2,1,0:T(8,128)S(1)}, s16[136,1024]{1,0:T(8,128)(2,1)S(1)}) custom-call(s32[8]{0:T(128)S(1)} %bitcast.17, f32[2,4,32,1024]{3,2,1,0:T(8,128)S(1)} %bitcast.8, f32[2,4,32,1024]{3,2,1,0:T(8,128)S(1)} %bitcast.11, bf16[2,4,32,1024]{3,2,1,0:T(8,128)(2,1)S(1)} %bitcast.14, bf16[5,32,1024]{2,1,0:T(8,128)(2,1)S(1)} %collective-permute-done.1.y_ref, ...), custom_call_target="tpu_custom_call" | custom-call | tf_op jit(solution)/shard_map/last_row/pallas_call | solution.py:487
  18.9 0.1 collective-permute-start.5
  19.0 0.0 copy-done.4
  19.0 3.9 %first_row.1.partial_ref = f32[3,4,32,1024]{3,2,1,0:T(8,128)} custom-call(s32[2]{0:T(128)S(1)} %copy-done.4, s32[8]{0:T(128)S(1)} %bitcast.18, f32[2,4,32,1024]{3,2,1,0:T(8,128)S(1)} %bitcast.9, f32[2,4,32,1024]{3,2,1,0:T(8,128)S(1)} %bitcast.12, bf16[2,4,32,1024]{3,2,1,0:T(8,128)(2,1)S(1)} %bitcast.15, ...), custom_call_target="tpu_custom_call" | custom-call | tf_op jit(solution)/shard_map/first_row/pallas_call | solution.py:500
  22.9 4.7 %collective-permute-done.5.code_ref = s16[136,1024]{1,0:T(8,128)(2,1)S(1)} collective-permute-done((s16[136,1024]{1,0:T(8,128)(2,1)S(1)}, s16[136,1024]{1,0:T(8,128)(2,1)S(1)}, u32[]{:S(2)}, u32[]{:S(2)}) %collective-permute-start.5) | collective-permute-done | bytes 278560 | tf_op jit(solution)/shard_map/ppermute | solution.py:499
  27.6 1.0 %place.1 = f32[3,4,32,1024]{3,2,1,0:T(8,128)} custom-call(bf16[144,128]{1,0:T(8,128)(2,1)S(1)} %collective-permute-done.early_a.straight_ref, s16[136,1024]{1,0:T(8,128)(2,1)S(1)} %collective-permute-done.5.code_ref, f32[3,4,32,1024]{3,2,1,0:T(8,128)} %first_row.1.partial_ref), custom_call_target="tpu_custom_call", output_to_operand_aliasing={{}: (2, {})} | custom-call | tf_op jit(solution)/shard_map/place/pallas_call | solution.py:509
Async XLA Ops:
  0.0 16.0 %copy-start.3 = (s32[1,1,8]{2,1,0:T(1,128)S(1)}, s32[1,1,8]{2,1,0:T(1,128)}, u32[]{:S(2)}) copy-start(s32[1,1,8]{2,1,0:T(1,128)} %param.8) | copy-start | bytes 100
  0.0 16.1 %copy-start.2 = (bf16[1,1,2,4,32,1024]{5,4,3,2,1,0:T(8,128)(2,1)S(1)}, bf16[1,1,2,4,32,1024]{5,4,3,2,1,0:T(8,128)(2,1)}, u32[]{:S(2)}) copy-start(bf16[1,1,2,4,32,1024]{5,4,3,2,1,0:T(8,128)(2,1)} %param.7) | copy-start | bytes 1572868
  0.0 16.1 %copy-start.1 = (f32[2,1,4,32,1024]{4,3,2,1,0:T(8,128)S(1)}, f32[2,1,4,32,1024]{4,3,2,1,0:T(8,128)}, u32[]{:S(2)}) copy-start(f32[2,1,4,32,1024]{4,3,2,1,0:T(8,128)} %param.6) | copy-start | bytes 3145732
  0.0 16.1 %copy-start = (f32[2,1,4,32,1024]{4,3,2,1,0:T(8,128)S(1)}, f32[2,1,4,32,1024]{4,3,2,1,0:T(8,128)}, u32[]{:S(2)}) copy-start(f32[2,1,4,32,1024]{4,3,2,1,0:T(8,128)} %param.5) | copy-start | bytes 3145732
  1.6 17.4 %copy-start.4 = (s32[2]{0:T(128)S(1)}, s32[2]{0:T(128)}, u32[]{:S(2)}) copy-start(s32[2]{0:T(128)} %owner_ref.1) | copy-start | bytes 28
  1.6 14.4 %collective-permute-start.1 = (bf16[5,32,1024]{2,1,0:T(8,128)(2,1)S(1)}, bf16[5,32,1024]{2,1,0:T(8,128)(2,1)S(1)}, u32[]{:S(2)}, u32[]{:S(2)}) collective-permute-start(bf16[5,32,1024]{2,1,0:T(8,128)(2,1)S(1)} %get-tuple-element.13), channel_id=1, source_target_pairs={{0,16},{16,0},{1,17},{17,1},{2,18},{18,2},{3,19},{19,3},{4,20},{20... | collective-permute-start | bytes 983048 | tf_op jit(solution)/shard_map/ppermute | solution.py:480
  4.7 11.4 %collective-permute-start = (bf16[144,128]{1,0:T(8,128)(2,1)S(1)}, bf16[144,128]{1,0:T(8,128)(2,1)S(1)}, u32[]{:S(2)}, u32[]{:S(2)}) collective-permute-start(bf16[144,128]{1,0:T(8,128)(2,1)S(1)} %get-tuple-element.12), channel_id=1, source_target_pairs={{0,1},{1,2},{2,3},{3,4},{4,5},{5,6},{6,7},{7,8},{8,9},{9,10},{10,1... | collective-permute-start | bytes 110600 | tf_op jit(solution)/shard_map/ppermute | solution.py:483
  4.7 11.4 %collective-permute-start.2 = (bf16[144,128]{1,0:T(8,128)(2,1)S(1)}, bf16[144,128]{1,0:T(8,128)(2,1)S(1)}, u32[]{:S(2)}, u32[]{:S(2)}) collective-permute-start(bf16[144,128]{1,0:T(8,128)(2,1)S(1)} %get-tuple-element.14), channel_id=1, source_target_pairs={{0,15},{1,0},{2,1},{3,2},{4,3},{5,4},{6,5},{7,6},{8,7},{9,8},{10,9... | collective-permute-start | bytes 110600 | tf_op jit(solution)/shard_map/ppermute | solution.py:481
  9.1 3.4 %collective-permute-start.3 = (bf16[64,128]{1,0:T(8,128)(2,1)S(1)}, bf16[64,128]{1,0:T(8,128)(2,1)S(1)}, u32[]{:S(2)}, u32[]{:S(2)}) collective-permute-start(bf16[64,128]{1,0:T(8,128)(2,1)S(1)} %get-tuple-element.15), channel_id=1, source_target_pairs={{0,31},{1,16},{2,17},{3,18},{4,19},{5,20},{6,21},{7,22},{8,23},{9,... | collective-permute-start | bytes 49160 | tf_op jit(solution)/shard_map/ppermute | solution.py:482
  9.3 6.8 %collective-permute-start.4 = (bf16[64,128]{1,0:T(8,128)(2,1)S(1)}, bf16[64,128]{1,0:T(8,128)(2,1)S(1)}, u32[]{:S(2)}, u32[]{:S(2)}) collective-permute-start(bf16[64,128]{1,0:T(8,128)(2,1)S(1)} %get-tuple-element.16), channel_id=1, source_target_pairs={{0,17},{1,18},{2,19},{3,20},{4,21},{5,22},{6,23},{7,24},{8,25},{9,... | collective-permute-start | bytes 49160 | tf_op jit(solution)/shard_map/ppermute | solution.py:484
  18.9 8.7 %collective-permute-start.5 = (s16[136,1024]{1,0:T(8,128)(2,1)S(1)}, s16[136,1024]{1,0:T(8,128)(2,1)S(1)}, u32[]{:S(2)}, u32[]{:S(2)}) collective-permute-start(s16[136,1024]{1,0:T(8,128)(2,1)S(1)} %get-tuple-element.17), channel_id=1, source_target_pairs={{0,1},{1,2},{2,3},{3,4},{4,5},{5,6},{6,7},{7,8},{8,9},{9,10},{10,1... | collective-permute-start | bytes 835592 | tf_op jit(solution)/shard_map/ppermute | solution.py:499

commit v3 on v0

--- a/solution.py
+++ b/solution.py
@@ -1,9 +1,20 @@
+import functools
+
 import jax
 import jax.numpy as jnp
 from jax import lax
+from jax.experimental import pallas as pl
+from jax.experimental.pallas import tpu as pltpu
 from jax.sharding import PartitionSpec as P
 
 STEPS = 2
+LANES = 128
+F32 = jnp.float32
+BF16 = jnp.bfloat16
+VMEM = pl.BlockSpec(memory_space=pltpu.VMEM)
+SMEM = pl.BlockSpec(memory_space=pltpu.SMEM)
+ANY = pl.BlockSpec(memory_space=pl.ANY)
+HBM = pl.BlockSpec(memory_space=pltpu.HBM)
 
 
 def extended_2(block, sides, width, periodic):
@@ -82,7 +93,7 @@
     return (placed, jnp.sum(valid_flags))
 
 
-def on_device(u_now, u_prev, coef_store, store_map, new_owner):
+def general_on_device(u_now, u_prev, coef_store, store_map, new_owner):
     state_now = u_now[:, 0]
     state_prev = u_prev[:, 0]
     blocks, fields, edge_cells, plane_cells = state_now.shape
@@ -114,7 +125,571 @@
     return result[:, None]
 
 
+def lane_ids():
+    return lax.broadcasted_iota(jnp.int32, (1, LANES), 1)
+
+
+def edge_start(lower, depth, size):
+    return pl.multiple_of(jnp.where(lower, depth - size, 0), size)
+
+
+def tag_values(map_ref, region):
+    numbers = [map_ref[region * 4 + s] for s in range(4)] + [map_ref[(1 - region) * 4 + s] for s in range(4)]
+    return [jnp.zeros((1, LANES), F32) + number.astype(F32) for number in numbers]
+
+
+def load_edges(u_ref, p_ref, coef_ref, ue_ref, pe_ref, ce_ref, region, lower, depth, sems):
+    edge8 = edge_start(lower, depth, 8)
+    edge16 = edge_start(lower, depth, 16)
+    return [
+        pltpu.make_async_copy(u_ref.at[:, :, pl.ds(edge8, 8), :], ue_ref, sems.at[0]),
+        pltpu.make_async_copy(p_ref.at[:, :, pl.ds(edge8, 8), :], pe_ref, sems.at[1]),
+        pltpu.make_async_copy(coef_ref.at[region, :, pl.ds(edge16, 16), :], ce_ref, sems.at[2]),
+    ]
+
+
+def pack_region_body(
+    map_hbm, u_ref, p_ref, coef_ref, y_ref, edges_ref, rows_ref, ue_ref, pe_ref, ce_ref, map_ref, sems
+):
+    fields = u_ref.shape[1]
+    depth = u_ref.shape[2]
+    region = lax.axis_index("region")
+    lower = region == 0
+    scalars = pltpu.make_async_copy(map_hbm, map_ref, sems.at[3])
+    bulk = pltpu.make_async_copy(coef_ref.at[1 - region], y_ref.at[0:4], sems.at[4])
+    copies = load_edges(u_ref, p_ref, coef_ref, ue_ref, pe_ref, ce_ref, region, lower, depth, sems)
+    for copy in [bulk, scalars] + copies:
+        copy.start()
+    for copy in copies:
+        copy.wait()
+    own_edge = jnp.where(lower, 7, 0)
+    own_next = jnp.where(lower, 6, 1)
+    for m in range(2):
+        for f in range(fields):
+            at = m * fields + f
+            near = ue_ref[m, f, pl.ds(own_edge, 1), :]
+            rows_ref[at : at + 1, :] = near
+            rows_ref[8 + at : 9 + at, :] = ue_ref[m, f, pl.ds(own_next, 1), :]
+            rows_ref[16 + at : 17 + at, :] = 2.0 * near - pe_ref[m, f, pl.ds(own_edge, 1), :]
+    for s in range(4):
+        piece = ce_ref[s].astype(F32)
+        rows_ref[24 + s : 25 + s, :] = jnp.where(lower, piece[15:16], piece[0:1])
+    scalars.wait()
+    for i, row in enumerate(tag_values(map_ref, region)):
+        rows_ref[28:29, i * LANES : (i + 1) * LANES] = row
+    rows_ref[29:32, :] = jnp.zeros((3, rows_ref.shape[1]), F32)
+    y_ref[4] = rows_ref[...].astype(BF16)
+    edges_ref[...] = rows_ref[...]
+    bulk.wait()
+
+
+def pack_ring_body(
+    owner_hbm, map_hbm, u_ref, p_ref, coef_ref, edges_ref, left_ref, right_ref, dleft_ref, dright_ref,
+    ua_ref, pa_ref, ca_ref, owner_ref, map_ref, sems
+):
+    fields = u_ref.shape[1]
+    depth = u_ref.shape[2]
+    last = u_ref.shape[3] - LANES
+    top = depth - 1
+    region = lax.axis_index("region")
+    lower = region == 0
+    other = 1 - region
+    copies = [
+        pltpu.make_async_copy(owner_hbm, owner_ref, sems.at[0]),
+        pltpu.make_async_copy(map_hbm, map_ref, sems.at[1]),
+        pltpu.make_async_copy(u_ref.at[0, :, :, 0:LANES], ua_ref.at[0], sems.at[2]),
+        pltpu.make_async_copy(u_ref.at[1, :, :, last : last + LANES], ua_ref.at[1], sems.at[3]),
+        pltpu.make_async_copy(p_ref.at[0, :, :, 0:LANES], pa_ref.at[0], sems.at[4]),
+        pltpu.make_async_copy(p_ref.at[1, :, :, last : last + LANES], pa_ref.at[1], sems.at[5]),
+        pltpu.make_async_copy(coef_ref.at[:, :, :, 0:LANES], ca_ref.at[0], sems.at[6]),
+        pltpu.make_async_copy(coef_ref.at[:, :, :, last : last + LANES], ca_ref.at[1], sems.at[7]),
+    ]
+    for copy in copies:
+        copy.start()
+    for copy in copies:
+        copy.wait()
+    lane = lane_ids()
+    tag_rows = tag_values(map_ref, region)
+    blank = jnp.zeros((1, LANES), F32)
+    flag = blank + jnp.where(owner_ref[1] != lax.axis_index("blk"), 1.0, 0.0).astype(F32)
+    for m, lanes, straight_ref, diag_ref in (
+        (0, slice(0, LANES), left_ref, dleft_ref),
+        (1, slice(last, last + LANES), right_ref, dright_ref),
+    ):
+        for f in range(fields):
+            now = ua_ref[m, f]
+            ahead = 2.0 * now - pa_ref[m, f]
+            piece = ca_ref[m, region, f].astype(F32)
+            if m == 0:
+                tile = jnp.where(
+                    lane < 64, now, jnp.where(lane < 96, pltpu.roll(ahead, 64, 1), pltpu.roll(piece, 96, 1))
+                )
+            else:
+                tile = jnp.where(
+                    lane >= 64, now, jnp.where(lane < 32, pltpu.roll(ahead, 32, 1), pltpu.roll(piece, 64, 1))
+                )
+            straight_ref[f * depth : (f + 1) * depth, :] = tile.astype(BF16)
+        far = [ca_ref[m, other, s].astype(F32) for s in range(4)]
+        extra = [jnp.where(lower, piece[0:1], piece[top:depth]) for piece in far] + tag_rows + [flag] + [blank] * 3
+        straight_ref[fields * depth : fields * depth + 16, :] = jnp.concatenate(extra, axis=0).astype(BF16)
+        plane = jnp.zeros((depth, LANES), F32)
+        for s in range(4):
+            shift = (32 * s if m == 0 else 32 + 32 * s) % LANES
+            moved = pltpu.roll(far[s], shift, 1) if shift else far[s]
+            plane = jnp.where((lane >= 32 * s) & (lane < 32 * s + 32), moved, plane)
+        diag_ref[0:depth, :] = plane.astype(BF16)
+        extra = (
+            [edges_ref[m * fields : m * fields + 4, lanes]]
+            + [edges_ref[8 + m * fields : 12 + m * fields, lanes]]
+            + [edges_ref[16 + m * fields : 20 + m * fields, lanes]]
+            + [edges_ref[24:28, lanes]]
+            + tag_rows
+            + [blank] * 8
+        )
+        diag_ref[depth : depth + 32, :] = jnp.concatenate(extra, axis=0).astype(BF16)
+
+
+def nine_sum(tiles, lane, first=0):
+    inside = lane % 32
+    low = inside != 0
+    high = inside != 31
+    rows = []
+    for tile in tiles:
+        rows.append(
+            tile
+            + jnp.where(low, pltpu.roll(tile, 1, 1), 0.0)
+            + jnp.where(high, pltpu.roll(tile, LANES - 1, 1), 0.0)
+        )
+    up = [pltpu.roll(row, 32, 1) for row in rows]
+    down = [pltpu.roll(row, LANES - 32, 1) for row in rows]
+    count = len(tiles)
+    result = []
+    for t in range(count):
+        before = up[t] if t == 0 else jnp.where(lane < 32, up[t - 1], up[t])
+        after = down[t] if t == count - 1 else jnp.where(lane >= 96, down[t + 1], down[t])
+        result.append(rows[t] + before + after)
+    return result
+
+
+def column_sum(tile, row_id, low_row, high_row):
+    depth = tile.shape[0]
+    above = pltpu.roll(tile, 1, 0)
+    below = pltpu.roll(tile, depth - 1, 0)
+    return tile + jnp.where(row_id == 0, low_row, above) + jnp.where(row_id == depth - 1, high_row, below)
+
+
+def local_body(u_ref, box_ref, rim_ref):
+    fields, depth, width = u_ref.shape[1:]
+    main = width // LANES
+    lower = lax.axis_index("region") == 0
+    lane = lane_ids()
+    row_id = lax.broadcasted_iota(jnp.int32, (depth, 1), 0)
+    for f in range(fields):
+        now = [u_ref[m, f, :, t * LANES : (t + 1) * LANES] for m in range(2) for t in range(main)]
+        sums = nine_sum(now, lane)
+        for i, (tile, total) in enumerate(zip(now, sums)):
+            m, t = divmod(i, main)
+            lanes = slice(t * LANES, (t + 1) * LANES)
+            rim_ref[m, f : f + 1, lanes] = jnp.where(lower, total[depth - 1 : depth], total[0:1])
+            box_ref[m, f, :, lanes] = column_sum(total, row_id, 0.0, 0.0) - 27.0 * tile
+    rim_ref[:, 4:8, :] = jnp.zeros((2, 4, width), F32)
+
+
+def tile_at(t):
+    return slice(t * LANES, (t + 1) * LANES)
+
+
+class Row:
+    def __init__(self, m, map_ref, u_ref, p_ref, coef_ref, y_ref, straight_ref, diag_ref, box_ref):
+        self.m = m
+        self.u, self.p, self.coef, self.y, self.box = u_ref, p_ref, coef_ref, y_ref, box_ref
+        self.straight, self.diag = straight_ref, diag_ref
+        self.fields, self.depth, self.width = u_ref.shape[1:]
+        self.main = self.width // LANES
+        self.region = lax.axis_index("region")
+        self.lower = self.region == 0
+        self.lane = lane_ids()
+        self.row_id = lax.broadcasted_iota(jnp.int32, (self.depth, 1), 0)
+        self.beside = 1 - m
+        self.local_lanes = slice(self.width - LANES, self.width) if m == 1 else slice(0, LANES)
+        fields, depth = self.fields, self.depth
+        self.extra_s = straight_ref[fields * depth : fields * depth + 16, :].astype(F32)
+        numbers = [map_ref[q] for q in range(8)]
+        self.places = []
+        for number in range(8):
+            place = jnp.int32(0)
+            for q in range(8):
+                place = jnp.where(numbers[q] == number, q, place)
+            self.places.append((place & 3, (place >> 2) == self.region))
+        planes = []
+        for s in range(4):
+            tile = straight_ref[s * depth : (s + 1) * depth, :].astype(F32)
+            planes.append(pltpu.roll(tile, 32 if m == 1 else 64, 1))
+        diag_tile = diag_ref[0:depth, :].astype(F32)
+        for s in range(4):
+            shift = (-32 * s if m == 1 else 96 - 32 * s) % LANES
+            planes.append(pltpu.roll(diag_tile, shift, 1) if shift else diag_tile)
+        self.planes = planes
+        self.tags = [self.extra_s[4 + i : 5 + i] for i in range(8)]
+        self.halo_base = 0 if m == 1 else fields
+
+    def with_sides(self, local, remote, middle):
+        return [local] + middle + [remote] if self.m == 1 else [remote] + middle + [local]
+
+    def coef_tile(self, number, lanes):
+        slot, held = self.places[number]
+        return jnp.where(held, self.coef[self.region, slot, :, lanes], self.y[slot, :, lanes]).astype(F32)
+
+    def other_column(self, rim_ref, near_ref, stepped_ref):
+        m, fields, depth, main = self.m, self.fields, self.depth, self.main
+        lane, lower = self.lane, self.lower
+        extra_y = self.y[4].astype(F32)
+        extra_d = self.diag[depth : depth + 32, :].astype(F32)
+        tags_d = [extra_d[16 + i : 17 + i] for i in range(8)]
+        tags_y = [extra_y[28:29, i * LANES : (i + 1) * LANES] for i in range(8)]
+        field_id = lax.broadcasted_iota(jnp.int32, (4, LANES), 0).astype(F32)
+
+        def edge_tiles(base_y, base_d):
+            middle = [extra_y[base_y + m * fields : base_y + m * fields + 4, tile_at(t)] for t in range(main)]
+            local = extra_y[base_y + self.beside * fields : base_y + self.beside * fields + 4, self.local_lanes]
+            return self.with_sides(local, extra_d[base_d : base_d + 4], middle)
+
+        near = edge_tiles(0, 0)
+        beyond = edge_tiles(8, 4)
+        ahead = edge_tiles(16, 8)
+
+        def other_row(s, lanes):
+            piece = self.coef[1 - self.region, s, :, lanes].astype(F32)
+            return jnp.where(lower, piece[0:1], piece[depth - 1 : depth])
+
+        def edge_coef(lanes, base):
+            total = jnp.zeros((4, LANES), F32)
+            for s in range(4):
+                total = total + jnp.where(tags_y[s] == field_id + base, extra_y[24 + s : 25 + s, lanes], 0.0)
+                total = total + jnp.where(tags_y[4 + s] == field_id + base, other_row(s, lanes), 0.0)
+            return total
+
+        corner = jnp.zeros((4, LANES), F32)
+        for s in range(4):
+            corner = corner + jnp.where(tags_d[s] == field_id + self.halo_base, extra_d[12 + s : 13 + s], 0.0)
+            corner = corner + jnp.where(tags_d[4 + s] == field_id + self.halo_base, self.extra_s[s : s + 1], 0.0)
+        edge_c = self.with_sides(
+            edge_coef(self.local_lanes, self.beside * fields),
+            corner,
+            [edge_coef(tile_at(t), m * fields) for t in range(main)],
+        )
+        near_sum = nine_sum(near, lane)
+        beyond_sum = nine_sum(beyond, lane)
+        border = main - 1 if m == 1 else 0
+        rims = self.with_sides(
+            rim_ref[self.beside, 0:4, self.local_lanes],
+            jnp.zeros((4, LANES), F32),
+            [rim_ref[m, 0:4, tile_at(t)] for t in range(main)],
+        )
+        own, outer = [], []
+        for f in range(fields):
+            tiles = self.border_tiles(f)
+            own.append(jnp.where(lower, tiles[0][depth - 1 : depth], tiles[0][0:1]))
+            outer.append(jnp.where(lower, tiles[1][depth - 1 : depth], tiles[1][0:1]))
+        pair = [jnp.concatenate(own, axis=0), jnp.concatenate(outer, axis=0)]
+        sums = nine_sum(pair if m == 1 else pair[::-1], lane)
+        side = main + 1 if m == 1 else 0
+        rims[side] = sums[1] if m == 1 else sums[0]
+        touched = sums[0] if m == 1 else sums[1]
+        facing = lane >= 96 if m == 1 else lane < 32
+        rims[border + 1] = jnp.where(facing, touched, rims[border + 1])
+        stepped = []
+        for t in range(main + 2):
+            box = near_sum[t] + beyond_sum[t] + rims[t]
+            stepped.append(ahead[t] + edge_c[t] * (box - 27.0 * near[t]))
+        stepped_sum = nine_sum(stepped, lane)
+        for t in range(main + 2):
+            near_ref[0:4, tile_at(t)] = near_sum[t]
+            stepped_ref[0:4, tile_at(t)] = stepped_sum[t]
+
+    def border_tiles(self, f):
+        border = self.main - 1 if self.m == 1 else 0
+        remote = self.straight[f * self.depth : (f + 1) * self.depth, :].astype(F32)
+        return self.u[self.m, f, :, tile_at(border)], remote
+
+    def rows(self, row):
+        return jnp.where(self.lower, 0.0, row), jnp.where(self.lower, row, 0.0)
+
+    def first_step(self, f, near_ref):
+        m, main, lane, fields = self.m, self.main, self.lane, self.fields
+        inner, remote = self.border_tiles(f)
+        local = self.u[self.beside, f, :, self.local_lanes]
+        pair = [inner, remote] if m == 1 else [remote, inner]
+        sums = nine_sum(pair, lane)
+        inner_sum, remote_sum = (sums[0], sums[1]) if m == 1 else (sums[1], sums[0])
+        facing = lane >= 96 if m == 1 else lane < 32
+        border = main - 1 if m == 1 else 0
+        now = self.with_sides(local, remote, [self.u[m, f, :, tile_at(t)] for t in range(main)])
+        halo_c = jnp.zeros((self.depth, LANES), F32)
+        for i in range(8):
+            halo_c = halo_c + jnp.where(self.tags[i] == F32(self.halo_base + f), self.planes[i], 0.0)
+        coef = self.with_sides(
+            self.coef_tile(self.beside * fields + f, self.local_lanes),
+            halo_c,
+            [self.coef_tile(m * fields + f, tile_at(t)) for t in range(main)],
+        )
+        drift = self.with_sides(
+            2.0 * local - self.p[self.beside, f, :, self.local_lanes],
+            pltpu.roll(remote, 64 if m == 1 else 96, 1),
+            [2.0 * now[t + 1] - self.p[m, f, :, tile_at(t)] for t in range(main)],
+        )
+        result = []
+        for t in range(main + 2):
+            remote_side = t == (main + 1 if m == 1 else 0)
+            low_row, high_row = self.rows(near_ref[f : f + 1, tile_at(t)])
+            if remote_side:
+                lap = column_sum(remote_sum, self.row_id, low_row, high_row) - 27.0 * remote
+            else:
+                if t == (0 if m == 1 else main + 1):
+                    lap = self.box[self.beside, f, :, self.local_lanes]
+                else:
+                    lap = self.box[m, f, :, tile_at(t - 1)]
+                lap = lap + jnp.where(self.row_id == 0, low_row, 0.0)
+                lap = lap + jnp.where(self.row_id == self.depth - 1, high_row, 0.0)
+                if t == border + 1:
+                    whole = column_sum(inner_sum, self.row_id, low_row, high_row) - 27.0 * inner
+                    lap = jnp.where(facing, whole, lap)
+            result.append(drift[t] + coef[t] * lap)
+        return result
+
+    def second_step(self, f, now, stepped_ref, write):
+        sums = nine_sum(now, self.lane)
+        for t in range(1, self.main + 1):
+            low_row, high_row = self.rows(stepped_ref[f : f + 1, tile_at(t)])
+            lanes = tile_at(t - 1)
+            lap = column_sum(sums[t], self.row_id, low_row, high_row) - 27.0 * now[t]
+            coef = self.coef_tile(self.m * self.fields + f, lanes)
+            write(f, lanes, 2.0 * now[t] - self.u[self.m, f, :, lanes] + coef * lap)
+
+
+CODES = 32000.0
+
+
+def code_writer(row_ref, code_ref, power_ref, first, count, depth):
+    def write(f, lanes, value):
+        at = f - first
+        row_ref[at, :, lanes] = value
+        size = jnp.maximum(jnp.max(jnp.abs(value), axis=0, keepdims=True), 1e-30)
+        power = jnp.ceil(jnp.log2(size))
+        code = jnp.floor(value * (CODES * jnp.exp2(-power)) + 0.5)
+        code_ref[at * depth : (at + 1) * depth, lanes] = code.astype(jnp.int32).astype(jnp.int16)
+        power_ref[at : at + 1, lanes] = power
+
+    return write
+
+
+def write_powers(power_ref, code_ref, count, depth):
+    power_ref[count:8, :] = jnp.zeros((8 - count, power_ref.shape[1]), F32)
+    code_ref[count * depth : count * depth + 8, :] = power_ref[...].astype(jnp.int32).astype(jnp.int16)
+
+
+def last_row_a_body(
+    map_ref, u_ref, p_ref, coef_ref, y_ref, straight_ref, diag_ref, box_ref, rim_ref,
+    row_ref, code_ref, near_ref, stepped_ref, power_ref
+):
+    count = row_ref.shape[0]
+    row = Row(1, map_ref, u_ref, p_ref, coef_ref, y_ref, straight_ref, diag_ref, box_ref)
+    row.other_column(rim_ref, near_ref, stepped_ref)
+    write = code_writer(row_ref, code_ref, power_ref, 0, count, row.depth)
+    for f in range(count):
+        row.second_step(f, row.first_step(f, near_ref), stepped_ref, write)
+    write_powers(power_ref, code_ref, count, row.depth)
+
+
+def last_row_b_body(
+    map_ref, u_ref, p_ref, coef_ref, y_ref, straight_ref, diag_ref, box_ref, near_ref, stepped_ref, early_a, early_b,
+    row_ref, code_ref, power_ref
+):
+    count = row_ref.shape[0]
+    row = Row(1, map_ref, u_ref, p_ref, coef_ref, y_ref, straight_ref, diag_ref, box_ref)
+    write = code_writer(row_ref, code_ref, power_ref, row.fields - count, count, row.depth)
+    for f in range(row.fields - count, row.fields):
+        row.second_step(f, row.first_step(f, near_ref), stepped_ref, write)
+    write_powers(power_ref, code_ref, count, row.depth)
+
+
+def first_row_body(
+    owner_ref, map_ref, u_ref, p_ref, coef_ref, y_ref, straight_ref, diag_ref, box_ref, rim_ref, last_a_ref, last_b_ref,
+    out_ref, near_ref, stepped_ref
+):
+    row = Row(0, map_ref, u_ref, p_ref, coef_ref, y_ref, straight_ref, diag_ref, box_ref)
+    arrives = row.extra_s[12:13] > 0.5
+    keeps = owner_ref[1] == lax.axis_index("blk")
+    half = last_a_ref.shape[0]
+
+    def write(f, lanes, value):
+        mine = last_a_ref[f, :, lanes] if f < half else last_b_ref[f - half, :, lanes]
+        kept = jnp.where(keeps, mine, 0.0)
+        out_ref[0, f, :, lanes] = value
+        out_ref[1, f, :, lanes] = jnp.where(arrives, value, kept)
+        out_ref[2, f, :, lanes] = jnp.where(arrives, kept, 0.0)
+
+    row.other_column(rim_ref, near_ref, stepped_ref)
+    for f in range(row.fields):
+        row.second_step(f, row.first_step(f, near_ref), stepped_ref, write)
+
+
+def place_body(first, straight_ref, code_ref, partial_ref, out_ref, row_ref, sems):
+    count, depth, width = row_ref.shape
+    rows = straight_ref.shape[0]
+    flag = jnp.max(straight_ref[rows - 16 : rows, :].astype(F32)[12:13])
+
+    @pl.when(flag > 0.5)
+    def _():
+        scale = jnp.exp2(code_ref[count * depth : count * depth + 8, :].astype(jnp.int32).astype(F32)) * (1.0 / CODES)
+        copies = []
+        for f in range(count):
+            code = code_ref[f * depth : (f + 1) * depth, :].astype(jnp.int32).astype(F32)
+            row_ref[f] = code * scale[f : f + 1]
+            copy = pltpu.make_async_copy(row_ref.at[f], out_ref.at[0, first + f], sems.at[f])
+            copy.start()
+            copies.append(copy)
+        for copy in copies:
+            copy.wait()
+
+
+def fast_on_device(u_now, u_prev, coef_store, store_map, new_owner):
+    blocks, _, fields, depth, width = u_now.shape
+    now = u_now.reshape(blocks, fields, depth, width)
+    prev = u_prev.reshape(blocks, fields, depth, width)
+    coef = coef_store[0, 0]
+    count = lax.axis_size("blk")
+    order = store_map.reshape(-1)
+    owner_hbm, order_hbm, now_hbm, prev_hbm, coef_hbm = (
+        pltpu.with_memory_space_constraint(array, pltpu.HBM) for array in (new_owner, order, now, prev, coef)
+    )
+    params = pltpu.CompilerParams(vmem_limit_bytes=48 * 1024 * 1024)
+
+    def call(body, name, out_shape, in_specs, out_specs, scratch, args, **options):
+        return pl.pallas_call(
+            body,
+            out_shape=out_shape,
+            in_specs=in_specs,
+            out_specs=out_specs,
+            scratch_shapes=scratch,
+            compiler_params=params,
+            name=name,
+            **options,
+        )(*args)
+
+    straight = jax.ShapeDtypeStruct((fields * depth + 16, LANES), BF16)
+    diag = jax.ShapeDtypeStruct((depth + 32, LANES), BF16)
+    y_out, edges = call(
+        pack_region_body,
+        "pack_region",
+        (jax.ShapeDtypeStruct((5, depth, width), BF16), jax.ShapeDtypeStruct((depth, width), F32)),
+        [HBM] * 4,
+        (VMEM, VMEM),
+        [
+            pltpu.VMEM((depth, width), F32),
+            pltpu.VMEM((blocks, fields, 8, width), F32),
+            pltpu.VMEM((blocks, fields, 8, width), F32),
+            pltpu.VMEM((4, 16, width), BF16),
+            pltpu.SMEM(order.shape, jnp.int32),
+            pltpu.SemaphoreType.DMA((5,)),
+        ],
+        (order_hbm, now_hbm, prev_hbm, coef_hbm),
+    )
+    left, right, dleft, dright = call(
+        pack_ring_body,
+        "pack_ring",
+        (straight, straight, diag, diag),
+        [HBM] * 5 + [VMEM],
+        (VMEM,) * 4,
+        [
+            pltpu.VMEM((2, fields, depth, LANES), F32),
+            pltpu.VMEM((2, fields, depth, LANES), F32),
+            pltpu.VMEM((2, 2, 4, depth, LANES), BF16),
+            pltpu.SMEM(new_owner.shape, jnp.int32),
+            pltpu.SMEM(order.shape, jnp.int32),
+            pltpu.SemaphoreType.DMA((8,)),
+        ],
+        (owner_hbm, order_hbm, now_hbm, prev_hbm, coef_hbm, edges),
+    )
+
+    swap = [(0, 1), (1, 0)]
+    forward = [(i, (i + 1) % count) for i in range(count)]
+    backward = [(i, (i - 1) % count) for i in range(count)]
+
+    def crossed(by):
+        return [(r * count + i, (1 - r) * count + (i + by) % count) for r in range(2) for i in range(count)]
+
+    y_in = lax.ppermute(y_out, "region", swap)
+    from_right = lax.ppermute(left, "blk", backward)
+    from_dright = lax.ppermute(dleft, ("region", "blk"), crossed(-1))
+    from_left = lax.ppermute(right, "blk", forward)
+    from_dleft = lax.ppermute(dright, ("region", "blk"), crossed(1))
+
+    box, rim = call(
+        local_body,
+        "local",
+        (jax.ShapeDtypeStruct(now.shape, F32), jax.ShapeDtypeStruct((blocks, 8, width), F32)),
+        [VMEM],
+        (VMEM, VMEM),
+        [],
+        (now,),
+    )
+    half = fields // 2
+    part = jax.ShapeDtypeStruct((half, depth, width), F32)
+    codes = jax.ShapeDtypeStruct((half * depth + 8, width), jnp.int16)
+    sums = jax.ShapeDtypeStruct((8, width + 2 * LANES), F32)
+    powers = pltpu.VMEM((8, width), F32)
+    last_a, code_a, near, stepped = call(
+        last_row_a_body,
+        "last_row_a",
+        (part, codes, sums, sums),
+        [SMEM] + [VMEM] * 8,
+        (VMEM,) * 4,
+        [powers],
+        (order, now, prev, coef, y_in, from_right, from_dright, box, rim),
+    )
+    arrived_a = lax.ppermute(code_a, "blk", forward)
+    last_b, code_b = call(
+        last_row_b_body,
+        "last_row_b",
+        (part, codes),
+        [SMEM] + [VMEM] * 9 + [ANY] * 2,
+        (VMEM,) * 2,
+        [powers],
+        (order, now, prev, coef, y_in, from_right, from_dright, box, near, stepped, from_left, from_dleft),
+    )
+    arrived_b = lax.ppermute(code_b, "blk", forward)
+    whole = jax.ShapeDtypeStruct((blocks + 1, fields, depth, width), F32)
+    result = call(
+        first_row_body,
+        "first_row",
+        whole,
+        [SMEM] * 2 + [VMEM] * 10,
+        VMEM,
+        [pltpu.VMEM((8, width + 2 * LANES), F32)] * 2,
+        (new_owner, order, now, prev, coef, y_in, from_left, from_dleft, box, rim, last_a, last_b),
+    )
+    for first, arrived in ((0, arrived_a), (half, arrived_b)):
+        result = call(
+            functools.partial(place_body, first),
+            "place",
+            whole,
+            [VMEM, VMEM, ANY],
+            ANY,
+            [pltpu.VMEM((half, depth, width), F32), pltpu.SemaphoreType.DMA((half,))],
+            (from_left, arrived, result),
+            input_output_aliases={2: 0},
+        )
+    return result[:, None]
+
+
 def solution(mesh):
+    def on_device(*args):
+        blocks = args[0].shape[0]
+        if lax.axis_size("region") == 2 and blocks == 2:
+            return fast_on_device(*args)
+        return general_on_device(*args)
+
     return jax.shard_map(
         on_device,
         mesh=mesh,

time: 75 us -> 30.2 us (0.40)
  other arithmetic: 16.5 us -> 0 us
  starting transfers between devices: 25.5 us -> 11.3 us
  waiting for transfers between devices: 20.6 us -> 6.53 us
  Pallas kernels: 0 us -> 12.1 us
  local copies, waits for them, and re-layouts: 9.23 us -> 0.02 us
  between operations: 2.7 us -> 0.11 us
    ppermute x10 -> x7, waiting for transfers between devices: 20.6 us -> 6.53 us  [the longest x1 3.59 us: fast_on_device(): from_dleft = lax.ppermute(dright, ('region', 'blk'), crossed(1))]
    pallas_call x0 -> x8, Pallas kernels: none -> 12.1 us  [call(): pl.pallas_call(body, out_shape=out_shape, in_specs=in_specs, out_specs=ou...]
    add x6 -> x0, other arithmetic: 10.9 us -> none  [the longest x2 6.98 us: stencil_step(): shifted[..., :width] * lower_mask + extended + shifted[..., 2:] * upper_mask]
    ppermute x10 -> x7, starting transfers between devices: 21.6 us -> 11.3 us  [the longest x1 4.39 us: fast_on_device(): from_dright = lax.ppermute(dleft, ('region', 'blk'), crossed(-1))]
    all_to_all x1 -> x0, starting transfers between devices: 3.92 us -> none  [on_device(): lax.all_to_all(store_local, 'region', split_axis=0, concat_axis=0, tiled=...]
    concatenate x2 -> x0, local copies, waits for them, and re-layouts: 3.89 us -> none  [stencil_step(): extended = jnp.concatenate([before_planes, padded, after_planes], axis=-1)]
    slice x5 -> x0, local copies, waits for them, and re-layouts: 2.73 us -> none  [the longest x1 1.35 us: on_device(): keep_first = (new_owner[0] == own_index).astype(jnp.int32).reshape(1)]
    select_n x4 -> x0, other arithmetic: 2.16 us -> none  [the longest x1 1.39 us: compact(): jnp.where(filled.reshape((slot_count,) + (1,) * (member.ndim - 1)), jnp.t...]
  transfers between devices with their start and end apart: 11 -> 7, of which waited for: 6 -> 3; matrix products, arithmetic and copies ran while one was open for 13% -> 0% of each run, Pallas kernels for 0% -> 33%
where the time goes in v3:
time: 30.2 us; the launch traced here: 30 us
  Pallas kernels  12.1 us (40%)
  starting transfers between devices  11.3 us (37%)
  waiting for transfers between devices  6.53 us (22%)
    pallas_call x8, Pallas kernels, call(): pl.pallas_call(body, out_shape=out_shape, in_specs=in_specs, out_specs=ou...  12.1 us
    ppermute x1, starting transfers between devices, fast_on_device(): from_dright = lax.ppermute(dleft, ('region', 'blk'), crossed(-1))  4.39 us
    ppermute x1, starting transfers between devices, fast_on_device(): from_right = lax.ppermute(left, 'blk', backward)  3.74 us
    ppermute x1, waiting for transfers between devices, fast_on_device(): from_dleft = lax.ppermute(dright, ('region', 'blk'), crossed(1))  3.59 us
    ppermute x1, starting transfers between devices, fast_on_device(): y_in = lax.ppermute(y_out, 'region', swap)  3.03 us
    ppermute x1, waiting for transfers between devices, fast_on_device(): arrived_b = lax.ppermute(code_b, 'blk', forward)  2.75 us
  transfers between devices with their start and end apart: 7, of which 3 were waited for; matrix products, arithmetic and copies ran while one was open for 0% of the time, Pallas kernels for 33%

profile of v3, /device:TPU:0, one launch (start us, length us, event | category | flops | bytes accessed | tf_op | source)
XLA Modules:
  0.0 30.0 jit_solution(691097214551175786)
XLA Ops:
  0.0 1.3 %pack_region.1 = (bf16[5,32,1024]{2,1,0:T(8,128)(2,1)S(1)}, f32[32,1024]{1,0:T(8,128)S(1)}) custom-call(s32[8]{0:T(128)} %bitcast.23, f32[2,4,32,1024]{3,2,1,0:T(8,128)} %bitcast.7, f32[2,4,32,1024]{3,2,1,0:T(8,128)} %bitcast.13, bf16[2,4,32,1024]{3,2,1,0:T(8,128)(2,1)} %bitcast.18), custom_call_target="tpu_custom_call" | custom-call | tf_op jit(solution)/shard_map/pack_region/pallas_call | solution.py:569
  1.3 0.0 copy-start
  1.3 3.0 %collective-permute-start.1 = (bf16[5,32,1024]{2,1,0:T(8,128)(2,1)S(1)}, bf16[5,32,1024]{2,1,0:T(8,128)(2,1)S(1)}, u32[]{:S(2)}, u32[]{:S(2)}) collective-permute-start(bf16[5,32,1024]{2,1,0:T(8,128)(2,1)S(1)} %get-tuple-element.21), channel_id=1, source_target_pairs={{0,16},{16,0},{1,17},{17,1},{2,18},{18,2},{3,19},{19,3},{4,20},{20... | collective-permute-start | bytes 983048 | tf_op jit(solution)/shard_map/ppermute | solution.py:622
  4.3 0.0 copy-start.1
  4.3 0.0 copy-start.2
  4.3 0.0 copy-start.3
  4.3 1.3 %pack_ring.1 = (bf16[144,128]{1,0:T(8,128)(2,1)S(1)}, bf16[144,128]{1,0:T(8,128)(2,1)S(1)}, bf16[64,128]{1,0:T(8,128)(2,1)S(1)}, bf16[64,128]{1,0:T(8,128)(2,1)S(1)}) custom-call(s32[2]{0:T(128)} %owner_ref.1, s32[8]{0:T(128)} %bitcast.24, f32[2,4,32,1024]{3,2,1,0:T(8,128)} %bitcast.8, f32[2,4,32,1024]{3,2,1,0:T(8,128)} %bitcast.14, ...), custom_call_target="tpu_custom_call" | custom-call | tf_op jit(solution)/shard_map/pack_ring/pallas_call | solution.py:569
  5.6 3.7 %collective-permute-start.2 = (bf16[144,128]{1,0:T(8,128)(2,1)S(1)}, bf16[144,128]{1,0:T(8,128)(2,1)S(1)}, u32[]{:S(2)}, u32[]{:S(2)}) collective-permute-start(bf16[144,128]{1,0:T(8,128)(2,1)S(1)} %get-tuple-element.22), channel_id=1, source_target_pairs={{0,15},{1,0},{2,1},{3,2},{4,3},{5,4},{6,5},{7,6},{8,7},{9,8},{10,9... | collective-permute-start | bytes 110600 | tf_op jit(solution)/shard_map/ppermute | solution.py:623
  9.4 0.0 collective-permute-start
  9.4 4.4 %collective-permute-start.3 = (bf16[64,128]{1,0:T(8,128)(2,1)S(1)}, bf16[64,128]{1,0:T(8,128)(2,1)S(1)}, u32[]{:S(2)}, u32[]{:S(2)}) collective-permute-start(bf16[64,128]{1,0:T(8,128)(2,1)S(1)} %get-tuple-element.23), channel_id=1, source_target_pairs={{0,31},{1,16},{2,17},{3,18},{4,19},{5,20},{6,21},{7,22},{8,23},{9,... | collective-permute-start | bytes 49160 | tf_op jit(solution)/shard_map/ppermute | solution.py:624
  13.8 0.0 collective-permute-start.4
  13.8 0.0 copy-done
  13.8 1.3 %local.1 = (f32[2,4,32,1024]{3,2,1,0:T(8,128)S(1)}, f32[2,8,1024]{2,1,0:T(8,128)S(1)}) custom-call(f32[2,4,32,1024]{3,2,1,0:T(8,128)S(1)} %bitcast.9), custom_call_target="tpu_custom_call" | custom-call | tf_op jit(solution)/shard_map/local/pallas_call | solution.py:569
  15.0 0.2 collective-permute-done.3.diag_ref
  15.2 0.0 collective-permute-done.2.straight_ref
  15.2 0.0 collective-permute-done.1.y_ref
  15.2 0.0 copy-done.1
  15.2 0.0 copy-done.2
  15.2 0.0 copy-done.3
  15.3 1.6 %last_row_a.1 = (f32[2,32,1024]{2,1,0:T(8,128)S(1)}, s16[72,1024]{1,0:T(8,128)(2,1)S(1)}, f32[8,1280]{1,0:T(8,128)S(1)}, f32[8,1280]{1,0:T(8,128)S(1)}) custom-call(s32[8]{0:T(128)S(1)} %bitcast.25, f32[2,4,32,1024]{3,2,1,0:T(8,128)S(1)} %bitcast.10, f32[2,4,32,1024]{3,2,1,0:T(8,128)S(1)} %bitcast.15, bf16[2,4,32,1024]{3,2,1,0:T(8,128)(2,1)S(1)} %bitcast.20, ...), custom_call_target="tpu_custom_call" | custom-call | tf_op jit(solution)/shard_map/last_row_a/pallas_call | solution.py:569
  16.9 0.1 collective-permute-start.6
  16.9 3.6 %collective-permute-done.4.early_b.diag_ref = bf16[64,128]{1,0:T(8,128)(2,1)S(1)} collective-permute-done((bf16[64,128]{1,0:T(8,128)(2,1)S(1)}, bf16[64,128]{1,0:T(8,128)(2,1)S(1)}, u32[]{:S(2)}, u32[]{:S(2)}) %collective-permute-start.4) | collective-permute-done | bytes 16416 | tf_op jit(solution)/shard_map/ppermute | solution.py:626
  20.5 0.0 collective-permute-done.early_a.straight_ref
  20.5 0.0 copy-start.4
  20.5 1.3 %last_row_b.1 = (f32[2,32,1024]{2,1,0:T(8,128)S(1)}, s16[72,1024]{1,0:T(8,128)(2,1)S(1)}) custom-call(s32[8]{0:T(128)S(1)} %bitcast.26, f32[2,4,32,1024]{3,2,1,0:T(8,128)S(1)} %bitcast.11, f32[2,4,32,1024]{3,2,1,0:T(8,128)S(1)} %bitcast.16, bf16[2,4,32,1024]{3,2,1,0:T(8,128)(2,1)S(1)} %bitcast.21, bf16[5,32,1024]{2,1,0:T(8,128)(2,1)S(1)} %collective-permute-done.1.y_ref, ...), custom_call_target="tpu_custom_call" | custom-call | tf_op jit(solution)/shard_map/last_row_b/pallas_call | solution.py:569
  21.9 0.1 collective-permute-start.5
  21.9 0.0 copy-done.4
  21.9 3.6 %first_row.1.partial_ref = f32[3,4,32,1024]{3,2,1,0:T(8,128)} custom-call(s32[2]{0:T(128)S(1)} %copy-done.4, s32[8]{0:T(128)S(1)} %bitcast.27, f32[2,4,32,1024]{3,2,1,0:T(8,128)S(1)} %bitcast.12, f32[2,4,32,1024]{3,2,1,0:T(8,128)S(1)} %bitcast.17, bf16[2,4,32,1024]{3,2,1,0:T(8,128)(2,1)S(1)} %bitcast.22, ...), custom_call_target="tpu_custom_call" | custom-call | tf_op jit(solution)/shard_map/first_row/pallas_call | solution.py:569
  25.6 0.0 collective-permute-done.6.code_ref
  25.6 0.9 %place.2.partial_ref = f32[3,4,32,1024]{3,2,1,0:T(8,128)} custom-call(bf16[144,128]{1,0:T(8,128)(2,1)S(1)} %collective-permute-done.early_a.straight_ref, s16[72,1024]{1,0:T(8,128)(2,1)S(1)} %collective-permute-done.6.code_ref, f32[3,4,32,1024]{3,2,1,0:T(8,128)} %first_row.1.partial_ref), custom_call_target="tpu_custom_call", output_to_operand_aliasing={{}: (2, {})} | custom-call | tf_op jit(solution)/shard_map/place/pallas_call | solution.py:569
  26.4 2.8 %collective-permute-done.5.code_ref = s16[72,1024]{1,0:T(8,128)(2,1)S(1)} collective-permute-done((s16[72,1024]{1,0:T(8,128)(2,1)S(1)}, s16[72,1024]{1,0:T(8,128)(2,1)S(1)}, u32[]{:S(2)}, u32[]{:S(2)}) %collective-permute-start.5) | collective-permute-done | bytes 147488 | tf_op jit(solution)/shard_map/ppermute | solution.py:661
  29.2 0.9 %place.3 = f32[3,4,32,1024]{3,2,1,0:T(8,128)} custom-call(bf16[144,128]{1,0:T(8,128)(2,1)S(1)} %collective-permute-done.early_a.straight_ref, s16[72,1024]{1,0:T(8,128)(2,1)S(1)} %collective-permute-done.5.code_ref, f32[3,4,32,1024]{3,2,1,0:T(8,128)} %place.2.partial_ref), custom_call_target="tpu_custom_call", output_to_operand_aliasing={{}: (2, {})} | custom-call | tf_op jit(solution)/shard_map/place/pallas_call | solution.py:569
Async XLA Ops:
  1.3 12.5 %copy-start = (f32[2,1,4,32,1024]{4,3,2,1,0:T(8,128)S(1)}, f32[2,1,4,32,1024]{4,3,2,1,0:T(8,128)}, u32[]{:S(2)}) copy-start(f32[2,1,4,32,1024]{4,3,2,1,0:T(8,128)} %param.5) | copy-start | bytes 3145732
  1.3 13.9 %collective-permute-start.1 = (bf16[5,32,1024]{2,1,0:T(8,128)(2,1)S(1)}, bf16[5,32,1024]{2,1,0:T(8,128)(2,1)S(1)}, u32[]{:S(2)}, u32[]{:S(2)}) collective-permute-start(bf16[5,32,1024]{2,1,0:T(8,128)(2,1)S(1)} %get-tuple-element.21), channel_id=1, source_target_pairs={{0,16},{16,0},{1,17},{17,1},{2,18},{18,2},{3,19},{19,3},{4,20},{20... | collective-permute-start | bytes 983048 | tf_op jit(solution)/shard_map/ppermute | solution.py:622
  4.3 10.9 %copy-start.1 = (f32[2,1,4,32,1024]{4,3,2,1,0:T(8,128)S(1)}, f32[2,1,4,32,1024]{4,3,2,1,0:T(8,128)}, u32[]{:S(2)}) copy-start(f32[2,1,4,32,1024]{4,3,2,1,0:T(8,128)} %param.6) | copy-start | bytes 3145732
  4.3 10.9 %copy-start.2 = (bf16[1,1,2,4,32,1024]{5,4,3,2,1,0:T(8,128)(2,1)S(1)}, bf16[1,1,2,4,32,1024]{5,4,3,2,1,0:T(8,128)(2,1)}, u32[]{:S(2)}) copy-start(bf16[1,1,2,4,32,1024]{5,4,3,2,1,0:T(8,128)(2,1)} %param.7) | copy-start | bytes 1572868
  4.3 10.9 %copy-start.3 = (s32[1,1,8]{2,1,0:T(1,128)S(1)}, s32[1,1,8]{2,1,0:T(1,128)}, u32[]{:S(2)}) copy-start(s32[1,1,8]{2,1,0:T(1,128)} %param.8) | copy-start | bytes 100
  5.6 9.6 %collective-permute-start.2 = (bf16[144,128]{1,0:T(8,128)(2,1)S(1)}, bf16[144,128]{1,0:T(8,128)(2,1)S(1)}, u32[]{:S(2)}, u32[]{:S(2)}) collective-permute-start(bf16[144,128]{1,0:T(8,128)(2,1)S(1)} %get-tuple-element.22), channel_id=1, source_target_pairs={{0,15},{1,0},{2,1},{3,2},{4,3},{5,4},{6,5},{7,6},{8,7},{9,8},{10,9... | collective-permute-start | bytes 110600 | tf_op jit(solution)/shard_map/ppermute | solution.py:623
  9.4 11.2 %collective-permute-start = (bf16[144,128]{1,0:T(8,128)(2,1)S(1)}, bf16[144,128]{1,0:T(8,128)(2,1)S(1)}, u32[]{:S(2)}, u32[]{:S(2)}) collective-permute-start(bf16[144,128]{1,0:T(8,128)(2,1)S(1)} %get-tuple-element.20), channel_id=1, source_target_pairs={{0,1},{1,2},{2,3},{3,4},{4,5},{5,6},{6,7},{7,8},{8,9},{9,10},{10,1... | collective-permute-start | bytes 110600 | tf_op jit(solution)/shard_map/ppermute | solution.py:625
  9.4 5.8 %collective-permute-start.3 = (bf16[64,128]{1,0:T(8,128)(2,1)S(1)}, bf16[64,128]{1,0:T(8,128)(2,1)S(1)}, u32[]{:S(2)}, u32[]{:S(2)}) collective-permute-start(bf16[64,128]{1,0:T(8,128)(2,1)S(1)} %get-tuple-element.23), channel_id=1, source_target_pairs={{0,31},{1,16},{2,17},{3,18},{4,19},{5,20},{6,21},{7,22},{8,23},{9,... | collective-permute-start | bytes 49160 | tf_op jit(solution)/shard_map/ppermute | solution.py:624
  13.8 6.8 %collective-permute-start.4 = (bf16[64,128]{1,0:T(8,128)(2,1)S(1)}, bf16[64,128]{1,0:T(8,128)(2,1)S(1)}, u32[]{:S(2)}, u32[]{:S(2)}) collective-permute-start(bf16[64,128]{1,0:T(8,128)(2,1)S(1)} %get-tuple-element.28), channel_id=1, source_target_pairs={{0,17},{1,18},{2,19},{3,20},{4,21},{5,22},{6,23},{7,24},{8,25},{9,... | collective-permute-start | bytes 49160 | tf_op jit(solution)/shard_map/ppermute | solution.py:626
  16.9 8.7 %collective-permute-start.6 = (s16[72,1024]{1,0:T(8,128)(2,1)S(1)}, s16[72,1024]{1,0:T(8,128)(2,1)S(1)}, u32[]{:S(2)}, u32[]{:S(2)}) collective-permute-start(s16[72,1024]{1,0:T(8,128)(2,1)S(1)} %get-tuple-element.30), channel_id=1, source_target_pairs={{0,1},{1,2},{2,3},{3,4},{4,5},{5,6},{6,7},{7,8},{8,9},{9,10},{10,1... | collective-permute-start | bytes 442376 | tf_op jit(solution)/shard_map/ppermute | solution.py:651
  20.5 1.4 %copy-start.4 = (s32[2]{0:T(128)S(1)}, s32[2]{0:T(128)}, u32[]{:S(2)}) copy-start(s32[2]{0:T(128)} %owner_ref.1) | copy-start | bytes 28
  21.9 7.3 %collective-permute-start.5 = (s16[72,1024]{1,0:T(8,128)(2,1)S(1)}, s16[72,1024]{1,0:T(8,128)(2,1)S(1)}, u32[]{:S(2)}, u32[]{:S(2)}) collective-permute-start(s16[72,1024]{1,0:T(8,128)(2,1)S(1)} %get-tuple-element.29), channel_id=1, source_target_pairs={{0,1},{1,2},{2,3},{3,4},{4,5},{5,6},{6,7},{7,8},{8,9},{9,10},{10,1... | collective-permute-start | bytes 442376 | tf_op jit(solution)/shard_map/ppermute | solution.py:661

commit v4 on v2

v4 whole, which is shorter than its diff:
```python
import functools

import jax
import jax.numpy as jnp
from jax import lax
from jax.experimental import pallas as pl
from jax.experimental.pallas import tpu as pltpu
from jax.sharding import PartitionSpec as P

STEPS = 2
LANES = 128
F32 = jnp.float32
BF16 = jnp.bfloat16
VMEM = pl.BlockSpec(memory_space=pltpu.VMEM)
SMEM = pl.BlockSpec(memory_space=pltpu.SMEM)
ANY = pl.BlockSpec(memory_space=pl.ANY)
HBM = pl.BlockSpec(memory_space=pltpu.HBM)


def extended_2(block, sides, width, periodic):
    for axis, dim in sides:
        count = lax.axis_size(axis)
        forward = [(i, i + 1) for i in range(count - 1)]
        if periodic:
            forward.append((count - 1, 0))
        backward = [(target, source) for source, target in forward]
        low = lax.ppermute(
            lax.slice_in_dim(block, block.shape[dim] - width, None, axis=dim), axis, forward
        )
        high = lax.ppermute(lax.slice_in_dim(block, 0, width, axis=dim), axis, backward)
        block = jnp.concatenate([low, block, high], axis=dim)
    return block


def shifted_2(value, axis, by):
    devices = lax.axis_size(axis)
    return lax.ppermute(value, axis, [(i, (i + by) % devices) for i in range(devices)])


def stencil_step(state_now, state_prev, coefficient, live_count):
    slot_count, field_count, edge_cells, plane_cells = state_now.shape
    padded = extended_2(state_now, (("region", 2),), 1, False)
    first_planes = padded[..., :edge_cells]
    last_planes = padded[..., plane_cells - edge_cells :]
    last_live = jnp.take(last_planes, live_count - 1, axis=0)
    rim_pair = jnp.stack([first_planes[0], last_live], axis=2)
    spread = extended_2(rim_pair.astype(jnp.bfloat16), (("blk", 2),), 1, True).astype(
        rim_pair.dtype
    )
    left_rim = spread[:, :, 0]
    right_rim = spread[:, :, 3]
    before_planes = jnp.concatenate([left_rim[None], last_planes[:-1]], axis=0)
    after_planes = jnp.pad(first_planes[1:], ((0, 1), (0, 0), (0, 0), (0, 0)))
    slot_ids = jnp.arange(slot_count)
    after_planes = jnp.where(
        (slot_ids == live_count - 1)[:, None, None, None], right_rim[None], after_planes
    )
    extended = jnp.concatenate([before_planes, padded, after_planes], axis=-1)
    width = extended.shape[-1]
    column = jnp.arange(width) % edge_cells
    lower_mask = (column != 0).astype(jnp.float32)
    upper_mask = (column != edge_cells - 1).astype(jnp.float32)
    margin = ((0, 0), (0, 0), (0, 0), (1, 1))
    shifted = jnp.pad(extended, margin)
    summed = shifted[..., :width] * lower_mask + extended + shifted[..., 2:] * upper_mask
    summed = (
        summed[..., : -2 * edge_cells]
        + summed[..., edge_cells:-edge_cells]
        + summed[..., 2 * edge_cells :]
    )
    box_sum = summed[:, :, :-2] + summed[:, :, 1:-1] + summed[:, :, 2:]
    laplace = box_sum - 27.0 * state_now
    return 2.0 * state_now - state_prev + coefficient.astype(jnp.float32) * laplace


def compact(members, valid_flags):
    slot_count = valid_flags.shape[0]
    place_index = jnp.cumsum(valid_flags) - 1
    target = jnp.arange(slot_count)
    chooser = (valid_flags[None, :] == 1) & (place_index[None, :] == target[:, None])
    source = jnp.sum(jnp.where(chooser, target[None, :], 0), axis=1)
    filled = jnp.sum(chooser.astype(jnp.int32), axis=1) > 0
    placed = tuple(
        (
            jnp.where(
                filled.reshape((slot_count,) + (1,) * (member.ndim - 1)),
                jnp.take(member, source, axis=0),
                jnp.zeros_like(member),
            )
            for member in members
        )
    )
    return (placed, jnp.sum(valid_flags))


def general_on_device(u_now, u_prev, coef_store, store_map, new_owner):
    state_now = u_now[:, 0]
    state_prev = u_prev[:, 0]
    blocks, fields, edge_cells, plane_cells = state_now.shape
    store_local = coef_store[0, 0]
    arrived = lax.all_to_all(store_local, "region", split_axis=0, concat_axis=0, tiled=True)
    flattened = arrived.reshape((-1,) + arrived.shape[2:])
    inverse = jnp.argsort(store_map[0, 0])
    coefficient = jnp.take(flattened, inverse, axis=0).reshape(
        blocks, fields, edge_cells, plane_cells
    )
    own_index = lax.axis_index("blk")
    goes_right = new_owner[blocks - 1] != own_index
    mark_right = goes_right.astype(jnp.float32).reshape(1)
    middle_flags = jnp.ones((blocks - 2,), jnp.int32)
    keep_first = (new_owner[0] == own_index).astype(jnp.int32).reshape(1)
    keep_last = (new_owner[blocks - 1] == own_index).astype(jnp.int32).reshape(1)
    for step_index in range(STEPS):
        state_now, state_prev = (
            stencil_step(state_now, state_prev, coefficient, blocks),
            state_now,
        )
    from_left = shifted_2((state_now[blocks - 1], mark_right), "blk", 1)
    valid_flags = jnp.concatenate(
        [(from_left[1] > 0.5).astype(jnp.int32), keep_first, middle_flags, keep_last]
    )
    stacked_now = jnp.concatenate([from_left[0][None], state_now], axis=0)
    placed, live_count = compact((stacked_now,), valid_flags)
    result = placed[0]
    return result[:, None]


def lane_ids():
    return lax.broadcasted_iota(jnp.int32, (1, LANES), 1)


def edge_start(lower, depth, size):
    return pl.multiple_of(jnp.where(lower, depth - size, 0), size)


def tag_values(map_ref, region):
    numbers = [map_ref[region * 4 + s] for s in range(4)] + [map_ref[(1 - region) * 4 + s] for s in range(4)]
    return [jnp.zeros((1, LANES), F32) + number.astype(F32) for number in numbers]


def pack_slab_body(coef_ref, slab_ref, sem):
    copy = pltpu.make_async_copy(coef_ref.at[1 - lax.axis_index("region")], slab_ref, sem)
    copy.start()
    copy.wait()


def pack_edges_body(
    owner_hbm, map_hbm, u_ref, p_ref, coef_ref, y_ref, left_ref, right_ref, dleft_ref, dright_ref,
    rows_ref, ue_ref, pe_ref, ce_ref, ua_ref, pa_ref, ca_ref, owner_ref, map_ref, sems
):
    fields = u_ref.shape[1]
    depth = u_ref.shape[2]
    last = u_ref.shape[3] - LANES
    top = depth - 1
    region = lax.axis_index("region")
    lower = region == 0
    other = 1 - region
    edge8 = edge_start(lower, depth, 8)
    edge16 = edge_start(lower, depth, 16)
    copies = [
        pltpu.make_async_copy(map_hbm, map_ref, sems.at[0]),
        pltpu.make_async_copy(u_ref.at[:, :, pl.ds(edge8, 8), :], ue_ref, sems.at[1]),
        pltpu.make_async_copy(p_ref.at[:, :, pl.ds(edge8, 8), :], pe_ref, sems.at[2]),
        pltpu.make_async_copy(coef_ref.at[region, :, pl.ds(edge16, 16), :], ce_ref, sems.at[3]),
        pltpu.make_async_copy(owner_hbm, owner_ref, sems.at[4]),
        pltpu.make_async_copy(u_ref.at[0, :, :, 0:LANES], ua_ref.at[0], sems.at[5]),
        pltpu.make_async_copy(u_ref.at[1, :, :, last : last + LANES], ua_ref.at[1], sems.at[6]),
        pltpu.make_async_copy(p_ref.at[0, :, :, 0:LANES], pa_ref.at[0], sems.at[7]),
        pltpu.make_async_copy(p_ref.at[1, :, :, last : last + LANES], pa_ref.at[1], sems.at[8]),
        pltpu.make_async_copy(coef_ref.at[:, :, :, 0:LANES], ca_ref.at[0], sems.at[9]),
        pltpu.make_async_copy(coef_ref.at[:, :, :, last : last + LANES], ca_ref.at[1], sems.at[10]),
    ]
    for copy in copies:
        copy.start()
    for copy in copies[:4]:
        copy.wait()
    lane = lane_ids()
    own_edge = jnp.where(lower, 7, 0)
    own_next = jnp.where(lower, 6, 1)
    for m in range(2):
        for f in range(fields):
            at = m * fields + f
            near = ue_ref[m, f, pl.ds(own_edge, 1), :]
            rows_ref[at : at + 1, :] = near
            rows_ref[8 + at : 9 + at, :] = ue_ref[m, f, pl.ds(own_next, 1), :]
            rows_ref[16 + at : 17 + at, :] = 2.0 * near - pe_ref[m, f, pl.ds(own_edge, 1), :]
    for s in range(4):
        piece = ce_ref[s].astype(F32)
        rows_ref[24 + s : 25 + s, :] = jnp.where(lower, piece[15:16], piece[0:1])
    tag_rows = tag_values(map_ref, region)
    for i, row in enumerate(tag_rows):
        rows_ref[28:29, i * LANES : (i + 1) * LANES] = row
    rows_ref[29:32, :] = jnp.zeros((3, rows_ref.shape[1]), F32)
    y_ref[...] = rows_ref[...].astype(BF16)
    for copy in copies[4:]:
        copy.wait()
    blank = jnp.zeros((1, LANES), F32)
    flag = blank + jnp.where(owner_ref[1] != lax.axis_index("blk"), 1.0, 0.0).astype(F32)
    for m, lanes, straight_ref, diag_ref in (
        (0, slice(0, LANES), left_ref, dleft_ref),
        (1, slice(last, last + LANES), right_ref, dright_ref),
    ):
        for f in range(fields):
            now = ua_ref[m, f]
            ahead = 2.0 * now - pa_ref[m, f]
            piece = ca_ref[m, region, f].astype(F32)
            if m == 0:
                tile = jnp.where(
                    lane < 64, now, jnp.where(lane < 96, pltpu.roll(ahead, 64, 1), pltpu.roll(piece, 96, 1))
                )
            else:
                tile = jnp.where(
                    lane >= 64, now, jnp.where(lane < 32, pltpu.roll(ahead, 32, 1), pltpu.roll(piece, 64, 1))
                )
            straight_ref[f * depth : (f + 1) * depth, :] = tile.astype(BF16)
        far = [ca_ref[m, other, s].astype(F32) for s in range(4)]
        extra = [jnp.where(lower, piece[0:1], piece[top:depth]) for piece in far] + tag_rows + [flag] + [blank] * 3
        straight_ref[fields * depth : fields * depth + 16, :] = jnp.concatenate(extra, axis=0).astype(BF16)
        plane = jnp.zeros((depth, LANES), F32)
        for s in range(4):
            shift = (32 * s if m == 0 else 32 + 32 * s) % LANES
            moved = pltpu.roll(far[s], shift, 1) if shift else far[s]
            plane = jnp.where((lane >= 32 * s) & (lane < 32 * s + 32), moved, plane)
        diag_ref[0:depth, :] = plane.astype(BF16)
        extra = (
            [rows_ref[m * fields : m * fields + 4, lanes]]
            + [rows_ref[8 + m * fields : 12 + m * fields, lanes]]
            + [rows_ref[16 + m * fields : 20 + m * fields, lanes]]
            + [rows_ref[24:28, lanes]]
            + tag_rows
            + [blank] * 8
        )
        diag_ref[depth : depth + 32, :] = jnp.concatenate(extra, axis=0).astype(BF16)
        rest = diag_ref.shape[0] - depth - 32
        diag_ref[depth + 32 :, :] = jnp.zeros((rest, LANES), BF16)


def nine_sum(tiles, lane, first=0):
    inside = lane % 32
    low = inside != 0
    high = inside != 31
    rows = []
    for tile in tiles:
        rows.append(
            tile
            + jnp.where(low, pltpu.roll(tile, 1, 1), 0.0)
            + jnp.where(high, pltpu.roll(tile, LANES - 1, 1), 0.0)
        )
    up = [pltpu.roll(row, 32, 1) for row in rows]
    down = [pltpu.roll(row, LANES - 32, 1) for row in rows]
    count = len(tiles)
    result = []
    for t in range(count):
        before = up[t] if t == 0 else jnp.where(lane < 32, up[t - 1], up[t])
        after = down[t] if t == count - 1 else jnp.where(lane >= 96, down[t + 1], down[t])
        result.append(rows[t] + before + after)
    return result


def column_sum(tile, row_id, low_row, high_row):
    depth = tile.shape[0]
    above = pltpu.roll(tile, 1, 0)
    below = pltpu.roll(tile, depth - 1, 0)
    return tile + jnp.where(row_id == 0, low_row, above) + jnp.where(row_id == depth - 1, high_row, below)


def local_body(u_ref, p_ref, box0_ref, box1_ref, drift_ref, rim_ref):
    fields, depth, width = u_ref.shape[1:]
    main = width // LANES
    lower = lax.axis_index("region") == 0
    lane = lane_ids()
    row_id = lax.broadcasted_iota(jnp.int32, (depth, 1), 0)
    boxes = (box0_ref, box1_ref)
    for f in range(fields):
        now = [u_ref[m, f, :, tile_at(t)] for m in range(2) for t in range(main)]
        sums = nine_sum(now, lane)
        for i, (tile, total) in enumerate(zip(now, sums)):
            m, t = divmod(i, main)
            lanes = tile_at(t)
            rim_ref[m, f : f + 1, lanes] = jnp.where(lower, total[depth - 1 : depth], total[0:1])
            boxes[m][f, :, lanes] = column_sum(total, row_id, 0.0, 0.0) - 27.0 * tile
            drift_ref[m, f, :, lanes] = 2.0 * tile - p_ref[m, f, :, lanes]
    rim_ref[:, 4:8, :] = jnp.zeros((2, 4, width), F32)


def tile_at(t):
    return slice(t * LANES, (t + 1) * LANES)


def with_sides(m, local, remote, middle):
    return [local] + middle + [remote] if m == 1 else [remote] + middle + [local]


def edge_body(
    m, u_ref, coef_ref, y_ref, straight_ref, diag_ref, beside_ref, rim_ref, box_in, box_ref, lap_ref, side_ref, stepped_ref
):
    fields, depth, width = u_ref.shape[1:]
    main = width // LANES
    region = lax.axis_index("region")
    lower = region == 0
    lane = lane_ids()
    row_id = lax.broadcasted_iota(jnp.int32, (depth, 1), 0)
    beside = 1 - m
    local_lanes = slice(width - LANES, width) if m == 1 else slice(0, LANES)
    border = main - 1 if m == 1 else 0
    side = main + 1 if m == 1 else 0
    facing = lane >= 96 if m == 1 else lane < 32
    halo_base = 0 if m == 1 else fields
    extra_s = straight_ref[fields * depth : fields * depth + 16, :].astype(F32)
    extra_d = diag_ref[depth : depth + 32, :].astype(F32)
    extra_y = y_ref[...].astype(F32)
    tags_s = [extra_s[4 + i : 5 + i] for i in range(8)]
    tags_d = [extra_d[16 + i : 17 + i] for i in range(8)]
    tags_y = [extra_y[28:29, i * LANES : (i + 1) * LANES] for i in range(8)]
    field_id = lax.broadcasted_iota(jnp.int32, (4, LANES), 0).astype(F32)

    planes = []
    for s in range(4):
        tile = straight_ref[s * depth : (s + 1) * depth, :].astype(F32)
        planes.append(pltpu.roll(tile, 32 if m == 1 else 64, 1))
    diag_tile = diag_ref[0:depth, :].astype(F32)
    for s in range(4):
        shift = (-32 * s if m == 1 else 96 - 32 * s) % LANES
        planes.append(pltpu.roll(diag_tile, shift, 1) if shift else diag_tile)

    def edge_tiles(base_y, base_d):
        middle = [extra_y[base_y + m * fields : base_y + m * fields + 4, tile_at(t)] for t in range(main)]
        local = extra_y[base_y + beside * fields : base_y + beside * fields + 4, local_lanes]
        return with_sides(m, local, extra_d[base_d : base_d + 4], middle)

    near = edge_tiles(0, 0)
    beyond = edge_tiles(8, 4)
    ahead = edge_tiles(16, 8)

    def other_row(s, lanes):
        piece = coef_ref[1 - region, s, :, lanes].astype(F32)
        return jnp.where(lower, piece[0:1], piece[depth - 1 : depth])

    def edge_coef(lanes, base):
        total = jnp.zeros((4, LANES), F32)
        for s in range(4):
            total = total + jnp.where(tags_y[s] == field_id + base, extra_y[24 + s : 25 + s, lanes], 0.0)
            total = total + jnp.where(tags_y[4 + s] == field_id + base, other_row(s, lanes), 0.0)
        return total

    corner = jnp.zeros((4, LANES), F32)
    for s in range(4):
        corner = corner + jnp.where(tags_d[s] == field_id + halo_base, extra_d[12 + s : 13 + s], 0.0)
        corner = corner + jnp.where(tags_d[4 + s] == field_id + halo_base, extra_s[s : s + 1], 0.0)
    edge_c = with_sides(
        m, edge_coef(local_lanes, beside * fields), corner, [edge_coef(tile_at(t), m * fields) for t in range(main)]
    )
    near_sum = nine_sum(near, lane)
    beyond_sum = nine_sum(beyond, lane)

    def rows(t, f):
        row = near_sum[t][f : f + 1]
        return jnp.where(lower, 0.0, row), jnp.where(lower, row, 0.0)

    own, outer = [], []
    for f in range(fields):
        inner = u_ref[m, f, :, tile_at(border)]
        remote = straight_ref[f * depth : (f + 1) * depth, :].astype(F32)
        sums = nine_sum(with_sides(m, remote, remote, [inner])[1:] if m == 1 else [remote, inner], lane)
        inner_sum, remote_sum = (sums[0], sums[1]) if m == 1 else (sums[1], sums[0])
        own.append(jnp.where(lower, inner_sum[depth - 1 : depth], inner_sum[0:1]))
        outer.append(jnp.where(lower, remote_sum[depth - 1 : depth], remote_sum[0:1]))
        halo_c = jnp.zeros((depth, LANES), F32)
        for i in range(8):
            halo_c = halo_c + jnp.where(tags_s[i] == F32(halo_base + f), planes[i], 0.0)
        low_row, high_row = rows(side, f)
        lap = column_sum(remote_sum, row_id, low_row, high_row) - 27.0 * remote
        side_ref[f] = pltpu.roll(remote, 64 if m == 1 else 96, 1) + halo_c * lap
        for t in range(main):
            low_row, high_row = rows(t + 1, f)
            if t == border:
                box = box_in[f, :, tile_at(t)]
                box = box + jnp.where(row_id == 0, low_row, 0.0) + jnp.where(row_id == depth - 1, high_row, 0.0)
                whole = column_sum(inner_sum, row_id, low_row, high_row) - 27.0 * inner
                box_ref[f, :, tile_at(t)] = jnp.where(facing, whole, box)
            else:
                box_ref[f, 0:1, tile_at(t)] = box_in[f, 0:1, tile_at(t)] + low_row
                box_ref[f, depth - 1 : depth, tile_at(t)] = box_in[f, depth - 1 : depth, tile_at(t)] + high_row
        lap = beside_ref[f, :, local_lanes]
        if m == 1:
            low_row, high_row = rows(0, f)
            lap = lap + jnp.where(row_id == 0, low_row, 0.0) + jnp.where(row_id == depth - 1, high_row, 0.0)
        lap_ref[f] = lap
    rims = with_sides(
        m,
        rim_ref[beside, 0:4, local_lanes],
        jnp.concatenate(outer, axis=0),
        [rim_ref[m, 0:4, tile_at(t)] for t in range(main)],
    )
    rims[border + 1] = jnp.where(facing, jnp.concatenate(own, axis=0), rims[border + 1])
    stepped = []
    for t in range(main + 2):
        box = near_sum[t] + beyond_sum[t] + rims[t]
        stepped.append(ahead[t] + edge_c[t] * (box - 27.0 * near[t]))
    stepped_sum = nine_sum(stepped, lane)
    for t in range(main + 2):
        stepped_ref[0:4, tile_at(t)] = stepped_sum[t]
    stepped_ref[4:8, :] = jnp.zeros((4, width + 2 * LANES), F32)


def steps(m, some, map_ref, u_ref, coef_ref, slab_ref, box_ref, drift_ref, lap_ref, side_ref, stepped_ref, write):
    fields, depth, width = u_ref.shape[1:]
    main = width // LANES
    region = lax.axis_index("region")
    lower = region == 0
    lane = lane_ids()
    row_id = lax.broadcasted_iota(jnp.int32, (depth, 1), 0)
    beside = 1 - m
    local_lanes = slice(width - LANES, width) if m == 1 else slice(0, LANES)
    numbers = [map_ref[q] for q in range(8)]

    def piece_of(number):
        place = jnp.int32(0)
        for q in range(8):
            place = jnp.where(numbers[q] == number, q, place)
        slot = place & 3
        held = (place >> 2) == region

        def tile(lanes):
            return jnp.where(held, coef_ref[region, slot, :, lanes], slab_ref[slot, :, lanes]).astype(F32)

        return tile

    for f in some:
        coef = piece_of(m * fields + f)
        coefs = [coef(tile_at(t)) for t in range(main)]
        local = drift_ref[beside, f, :, local_lanes] + piece_of(beside * fields + f)(local_lanes) * lap_ref[f]
        middle = [drift_ref[m, f, :, tile_at(t)] + coefs[t] * box_ref[f, :, tile_at(t)] for t in range(main)]
        now = with_sides(m, local, side_ref[f], middle)
        sums = nine_sum(now, lane)
        for t in range(main):
            row = stepped_ref[f : f + 1, tile_at(t + 1)]
            low_row, high_row = jnp.where(lower, 0.0, row), jnp.where(lower, row, 0.0)
            lap = column_sum(sums[t + 1], row_id, low_row, high_row) - 27.0 * middle[t]
            write(f, tile_at(t), 2.0 * middle[t] - u_ref[m, f, :, tile_at(t)] + coefs[t] * lap)


CODES = 32000.0


def code_writer(row_ref, code_ref, power_ref, first, count, depth):
    def write(f, lanes, value):
        at = f - first
        row_ref[at, :, lanes] = value
        size = jnp.maximum(jnp.max(jnp.abs(value), axis=0, keepdims=True), 1e-30)
        power = jnp.ceil(jnp.log2(size))
        code = jnp.floor(value * (CODES * jnp.exp2(-power)) + 0.5)
        code_ref[at * depth : (at + 1) * depth, lanes] = code.astype(jnp.int32).astype(jnp.int16)
        power_ref[at : at + 1, lanes] = power

    return write


def write_powers(power_ref, code_ref, count, depth):
    power_ref[count:8, :] = jnp.zeros((8 - count, power_ref.shape[1]), F32)
    code_ref[count * depth : count * depth + 8, :] = power_ref[...].astype(jnp.int32).astype(jnp.int16)


def last_row_body(
    first, map_ref, u_ref, coef_ref, slab_ref, box_ref, drift_ref, lap_ref, side_ref, stepped_ref, *rest
):
    row_ref, code_ref, power_ref = rest[-3:]
    count, depth, _ = row_ref.shape
    write = code_writer(row_ref, code_ref, power_ref, first, count, depth)
    some = range(first, first + count)
    steps(1, some, map_ref, u_ref, coef_ref, slab_ref, box_ref, drift_ref, lap_ref, side_ref, stepped_ref, write)
    write_powers(power_ref, code_ref, count, depth)


def first_row_body(
    owner_ref, map_ref, u_ref, coef_ref, slab_ref, box_ref, drift_ref, lap_ref, side_ref, stepped_ref, straight_ref,
    last_a_ref, last_b_ref, out_ref
):
    fields, depth = u_ref.shape[1:3]
    extra = straight_ref[fields * depth : fields * depth + 16, :].astype(F32)
    arrives = extra[12:13] > 0.5
    keeps = owner_ref[1] == lax.axis_index("blk")
    half = last_a_ref.shape[0]

    def write(f, lanes, value):
        mine = last_a_ref[f, :, lanes] if f < half else last_b_ref[f - half, :, lanes]
        kept = jnp.where(keeps, mine, 0.0)
        out_ref[0, f, :, lanes] = value
        out_ref[1, f, :, lanes] = jnp.where(arrives, value, kept)
        out_ref[2, f, :, lanes] = jnp.where(arrives, kept, 0.0)

    some = range(fields)
    steps(0, some, map_ref, u_ref, coef_ref, slab_ref, box_ref, drift_ref, lap_ref, side_ref, stepped_ref, write)


def place_body(first, straight_ref, code_ref, partial_ref, out_ref, row_ref, sems):
    count, depth, width = row_ref.shape
    rows = straight_ref.shape[0]
    flag = jnp.max(straight_ref[rows - 16 : rows, :].astype(F32)[12:13])

    @pl.when(flag > 0.5)
    def _():
        scale = jnp.exp2(code_ref[count * depth : count * depth + 8, :].astype(jnp.int32).astype(F32)) * (1.0 / CODES)
        copies = []
        for f in range(count):
            code = code_ref[f * depth : (f + 1) * depth, :].astype(jnp.int32).astype(F32)
            row_ref[f] = code * scale[f : f + 1]
            copy = pltpu.make_async_copy(row_ref.at[f], out_ref.at[0, first + f], sems.at[f])
            copy.start()
            copies.append(copy)
        for copy in copies:
            copy.wait()


def fast_on_device(u_now, u_prev, coef_store, store_map, new_owner):
    blocks, _, fields, depth, width = u_now.shape
    now = u_now.reshape(blocks, fields, depth, width)
    prev = u_prev.reshape(blocks, fields, depth, width)
    coef = coef_store[0, 0]
    count = lax.axis_size("blk")
    order = store_map.reshape(-1)
    owner_hbm, order_hbm, now_hbm, prev_hbm, coef_hbm = (
        pltpu.with_memory_space_constraint(array, pltpu.HBM) for array in (new_owner, order, now, prev, coef)
    )
    params = pltpu.CompilerParams(vmem_limit_bytes=48 * 1024 * 1024)

    def call(body, name, out_shape, in_specs, out_specs, scratch, args, **options):
        return pl.pallas_call(
            body,
            out_shape=out_shape,
            in_specs=in_specs,
            out_specs=out_specs,
            scratch_shapes=scratch,
            compiler_params=params,
            name=name,
            **options,
        )(*args)

    slab_shape = jax.ShapeDtypeStruct(coef.shape[1:], BF16)
    slab_out = call(pack_slab_body, "pack_slab", slab_shape, [HBM], VMEM, [pltpu.SemaphoreType.DMA], (coef_hbm,))
    message = jax.ShapeDtypeStruct((fields * depth + 16, LANES), BF16)
    y_out, left, right, dleft, dright = call(
        pack_edges_body,
        "pack_edges",
        (jax.ShapeDtypeStruct((depth, width), BF16),) + (message,) * 4,
        [HBM] * 5,
        (VMEM,) * 5,
        [
            pltpu.VMEM((depth, width), F32),
            pltpu.VMEM((blocks, fields, 8, width), F32),
            pltpu.VMEM((blocks, fields, 8, width), F32),
            pltpu.VMEM((4, 16, width), BF16),
            pltpu.VMEM((2, fields, depth, LANES), F32),
            pltpu.VMEM((2, fields, depth, LANES), F32),
            pltpu.VMEM((2, 2, 4, depth, LANES), BF16),
            pltpu.SMEM(new_owner.shape, jnp.int32),
            pltpu.SMEM(order.shape, jnp.int32),
            pltpu.SemaphoreType.DMA((11,)),
        ],
        (owner_hbm, order_hbm, now_hbm, prev_hbm, coef_hbm),
    )

    swap = [(0, 1), (1, 0)]
    forward = [(i, (i + 1) % count) for i in range(count)]
    backward = [(i, (i - 1) % count) for i in range(count)]

    def crossed(by):
        return [(r * count + i, (1 - r) * count + (i + by) % count) for r in range(2) for i in range(count)]

    slab = lax.ppermute(slab_out, "region", swap)
    y_in = lax.ppermute(y_out, "region", swap)
    from_right = lax.ppermute(left, "blk", backward)
    from_dright = lax.ppermute(dleft, ("region", "blk"), crossed(-1))
    from_left = lax.ppermute(right, "blk", forward)
    from_dleft = lax.ppermute(dright, ("region", "blk"), crossed(1))

    row = jax.ShapeDtypeStruct((fields, depth, width), F32)
    box0, box1, drift, rim = call(
        local_body,
        "local",
        (row, row, jax.ShapeDtypeStruct(now.shape, F32), jax.ShapeDtypeStruct((blocks, 8, width), F32)),
        [VMEM] * 2,
        (VMEM,) * 4,
        [],
        (now, prev),
    )
    tiles = jax.ShapeDtypeStruct((fields, depth, LANES), F32)
    edge_outs = (row, tiles, tiles, jax.ShapeDtypeStruct((8, width + 2 * LANES), F32))

    def edges(m, straight, diag, beside, own):
        return call(
            functools.partial(edge_body, m),
            "edges",
            edge_outs,
            [VMEM] * 8,
            (VMEM,) * 4,
            [],
            (now, coef, y_in, straight, diag, beside, rim, own),
            input_output_aliases={7: 0},
        )

    half = fields // 2
    part = jax.ShapeDtypeStruct((half, depth, width), F32)
    codes = jax.ShapeDtypeStruct((half * depth + 8, width), jnp.int16)

    def last_row(first, *early):
        return call(
            functools.partial(last_row_body, first),
            "last_row",
            (part, codes),
            [SMEM] + [VMEM] * 8 + [ANY] * len(early),
            (VMEM,) * 2,
            [pltpu.VMEM((8, width), F32)],
            (order, now, coef, slab, box1, drift, lap1, side1, stepped1) + early,
        )

    box1, lap1, side1, stepped1 = edges(1, from_right, from_dright, box0, box1)
    last_a, code_a = last_row(0)
    arrived_a = lax.ppermute(code_a, "blk", forward)
    last_b, code_b = last_row(half, from_left, from_dleft)
    arrived_b = lax.ppermute(code_b, "blk", forward)
    box0, lap0, side0, stepped0 = edges(0, from_left, from_dleft, box1, box0)
    whole = jax.ShapeDtypeStruct((blocks + 1, fields, depth, width), F32)
    result = call(
        first_row_body,
        "first_row",
        whole,
        [SMEM] * 2 + [VMEM] * 11,
        VMEM,
        [],
        (new_owner, order, now, coef, slab, box0, drift, lap0, side0, stepped0, from_left, last_a, last_b),
    )
    for first, arrived in ((0, arrived_a), (half, arrived_b)):
        result = call(
            functools.partial(place_body, first),
            "place",
            whole,
            [VMEM, VMEM, ANY],
            ANY,
            [pltpu.VMEM((half, depth, width), F32), pltpu.SemaphoreType.DMA((half,))],
            (from_left, arrived, result),
            input_output_aliases={2: 0},
        )
    return result[:, None]


def solution(mesh):
    def on_device(*args):
        blocks = args[0].shape[0]
        if lax.axis_size("region") == 2 and blocks == 2:
            return fast_on_device(*args)
        return general_on_device(*args)

    return jax.shard_map(
        on_device,
        mesh=mesh,
        in_specs=(
            P("blk", "region", None, None, None),
            P("blk", "region", None, None, None),
            P("blk", "region", None, None, None, None),
            P("blk", "region", None),
            P("blk"),
        ),
        out_specs=P("blk", "region", None, None, None),
        check_vma=False,
    )
```

time: 28.7 us -> 27.9 us (0.972)
  waiting for transfers between devices: 9.9 us -> 6.8 us
  Pallas kernels: 9.29 us -> 11.6 us
    ppermute x1 -> x3, starting transfers between devices: 0.06 us -> 3.15 us  [the longest x1 3.03 us: fast_on_device(): slab = lax.ppermute(slab_out, 'region', swap)]
    ppermute x1, waiting for transfers between devices: 3.5 us -> 0.91 us  [fast_on_device(): from_dleft = lax.ppermute(dright, ('region', 'blk'), crossed(1))]
    ppermute x1, starting transfers between devices: 3.05 us -> 0.51 us  [fast_on_device(): y_in = lax.ppermute(y_out, 'region', swap)]
    pallas_call x4 -> x10, Pallas kernels: 9.29 us -> 11.6 us  [call(): pl.pallas_call(body, out_shape=out_shape, in_specs=in_specs, out_specs=ou...]
    ppermute x1, waiting for transfers between devices: 0.01 us -> 1.76 us  [fast_on_device(): from_left = lax.ppermute(right, 'blk', forward)]
    ppermute x1 -> x3, waiting for transfers between devices: 4.73 us -> 3.08 us  [the longest x1 3.03 us: fast_on_device(): arrived_b = lax.ppermute(code_b, 'blk', forward)]
    ppermute x1, starting transfers between devices: 0.15 us -> 1.65 us  [fast_on_device(): from_dright = lax.ppermute(dleft, ('region', 'blk'), crossed(-1))]
    ppermute x1, starting transfers between devices: 1.6 us -> 0.1 us  [fast_on_device(): from_dleft = lax.ppermute(dright, ('region', 'blk'), crossed(1))]
  transfers between devices with their start and end apart: 6 -> 8, of which waited for: 3 -> 5; matrix products, arithmetic and copies ran while one was open for 0% -> 0% of each run, Pallas kernels for 14% -> 35%
where the time goes in v4:
time: 27.9 us; the launch traced here: 27.7 us
  Pallas kernels  11.6 us (42%)
  starting transfers between devices  9.14 us (33%)
  waiting for transfers between devices  6.8 us (24%)
    pallas_call x10, Pallas kernels, call(): pl.pallas_call(body, out_shape=out_shape, in_specs=in_specs, out_specs=ou...  11.6 us
    ppermute x1, starting transfers between devices, fast_on_device(): from_right = lax.ppermute(left, 'blk', backward)  3.74 us
    ppermute x1, starting transfers between devices, fast_on_device(): slab = lax.ppermute(slab_out, 'region', swap)  3.03 us
    ppermute x1, waiting for transfers between devices, fast_on_device(): arrived_b = lax.ppermute(code_b, 'blk', forward)  3.03 us
    ppermute x1, waiting for transfers between devices, fast_on_device(): from_left = lax.ppermute(right, 'blk', forward)  1.76 us
    ppermute x1, starting transfers between devices, fast_on_device(): from_dright = lax.ppermute(dleft, ('region', 'blk'), crossed(-1))  1.65 us
    ppermute x1, waiting for transfers between devices, fast_on_device(): from_dleft = lax.ppermute(dright, ('region', 'blk'), crossed(1))  0.91 us
    ppermute x1, waiting for transfers between devices, fast_on_device(): from_dright = lax.ppermute(dleft, ('region', 'blk'), crossed(-1))  0.68 us
  transfers between devices with their start and end apart: 8, of which 5 were waited for; matrix products, arithmetic and copies ran while one was open for 0% of the time, Pallas kernels for 35%

profile of v4, /device:TPU:0, one launch (start us, length us, event | category | flops | bytes accessed | tf_op | source)
XLA Modules:
  0.0 27.7 jit_solution(13996067043535725494)
XLA Ops:
  0.0 0.0 copy-start
  0.0 0.0 copy-start.2
  0.0 1.1 %pack_slab.1 = bf16[4,32,1024]{2,1,0:T(8,128)(2,1)S(1)} custom-call(bf16[2,4,32,1024]{3,2,1,0:T(8,128)(2,1)} %bitcast.14), custom_call_target="tpu_custom_call" | custom-call | tf_op jit(solution)/shard_map/pack_slab/pallas_call | solution.py:528
  1.1 3.0 %collective-permute-start.1 = (bf16[4,32,1024]{2,1,0:T(8,128)(2,1)S(1)}, bf16[4,32,1024]{2,1,0:T(8,128)(2,1)S(1)}, u32[]{:S(2)}, u32[]{:S(2)}) collective-permute-start(bf16[4,32,1024]{2,1,0:T(8,128)(2,1)S(1)} %pack_slab.1), channel_id=1, source_target_pairs={{0,16},{16,0},{1,17},{17,1},{2,18},{18,2},{3,19},{19,3},{4,20},{20... | collective-permute-start | bytes 786440 | tf_op jit(solution)/shard_map/ppermute | solution.py:570
  4.2 1.4 %pack_edges.1 = (bf16[32,1024]{1,0:T(8,128)(2,1)S(1)}, bf16[144,128]{1,0:T(8,128)(2,1)S(1)}, bf16[144,128]{1,0:T(8,128)(2,1)S(1)}, bf16[144,128]{1,0:T(8,128)(2,1)S(1)}, bf16[144,128]{1,0:T(8,128)(2,1)S(1)}) custom-call(s32[2]{0:T(128)} %owner_ref.1, s32[8]{0:T(128)} %bitcast.23, f32[2,4,32,1024]{3,2,1,0:T(8,128)} %bitcast.7, f32[2,4,32,1024]{3,2,1,0:T(8,128)} %bitcast.21, ...), custom_call_target="tpu_custom_call" | custom-call | tf_op jit(solution)/shard_map/pack_edges/pallas_call | solution.py:528
  5.5 0.0 copy-start.1
  5.5 3.7 %collective-permute-start.3 = (bf16[144,128]{1,0:T(8,128)(2,1)S(1)}, bf16[144,128]{1,0:T(8,128)(2,1)S(1)}, u32[]{:S(2)}, u32[]{:S(2)}) collective-permute-start(bf16[144,128]{1,0:T(8,128)(2,1)S(1)} %get-tuple-element.28), channel_id=1, source_target_pairs={{0,15},{1,0},{2,1},{3,2},{4,3},{5,4},{6,5},{7,6},{8,7},{9,8},{10,9... | collective-permute-start | bytes 110600 | tf_op jit(solution)/shard_map/ppermute | solution.py:572
  9.3 0.5 %collective-permute-start.2 = (bf16[32,1024]{1,0:T(8,128)(2,1)S(1)}, bf16[32,1024]{1,0:T(8,128)(2,1)S(1)}, u32[]{:S(2)}, u32[]{:S(2)}) collective-permute-start(bf16[32,1024]{1,0:T(8,128)(2,1)S(1)} %get-tuple-element.27), channel_id=1, source_target_pairs={{0,16},{16,0},{1,17},{17,1},{2,18},{18,2},{3,19},{19,3},{4,20},{20... | collective-permute-start | bytes 196616 | tf_op jit(solution)/shard_map/ppermute | solution.py:571
  9.8 1.6 %collective-permute-start.4 = (bf16[144,128]{1,0:T(8,128)(2,1)S(1)}, bf16[144,128]{1,0:T(8,128)(2,1)S(1)}, u32[]{:S(2)}, u32[]{:S(2)}) collective-permute-start(bf16[144,128]{1,0:T(8,128)(2,1)S(1)} %get-tuple-element.29), channel_id=1, source_target_pairs={{0,31},{1,16},{2,17},{3,18},{4,19},{5,20},{6,21},{7,22},{8,23},{9,... | collective-permute-start | bytes 110600 | tf_op jit(solution)/shard_map/ppermute | solution.py:573
  11.4 0.0 collective-permute-start
  11.4 0.0 collective-permute-done.3.straight_ref
  11.4 0.1 collective-permute-start.5
  11.5 0.0 copy-done
  11.5 0.0 copy-done.2
  11.5 1.3 %local.1 = (f32[4,32,1024]{2,1,0:T(8,128)S(1)}, f32[4,32,1024]{2,1,0:T(8,128)S(1)}, f32[2,4,32,1024]{3,2,1,0:T(8,128)S(1)}, f32[2,8,1024]{2,1,0:T(8,128)S(1)}) custom-call(f32[2,4,32,1024]{3,2,1,0:T(8,128)S(1)} %bitcast.8, f32[2,4,32,1024]{3,2,1,0:T(8,128)S(1)} %bitcast.22), custom_call_target="tpu_custom_call" | custom-call | tf_op jit(solution)/shard_map/local/pallas_call | solution.py:528
  12.8 0.0 copy-start.3
  12.8 0.7 %collective-permute-done.4.diag_ref = bf16[144,128]{1,0:T(8,128)(2,1)S(1)} collective-permute-done((bf16[144,128]{1,0:T(8,128)(2,1)S(1)}, bf16[144,128]{1,0:T(8,128)(2,1)S(1)}, u32[]{:S(2)}, u32[]{:S(2)}) %collective-permute-start.4) | collective-permute-done | bytes 36896 | tf_op jit(solution)/shard_map/ppermute | solution.py:573
  13.5 0.4 %collective-permute-done.2.y_ref = bf16[32,1024]{1,0:T(8,128)(2,1)S(1)} collective-permute-done((bf16[32,1024]{1,0:T(8,128)(2,1)S(1)}, bf16[32,1024]{1,0:T(8,128)(2,1)S(1)}, u32[]{:S(2)}, u32[]{:S(2)}) %collective-permute-start.2) | collective-permute-done | bytes 65568 | tf_op jit(solution)/shard_map/ppermute | solution.py:571
  13.9 0.0 copy-done.1
  13.9 0.6 %edges.2 = (f32[4,32,1024]{2,1,0:T(8,128)S(1)}, f32[4,32,128]{2,1,0:T(8,128)S(1)}, f32[4,32,128]{2,1,0:T(8,128)S(1)}, f32[8,1280]{1,0:T(8,128)S(1)}) custom-call(f32[2,4,32,1024]{3,2,1,0:T(8,128)S(1)} %bitcast.9, bf16[2,4,32,1024]{3,2,1,0:T(8,128)(2,1)S(1)} %bitcast.16, ...), custom_call_target="tpu_custom_call", output_to_operand_aliasing={{0}: (7, {})} | custom-call | tf_op jit(solution)/shard_map/edges/pallas_call | solution.py:528
  14.5 0.0 collective-permute-done.1.slab_ref
  14.5 0.0 copy-done.3
  14.5 1.1 %last_row.3 = (f32[2,32,1024]{2,1,0:T(8,128)S(1)}, s16[72,1024]{1,0:T(8,128)(2,1)S(1)}) custom-call(s32[8]{0:T(128)S(1)} %bitcast.24, f32[2,4,32,1024]{3,2,1,0:T(8,128)S(1)} %bitcast.10, bf16[2,4,32,1024]{3,2,1,0:T(8,128)(2,1)S(1)} %bitcast.17, bf16[4,32,1024]{2,1,0:T(8,128)(2,1)S(1)} %collective-permute-done.1.slab_ref, ...), custom_call_target="tpu_custom_call" | custom-call | tf_op jit(solution)/shard_map/last_row/pallas_call | solution.py:528
  15.7 0.1 collective-permute-start.7
  15.7 1.8 %collective-permute-done.rest_0_.straight_ref = bf16[144,128]{1,0:T(8,128)(2,1)S(1)} collective-permute-done((bf16[144,128]{1,0:T(8,128)(2,1)S(1)}, bf16[144,128]{1,0:T(8,128)(2,1)S(1)}, u32[]{:S(2)}, u32[]{:S(2)}) %collective-permute-start) | collective-permute-done | bytes 36896 | tf_op jit(solution)/shard_map/ppermute | solution.py:574
  17.5 0.9 %collective-permute-done.5.rest_1_.diag_ref = bf16[144,128]{1,0:T(8,128)(2,1)S(1)} collective-permute-done((bf16[144,128]{1,0:T(8,128)(2,1)S(1)}, bf16[144,128]{1,0:T(8,128)(2,1)S(1)}, u32[]{:S(2)}, u32[]{:S(2)}) %collective-permute-start.5) | collective-permute-done | bytes 36896 | tf_op jit(solution)/shard_map/ppermute | solution.py:575
  18.4 1.1 %last_row.2 = (f32[2,32,1024]{2,1,0:T(8,128)S(1)}, s16[72,1024]{1,0:T(8,128)(2,1)S(1)}) custom-call(s32[8]{0:T(128)S(1)} %bitcast.25, f32[2,4,32,1024]{3,2,1,0:T(8,128)S(1)} %bitcast.11, bf16[2,4,32,1024]{3,2,1,0:T(8,128)(2,1)S(1)} %bitcast.18, bf16[4,32,1024]{2,1,0:T(8,128)(2,1)S(1)} %collective-permute-done.1.slab_ref, ...), custom_call_target="tpu_custom_call" | custom-call | tf_op jit(solution)/shard_map/last_row/pallas_call | solution.py:528
  19.6 0.0 copy-start.4
  19.6 0.1 collective-permute-start.6
  19.6 0.6 %edges.3 = (f32[4,32,1024]{2,1,0:T(8,128)S(1)}, f32[4,32,128]{2,1,0:T(8,128)S(1)}, f32[4,32,128]{2,1,0:T(8,128)S(1)}, f32[8,1280]{1,0:T(8,128)S(1)}) custom-call(f32[2,4,32,1024]{3,2,1,0:T(8,128)S(1)} %bitcast.12, bf16[2,4,32,1024]{3,2,1,0:T(8,128)(2,1)S(1)} %bitcast.19, ...), custom_call_target="tpu_custom_call", output_to_operand_aliasing={{0}: (7, {})} | custom-call | tf_op jit(solution)/shard_map/edges/pallas_call | solution.py:528
  20.3 0.0 copy-done.4
  20.3 2.7 %first_row.1.partial_ref = f32[3,4,32,1024]{3,2,1,0:T(8,128)} custom-call(s32[2]{0:T(128)S(1)} %copy-done.4, s32[8]{0:T(128)S(1)} %bitcast.26, f32[2,4,32,1024]{3,2,1,0:T(8,128)S(1)} %bitcast.13, bf16[2,4,32,1024]{3,2,1,0:T(8,128)(2,1)S(1)} %bitcast.20, bf16[4,32,1024]{2,1,0:T(8,128)(2,1)S(1)} %collective-permute-done.1.slab_ref, ...), custom_call_target="tpu_custom_call" | custom-call | tf_op jit(solution)/shard_map/first_row/pallas_call | solution.py:528
  23.0 0.0 collective-permute-done.7.code_ref
  23.0 0.9 %place.2.partial_ref = f32[3,4,32,1024]{3,2,1,0:T(8,128)} custom-call(bf16[144,128]{1,0:T(8,128)(2,1)S(1)} %collective-permute-done.rest_0_.straight_ref, s16[72,1024]{1,0:T(8,128)(2,1)S(1)} %collective-permute-done.7.code_ref, f32[3,4,32,1024]{3,2,1,0:T(8,128)} %first_row.1.partial_ref), custom_call_target="tpu_custom_call", output_to_operand_aliasing={{}: (2, {})} | custom-call | tf_op jit(solution)/shard_map/place/pallas_call | solution.py:528
  23.9 3.0 %collective-permute-done.6.code_ref = s16[72,1024]{1,0:T(8,128)(2,1)S(1)} collective-permute-done((s16[72,1024]{1,0:T(8,128)(2,1)S(1)}, s16[72,1024]{1,0:T(8,128)(2,1)S(1)}, u32[]{:S(2)}, u32[]{:S(2)}) %collective-permute-start.6) | collective-permute-done | bytes 147488 | tf_op jit(solution)/shard_map/ppermute | solution.py:621
  26.9 0.9 %place.3 = f32[3,4,32,1024]{3,2,1,0:T(8,128)} custom-call(bf16[144,128]{1,0:T(8,128)(2,1)S(1)} %collective-permute-done.rest_0_.straight_ref, s16[72,1024]{1,0:T(8,128)(2,1)S(1)} %collective-permute-done.6.code_ref, f32[3,4,32,1024]{3,2,1,0:T(8,128)} %place.2.partial_ref), custom_call_target="tpu_custom_call", output_to_operand_aliasing={{}: (2, {})} | custom-call | tf_op jit(solution)/shard_map/place/pallas_call | solution.py:528
Async XLA Ops:
  0.0 11.5 %copy-start = (f32[2,1,4,32,1024]{4,3,2,1,0:T(8,128)S(1)}, f32[2,1,4,32,1024]{4,3,2,1,0:T(8,128)}, u32[]{:S(2)}) copy-start(f32[2,1,4,32,1024]{4,3,2,1,0:T(8,128)} %param.5) | copy-start | bytes 3145732
  0.0 11.5 %copy-start.2 = (f32[2,1,4,32,1024]{4,3,2,1,0:T(8,128)S(1)}, f32[2,1,4,32,1024]{4,3,2,1,0:T(8,128)}, u32[]{:S(2)}) copy-start(f32[2,1,4,32,1024]{4,3,2,1,0:T(8,128)} %param.6) | copy-start | bytes 3145732
  1.1 13.4 %collective-permute-start.1 = (bf16[4,32,1024]{2,1,0:T(8,128)(2,1)S(1)}, bf16[4,32,1024]{2,1,0:T(8,128)(2,1)S(1)}, u32[]{:S(2)}, u32[]{:S(2)}) collective-permute-start(bf16[4,32,1024]{2,1,0:T(8,128)(2,1)S(1)} %pack_slab.1), channel_id=1, source_target_pairs={{0,16},{16,0},{1,17},{17,1},{2,18},{18,2},{3,19},{19,3},{4,20},{20... | collective-permute-start | bytes 786440 | tf_op jit(solution)/shard_map/ppermute | solution.py:570
  5.5 8.3 %copy-start.1 = (bf16[1,1,2,4,32,1024]{5,4,3,2,1,0:T(8,128)(2,1)S(1)}, bf16[1,1,2,4,32,1024]{5,4,3,2,1,0:T(8,128)(2,1)}, u32[]{:S(2)}) copy-start(bf16[1,1,2,4,32,1024]{5,4,3,2,1,0:T(8,128)(2,1)} %param.7) | copy-start | bytes 1572868
  5.5 5.9 %collective-permute-start.3 = (bf16[144,128]{1,0:T(8,128)(2,1)S(1)}, bf16[144,128]{1,0:T(8,128)(2,1)S(1)}, u32[]{:S(2)}, u32[]{:S(2)}) collective-permute-start(bf16[144,128]{1,0:T(8,128)(2,1)S(1)} %get-tuple-element.28), channel_id=1, source_target_pairs={{0,15},{1,0},{2,1},{3,2},{4,3},{5,4},{6,5},{7,6},{8,7},{9,8},{10,9... | collective-permute-start | bytes 110600 | tf_op jit(solution)/shard_map/ppermute | solution.py:572
  9.3 4.6 %collective-permute-start.2 = (bf16[32,1024]{1,0:T(8,128)(2,1)S(1)}, bf16[32,1024]{1,0:T(8,128)(2,1)S(1)}, u32[]{:S(2)}, u32[]{:S(2)}) collective-permute-start(bf16[32,1024]{1,0:T(8,128)(2,1)S(1)} %get-tuple-element.27), channel_id=1, source_target_pairs={{0,16},{16,0},{1,17},{17,1},{2,18},{18,2},{3,19},{19,3},{4,20},{20... | collective-permute-start | bytes 196616 | tf_op jit(solution)/shard_map/ppermute | solution.py:571
  9.8 3.7 %collective-permute-start.4 = (bf16[144,128]{1,0:T(8,128)(2,1)S(1)}, bf16[144,128]{1,0:T(8,128)(2,1)S(1)}, u32[]{:S(2)}, u32[]{:S(2)}) collective-permute-start(bf16[144,128]{1,0:T(8,128)(2,1)S(1)} %get-tuple-element.29), channel_id=1, source_target_pairs={{0,31},{1,16},{2,17},{3,18},{4,19},{5,20},{6,21},{7,22},{8,23},{9,... | collective-permute-start | bytes 110600 | tf_op jit(solution)/shard_map/ppermute | solution.py:573
  11.4 6.1 %collective-permute-start = (bf16[144,128]{1,0:T(8,128)(2,1)S(1)}, bf16[144,128]{1,0:T(8,128)(2,1)S(1)}, u32[]{:S(2)}, u32[]{:S(2)}) collective-permute-start(bf16[144,128]{1,0:T(8,128)(2,1)S(1)} %get-tuple-element.26), channel_id=1, source_target_pairs={{0,1},{1,2},{2,3},{3,4},{4,5},{5,6},{6,7},{7,8},{8,9},{9,10},{10,1... | collective-permute-start | bytes 110600 | tf_op jit(solution)/shard_map/ppermute | solution.py:574
  11.4 7.0 %collective-permute-start.5 = (bf16[144,128]{1,0:T(8,128)(2,1)S(1)}, bf16[144,128]{1,0:T(8,128)(2,1)S(1)}, u32[]{:S(2)}, u32[]{:S(2)}) collective-permute-start(bf16[144,128]{1,0:T(8,128)(2,1)S(1)} %get-tuple-element.38), channel_id=1, source_target_pairs={{0,17},{1,18},{2,19},{3,20},{4,21},{5,22},{6,23},{7,24},{8,25},{9,... | collective-permute-start | bytes 110600 | tf_op jit(solution)/shard_map/ppermute | solution.py:575
  12.8 1.7 %copy-start.3 = (s32[1,1,8]{2,1,0:T(1,128)S(1)}, s32[1,1,8]{2,1,0:T(1,128)}, u32[]{:S(2)}) copy-start(s32[1,1,8]{2,1,0:T(1,128)} %param.8) | copy-start | bytes 100
  15.7 7.3 %collective-permute-start.7 = (s16[72,1024]{1,0:T(8,128)(2,1)S(1)}, s16[72,1024]{1,0:T(8,128)(2,1)S(1)}, u32[]{:S(2)}, u32[]{:S(2)}) collective-permute-start(s16[72,1024]{1,0:T(8,128)(2,1)S(1)} %get-tuple-element.40), channel_id=1, source_target_pairs={{0,1},{1,2},{2,3},{3,4},{4,5},{5,6},{6,7},{7,8},{8,9},{9,10},{10,1... | collective-permute-start | bytes 442376 | tf_op jit(solution)/shard_map/ppermute | solution.py:619
  19.6 0.7 %copy-start.4 = (s32[2]{0:T(128)S(1)}, s32[2]{0:T(128)}, u32[]{:S(2)}) copy-start(s32[2]{0:T(128)} %owner_ref.1) | copy-start | bytes 28
  19.6 7.3 %collective-permute-start.6 = (s16[72,1024]{1,0:T(8,128)(2,1)S(1)}, s16[72,1024]{1,0:T(8,128)(2,1)S(1)}, u32[]{:S(2)}, u32[]{:S(2)}) collective-permute-start(s16[72,1024]{1,0:T(8,128)(2,1)S(1)} %get-tuple-element.39), channel_id=1, source_target_pairs={{0,1},{1,2},{2,3},{3,4},{4,5},{5,6},{6,7},{7,8},{8,9},{9,10},{10,1... | collective-permute-start | bytes 442376 | tf_op jit(solution)/shard_map/ppermute | solution.py:621

commit v5 on v0

--- a/solution.py
+++ b/solution.py
@@ -1,9 +1,20 @@
+import functools
+
 import jax
 import jax.numpy as jnp
 from jax import lax
+from jax.experimental import pallas as pl
+from jax.experimental.pallas import tpu as pltpu
 from jax.sharding import PartitionSpec as P
 
 STEPS = 2
+LANES = 128
+F32 = jnp.float32
+BF16 = jnp.bfloat16
+VMEM = pl.BlockSpec(memory_space=pltpu.VMEM)
+SMEM = pl.BlockSpec(memory_space=pltpu.SMEM)
+ANY = pl.BlockSpec(memory_space=pl.ANY)
+HBM = pl.BlockSpec(memory_space=pltpu.HBM)
 
 
 def extended_2(block, sides, width, periodic):
@@ -82,7 +93,7 @@
     return (placed, jnp.sum(valid_flags))
 
 
-def on_device(u_now, u_prev, coef_store, store_map, new_owner):
+def general_on_device(u_now, u_prev, coef_store, store_map, new_owner):
     state_now = u_now[:, 0]
     state_prev = u_prev[:, 0]
     blocks, fields, edge_cells, plane_cells = state_now.shape
@@ -114,7 +125,726 @@
     return result[:, None]
 
 
+def lane_ids():
+    return lax.broadcasted_iota(jnp.int32, (1, LANES), 1)
+
+
+def edge_start(lower, depth, size):
+    return pl.multiple_of(jnp.where(lower, depth - size, 0), size)
+
+
+def tag_values(map_ref, region):
+    numbers = [map_ref[region * 4 + s] for s in range(4)] + [map_ref[(1 - region) * 4 + s] for s in range(4)]
+    return [jnp.zeros((1, LANES), F32) + number.astype(F32) for number in numbers]
+
+
+def pack_slab_body(coef_ref, slab_ref, sems):
+    other = 1 - lax.axis_index("region")
+    half = coef_ref.shape[2] // 2
+    copies = []
+    for s in range(4):
+        for h in range(2):
+            part = slice(h * half, (h + 1) * half)
+            copies.append(
+                pltpu.make_async_copy(coef_ref.at[other, s, part], slab_ref.at[s, part], sems.at[2 * s + h])
+            )
+    for copy in copies:
+        copy.start()
+    for copy in copies:
+        copy.wait()
+
+
+def pack_edges_body(
+    map_hbm, u_ref, p_ref, coef_ref, y_ref, straight_ref, diag_ref,
+    rows_ref, ue_ref, pe_ref, ce_ref, ua_ref, pa_ref, ca_ref, map_ref, sems
+):
+    fields = u_ref.shape[1]
+    depth = u_ref.shape[2]
+    top = depth - 1
+    region = lax.axis_index("region")
+    lower = region == 0
+    other = 1 - region
+    edge8 = edge_start(lower, depth, 8)
+    edge16 = edge_start(lower, depth, 16)
+    copies = [
+        pltpu.make_async_copy(map_hbm, map_ref, sems.at[0]),
+        pltpu.make_async_copy(u_ref.at[:, :, pl.ds(edge8, 8), :], ue_ref, sems.at[1]),
+        pltpu.make_async_copy(p_ref.at[:, :, pl.ds(edge8, 8), :], pe_ref, sems.at[2]),
+        pltpu.make_async_copy(coef_ref.at[region, :, pl.ds(edge16, 16), :], ce_ref, sems.at[3]),
+        pltpu.make_async_copy(u_ref.at[0, :, :, 0:LANES], ua_ref, sems.at[4]),
+        pltpu.make_async_copy(p_ref.at[0, :, :, 0:LANES], pa_ref, sems.at[5]),
+        pltpu.make_async_copy(coef_ref.at[:, :, :, 0:LANES], ca_ref, sems.at[6]),
+    ]
+    for copy in copies:
+        copy.start()
+    for copy in copies[:4]:
+        copy.wait()
+    lane = lane_ids()
+    own_edge = jnp.where(lower, 7, 0)
+    own_next = jnp.where(lower, 6, 1)
+    for m in range(2):
+        for f in range(fields):
+            at = m * fields + f
+            near = ue_ref[m, f, pl.ds(own_edge, 1), :]
+            rows_ref[at : at + 1, :] = near
+            rows_ref[8 + at : 9 + at, :] = ue_ref[m, f, pl.ds(own_next, 1), :]
+            rows_ref[16 + at : 17 + at, :] = 2.0 * near - pe_ref[m, f, pl.ds(own_edge, 1), :]
+    for s in range(4):
+        piece = ce_ref[s].astype(F32)
+        rows_ref[24 + s : 25 + s, :] = jnp.where(lower, piece[15:16], piece[0:1])
+    tag_rows = tag_values(map_ref, region)
+    for i, row in enumerate(tag_rows):
+        rows_ref[28:29, i * LANES : (i + 1) * LANES] = row
+    rows_ref[29:32, :] = jnp.zeros((3, rows_ref.shape[1]), F32)
+    y_ref[...] = rows_ref[...].astype(BF16)
+    for copy in copies[4:]:
+        copy.wait()
+    blank = jnp.zeros((1, LANES), F32)
+    for f in range(fields):
+        now = ua_ref[f]
+        ahead = 2.0 * now - pa_ref[f]
+        piece = ca_ref[region, f].astype(F32)
+        tile = jnp.where(
+            lane < 64, now, jnp.where(lane < 96, pltpu.roll(ahead, 64, 1), pltpu.roll(piece, 96, 1))
+        )
+        straight_ref[f * depth : (f + 1) * depth, :] = tile.astype(BF16)
+    far = [ca_ref[other, s].astype(F32) for s in range(4)]
+    extra = [jnp.where(lower, piece[0:1], piece[top:depth]) for piece in far] + tag_rows + [blank] * 4
+    straight_ref[fields * depth : fields * depth + 16, :] = jnp.concatenate(extra, axis=0).astype(BF16)
+    plane = jnp.zeros((depth, LANES), F32)
+    for s in range(4):
+        moved = pltpu.roll(far[s], 32 * s, 1) if s else far[s]
+        plane = jnp.where((lane >= 32 * s) & (lane < 32 * s + 32), moved, plane)
+    diag_ref[0:depth, :] = plane.astype(BF16)
+    edges = [rows_ref[base : base + 4, 0:LANES] for base in (0, 8, 16, 24)]
+    extra = edges + tag_rows + [blank] * 8
+    diag_ref[depth : depth + 32, :] = jnp.concatenate(extra, axis=0).astype(BF16)
+
+
+def nine_sum(tiles, lane, first=0):
+    inside = lane % 32
+    low = inside != 0
+    high = inside != 31
+    rows = []
+    for tile in tiles:
+        rows.append(
+            tile
+            + jnp.where(low, pltpu.roll(tile, 1, 1), 0.0)
+            + jnp.where(high, pltpu.roll(tile, LANES - 1, 1), 0.0)
+        )
+    up = [pltpu.roll(row, 32, 1) for row in rows]
+    down = [pltpu.roll(row, LANES - 32, 1) for row in rows]
+    count = len(tiles)
+    result = []
+    for t in range(count):
+        before = up[t] if t == 0 else jnp.where(lane < 32, up[t - 1], up[t])
+        after = down[t] if t == count - 1 else jnp.where(lane >= 96, down[t + 1], down[t])
+        result.append(rows[t] + before + after)
+    return result
+
+
+def column_sum(tile, row_id, low_row, high_row):
+    depth = tile.shape[0]
+    above = pltpu.roll(tile, 1, 0)
+    below = pltpu.roll(tile, depth - 1, 0)
+    return tile + jnp.where(row_id == 0, low_row, above) + jnp.where(row_id == depth - 1, high_row, below)
+
+
+def local_body(u_ref, p_ref, box0_ref, box1_ref, drift_ref, rim_ref):
+    fields, depth, width = u_ref.shape[1:]
+    main = width // LANES
+    lower = lax.axis_index("region") == 0
+    lane = lane_ids()
+    row_id = lax.broadcasted_iota(jnp.int32, (depth, 1), 0)
+    boxes = (box0_ref, box1_ref)
+    for f in range(fields):
+        now = [u_ref[m, f, :, tile_at(t)] for m in range(2) for t in range(main)]
+        sums = nine_sum(now, lane)
+        for i, (tile, total) in enumerate(zip(now, sums)):
+            m, t = divmod(i, main)
+            lanes = tile_at(t)
+            rim_ref[m, f : f + 1, lanes] = jnp.where(lower, total[depth - 1 : depth], total[0:1])
+            boxes[m][f, :, lanes] = column_sum(total, row_id, 0.0, 0.0) - 27.0 * tile
+            drift_ref[m, f, :, lanes] = 2.0 * tile - p_ref[m, f, :, lanes]
+    rim_ref[:, 4:8, :] = jnp.zeros((2, 4, width), F32)
+
+
+def tile_at(t):
+    return slice(t * LANES, (t + 1) * LANES)
+
+
+class ColumnEdge:
+    def __init__(self, coef_ref, y_ref):
+        self.region = lax.axis_index("region")
+        self.lower = self.region == 0
+        self.coef = coef_ref
+        self.depth = coef_ref.shape[2]
+        self.extra = y_ref[...].astype(F32)
+        self.tags = [self.extra[28:29, i * LANES : (i + 1) * LANES] for i in range(8)]
+        self.field_id = lax.broadcasted_iota(jnp.int32, (4, LANES), 0).astype(F32)
+
+    def near(self, m, lanes):
+        return self.extra[4 * m : 4 * m + 4, lanes]
+
+    def beyond(self, m, lanes):
+        return self.extra[8 + 4 * m : 12 + 4 * m, lanes]
+
+    def ahead(self, m, lanes):
+        return self.extra[16 + 4 * m : 20 + 4 * m, lanes]
+
+    def coefs(self, m, lanes):
+        total = jnp.zeros((4, LANES), F32)
+        for s in range(4):
+            piece = self.coef[1 - self.region, s, :, lanes].astype(F32)
+            held = jnp.where(self.lower, piece[0:1], piece[self.depth - 1 : self.depth])
+            total = total + jnp.where(self.tags[s] == self.field_id + 4 * m, self.extra[24 + s : 25 + s, lanes], 0.0)
+            total = total + jnp.where(self.tags[4 + s] == self.field_id + 4 * m, held, 0.0)
+        return total
+
+    def own(self, tile):
+        return jnp.where(self.lower, tile[self.depth - 1 : self.depth], tile[0:1])
+
+    def rows(self, row):
+        return jnp.where(self.lower, 0.0, row), jnp.where(self.lower, row, 0.0)
+
+
+def last_edges_body(
+    u_ref, coef_ref, y_ref, straight_ref, diag_ref, box0_ref, rim_ref, box_in, box_ref, lap_ref, side_ref, sums_ref, tail_ref
+):
+    fields, depth, width = u_ref.shape[1:]
+    main = width // LANES
+    lane = lane_ids()
+    row_id = lax.broadcasted_iota(jnp.int32, (depth, 1), 0)
+    column = ColumnEdge(coef_ref, y_ref)
+    before = slice(width - LANES, width)
+    facing = lane >= 96
+    extra_s = straight_ref[fields * depth : fields * depth + 16, :].astype(F32)
+    extra_d = diag_ref[depth : depth + 32, :].astype(F32)
+    tags_s = [extra_s[4 + i : 5 + i] for i in range(8)]
+    tags_d = [extra_d[16 + i : 17 + i] for i in range(8)]
+
+    planes = []
+    for s in range(4):
+        planes.append(pltpu.roll(straight_ref[s * depth : (s + 1) * depth, :].astype(F32), 32, 1))
+    diag_tile = diag_ref[0:depth, :].astype(F32)
+    for s in range(4):
+        planes.append(pltpu.roll(diag_tile, LANES - 32 * s, 1) if s else diag_tile)
+
+    def edge_tiles(of, base):
+        return [of(0, before)] + [of(1, tile_at(t)) for t in range(main)] + [extra_d[base : base + 4]]
+
+    near = edge_tiles(column.near, 0)
+    beyond = edge_tiles(column.beyond, 4)
+    ahead = edge_tiles(column.ahead, 8)
+    corner = jnp.zeros((4, LANES), F32)
+    for s in range(4):
+        corner = corner + jnp.where(tags_d[s] == column.field_id, extra_d[12 + s : 13 + s], 0.0)
+        corner = corner + jnp.where(tags_d[4 + s] == column.field_id, extra_s[s : s + 1], 0.0)
+    edge_c = [column.coefs(0, before)] + [column.coefs(1, tile_at(t)) for t in range(main)] + [corner]
+    near_sum = nine_sum(near, lane)
+    beyond_sum = nine_sum(beyond, lane)
+
+    own, outer = [], []
+    for f in range(fields):
+        inner = u_ref[1, f, :, tile_at(main - 1)]
+        remote = straight_ref[f * depth : (f + 1) * depth, :].astype(F32)
+        inner_sum, remote_sum = nine_sum([inner, remote], lane)
+        own.append(column.own(inner_sum))
+        outer.append(column.own(remote_sum))
+        halo_c = jnp.zeros((depth, LANES), F32)
+        for i in range(8):
+            halo_c = halo_c + jnp.where(tags_s[i] == F32(f), planes[i], 0.0)
+        low_row, high_row = column.rows(near_sum[main + 1][f : f + 1])
+        lap = column_sum(remote_sum, row_id, low_row, high_row) - 27.0 * remote
+        side_ref[f] = pltpu.roll(remote, 64, 1) + halo_c * lap
+        for t in range(main):
+            low_row, high_row = column.rows(near_sum[t + 1][f : f + 1])
+            lanes = tile_at(t)
+            if t == main - 1:
+                box = box_in[f, :, lanes]
+                box = box + jnp.where(row_id == 0, low_row, 0.0) + jnp.where(row_id == depth - 1, high_row, 0.0)
+                whole = column_sum(inner_sum, row_id, low_row, high_row) - 27.0 * inner
+                box_ref[f, :, lanes] = jnp.where(facing, whole, box)
+            else:
+                box_ref[f, 0:1, lanes] = box_in[f, 0:1, lanes] + low_row
+                box_ref[f, depth - 1 : depth, lanes] = box_in[f, depth - 1 : depth, lanes] + high_row
+        low_row, high_row = column.rows(near_sum[0][f : f + 1])
+        lap = box0_ref[f, :, before]
+        lap_ref[f] = lap + jnp.where(row_id == 0, low_row, 0.0) + jnp.where(row_id == depth - 1, high_row, 0.0)
+    rims = [rim_ref[0, 0:4, before]] + [rim_ref[1, 0:4, tile_at(t)] for t in range(main)]
+    rims.append(jnp.concatenate(outer, axis=0))
+    rims[main] = jnp.where(facing, jnp.concatenate(own, axis=0), rims[main])
+    stepped = []
+    for t in range(main + 2):
+        box = near_sum[t] + beyond_sum[t] + rims[t]
+        stepped.append(ahead[t] + edge_c[t] * (box - 27.0 * near[t]))
+    stepped_sum = nine_sum(stepped, lane)
+    for t in range(main):
+        sums_ref[0:4, tile_at(t)] = stepped_sum[t + 1]
+    sums_ref[4:8, :] = jnp.zeros((4, width), F32)
+    tail_ref[0:4, :] = stepped[main]
+    tail_ref[4:8, :] = jnp.zeros((4, LANES), F32)
+
+
+def first_edges_body(
+    u_ref, coef_ref, y_ref, box1_ref, rim_ref, box_in, box_ref, sums_ref, tail_ref
+):
+    fields, depth, width = u_ref.shape[1:]
+    main = width // LANES
+    lane = lane_ids()
+    column = ColumnEdge(coef_ref, y_ref)
+    after = slice(0, LANES)
+
+    def edge_tiles(of):
+        return [of(0, tile_at(t)) for t in range(main)] + [of(1, after)]
+
+    near = edge_tiles(column.near)
+    near_sum = nine_sum(near, lane)
+    beyond_sum = nine_sum(edge_tiles(column.beyond), lane)
+    ahead = edge_tiles(column.ahead)
+    edge_c = edge_tiles(column.coefs)
+    for f in range(fields):
+        for t in range(main):
+            low_row, high_row = column.rows(near_sum[t][f : f + 1])
+            lanes = tile_at(t)
+            box_ref[f, 0:1, lanes] = box_in[f, 0:1, lanes] + low_row
+            box_ref[f, depth - 1 : depth, lanes] = box_in[f, depth - 1 : depth, lanes] + high_row
+    rims = [rim_ref[0, 0:4, tile_at(t)] for t in range(main)] + [rim_ref[1, 0:4, after]]
+    stepped = []
+    for t in range(main + 1):
+        box = near_sum[t] + beyond_sum[t] + rims[t]
+        stepped.append(ahead[t] + edge_c[t] * (box - 27.0 * near[t]))
+    stepped_sum = nine_sum(stepped, lane)
+    for t in range(main):
+        sums_ref[0:4, tile_at(t)] = stepped_sum[t]
+    sums_ref[4:8, :] = jnp.zeros((4, width), F32)
+    tail_ref[0:4, :] = stepped[1]
+    tail_ref[4:8, :] = jnp.zeros((4, LANES), F32)
+
+
+class Pieces:
+    def __init__(self, map_ref, coef_ref, slab_ref):
+        self.coef, self.slab = coef_ref, slab_ref
+        self.region = lax.axis_index("region")
+        self.numbers = [map_ref[q] for q in range(8)]
+
+    def piece(self, number):
+        place = jnp.int32(0)
+        for q in range(8):
+            place = jnp.where(self.numbers[q] == number, q, place)
+        slot = place & 3
+        held = (place >> 2) == self.region
+
+        def tile(lanes):
+            return jnp.where(held, self.coef[self.region, slot, :, lanes], self.slab[slot, :, lanes]).astype(F32)
+
+        return tile
+
+
+def second_step(now, before, total, coef, row_id, row, lower):
+    low_row, high_row = jnp.where(lower, 0.0, row), jnp.where(lower, row, 0.0)
+    lap = column_sum(total, row_id, low_row, high_row) - 27.0 * now
+    return 2.0 * now - before + coef * lap
+
+
+CODES = 32000.0
+
+
+def power_of(size):
+    return jnp.ceil(jnp.log2(jnp.maximum(size, 1e-30)))
+
+
+def coded(value, power):
+    return jnp.floor(value * (CODES * jnp.exp2(-power)) + 0.5)
+
+
+def narrow(value):
+    return value.astype(jnp.int32).astype(jnp.int16)
+
+
+def wide(code):
+    return code.astype(jnp.int32).astype(F32)
+
+
+def scale_of(power):
+    return jnp.exp2(power) * (1.0 / CODES)
+
+
+def last_row_body(
+    first, map_ref, u_ref, coef_ref, slab_ref, box_ref, drift_ref, lap_ref, side_ref, sums_ref, *rest
+):
+    if first == 0:
+        owner_ref, y_ref, tail_ref, row_ref, code_ref, power_ref, extra_ref = rest
+    else:
+        row_ref, code_ref, power_ref = rest
+    count, depth, width = row_ref.shape
+    fields = u_ref.shape[1]
+    main = width // LANES
+    lane = lane_ids()
+    row_id = lax.broadcasted_iota(jnp.int32, (depth, 1), 0)
+    pieces = Pieces(map_ref, coef_ref, slab_ref)
+    lower = pieces.region == 0
+    before = slice(width - LANES, width)
+    base = count * depth
+    last_tiles = []
+    for f in range(first, first + count):
+        coef = pieces.piece(fields + f)
+        coefs = [coef(tile_at(t)) for t in range(main)]
+        middle = [drift_ref[1, f, :, tile_at(t)] + coefs[t] * box_ref[f, :, tile_at(t)] for t in range(main)]
+        local = drift_ref[0, f, :, before] + pieces.piece(f)(before) * lap_ref[f]
+        sums = nine_sum([local] + middle + [side_ref[f]], lane)
+        at = f - first
+        for t in range(main):
+            lanes = tile_at(t)
+            row = sums_ref[f : f + 1, lanes]
+            value = second_step(middle[t], u_ref[1, f, :, lanes], sums[t + 1], coefs[t], row_id, row, lower)
+            row_ref[at, :, lanes] = value
+            power = power_of(jnp.max(jnp.abs(value), axis=0, keepdims=True))
+            code_ref[at * depth : (at + 1) * depth, lanes] = narrow(coded(value, power))
+            power_ref[at : at + 1, lanes] = power
+        last_tiles.append(middle[main - 1])
+    power_ref[count:8, :] = jnp.zeros((8 - count, width), F32)
+    code_ref[base : base + 8, :] = narrow(power_ref[...])
+    if first == 0:
+        near = y_ref[0:16, before].astype(F32)
+        extra_ref[2:3, :] = jnp.zeros((1, width), F32) + jnp.where(owner_ref[1] != lax.axis_index("blk"), 1.0, 0.0)
+        extra_ref[3:8, :] = jnp.zeros((5, width), F32)
+        for f in range(fields):
+            if f < count:
+                stepped = last_tiles[f]
+            else:
+                stepped = drift_ref[1, f, :, before] + pieces.piece(fields + f)(before) * box_ref[f, :, before]
+            both = jnp.where(lane >= 96, u_ref[1, f, :, before], pltpu.roll(stepped, 96, 1))
+            rows = [near[4 + f : 5 + f], near[12 + f : 13 + f], tail_ref[f : f + 1, :]]
+            size = jnp.max(jnp.abs(both), axis=0, keepdims=True)
+            for row in rows:
+                size = jnp.maximum(size, jnp.abs(row))
+            power = power_of(size)
+            codes = narrow(coded(both, power))
+            here, there = tile_at(f), tile_at(fields + f)
+            code_ref[base + 8 : base + 8 + depth // 2, here] = codes[0 : depth // 2]
+            code_ref[base + 8 : base + 8 + depth // 2, there] = codes[depth // 2 : depth]
+            extra_ref[0:1, here] = power
+            extra_ref[0:1, there] = coded(rows[0], power)
+            extra_ref[1:2, here] = coded(rows[1], power)
+            extra_ref[1:2, there] = coded(rows[2], power)
+        code_ref[base + 8 + depth // 2 : base + 16 + depth // 2, :] = narrow(extra_ref[...])
+
+
+def first_row_body(map_ref, u_ref, coef_ref, slab_ref, box_ref, box1_ref, drift_ref, sums_ref, row_ref):
+    fields, depth, width = u_ref.shape[1:]
+    main = width // LANES
+    lane = lane_ids()
+    row_id = lax.broadcasted_iota(jnp.int32, (depth, 1), 0)
+    pieces = Pieces(map_ref, coef_ref, slab_ref)
+    lower = pieces.region == 0
+    after = slice(0, LANES)
+    for f in range(fields):
+        coef = pieces.piece(f)
+        coefs = [coef(tile_at(t)) for t in range(main)]
+        now = [drift_ref[0, f, :, tile_at(t)] + coefs[t] * box_ref[f, :, tile_at(t)] for t in range(main)]
+        local = drift_ref[1, f, :, after] + pieces.piece(fields + f)(after) * box1_ref[f, :, after]
+        sums = nine_sum(now + [local], lane)
+        for t in range(1, main):
+            lanes = tile_at(t)
+            row = sums_ref[f : f + 1, lanes]
+            row_ref[f, :, lanes] = second_step(now[t], u_ref[0, f, :, lanes], sums[t], coefs[t], row_id, row, lower)
+
+
+def arrival(code_ref):
+    rows = code_ref.shape[0]
+    return jnp.max(wide(code_ref[rows - 8 : rows, :])[2:3]) > 0.5
+
+
+def place_codes(code_ref, first, count, depth, row_ref, out_ref, sems, base):
+    scale = scale_of(wide(code_ref[count * depth : count * depth + 8, :]))
+    part = depth // 2
+    copies = []
+    for f in range(count):
+        for h in range(2):
+            rows = slice(h * part, (h + 1) * part)
+            start = f * depth + h * part
+            row_ref[f, rows] = wide(code_ref[start : start + part, :]) * scale[f : f + 1]
+            sem = sems.at[base + 2 * f + h]
+            copies.append(pltpu.make_async_copy(row_ref.at[f, rows], out_ref.at[0, first + f, rows], sem))
+            copies[-1].start()
+    return copies
+
+
+def finish_body(
+    owner_ref, map_ref, u_ref, coef_ref, slab_ref, y_ref, box_ref, drift_ref, tail_ref, code_ref, row_ref,
+    last_a_ref, last_b_ref, out_ref, tile_ref, zero_ref, arrived_ref, sems
+):
+    fields, depth, width = u_ref.shape[1:]
+    half = last_a_ref.shape[0]
+    base = half * depth
+    lane = lane_ids()
+    row_id = lax.broadcasted_iota(jnp.int32, (depth, 1), 0)
+    arrives = arrival(code_ref)
+    slot = jnp.where(arrives, 1, 0)
+    keeps = owner_ref[1] == lax.axis_index("blk")
+
+    def row_copies(at, sources, base):
+        return [
+            pltpu.make_async_copy(source, out_ref.at[at, f], sems.at[base + f]) for f, source in enumerate(sources)
+        ]
+
+    mine = [last_a_ref.at[f] for f in range(half)] + [last_b_ref.at[f] for f in range(fields - half)]
+    kept = row_copies(slot + 1, mine, 0)
+    blank = row_copies(slot + 1, [zero_ref] * fields, 0)
+    third = row_copies(2, [zero_ref] * fields, fields)
+    rest = slice(LANES, width)
+    firsts = [
+        pltpu.make_async_copy(row_ref.at[f, :, rest], out_ref.at[slot, f, :, rest], sems.at[2 * fields + f])
+        for f in range(fields)
+    ]
+    for copy in firsts:
+        copy.start()
+
+    @pl.when(keeps)
+    def _():
+        for copy in kept:
+            copy.start()
+
+    zero_ref[...] = jnp.zeros(zero_ref.shape, F32)
+
+    @pl.when(jnp.logical_not(keeps))
+    def _():
+        for copy in blank:
+            copy.start()
+
+    @pl.when(jnp.logical_not(arrives))
+    def _():
+        for copy in third:
+            copy.start()
+
+    column = ColumnEdge(coef_ref, y_ref)
+    pieces = Pieces(map_ref, coef_ref, slab_ref)
+    extra = wide(code_ref[base + 8 + depth // 2 : base + 16 + depth // 2, :])
+    tile0, tile1 = tile_at(0), tile_at(1)
+    near = column.near(0, tile0)
+    corners = [[], [], []]
+    rims, before, stepped, nexts, coefs = [], [], [], [], []
+    for f in range(fields):
+        here, there = tile_at(f), tile_at(fields + f)
+        scale = scale_of(extra[0:1, here])
+        corners[0].append(extra[0:1, there] * scale)
+        corners[1].append(extra[1:2, here] * scale)
+        corners[2].append(extra[1:2, there] * scale)
+        upper = wide(code_ref[base + 8 : base + 8 + depth // 2, here])
+        under = wide(code_ref[base + 8 : base + 8 + depth // 2, there])
+        before.append(jnp.concatenate([upper, under], axis=0) * scale)
+    corners = [jnp.concatenate(rows, axis=0) for rows in corners]
+    near_sum = nine_sum([corners[0], near, column.near(0, tile1)], lane)[1]
+    beyond_sum = nine_sum([corners[1], column.beyond(0, tile0), column.beyond(0, tile1)], lane)[1]
+    for f in range(fields):
+        now = u_ref[0, f, :, tile0]
+        total = nine_sum([before[f], now, u_ref[0, f, :, tile1]], lane)[1]
+        rims.append(column.own(total))
+        low_row, high_row = column.rows(near_sum[f : f + 1])
+        lap = column_sum(total, row_id, low_row, high_row) - 27.0 * now
+        coef = pieces.piece(f)
+        coefs.append(coef(tile0))
+        stepped.append(drift_ref[0, f, :, tile0] + coefs[f] * lap)
+        nexts.append(drift_ref[0, f, :, tile1] + coef(tile1) * box_ref[f, :, tile1])
+    box = near_sum + beyond_sum + jnp.concatenate(rims, axis=0)
+    edge = column.ahead(0, tile0) + column.coefs(0, tile0) * (box - 27.0 * near)
+    edge_sum = nine_sum([corners[2], edge, tail_ref[0:4, :]], lane)[1]
+    for f in range(fields):
+        total = nine_sum([pltpu.roll(before[f], 32, 1), stepped[f], nexts[f]], lane)[1]
+        row = edge_sum[f : f + 1]
+        tile_ref[f] = second_step(stepped[f], u_ref[0, f, :, tile0], total, coefs[f], row_id, row, column.lower)
+    last = pltpu.make_async_copy(tile_ref, out_ref.at[slot, :, :, tile0], sems.at[3 * fields])
+    last.start()
+
+    @pl.when(arrives)
+    def _():
+        for copy in place_codes(code_ref, 0, half, depth, arrived_ref, out_ref, sems, 3 * fields + 1):
+            copy.wait()
+
+    @pl.when(keeps)
+    def _():
+        for copy in kept:
+            copy.wait()
+
+    @pl.when(jnp.logical_not(keeps))
+    def _():
+        for copy in blank:
+            copy.wait()
+
+    @pl.when(jnp.logical_not(arrives))
+    def _():
+        for copy in third:
+            copy.wait()
+
+    for copy in firsts:
+        copy.wait()
+    last.wait()
+
+
+def place_body(first, code_a_ref, code_ref, partial_ref, out_ref, row_ref, sems):
+    count, depth, _ = row_ref.shape
+
+    @pl.when(arrival(code_a_ref))
+    def _():
+        for copy in place_codes(code_ref, first, count, depth, row_ref, out_ref, sems, 0):
+            copy.wait()
+
+
+def fast_on_device(u_now, u_prev, coef_store, store_map, new_owner):
+    blocks, _, fields, depth, width = u_now.shape
+    now = u_now.reshape(blocks, fields, depth, width)
+    prev = u_prev.reshape(blocks, fields, depth, width)
+    coef = coef_store[0, 0]
+    count = lax.axis_size("blk")
+    order = store_map.reshape(-1)
+    owner_hbm, order_hbm, now_hbm, prev_hbm, coef_hbm = (
+        pltpu.with_memory_space_constraint(array, pltpu.HBM) for array in (new_owner, order, now, prev, coef)
+    )
+    params = pltpu.CompilerParams(vmem_limit_bytes=48 * 1024 * 1024)
+
+    def call(body, name, out_shape, in_specs, out_specs, scratch, args, **options):
+        return pl.pallas_call(
+            body,
+            out_shape=out_shape,
+            in_specs=in_specs,
+            out_specs=out_specs,
+            scratch_shapes=scratch,
+            compiler_params=params,
+            name=name,
+            **options,
+        )(*args)
+
+    slab_shape = jax.ShapeDtypeStruct(coef.shape[1:], BF16)
+    slab_out = call(pack_slab_body, "pack_slab", slab_shape, [HBM], VMEM, [pltpu.SemaphoreType.DMA((8,))], (coef_hbm,))
+    straight = jax.ShapeDtypeStruct((fields * depth + 16, LANES), BF16)
+    diag = jax.ShapeDtypeStruct((depth + 32, LANES), BF16)
+    y_out, left, dleft = call(
+        pack_edges_body,
+        "pack_edges",
+        (jax.ShapeDtypeStruct((depth, width), BF16), straight, diag),
+        [HBM] * 4,
+        (VMEM,) * 3,
+        [
+            pltpu.VMEM((depth, width), F32),
+            pltpu.VMEM((blocks, fields, 8, width), F32),
+            pltpu.VMEM((blocks, fields, 8, width), F32),
+            pltpu.VMEM((4, 16, width), BF16),
+            pltpu.VMEM((fields, depth, LANES), F32),
+            pltpu.VMEM((fields, depth, LANES), F32),
+            pltpu.VMEM((2, 4, depth, LANES), BF16),
+            pltpu.SMEM(order.shape, jnp.int32),
+            pltpu.SemaphoreType.DMA((7,)),
+        ],
+        (order_hbm, now_hbm, prev_hbm, coef_hbm),
+    )
+
+    swap = [(0, 1), (1, 0)]
+    forward = [(i, (i + 1) % count) for i in range(count)]
+    backward = [(i, (i - 1) % count) for i in range(count)]
+    crossed = [(r * count + i, (1 - r) * count + (i - 1) % count) for r in range(2) for i in range(count)]
+    slab = lax.ppermute(slab_out, "region", swap)
+    y_in = lax.ppermute(y_out, "region", swap)
+    from_right = lax.ppermute(left, "blk", backward)
+    from_dright = lax.ppermute(dleft, ("region", "blk"), crossed)
+
+    row = jax.ShapeDtypeStruct((fields, depth, width), F32)
+    box0, box1, drift, rim = call(
+        local_body,
+        "local",
+        (row, row, jax.ShapeDtypeStruct(now.shape, F32), jax.ShapeDtypeStruct((blocks, 8, width), F32)),
+        [VMEM] * 2,
+        (VMEM,) * 4,
+        [],
+        (now, prev),
+    )
+    tiles = jax.ShapeDtypeStruct((fields, depth, LANES), F32)
+    sums = jax.ShapeDtypeStruct((8, width), F32)
+    tail = jax.ShapeDtypeStruct((8, LANES), F32)
+    box1, lap1, side1, sums1, tail1 = call(
+        last_edges_body,
+        "last_edges",
+        (row, tiles, tiles, sums, tail),
+        [VMEM] * 8,
+        (VMEM,) * 5,
+        [],
+        (now, coef, y_in, from_right, from_dright, box0, rim, box1),
+        input_output_aliases={7: 0},
+    )
+    half = fields // 2
+    part = jax.ShapeDtypeStruct((half, depth, width), F32)
+    codes = jax.ShapeDtypeStruct((half * depth + 8, width), jnp.int16)
+    more_codes = jax.ShapeDtypeStruct((half * depth + depth // 2 + 16, width), jnp.int16)
+    stepping = (order, now, coef, slab, box1, drift, lap1, side1, sums1)
+    powers = pltpu.VMEM((8, width), F32)
+    last_a, code_a = call(
+        functools.partial(last_row_body, 0),
+        "last_row",
+        (part, more_codes),
+        [SMEM] + [VMEM] * 8 + [SMEM] + [VMEM] * 2,
+        (VMEM,) * 2,
+        [powers, powers],
+        stepping + (new_owner, y_in, tail1),
+    )
+    arrived_a = lax.ppermute(code_a, "blk", forward)
+    last_b, code_b = call(
+        functools.partial(last_row_body, half), "last_row", (part, codes), [SMEM] + [VMEM] * 8, (VMEM,) * 2, [powers], stepping
+    )
+    arrived_b = lax.ppermute(code_b, "blk", forward)
+    box0, sums0, tail0 = call(
+        first_edges_body,
+        "first_edges",
+        (row, sums, tail),
+        [VMEM] * 6,
+        (VMEM,) * 3,
+        [],
+        (now, coef, y_in, box1, rim, box0),
+        input_output_aliases={5: 0},
+    )
+    first = call(
+        first_row_body,
+        "first_row",
+        row,
+        [SMEM] + [VMEM] * 7,
+        VMEM,
+        [],
+        (order, now, coef, slab, box0, box1, drift, sums0),
+    )
+    whole = jax.ShapeDtypeStruct((blocks + 1, fields, depth, width), F32)
+    result = call(
+        finish_body,
+        "finish",
+        whole,
+        [SMEM] * 2 + [VMEM] * 11,
+        ANY,
+        [
+            pltpu.VMEM((fields, depth, LANES), F32),
+            pltpu.VMEM((depth, width), F32),
+            pltpu.VMEM((half, depth, width), F32),
+            pltpu.SemaphoreType.DMA((3 * fields + 1 + 2 * half,)),
+        ],
+        (new_owner, order, now, coef, slab, y_in, box0, drift, tail0, arrived_a, first, last_a, last_b),
+    )
+    result = call(
+        functools.partial(place_body, half),
+        "place",
+        whole,
+        [VMEM, VMEM, ANY],
+        ANY,
+        [pltpu.VMEM((half, depth, width), F32), pltpu.SemaphoreType.DMA((2 * half,))],
+        (arrived_a, arrived_b, result),
+        input_output_aliases={2: 0},
+    )
+    return result[:, None]
+
+
 def solution(mesh):
+    def on_device(*args):
+        blocks = args[0].shape[0]
+        if lax.axis_size("region") == 2 and blocks == 2:
+            return fast_on_device(*args)
+        return general_on_device(*args)
+
     return jax.shard_map(
         on_device,
         mesh=mesh,

time: 75 us -> 26.3 us (0.35)
  waiting for transfers between devices: 20.6 us -> 3.99 us
  other arithmetic: 16.5 us -> 0 us
  starting transfers between devices: 25.5 us -> 10.2 us
  Pallas kernels: 0 us -> 11.8 us
  local copies, waits for them, and re-layouts: 9.23 us -> 0.03 us
  between operations: 2.7 us -> 0.14 us
    ppermute x10 -> x6, waiting for transfers between devices: 20.6 us -> 3.99 us  [the longest x1 3.83 us: fast_on_device(): arrived_a = lax.ppermute(code_a, 'blk', forward)]
    pallas_call x0 -> x10, Pallas kernels: none -> 11.8 us  [call(): pl.pallas_call(body, out_shape=out_shape, in_specs=in_specs, out_specs=ou...]
    ppermute x10 -> x6, starting transfers between devices: 21.6 us -> 10.2 us  [the longest x1 3.88 us: fast_on_device(): from_right = lax.ppermute(left, 'blk', backward)]
    add x6 -> x0, other arithmetic: 10.9 us -> none  [the longest x2 6.98 us: stencil_step(): shifted[..., :width] * lower_mask + extended + shifted[..., 2:] * upper_mask]
    all_to_all x1 -> x0, starting transfers between devices: 3.92 us -> none  [on_device(): lax.all_to_all(store_local, 'region', split_axis=0, concat_axis=0, tiled=...]
    concatenate x2 -> x0, local copies, waits for them, and re-layouts: 3.89 us -> none  [stencil_step(): extended = jnp.concatenate([before_planes, padded, after_planes], axis=-1)]
    slice x5 -> x0, local copies, waits for them, and re-layouts: 2.73 us -> none  [the longest x1 1.35 us: on_device(): keep_first = (new_owner[0] == own_index).astype(jnp.int32).reshape(1)]
    select_n x4 -> x0, other arithmetic: 2.16 us -> none  [the longest x1 1.39 us: compact(): jnp.where(filled.reshape((slot_count,) + (1,) * (member.ndim - 1)), jnp.t...]
  transfers between devices with their start and end apart: 11 -> 6, of which waited for: 6 -> 2; matrix products, arithmetic and copies ran while one was open for 13% -> 0% of each run, Pallas kernels for 0% -> 33%
where the time goes in v5:
time: 26.3 us; the launch traced here: 26.2 us
  Pallas kernels  11.8 us (45%)
  starting transfers between devices  10.2 us (39%)
  waiting for transfers between devices  3.99 us (15%)
    pallas_call x10, Pallas kernels, call(): pl.pallas_call(body, out_shape=out_shape, in_specs=in_specs, out_specs=ou...  11.8 us
    ppermute x1, starting transfers between devices, fast_on_device(): from_right = lax.ppermute(left, 'blk', backward)  3.88 us
    ppermute x1, waiting for transfers between devices, fast_on_device(): arrived_a = lax.ppermute(code_a, 'blk', forward)  3.83 us
    ppermute x1, starting transfers between devices, fast_on_device(): slab = lax.ppermute(slab_out, 'region', swap)  3.03 us
    ppermute x1, starting transfers between devices, fast_on_device(): from_dright = lax.ppermute(dleft, ('region', 'blk'), crossed)  2.19 us
    ppermute x1, starting transfers between devices, fast_on_device(): arrived_b = lax.ppermute(code_b, 'blk', forward)  0.99 us
  transfers between devices with their start and end apart: 6, of which 2 were waited for; matrix products, arithmetic and copies ran while one was open for 0% of the time, Pallas kernels for 33%

profile of v5, /device:TPU:0, one launch (start us, length us, event | category | flops | bytes accessed | tf_op | source)
XLA Modules:
  0.0 26.2 jit_solution(9759254298713189057)
XLA Ops:
  0.0 0.0 copy-start
  0.0 0.0 copy-start.2
  0.0 1.1 %pack_slab.1 = bf16[4,32,1024]{2,1,0:T(8,128)(2,1)S(1)} custom-call(bf16[2,4,32,1024]{3,2,1,0:T(8,128)(2,1)} %bitcast.15), custom_call_target="tpu_custom_call" | custom-call | tf_op jit(solution)/shard_map/pack_slab/pallas_call | solution.py:707
  1.1 3.0 %collective-permute-start = (bf16[4,32,1024]{2,1,0:T(8,128)(2,1)S(1)}, bf16[4,32,1024]{2,1,0:T(8,128)(2,1)S(1)}, u32[]{:S(2)}, u32[]{:S(2)}) collective-permute-start(bf16[4,32,1024]{2,1,0:T(8,128)(2,1)S(1)} %pack_slab.1), channel_id=1, source_target_pairs={{0,16},{16,0},{1,17},{17,1},{2,18},{18,2},{3,19},{19,3},{4,20},{20... | collective-permute-start | bytes 786440 | tf_op jit(solution)/shard_map/ppermute | solution.py:746
  4.1 1.3 %pack_edges.1 = (bf16[32,1024]{1,0:T(8,128)(2,1)S(1)}, bf16[144,128]{1,0:T(8,128)(2,1)S(1)}, bf16[64,128]{1,0:T(8,128)(2,1)S(1)}) custom-call(s32[8]{0:T(128)} %bitcast.25, f32[2,4,32,1024]{3,2,1,0:T(8,128)} %bitcast.7, f32[2,4,32,1024]{3,2,1,0:T(8,128)} %bitcast.23, bf16[2,4,32,1024]{3,2,1,0:T(8,128)(2,1)} %bitcast.16), custom_call_target="tpu_custom_call" | custom-call | tf_op jit(solution)/shard_map/pack_edges/pallas_call | solution.py:707
  5.4 0.0 copy-start.1
  5.4 0.1 collective-permute-start.1
  5.5 3.9 %collective-permute-start.2 = (bf16[144,128]{1,0:T(8,128)(2,1)S(1)}, bf16[144,128]{1,0:T(8,128)(2,1)S(1)}, u32[]{:S(2)}, u32[]{:S(2)}) collective-permute-start(bf16[144,128]{1,0:T(8,128)(2,1)S(1)} %get-tuple-element.25), channel_id=1, source_target_pairs={{0,15},{1,0},{2,1},{3,2},{4,3},{5,4},{6,5},{7,6},{8,7},{9,8},{10,9... | collective-permute-start | bytes 110600 | tf_op jit(solution)/shard_map/ppermute | solution.py:748
  9.4 2.2 %collective-permute-start.3 = (bf16[64,128]{1,0:T(8,128)(2,1)S(1)}, bf16[64,128]{1,0:T(8,128)(2,1)S(1)}, u32[]{:S(2)}, u32[]{:S(2)}) collective-permute-start(bf16[64,128]{1,0:T(8,128)(2,1)S(1)} %get-tuple-element.26), channel_id=1, source_target_pairs={{0,31},{1,16},{2,17},{3,18},{4,19},{5,20},{6,21},{7,22},{8,23},{9,... | collective-permute-start | bytes 49160 | tf_op jit(solution)/shard_map/ppermute | solution.py:749
  11.6 0.0 copy-done
  11.6 0.0 copy-done.2
  11.6 1.3 %local.1 = (f32[4,32,1024]{2,1,0:T(8,128)S(1)}, f32[4,32,1024]{2,1,0:T(8,128)S(1)}, f32[2,4,32,1024]{3,2,1,0:T(8,128)S(1)}, f32[2,8,1024]{2,1,0:T(8,128)S(1)}) custom-call(f32[2,4,32,1024]{3,2,1,0:T(8,128)S(1)} %bitcast.8, f32[2,4,32,1024]{3,2,1,0:T(8,128)S(1)} %bitcast.24), custom_call_target="tpu_custom_call" | custom-call | tf_op jit(solution)/shard_map/local/pallas_call | solution.py:707
  12.9 0.0 copy-start.3
  12.9 0.0 copy-start.4
  12.9 0.1 collective-permute-done.3.diag_ref
  13.1 0.0 collective-permute-done.2.straight_ref
  13.1 0.0 collective-permute-done.1.y_ref.rest_1_
  13.1 0.0 copy-done.1
  13.1 0.6 %last_edges.1 = (f32[4,32,1024]{2,1,0:T(8,128)S(1)}, f32[4,32,128]{2,1,0:T(8,128)S(1)}, f32[4,32,128]{2,1,0:T(8,128)S(1)}, f32[8,1024]{1,0:T(8,128)S(1)}, f32[8,128]{1,0:T(8,128)S(1)}) custom-call(f32[2,4,32,1024]{3,2,1,0:T(8,128)S(1)} %bitcast.9, bf16[2,4,32,1024]{3,2,1,0:T(8,128)(2,1)S(1)} %bitcast.17, ...), custom_call_target="tpu_custom_call", output_to_operand_aliasing={{0}: (7, {})} | custom-call | tf_op jit(solution)/shard_map/last_edges/pallas_call | solution.py:707
  13.7 0.0 collective-permute-done.slab_ref
  13.7 0.0 copy-done.3
  13.7 0.0 copy-done.4
  13.7 1.2 %last_row.2 = (f32[2,32,1024]{2,1,0:T(8,128)S(1)}, s16[96,1024]{1,0:T(8,128)(2,1)S(1)}) custom-call(s32[8]{0:T(128)S(1)} %bitcast.26, f32[2,4,32,1024]{3,2,1,0:T(8,128)S(1)} %bitcast.10, bf16[2,4,32,1024]{3,2,1,0:T(8,128)(2,1)S(1)} %bitcast.18, bf16[4,32,1024]{2,1,0:T(8,128)(2,1)S(1)} %collective-permute-done.slab_ref, ...), custom_call_target="tpu_custom_call" | custom-call | tf_op jit(solution)/shard_map/last_row/pallas_call | solution.py:707
  14.9 0.1 collective-permute-start.4
  15.0 1.1 %last_row.3 = (f32[2,32,1024]{2,1,0:T(8,128)S(1)}, s16[72,1024]{1,0:T(8,128)(2,1)S(1)}) custom-call(s32[8]{0:T(128)S(1)} %bitcast.27, f32[2,4,32,1024]{3,2,1,0:T(8,128)S(1)} %bitcast.11, bf16[2,4,32,1024]{3,2,1,0:T(8,128)(2,1)S(1)} %bitcast.19, bf16[4,32,1024]{2,1,0:T(8,128)(2,1)S(1)} %collective-permute-done.slab_ref, ...), custom_call_target="tpu_custom_call" | custom-call | tf_op jit(solution)/shard_map/last_row/pallas_call | solution.py:707
  16.2 1.0 %collective-permute-start.5 = (s16[72,1024]{1,0:T(8,128)(2,1)S(1)}, s16[72,1024]{1,0:T(8,128)(2,1)S(1)}, u32[]{:S(2)}, u32[]{:S(2)}) collective-permute-start(s16[72,1024]{1,0:T(8,128)(2,1)S(1)} %get-tuple-element.37), channel_id=1, source_target_pairs={{0,1},{1,2},{2,3},{3,4},{4,5},{5,6},{6,7},{7,8},{8,9},{9,10},{10,1... | collective-permute-start | bytes 442376 | tf_op jit(solution)/shard_map/ppermute | solution.py:793
  17.2 0.4 %first_edges.1 = (f32[4,32,1024]{2,1,0:T(8,128)S(1)}, f32[8,1024]{1,0:T(8,128)S(1)}, f32[8,128]{1,0:T(8,128)S(1)}) custom-call(f32[2,4,32,1024]{3,2,1,0:T(8,128)S(1)} %bitcast.12, bf16[2,4,32,1024]{3,2,1,0:T(8,128)(2,1)S(1)} %bitcast.20, bf16[32,1024]{1,0:T(8,128)(2,1)S(1)} %collective-permute-done.1.y_ref.rest_1_, ...), custom_call_target="tpu_custom_call", output_to_operand_aliasing={{0}: (5, {})} | custom-call | tf_op jit(solution)/shard_map/first_edges/pallas_call | solution.py:707
  17.5 1.4 %first_row.1.row_ref = f32[4,32,1024]{2,1,0:T(8,128)S(1)} custom-call(s32[8]{0:T(128)S(1)} %bitcast.28, f32[2,4,32,1024]{3,2,1,0:T(8,128)S(1)} %bitcast.13, bf16[2,4,32,1024]{3,2,1,0:T(8,128)(2,1)S(1)} %bitcast.21, bf16[4,32,1024]{2,1,0:T(8,128)(2,1)S(1)} %collective-permute-done.slab_ref, f32[4,32,1024]{2,1,0:T(8,128)S(1)} %get-tuple-element.38.box_ref, ...), custom_call_target="tpu_custom_call" | custom-call | tf_op jit(solution)/shard_map/first_row/pallas_call | solution.py:707
  19.0 3.8 %collective-permute-done.4.code_ref.code_a_ref = s16[96,1024]{1,0:T(8,128)(2,1)S(1)} collective-permute-done((s16[96,1024]{1,0:T(8,128)(2,1)S(1)}, s16[96,1024]{1,0:T(8,128)(2,1)S(1)}, u32[]{:S(2)}, u32[]{:S(2)}) %collective-permute-start.4) | collective-permute-done | bytes 196640 | tf_op jit(solution)/shard_map/ppermute | solution.py:789
  22.8 2.5 %finish.1.partial_ref = f32[3,4,32,1024]{3,2,1,0:T(8,128)} custom-call(s32[2]{0:T(128)S(1)} %copy-done.4, s32[8]{0:T(128)S(1)} %bitcast.29, f32[2,4,32,1024]{3,2,1,0:T(8,128)S(1)} %bitcast.14, bf16[2,4,32,1024]{3,2,1,0:T(8,128)(2,1)S(1)} %bitcast.22, bf16[4,32,1024]{2,1,0:T(8,128)(2,1)S(1)} %collective-permute-done.slab_ref, ...), custom_call_target="tpu_custom_call" | custom-call | tf_op jit(solution)/shard_map/finish/pallas_call | solution.py:707
  25.3 0.0 collective-permute-done.5.code_ref
  25.3 0.9 %place.1 = f32[3,4,32,1024]{3,2,1,0:T(8,128)} custom-call(s16[96,1024]{1,0:T(8,128)(2,1)S(1)} %collective-permute-done.4.code_ref.code_a_ref, s16[72,1024]{1,0:T(8,128)(2,1)S(1)} %collective-permute-done.5.code_ref, f32[3,4,32,1024]{3,2,1,0:T(8,128)} %finish.1.partial_ref), custom_call_target="tpu_custom_call", output_to_operand_aliasing={{}: (2, {})} | custom-call | tf_op jit(solution)/shard_map/place/pallas_call | solution.py:707
Async XLA Ops:
  0.0 11.6 %copy-start = (f32[2,1,4,32,1024]{4,3,2,1,0:T(8,128)S(1)}, f32[2,1,4,32,1024]{4,3,2,1,0:T(8,128)}, u32[]{:S(2)}) copy-start(f32[2,1,4,32,1024]{4,3,2,1,0:T(8,128)} %param.5) | copy-start | bytes 3145732
  0.0 11.6 %copy-start.2 = (f32[2,1,4,32,1024]{4,3,2,1,0:T(8,128)S(1)}, f32[2,1,4,32,1024]{4,3,2,1,0:T(8,128)}, u32[]{:S(2)}) copy-start(f32[2,1,4,32,1024]{4,3,2,1,0:T(8,128)} %param.6) | copy-start | bytes 3145732
  1.1 12.6 %collective-permute-start = (bf16[4,32,1024]{2,1,0:T(8,128)(2,1)S(1)}, bf16[4,32,1024]{2,1,0:T(8,128)(2,1)S(1)}, u32[]{:S(2)}, u32[]{:S(2)}) collective-permute-start(bf16[4,32,1024]{2,1,0:T(8,128)(2,1)S(1)} %pack_slab.1), channel_id=1, source_target_pairs={{0,16},{16,0},{1,17},{17,1},{2,18},{18,2},{3,19},{19,3},{4,20},{20... | collective-permute-start | bytes 786440 | tf_op jit(solution)/shard_map/ppermute | solution.py:746
  5.4 7.6 %copy-start.1 = (bf16[1,1,2,4,32,1024]{5,4,3,2,1,0:T(8,128)(2,1)S(1)}, bf16[1,1,2,4,32,1024]{5,4,3,2,1,0:T(8,128)(2,1)}, u32[]{:S(2)}) copy-start(bf16[1,1,2,4,32,1024]{5,4,3,2,1,0:T(8,128)(2,1)} %param.7) | copy-start | bytes 1572868
  5.4 7.6 %collective-permute-start.1 = (bf16[32,1024]{1,0:T(8,128)(2,1)S(1)}, bf16[32,1024]{1,0:T(8,128)(2,1)S(1)}, u32[]{:S(2)}, u32[]{:S(2)}) collective-permute-start(bf16[32,1024]{1,0:T(8,128)(2,1)S(1)} %get-tuple-element.24), channel_id=1, source_target_pairs={{0,16},{16,0},{1,17},{17,1},{2,18},{18,2},{3,19},{19,3},{4,20},{20... | collective-permute-start | bytes 196616 | tf_op jit(solution)/shard_map/ppermute | solution.py:747
  5.5 7.5 %collective-permute-start.2 = (bf16[144,128]{1,0:T(8,128)(2,1)S(1)}, bf16[144,128]{1,0:T(8,128)(2,1)S(1)}, u32[]{:S(2)}, u32[]{:S(2)}) collective-permute-start(bf16[144,128]{1,0:T(8,128)(2,1)S(1)} %get-tuple-element.25), channel_id=1, source_target_pairs={{0,15},{1,0},{2,1},{3,2},{4,3},{5,4},{6,5},{7,6},{8,7},{9,8},{10,9... | collective-permute-start | bytes 110600 | tf_op jit(solution)/shard_map/ppermute | solution.py:748
  9.4 3.6 %collective-permute-start.3 = (bf16[64,128]{1,0:T(8,128)(2,1)S(1)}, bf16[64,128]{1,0:T(8,128)(2,1)S(1)}, u32[]{:S(2)}, u32[]{:S(2)}) collective-permute-start(bf16[64,128]{1,0:T(8,128)(2,1)S(1)} %get-tuple-element.26), channel_id=1, source_target_pairs={{0,31},{1,16},{2,17},{3,18},{4,19},{5,20},{6,21},{7,22},{8,23},{9,... | collective-permute-start | bytes 49160 | tf_op jit(solution)/shard_map/ppermute | solution.py:749
  12.9 0.8 %copy-start.3 = (s32[1,1,8]{2,1,0:T(1,128)S(1)}, s32[1,1,8]{2,1,0:T(1,128)}, u32[]{:S(2)}) copy-start(s32[1,1,8]{2,1,0:T(1,128)} %param.8) | copy-start | bytes 100
  12.9 0.8 %copy-start.4 = (s32[2]{0:T(128)S(1)}, s32[2]{0:T(128)}, u32[]{:S(2)}) copy-start(s32[2]{0:T(128)} %owner_ref.1) | copy-start | bytes 28
  14.9 7.8 %collective-permute-start.4 = (s16[96,1024]{1,0:T(8,128)(2,1)S(1)}, s16[96,1024]{1,0:T(8,128)(2,1)S(1)}, u32[]{:S(2)}, u32[]{:S(2)}) collective-permute-start(s16[96,1024]{1,0:T(8,128)(2,1)S(1)} %get-tuple-element.36), channel_id=1, source_target_pairs={{0,1},{1,2},{2,3},{3,4},{4,5},{5,6},{6,7},{7,8},{8,9},{9,10},{10,1... | collective-permute-start | bytes 589832 | tf_op jit(solution)/shard_map/ppermute | solution.py:789
  16.2 9.1 %collective-permute-start.5 = (s16[72,1024]{1,0:T(8,128)(2,1)S(1)}, s16[72,1024]{1,0:T(8,128)(2,1)S(1)}, u32[]{:S(2)}, u32[]{:S(2)}) collective-permute-start(s16[72,1024]{1,0:T(8,128)(2,1)S(1)} %get-tuple-element.37), channel_id=1, source_target_pairs={{0,1},{1,2},{2,3},{3,4},{4,5},{5,6},{6,7},{7,8},{8,9},{9,10},{10,1... | collective-permute-start | bytes 442376 | tf_op jit(solution)/shard_map/ppermute | solution.py:793

commit v6 on v5

--- a/solution.py
+++ b/solution.py
@@ -138,67 +138,52 @@
     return [jnp.zeros((1, LANES), F32) + number.astype(F32) for number in numbers]
 
 
-def pack_slab_body(coef_ref, slab_ref, sems):
-    other = 1 - lax.axis_index("region")
-    half = coef_ref.shape[2] // 2
-    copies = []
-    for s in range(4):
-        for h in range(2):
-            part = slice(h * half, (h + 1) * half)
-            copies.append(
-                pltpu.make_async_copy(coef_ref.at[other, s, part], slab_ref.at[s, part], sems.at[2 * s + h])
-            )
+def edge_copies(u_ref, p_ref, coef_ref, ue_ref, pe_ref, ce_ref, some, region, sems):
+    lower = region == 0
+    depth = u_ref.shape[2]
+    edge8 = edge_start(lower, depth, 8)
+    edge16 = edge_start(lower, depth, 16)
+    rows, lanes = some
+    return [
+        pltpu.make_async_copy(u_ref.at[rows, :, pl.ds(edge8, 8), lanes], ue_ref, sems.at[0]),
+        pltpu.make_async_copy(p_ref.at[rows, :, pl.ds(edge8, 8), lanes], pe_ref, sems.at[1]),
+        pltpu.make_async_copy(coef_ref.at[region, :, pl.ds(edge16, 16), lanes], ce_ref, sems.at[2]),
+    ]
+
+
+def edge_rows(ue_ref, pe_ref, m, f, lower):
+    own_edge = jnp.where(lower, 7, 0)
+    own_next = jnp.where(lower, 6, 1)
+    near = ue_ref[m, f, pl.ds(own_edge, 1), :]
+    return near, ue_ref[m, f, pl.ds(own_next, 1), :], 2.0 * near - pe_ref[m, f, pl.ds(own_edge, 1), :]
+
+
+def edge_piece(ce_ref, s, lower):
+    piece = ce_ref[s].astype(F32)
+    return jnp.where(lower, piece[15:16], piece[0:1])
+
+
+def pack_back_body(
+    map_hbm, u_ref, p_ref, coef_ref, straight_ref, diag_ref, ue_ref, pe_ref, ce_ref, ua_ref, pa_ref, ca_ref, map_ref, sems
+):
+    fields = u_ref.shape[1]
+    depth = u_ref.shape[2]
+    region = lax.axis_index("region")
+    lower = region == 0
+    other = 1 - region
+    front = slice(0, LANES)
+    copies = [
+        pltpu.make_async_copy(map_hbm, map_ref, sems.at[3]),
+        pltpu.make_async_copy(u_ref.at[0, :, :, front], ua_ref, sems.at[4]),
+        pltpu.make_async_copy(p_ref.at[0, :, :, front], pa_ref, sems.at[5]),
+        pltpu.make_async_copy(coef_ref.at[:, :, :, front], ca_ref, sems.at[6]),
+    ] + edge_copies(u_ref, p_ref, coef_ref, ue_ref, pe_ref, ce_ref, (slice(0, 1), front), region, sems)
     for copy in copies:
         copy.start()
     for copy in copies:
         copy.wait()
-
-
-def pack_edges_body(
-    map_hbm, u_ref, p_ref, coef_ref, y_ref, straight_ref, diag_ref,
-    rows_ref, ue_ref, pe_ref, ce_ref, ua_ref, pa_ref, ca_ref, map_ref, sems
-):
-    fields = u_ref.shape[1]
-    depth = u_ref.shape[2]
-    top = depth - 1
-    region = lax.axis_index("region")
-    lower = region == 0
-    other = 1 - region
-    edge8 = edge_start(lower, depth, 8)
-    edge16 = edge_start(lower, depth, 16)
-    copies = [
-        pltpu.make_async_copy(map_hbm, map_ref, sems.at[0]),
-        pltpu.make_async_copy(u_ref.at[:, :, pl.ds(edge8, 8), :], ue_ref, sems.at[1]),
-        pltpu.make_async_copy(p_ref.at[:, :, pl.ds(edge8, 8), :], pe_ref, sems.at[2]),
-        pltpu.make_async_copy(coef_ref.at[region, :, pl.ds(edge16, 16), :], ce_ref, sems.at[3]),
-        pltpu.make_async_copy(u_ref.at[0, :, :, 0:LANES], ua_ref, sems.at[4]),
-        pltpu.make_async_copy(p_ref.at[0, :, :, 0:LANES], pa_ref, sems.at[5]),
-        pltpu.make_async_copy(coef_ref.at[:, :, :, 0:LANES], ca_ref, sems.at[6]),
-    ]
-    for copy in copies:
-        copy.start()
-    for copy in copies[:4]:
-        copy.wait()
     lane = lane_ids()
-    own_edge = jnp.where(lower, 7, 0)
-    own_next = jnp.where(lower, 6, 1)
-    for m in range(2):
-        for f in range(fields):
-            at = m * fields + f
-            near = ue_ref[m, f, pl.ds(own_edge, 1), :]
-            rows_ref[at : at + 1, :] = near
-            rows_ref[8 + at : 9 + at, :] = ue_ref[m, f, pl.ds(own_next, 1), :]
-            rows_ref[16 + at : 17 + at, :] = 2.0 * near - pe_ref[m, f, pl.ds(own_edge, 1), :]
-    for s in range(4):
-        piece = ce_ref[s].astype(F32)
-        rows_ref[24 + s : 25 + s, :] = jnp.where(lower, piece[15:16], piece[0:1])
     tag_rows = tag_values(map_ref, region)
-    for i, row in enumerate(tag_rows):
-        rows_ref[28:29, i * LANES : (i + 1) * LANES] = row
-    rows_ref[29:32, :] = jnp.zeros((3, rows_ref.shape[1]), F32)
-    y_ref[...] = rows_ref[...].astype(BF16)
-    for copy in copies[4:]:
-        copy.wait()
     blank = jnp.zeros((1, LANES), F32)
     for f in range(fields):
         now = ua_ref[f]
@@ -209,16 +194,49 @@
         )
         straight_ref[f * depth : (f + 1) * depth, :] = tile.astype(BF16)
     far = [ca_ref[other, s].astype(F32) for s in range(4)]
-    extra = [jnp.where(lower, piece[0:1], piece[top:depth]) for piece in far] + tag_rows + [blank] * 4
+    extra = [jnp.where(lower, piece[0:1], piece[depth - 1 : depth]) for piece in far] + tag_rows + [blank] * 4
     straight_ref[fields * depth : fields * depth + 16, :] = jnp.concatenate(extra, axis=0).astype(BF16)
     plane = jnp.zeros((depth, LANES), F32)
     for s in range(4):
         moved = pltpu.roll(far[s], 32 * s, 1) if s else far[s]
         plane = jnp.where((lane >= 32 * s) & (lane < 32 * s + 32), moved, plane)
     diag_ref[0:depth, :] = plane.astype(BF16)
-    edges = [rows_ref[base : base + 4, 0:LANES] for base in (0, 8, 16, 24)]
-    extra = edges + tag_rows + [blank] * 8
+    rows = [edge_rows(ue_ref, pe_ref, 0, f, lower) for f in range(fields)]
+    extra = [row[kind] for kind in range(3) for row in rows]
+    extra += [edge_piece(ce_ref, s, lower) for s in range(4)] + tag_rows + [blank] * 8
     diag_ref[depth : depth + 32, :] = jnp.concatenate(extra, axis=0).astype(BF16)
+
+
+def pack_region_body(map_hbm, u_ref, p_ref, coef_ref, y_ref, rows_ref, ue_ref, pe_ref, ce_ref, map_ref, sems):
+    fields, depth, width = u_ref.shape[1:]
+    region = lax.axis_index("region")
+    lower = region == 0
+    other = 1 - region
+    half = depth // 2
+    slab = []
+    for s in range(4):
+        for h in range(2):
+            part = slice(h * half, (h + 1) * half)
+            slab.append(pltpu.make_async_copy(coef_ref.at[other, s, part], y_ref.at[s, part], sems.at[4 + 2 * s + h]))
+    copies = [pltpu.make_async_copy(map_hbm, map_ref, sems.at[3])]
+    copies += edge_copies(u_ref, p_ref, coef_ref, ue_ref, pe_ref, ce_ref, (slice(0, 2), slice(0, width)), region, sems)
+    for copy in copies + slab:
+        copy.start()
+    for copy in copies:
+        copy.wait()
+    for m in range(2):
+        for f in range(fields):
+            for kind, row in enumerate(edge_rows(ue_ref, pe_ref, m, f, lower)):
+                at = 8 * kind + m * fields + f
+                rows_ref[at : at + 1, :] = row
+    for s in range(4):
+        rows_ref[24 + s : 25 + s, :] = edge_piece(ce_ref, s, lower)
+    for i, row in enumerate(tag_values(map_ref, region)):
+        rows_ref[28:29, i * LANES : (i + 1) * LANES] = row
+    rows_ref[29:32, :] = jnp.zeros((3, width), F32)
+    y_ref[4] = rows_ref[...].astype(BF16)
+    for copy in slab:
+        copy.wait()
 
 
 def nine_sum(tiles, lane, first=0):
@@ -279,7 +297,7 @@
         self.lower = self.region == 0
         self.coef = coef_ref
         self.depth = coef_ref.shape[2]
-        self.extra = y_ref[...].astype(F32)
+        self.extra = y_ref[4].astype(F32)
         self.tags = [self.extra[28:29, i * LANES : (i + 1) * LANES] for i in range(8)]
         self.field_id = lax.broadcasted_iota(jnp.int32, (4, LANES), 0).astype(F32)
 
@@ -308,27 +326,48 @@
         return jnp.where(self.lower, 0.0, row), jnp.where(self.lower, row, 0.0)
 
 
-def last_edges_body(
-    u_ref, coef_ref, y_ref, straight_ref, diag_ref, box0_ref, rim_ref, box_in, box_ref, lap_ref, side_ref, sums_ref, tail_ref
-):
+def border_body(u_ref, straight_ref, diag_ref, box_in, box_ref, side_lap_ref, side_coef_ref, rim_ref):
     fields, depth, width = u_ref.shape[1:]
-    main = width // LANES
     lane = lane_ids()
     row_id = lax.broadcasted_iota(jnp.int32, (depth, 1), 0)
-    column = ColumnEdge(coef_ref, y_ref)
+    lower = lax.axis_index("region") == 0
     before = slice(width - LANES, width)
     facing = lane >= 96
-    extra_s = straight_ref[fields * depth : fields * depth + 16, :].astype(F32)
-    extra_d = diag_ref[depth : depth + 32, :].astype(F32)
-    tags_s = [extra_s[4 + i : 5 + i] for i in range(8)]
-    tags_d = [extra_d[16 + i : 17 + i] for i in range(8)]
-
+    tags = [straight_ref[fields * depth : fields * depth + 16, :].astype(F32)[4 + i : 5 + i] for i in range(8)]
     planes = []
     for s in range(4):
         planes.append(pltpu.roll(straight_ref[s * depth : (s + 1) * depth, :].astype(F32), 32, 1))
     diag_tile = diag_ref[0:depth, :].astype(F32)
     for s in range(4):
         planes.append(pltpu.roll(diag_tile, LANES - 32 * s, 1) if s else diag_tile)
+    for f in range(fields):
+        inner = u_ref[1, f, :, before]
+        remote = straight_ref[f * depth : (f + 1) * depth, :].astype(F32)
+        inner_sum, remote_sum = nine_sum([inner, remote], lane)
+        for i, tile in enumerate((inner_sum, remote_sum)):
+            rim_ref[i, f : f + 1, :] = jnp.where(lower, tile[depth - 1 : depth], tile[0:1])
+        halo_c = jnp.zeros((depth, LANES), F32)
+        for i in range(8):
+            halo_c = halo_c + jnp.where(tags[i] == F32(f), planes[i], 0.0)
+        side_coef_ref[f] = halo_c
+        side_lap_ref[f] = column_sum(remote_sum, row_id, 0.0, 0.0) - 27.0 * remote
+        whole = column_sum(inner_sum, row_id, 0.0, 0.0) - 27.0 * inner
+        box_ref[f, :, before] = jnp.where(facing, whole, box_in[f, :, before])
+    rim_ref[:, 4:8, :] = jnp.zeros((2, 4, LANES), F32)
+
+
+def last_edges(
+    coef_ref, y_ref, straight_ref, diag_ref, box0_ref, rim_ref, side_lap_ref, side_coef_ref, side_rim_ref, box_in,
+    box_ref, lap_ref, side_ref, sums_ref
+):
+    fields, depth, width = box_in.shape
+    main = width // LANES
+    lane = lane_ids()
+    column = ColumnEdge(coef_ref, y_ref)
+    before = slice(width - LANES, width)
+    extra_s = straight_ref[fields * depth : fields * depth + 16, :].astype(F32)
+    extra_d = diag_ref[depth : depth + 32, :].astype(F32)
+    tags_d = [extra_d[16 + i : 17 + i] for i in range(8)]
 
     def edge_tiles(of, base):
         return [of(0, before)] + [of(1, tile_at(t)) for t in range(main)] + [extra_d[base : base + 4]]
@@ -343,37 +382,25 @@
     edge_c = [column.coefs(0, before)] + [column.coefs(1, tile_at(t)) for t in range(main)] + [corner]
     near_sum = nine_sum(near, lane)
     beyond_sum = nine_sum(beyond, lane)
-
-    own, outer = [], []
+    top = slice(0, 1)
+    bottom = slice(depth - 1, depth)
     for f in range(fields):
-        inner = u_ref[1, f, :, tile_at(main - 1)]
-        remote = straight_ref[f * depth : (f + 1) * depth, :].astype(F32)
-        inner_sum, remote_sum = nine_sum([inner, remote], lane)
-        own.append(column.own(inner_sum))
-        outer.append(column.own(remote_sum))
-        halo_c = jnp.zeros((depth, LANES), F32)
-        for i in range(8):
-            halo_c = halo_c + jnp.where(tags_s[i] == F32(f), planes[i], 0.0)
-        low_row, high_row = column.rows(near_sum[main + 1][f : f + 1])
-        lap = column_sum(remote_sum, row_id, low_row, high_row) - 27.0 * remote
-        side_ref[f] = pltpu.roll(remote, 64, 1) + halo_c * lap
         for t in range(main):
             low_row, high_row = column.rows(near_sum[t + 1][f : f + 1])
             lanes = tile_at(t)
-            if t == main - 1:
-                box = box_in[f, :, lanes]
-                box = box + jnp.where(row_id == 0, low_row, 0.0) + jnp.where(row_id == depth - 1, high_row, 0.0)
-                whole = column_sum(inner_sum, row_id, low_row, high_row) - 27.0 * inner
-                box_ref[f, :, lanes] = jnp.where(facing, whole, box)
-            else:
-                box_ref[f, 0:1, lanes] = box_in[f, 0:1, lanes] + low_row
-                box_ref[f, depth - 1 : depth, lanes] = box_in[f, depth - 1 : depth, lanes] + high_row
+            box_ref[f, top, lanes] = box_in[f, top, lanes] + low_row
+            box_ref[f, bottom, lanes] = box_in[f, bottom, lanes] + high_row
+        remote = straight_ref[f * depth : (f + 1) * depth, :].astype(F32)
+        side_ref[f] = pltpu.roll(remote, 64, 1) + side_coef_ref[f] * side_lap_ref[f]
+        low_row, high_row = column.rows(near_sum[main + 1][f : f + 1])
+        side_ref[f, top] += side_coef_ref[f, top] * low_row
+        side_ref[f, bottom] += side_coef_ref[f, bottom] * high_row
         low_row, high_row = column.rows(near_sum[0][f : f + 1])
-        lap = box0_ref[f, :, before]
-        lap_ref[f] = lap + jnp.where(row_id == 0, low_row, 0.0) + jnp.where(row_id == depth - 1, high_row, 0.0)
-    rims = [rim_ref[0, 0:4, before]] + [rim_ref[1, 0:4, tile_at(t)] for t in range(main)]
-    rims.append(jnp.concatenate(outer, axis=0))
-    rims[main] = jnp.where(facing, jnp.concatenate(own, axis=0), rims[main])
+        lap_ref[f] = box0_ref[f, :, before]
+        lap_ref[f, top] += low_row
+        lap_ref[f, bottom] += high_row
+    rims = [rim_ref[0, 0:4, before]] + [rim_ref[1, 0:4, tile_at(t)] for t in range(main)] + [side_rim_ref[1, 0:4, :]]
+    rims[main] = jnp.where(lane >= 96, side_rim_ref[0, 0:4, :], rims[main])
     stepped = []
     for t in range(main + 2):
         box = near_sum[t] + beyond_sum[t] + rims[t]
@@ -382,8 +409,7 @@
     for t in range(main):
         sums_ref[0:4, tile_at(t)] = stepped_sum[t + 1]
     sums_ref[4:8, :] = jnp.zeros((4, width), F32)
-    tail_ref[0:4, :] = stepped[main]
-    tail_ref[4:8, :] = jnp.zeros((4, LANES), F32)
+    return stepped[main]
 
 
 def first_edges_body(
@@ -470,19 +496,33 @@
     return jnp.exp2(power) * (1.0 / CODES)
 
 
-def last_row_body(
-    first, map_ref, u_ref, coef_ref, slab_ref, box_ref, drift_ref, lap_ref, side_ref, sums_ref, *rest
+def last_row_a_body(
+    map_ref, owner_ref, u_ref, coef_ref, y_ref, straight_ref, diag_ref, box0_ref, rim_ref, side_lap_ref, side_coef_ref,
+    side_rim_ref, drift_ref, box_in, box_ref, lap_ref, side_ref, sums_ref, row_ref, code_ref, power_ref, extra_ref
 ):
-    if first == 0:
-        owner_ref, y_ref, tail_ref, row_ref, code_ref, power_ref, extra_ref = rest
-    else:
-        row_ref, code_ref, power_ref = rest
+    tail = last_edges(
+        coef_ref, y_ref, straight_ref, diag_ref, box0_ref, rim_ref, side_lap_ref, side_coef_ref, side_rim_ref, box_in,
+        box_ref, lap_ref, side_ref, sums_ref
+    )
+    more = (owner_ref, tail, extra_ref)
+    refs = (map_ref, u_ref, coef_ref, y_ref, box_ref, drift_ref, lap_ref, side_ref, sums_ref, row_ref, code_ref, power_ref)
+    last_row(0, *refs, more=more)
+
+
+def last_row_b_body(first, *refs):
+    last_row(first, *refs)
+
+
+def last_row(
+    first, map_ref, u_ref, coef_ref, y_ref, box_ref, drift_ref, lap_ref, side_ref, sums_ref, row_ref, code_ref, power_ref,
+    more=None
+):
     count, depth, width = row_ref.shape
     fields = u_ref.shape[1]
     main = width // LANES
     lane = lane_ids()
     row_id = lax.broadcasted_iota(jnp.int32, (depth, 1), 0)
-    pieces = Pieces(map_ref, coef_ref, slab_ref)
+    pieces = Pieces(map_ref, coef_ref, y_ref)
     lower = pieces.region == 0
     before = slice(width - LANES, width)
     base = count * depth
@@ -505,8 +545,9 @@
         last_tiles.append(middle[main - 1])
     power_ref[count:8, :] = jnp.zeros((8 - count, width), F32)
     code_ref[base : base + 8, :] = narrow(power_ref[...])
-    if first == 0:
-        near = y_ref[0:16, before].astype(F32)
+    if more is not None:
+        owner_ref, tail, extra_ref = more
+        near = y_ref[4, 0:16, before].astype(F32)
         extra_ref[2:3, :] = jnp.zeros((1, width), F32) + jnp.where(owner_ref[1] != lax.axis_index("blk"), 1.0, 0.0)
         extra_ref[3:8, :] = jnp.zeros((5, width), F32)
         for f in range(fields):
@@ -515,7 +556,7 @@
             else:
                 stepped = drift_ref[1, f, :, before] + pieces.piece(fields + f)(before) * box_ref[f, :, before]
             both = jnp.where(lane >= 96, u_ref[1, f, :, before], pltpu.roll(stepped, 96, 1))
-            rows = [near[4 + f : 5 + f], near[12 + f : 13 + f], tail_ref[f : f + 1, :]]
+            rows = [near[4 + f : 5 + f], near[12 + f : 13 + f], tail[f : f + 1]]
             size = jnp.max(jnp.abs(both), axis=0, keepdims=True)
             for row in rows:
                 size = jnp.maximum(size, jnp.abs(row))
@@ -531,12 +572,12 @@
         code_ref[base + 8 + depth // 2 : base + 16 + depth // 2, :] = narrow(extra_ref[...])
 
 
-def first_row_body(map_ref, u_ref, coef_ref, slab_ref, box_ref, box1_ref, drift_ref, sums_ref, row_ref):
+def first_row_body(map_ref, u_ref, coef_ref, y_ref, box_ref, box1_ref, drift_ref, sums_ref, row_ref):
     fields, depth, width = u_ref.shape[1:]
     main = width // LANES
     lane = lane_ids()
     row_id = lax.broadcasted_iota(jnp.int32, (depth, 1), 0)
-    pieces = Pieces(map_ref, coef_ref, slab_ref)
+    pieces = Pieces(map_ref, coef_ref, y_ref)
     lower = pieces.region == 0
     after = slice(0, LANES)
     for f in range(fields):
@@ -553,73 +594,105 @@
 
 def arrival(code_ref):
     rows = code_ref.shape[0]
-    return jnp.max(wide(code_ref[rows - 8 : rows, :])[2:3]) > 0.5
-
-
-def place_codes(code_ref, first, count, depth, row_ref, out_ref, sems, base):
-    scale = scale_of(wide(code_ref[count * depth : count * depth + 8, :]))
+    return jnp.max(wide(code_ref[rows - 8 : rows, 0:LANES])[2:3]) > 0.5
+
+
+def code_copies(first, count, depth, row_ref, out_ref, sems, base):
     part = depth // 2
     copies = []
     for f in range(count):
         for h in range(2):
             rows = slice(h * part, (h + 1) * part)
-            start = f * depth + h * part
-            row_ref[f, rows] = wide(code_ref[start : start + part, :]) * scale[f : f + 1]
             sem = sems.at[base + 2 * f + h]
             copies.append(pltpu.make_async_copy(row_ref.at[f, rows], out_ref.at[0, first + f, rows], sem))
-            copies[-1].start()
     return copies
 
 
+def place_codes(code_ref, first, count, depth, row_ref, out_ref, sems, base):
+    scale = scale_of(wide(code_ref[count * depth : count * depth + 8, :]))
+    part = depth // 2
+    for i, copy in enumerate(code_copies(first, count, depth, row_ref, out_ref, sems, base)):
+        f, h = divmod(i, 2)
+        row_ref[f, h * part : (h + 1) * part] = wide(code_ref[i * part : (i + 1) * part, :]) * scale[f : f + 1]
+        copy.start()
+
+
+def first_copies(row_ref, out_ref, at, sems, base):
+    fields, _, width = row_ref.shape
+    rest = slice(LANES, width)
+    return [
+        pltpu.make_async_copy(row_ref.at[f, :, rest], out_ref.at[at, f, :, rest], sems.at[base + f])
+        for f in range(fields)
+    ]
+
+
+def last_copies(last_a_ref, last_b_ref, out_ref, at, sems, base):
+    half = last_a_ref.shape[0]
+    sources = [last_a_ref.at[f] for f in range(half)] + [last_b_ref.at[f] for f in range(half)]
+    return [pltpu.make_async_copy(source, out_ref.at[at, f], sems.at[base + f]) for f, source in enumerate(sources)]
+
+
+def rows_body(owner_ref, row_ref, last_a_ref, last_b_ref, out_ref, zero_ref, sems):
+    fields = row_ref.shape[0]
+    keeps = owner_ref[1] == lax.axis_index("blk")
+    zero_ref[...] = jnp.zeros(zero_ref.shape, F32)
+
+    def zeros(at, base):
+        return [pltpu.make_async_copy(zero_ref, out_ref.at[at, f], sems.at[base + f]) for f in range(fields)]
+
+    always = first_copies(row_ref, out_ref, 0, sems, 0) + zeros(2, fields)
+    kept = last_copies(last_a_ref, last_b_ref, out_ref, 1, sems, 2 * fields)
+    gone = zeros(1, 2 * fields)
+
+    def all_of(act):
+        for copy in always:
+            act(copy)
+
+        @pl.when(keeps)
+        def _():
+            for copy in kept:
+                act(copy)
+
+        @pl.when(jnp.logical_not(keeps))
+        def _():
+            for copy in gone:
+                act(copy)
+
+    all_of(lambda copy: copy.start())
+    all_of(lambda copy: copy.wait())
+
+
 def finish_body(
-    owner_ref, map_ref, u_ref, coef_ref, slab_ref, y_ref, box_ref, drift_ref, tail_ref, code_ref, row_ref,
-    last_a_ref, last_b_ref, out_ref, tile_ref, zero_ref, arrived_ref, sems
+    owner_ref, map_ref, u_ref, coef_ref, y_ref, box_ref, drift_ref, tail_ref, code_ref, row_ref,
+    last_a_ref, last_b_ref, partial_ref, out_ref, tile_ref, arrived_ref, sems
 ):
     fields, depth, width = u_ref.shape[1:]
-    half = last_a_ref.shape[0]
+    half = arrived_ref.shape[0]
     base = half * depth
     lane = lane_ids()
     row_id = lax.broadcasted_iota(jnp.int32, (depth, 1), 0)
     arrives = arrival(code_ref)
     slot = jnp.where(arrives, 1, 0)
-    keeps = owner_ref[1] == lax.axis_index("blk")
-
-    def row_copies(at, sources, base):
-        return [
-            pltpu.make_async_copy(source, out_ref.at[at, f], sems.at[base + f]) for f, source in enumerate(sources)
-        ]
-
-    mine = [last_a_ref.at[f] for f in range(half)] + [last_b_ref.at[f] for f in range(fields - half)]
-    kept = row_copies(slot + 1, mine, 0)
-    blank = row_copies(slot + 1, [zero_ref] * fields, 0)
-    third = row_copies(2, [zero_ref] * fields, fields)
-    rest = slice(LANES, width)
-    firsts = [
-        pltpu.make_async_copy(row_ref.at[f, :, rest], out_ref.at[slot, f, :, rest], sems.at[2 * fields + f])
-        for f in range(fields)
-    ]
-    for copy in firsts:
-        copy.start()
-
-    @pl.when(keeps)
+    moves_on = jnp.logical_and(arrives, owner_ref[1] == lax.axis_index("blk"))
+    firsts = first_copies(row_ref, out_ref, 1, sems, 1 + 2 * half)
+    lasts = last_copies(last_a_ref, last_b_ref, out_ref, 2, sems, 1 + 2 * half + fields)
+
+    @pl.when(arrives)
     def _():
-        for copy in kept:
+        for copy in firsts:
             copy.start()
 
-    zero_ref[...] = jnp.zeros(zero_ref.shape, F32)
-
-    @pl.when(jnp.logical_not(keeps))
+    @pl.when(moves_on)
     def _():
-        for copy in blank:
+        for copy in lasts:
             copy.start()
 
-    @pl.when(jnp.logical_not(arrives))
+    @pl.when(arrives)
     def _():
-        for copy in third:
-            copy.start()
+        place_codes(code_ref, 0, half, depth, arrived_ref, out_ref, sems, 1)
 
     column = ColumnEdge(coef_ref, y_ref)
-    pieces = Pieces(map_ref, coef_ref, slab_ref)
+    pieces = Pieces(map_ref, coef_ref, y_ref)
     extra = wide(code_ref[base + 8 + depth // 2 : base + 16 + depth // 2, :])
     tile0, tile1 = tile_at(0), tile_at(1)
     near = column.near(0, tile0)
@@ -654,31 +727,21 @@
         total = nine_sum([pltpu.roll(before[f], 32, 1), stepped[f], nexts[f]], lane)[1]
         row = edge_sum[f : f + 1]
         tile_ref[f] = second_step(stepped[f], u_ref[0, f, :, tile0], total, coefs[f], row_id, row, column.lower)
-    last = pltpu.make_async_copy(tile_ref, out_ref.at[slot, :, :, tile0], sems.at[3 * fields])
+    last = pltpu.make_async_copy(tile_ref, out_ref.at[slot, :, :, tile0], sems.at[0])
     last.start()
 
     @pl.when(arrives)
     def _():
-        for copy in place_codes(code_ref, 0, half, depth, arrived_ref, out_ref, sems, 3 * fields + 1):
+        for copy in code_copies(0, half, depth, arrived_ref, out_ref, sems, 1):
             copy.wait()
-
-    @pl.when(keeps)
+        for copy in firsts:
+            copy.wait()
+
+    @pl.when(moves_on)
     def _():
-        for copy in kept:
+        for copy in lasts:
             copy.wait()
 
-    @pl.when(jnp.logical_not(keeps))
-    def _():
-        for copy in blank:
-            copy.wait()
-
-    @pl.when(jnp.logical_not(arrives))
-    def _():
-        for copy in third:
-            copy.wait()
-
-    for copy in firsts:
-        copy.wait()
     last.wait()
 
 
@@ -687,7 +750,8 @@
 
     @pl.when(arrival(code_a_ref))
     def _():
-        for copy in place_codes(code_ref, first, count, depth, row_ref, out_ref, sems, 0):
+        place_codes(code_ref, first, count, depth, row_ref, out_ref, sems, 0)
+        for copy in code_copies(first, count, depth, row_ref, out_ref, sems, 0):
             copy.wait()
 
 
@@ -698,8 +762,8 @@
     coef = coef_store[0, 0]
     count = lax.axis_size("blk")
     order = store_map.reshape(-1)
-    owner_hbm, order_hbm, now_hbm, prev_hbm, coef_hbm = (
-        pltpu.with_memory_space_constraint(array, pltpu.HBM) for array in (new_owner, order, now, prev, coef)
+    order_hbm, now_hbm, prev_hbm, coef_hbm = (
+        pltpu.with_memory_space_constraint(array, pltpu.HBM) for array in (order, now, prev, coef)
     )
     params = pltpu.CompilerParams(vmem_limit_bytes=48 * 1024 * 1024)
 
@@ -715,35 +779,47 @@
             **options,
         )(*args)
 
-    slab_shape = jax.ShapeDtypeStruct(coef.shape[1:], BF16)
-    slab_out = call(pack_slab_body, "pack_slab", slab_shape, [HBM], VMEM, [pltpu.SemaphoreType.DMA((8,))], (coef_hbm,))
     straight = jax.ShapeDtypeStruct((fields * depth + 16, LANES), BF16)
     diag = jax.ShapeDtypeStruct((depth + 32, LANES), BF16)
-    y_out, left, dleft = call(
-        pack_edges_body,
-        "pack_edges",
-        (jax.ShapeDtypeStruct((depth, width), BF16), straight, diag),
+    sources = (order_hbm, now_hbm, prev_hbm, coef_hbm)
+    y_out = call(
+        pack_region_body,
+        "pack_region",
+        jax.ShapeDtypeStruct((5, depth, width), BF16),
         [HBM] * 4,
-        (VMEM,) * 3,
+        VMEM,
         [
             pltpu.VMEM((depth, width), F32),
             pltpu.VMEM((blocks, fields, 8, width), F32),
             pltpu.VMEM((blocks, fields, 8, width), F32),
             pltpu.VMEM((4, 16, width), BF16),
+            pltpu.SMEM(order.shape, jnp.int32),
+            pltpu.SemaphoreType.DMA((12,)),
+        ],
+        sources,
+    )
+    left, dleft = call(
+        pack_back_body,
+        "pack_back",
+        (straight, diag),
+        [HBM] * 4,
+        (VMEM,) * 2,
+        [
+            pltpu.VMEM((1, fields, 8, LANES), F32),
+            pltpu.VMEM((1, fields, 8, LANES), F32),
+            pltpu.VMEM((4, 16, LANES), BF16),
             pltpu.VMEM((fields, depth, LANES), F32),
             pltpu.VMEM((fields, depth, LANES), F32),
             pltpu.VMEM((2, 4, depth, LANES), BF16),
             pltpu.SMEM(order.shape, jnp.int32),
             pltpu.SemaphoreType.DMA((7,)),
         ],
-        (order_hbm, now_hbm, prev_hbm, coef_hbm),
-    )
-
+        sources,
+    )
     swap = [(0, 1), (1, 0)]
     forward = [(i, (i + 1) % count) for i in range(count)]
     backward = [(i, (i - 1) % count) for i in range(count)]
     crossed = [(r * count + i, (1 - r) * count + (i - 1) % count) for r in range(2) for i in range(count)]
-    slab = lax.ppermute(slab_out, "region", swap)
     y_in = lax.ppermute(y_out, "region", swap)
     from_right = lax.ppermute(left, "blk", backward)
     from_dright = lax.ppermute(dleft, ("region", "blk"), crossed)
@@ -761,34 +837,41 @@
     tiles = jax.ShapeDtypeStruct((fields, depth, LANES), F32)
     sums = jax.ShapeDtypeStruct((8, width), F32)
     tail = jax.ShapeDtypeStruct((8, LANES), F32)
-    box1, lap1, side1, sums1, tail1 = call(
-        last_edges_body,
-        "last_edges",
-        (row, tiles, tiles, sums, tail),
-        [VMEM] * 8,
-        (VMEM,) * 5,
+    box1, side_lap, side_coef, side_rim = call(
+        border_body,
+        "border",
+        (row, tiles, tiles, jax.ShapeDtypeStruct((2, 8, LANES), F32)),
+        [VMEM] * 4,
+        (VMEM,) * 4,
         [],
-        (now, coef, y_in, from_right, from_dright, box0, rim, box1),
-        input_output_aliases={7: 0},
+        (now, from_right, from_dright, box1),
+        input_output_aliases={3: 0},
+        cost_estimate=pl.CostEstimate(flops=0, transcendentals=0, bytes_accessed=40_000_000),
     )
     half = fields // 2
     part = jax.ShapeDtypeStruct((half, depth, width), F32)
     codes = jax.ShapeDtypeStruct((half * depth + 8, width), jnp.int16)
     more_codes = jax.ShapeDtypeStruct((half * depth + depth // 2 + 16, width), jnp.int16)
-    stepping = (order, now, coef, slab, box1, drift, lap1, side1, sums1)
     powers = pltpu.VMEM((8, width), F32)
-    last_a, code_a = call(
-        functools.partial(last_row_body, 0),
+    box1, lap1, side1, sums1, last_a, code_a = call(
+        last_row_a_body,
         "last_row",
-        (part, more_codes),
-        [SMEM] + [VMEM] * 8 + [SMEM] + [VMEM] * 2,
-        (VMEM,) * 2,
+        (row, tiles, tiles, sums, part, more_codes),
+        [SMEM] * 2 + [VMEM] * 12,
+        (VMEM,) * 6,
         [powers, powers],
-        stepping + (new_owner, y_in, tail1),
+        (order, new_owner, now, coef, y_in, from_right, from_dright, box0, rim, side_lap, side_coef, side_rim, drift, box1),
+        input_output_aliases={13: 0},
     )
     arrived_a = lax.ppermute(code_a, "blk", forward)
     last_b, code_b = call(
-        functools.partial(last_row_body, half), "last_row", (part, codes), [SMEM] + [VMEM] * 8, (VMEM,) * 2, [powers], stepping
+        functools.partial(last_row_b_body, half),
+        "last_row",
+        (part, codes),
+        [SMEM] + [VMEM] * 8,
+        (VMEM,) * 2,
+        [powers],
+        (order, now, coef, y_in, box1, drift, lap1, side1, sums1),
     )
     arrived_b = lax.ppermute(code_b, "blk", forward)
     box0, sums0, tail0 = call(
@@ -808,34 +891,44 @@
         [SMEM] + [VMEM] * 7,
         VMEM,
         [],
-        (order, now, coef, slab, box0, box1, drift, sums0),
+        (order, now, coef, y_in, box0, box1, drift, sums0),
     )
     whole = jax.ShapeDtypeStruct((blocks + 1, fields, depth, width), F32)
-    result = call(
+    placed = call(
+        rows_body,
+        "rows",
+        whole,
+        [SMEM] + [VMEM] * 3,
+        ANY,
+        [pltpu.VMEM((depth, width), F32), pltpu.SemaphoreType.DMA((3 * fields,))],
+        (new_owner, first, last_a, last_b),
+    )
+    arrived_half = pltpu.VMEM((half, depth, width), F32)
+    placed = call(
         finish_body,
         "finish",
         whole,
-        [SMEM] * 2 + [VMEM] * 11,
+        [SMEM] * 2 + [VMEM] * 10 + [ANY],
         ANY,
         [
             pltpu.VMEM((fields, depth, LANES), F32),
-            pltpu.VMEM((depth, width), F32),
-            pltpu.VMEM((half, depth, width), F32),
-            pltpu.SemaphoreType.DMA((3 * fields + 1 + 2 * half,)),
+            arrived_half,
+            pltpu.SemaphoreType.DMA((1 + 2 * half + 2 * fields,)),
         ],
-        (new_owner, order, now, coef, slab, y_in, box0, drift, tail0, arrived_a, first, last_a, last_b),
-    )
-    result = call(
+        (new_owner, order, now, coef, y_in, box0, drift, tail0, arrived_a, first, last_a, last_b, placed),
+        input_output_aliases={12: 0},
+    )
+    placed = call(
         functools.partial(place_body, half),
         "place",
         whole,
         [VMEM, VMEM, ANY],
         ANY,
-        [pltpu.VMEM((half, depth, width), F32), pltpu.SemaphoreType.DMA((2 * half,))],
-        (arrived_a, arrived_b, result),
+        [arrived_half, pltpu.SemaphoreType.DMA((2 * half,))],
+        (arrived_a, arrived_b, placed),
         input_output_aliases={2: 0},
     )
-    return result[:, None]
+    return placed[:, None]
 
 
 def solution(mesh):

time: 26.3 us -> 25.7 us (0.977)
  Pallas kernels: 11.8 us -> 13.4 us
  waiting for transfers between devices: 3.99 us -> 2.66 us
  starting transfers between devices: 10.2 us -> 9.24 us
    ppermute x1 -> x0, starting transfers between devices: 3.03 us -> none  [fast_on_device(): slab = lax.ppermute(slab_out, 'region', swap)]
    ppermute x1, starting transfers between devices: 0.1 us -> 3.03 us  [fast_on_device(): y_in = lax.ppermute(y_out, 'region', swap)]
    ppermute x1, waiting for transfers between devices: 3.83 us -> 1.62 us  [fast_on_device(): arrived_a = lax.ppermute(code_a, 'blk', forward)]
    pallas_call x10 -> x11, Pallas kernels: 11.8 us -> 13.4 us  [call(): pl.pallas_call(body, out_shape=out_shape, in_specs=in_specs, out_specs=ou...]
    ppermute x1, starting transfers between devices: 2.19 us -> 0.94 us  [fast_on_device(): from_dright = lax.ppermute(dleft, ('region', 'blk'), crossed)]
    ppermute x1, waiting for transfers between devices: 0.15 us -> 1.04 us  [fast_on_device(): from_dright = lax.ppermute(dleft, ('region', 'blk'), crossed)]
    ppermute x1, starting transfers between devices: 0.99 us -> 1.47 us  [fast_on_device(): arrived_b = lax.ppermute(code_b, 'blk', forward)]
  transfers between devices with their start and end apart: 6 -> 5, of which waited for: 2 -> 2; matrix products, arithmetic and copies ran while one was open for 0% -> 0% of each run, Pallas kernels for 33% -> 39%
where the time goes in v6:
time: 25.7 us; the launch traced here: 25.5 us
  Pallas kernels  13.4 us (52%)
  starting transfers between devices  9.24 us (36%)
  waiting for transfers between devices  2.66 us (10%)
    pallas_call x11, Pallas kernels, call(): pl.pallas_call(body, out_shape=out_shape, in_specs=in_specs, out_specs=ou...  13.4 us
    ppermute x1, starting transfers between devices, fast_on_device(): from_right = lax.ppermute(left, 'blk', backward)  3.74 us
    ppermute x1, starting transfers between devices, fast_on_device(): y_in = lax.ppermute(y_out, 'region', swap)  3.03 us
    ppermute x1, waiting for transfers between devices, fast_on_device(): arrived_a = lax.ppermute(code_a, 'blk', forward)  1.62 us
    ppermute x1, starting transfers between devices, fast_on_device(): arrived_b = lax.ppermute(code_b, 'blk', forward)  1.47 us
    ppermute x1, waiting for transfers between devices, fast_on_device(): from_dright = lax.ppermute(dleft, ('region', 'blk'), crossed)  1.04 us
    ppermute x1, starting transfers between devices, fast_on_device(): from_dright = lax.ppermute(dleft, ('region', 'blk'), crossed)  0.94 us
  transfers between devices with their start and end apart: 5, of which 2 were waited for; matrix products, arithmetic and copies ran while one was open for 0% of the time, Pallas kernels for 39%

profile of v6, /device:TPU:0, one launch (start us, length us, event | category | flops | bytes accessed | tf_op | source)
XLA Modules:
  0.0 25.5 jit_solution(7718709160630991866)
XLA Ops:
  0.0 1.2 %pack_region.1 = bf16[5,32,1024]{2,1,0:T(8,128)(2,1)S(1)} custom-call(s32[8]{0:T(128)} %bitcast.26, f32[2,4,32,1024]{3,2,1,0:T(8,128)} %bitcast.7, f32[2,4,32,1024]{3,2,1,0:T(8,128)} %bitcast.23, bf16[2,4,32,1024]{3,2,1,0:T(8,128)(2,1)} %bitcast.16), custom_call_target="tpu_custom_call" | custom-call | tf_op jit(solution)/shard_map/pack_region/pallas_call | solution.py:771
  1.3 0.0 copy-start
  1.3 0.0 copy-start.2
  1.3 3.0 %collective-permute-start = (bf16[5,32,1024]{2,1,0:T(8,128)(2,1)S(1)}, bf16[5,32,1024]{2,1,0:T(8,128)(2,1)S(1)}, u32[]{:S(2)}, u32[]{:S(2)}) collective-permute-start(bf16[5,32,1024]{2,1,0:T(8,128)(2,1)S(1)} %pack_region.1), channel_id=1, source_target_pairs={{0,16},{16,0},{1,17},{17,1},{2,18},{18,2},{3,19},{19,3},{4,20},{20... | collective-permute-start | bytes 983048 | tf_op jit(solution)/shard_map/ppermute | solution.py:823
  4.3 1.1 %pack_back.1 = (bf16[144,128]{1,0:T(8,128)(2,1)S(1)}, bf16[64,128]{1,0:T(8,128)(2,1)S(1)}) custom-call(s32[8]{0:T(128)} %bitcast.27, f32[2,4,32,1024]{3,2,1,0:T(8,128)} %bitcast.8, f32[2,4,32,1024]{3,2,1,0:T(8,128)} %bitcast.24, bf16[2,4,32,1024]{3,2,1,0:T(8,128)(2,1)} %bitcast.17), custom_call_target="tpu_custom_call" | custom-call | tf_op jit(solution)/shard_map/pack_back/pallas_call | solution.py:771
  5.4 3.7 %collective-permute-start.1 = (bf16[144,128]{1,0:T(8,128)(2,1)S(1)}, bf16[144,128]{1,0:T(8,128)(2,1)S(1)}, u32[]{:S(2)}, u32[]{:S(2)}) collective-permute-start(bf16[144,128]{1,0:T(8,128)(2,1)S(1)} %get-tuple-element.26), channel_id=1, source_target_pairs={{0,15},{1,0},{2,1},{3,2},{4,3},{5,4},{6,5},{7,6},{8,7},{9,8},{10,9... | collective-permute-start | bytes 110600 | tf_op jit(solution)/shard_map/ppermute | solution.py:824
  9.1 0.0 copy-start.1
  9.1 0.0 copy-start.3
  9.1 0.0 copy-start.4
  9.1 0.9 %collective-permute-start.2 = (bf16[64,128]{1,0:T(8,128)(2,1)S(1)}, bf16[64,128]{1,0:T(8,128)(2,1)S(1)}, u32[]{:S(2)}, u32[]{:S(2)}) collective-permute-start(bf16[64,128]{1,0:T(8,128)(2,1)S(1)} %get-tuple-element.27), channel_id=1, source_target_pairs={{0,31},{1,16},{2,17},{3,18},{4,19},{5,20},{6,21},{7,22},{8,23},{9,... | collective-permute-start | bytes 49160 | tf_op jit(solution)/shard_map/ppermute | solution.py:825
  10.1 0.0 copy-done
  10.1 0.0 copy-done.2
  10.1 1.3 %local.1 = (f32[4,32,1024]{2,1,0:T(8,128)S(1)}, f32[4,32,1024]{2,1,0:T(8,128)S(1)}, f32[2,4,32,1024]{3,2,1,0:T(8,128)S(1)}, f32[2,8,1024]{2,1,0:T(8,128)S(1)}) custom-call(f32[2,4,32,1024]{3,2,1,0:T(8,128)S(1)} %bitcast.9, f32[2,4,32,1024]{3,2,1,0:T(8,128)S(1)} %bitcast.25), custom_call_target="tpu_custom_call" | custom-call | tf_op jit(solution)/shard_map/local/pallas_call | solution.py:771
  11.3 1.0 %collective-permute-done.2.diag_ref = bf16[64,128]{1,0:T(8,128)(2,1)S(1)} collective-permute-done((bf16[64,128]{1,0:T(8,128)(2,1)S(1)}, bf16[64,128]{1,0:T(8,128)(2,1)S(1)}, u32[]{:S(2)}, u32[]{:S(2)}) %collective-permute-start.2) | collective-permute-done | bytes 16416 | tf_op jit(solution)/shard_map/ppermute | solution.py:825
  12.4 0.0 collective-permute-done.1.straight_ref
  12.4 0.3 %border.1 = (f32[4,32,1024]{2,1,0:T(8,128)S(1)}, f32[4,32,128]{2,1,0:T(8,128)S(1)}, f32[4,32,128]{2,1,0:T(8,128)S(1)}, f32[2,8,128]{2,1,0:T(8,128)S(1)}) custom-call(f32[2,4,32,1024]{3,2,1,0:T(8,128)S(1)} %bitcast.10, bf16[144,128]{1,0:T(8,128)(2,1)S(1)} %collective-permute-done.1.straight_ref, ...), custom_call_target="tpu_custom_call", output_to_operand_aliasing={{0}: (3, {})} | custom-call | bytes 40000000 | tf_op jit(solution)/shard_map/border/pallas_call | solution.py:771
  12.7 0.0 collective-permute-done.y_ref.refs_3_
  12.7 0.0 copy-done.1
  12.8 0.0 copy-done.3
  12.8 0.0 copy-done.4
  12.8 1.4 %last_row.2 = (f32[4,32,1024]{2,1,0:T(8,128)S(1)}, f32[4,32,128]{2,1,0:T(8,128)S(1)}, f32[4,32,128]{2,1,0:T(8,128)S(1)}, f32[8,1024]{1,0:T(8,128)S(1)}, f32[2,32...) custom-call(s32[8]{0:T(128)S(1)} %bitcast.28, s32[2]{0:T(128)S(1)} %copy-done.4, ...), custom_call_target="tpu_custom_call", output_to_operand_aliasing={{0}: (13, {})} | custom-call | tf_op jit(solution)/shard_map/last_row/pallas_call | solution.py:771
  14.2 0.1 collective-permute-start.3
  14.3 1.1 %last_row.3 = (f32[2,32,1024]{2,1,0:T(8,128)S(1)}, s16[72,1024]{1,0:T(8,128)(2,1)S(1)}) custom-call(s32[8]{0:T(128)S(1)} %bitcast.29, f32[2,4,32,1024]{3,2,1,0:T(8,128)S(1)} %bitcast.12, bf16[2,4,32,1024]{3,2,1,0:T(8,128)(2,1)S(1)} %bitcast.19, bf16[5,32,1024]{2,1,0:T(8,128)(2,1)S(1)} %collective-permute-done.y_ref.refs_3_, ...), custom_call_target="tpu_custom_call" | custom-call | tf_op jit(solution)/shard_map/last_row/pallas_call | solution.py:771
  15.4 1.5 %collective-permute-start.4 = (s16[72,1024]{1,0:T(8,128)(2,1)S(1)}, s16[72,1024]{1,0:T(8,128)(2,1)S(1)}, u32[]{:S(2)}, u32[]{:S(2)}) collective-permute-start(s16[72,1024]{1,0:T(8,128)(2,1)S(1)} %get-tuple-element.41), channel_id=1, source_target_pairs={{0,1},{1,2},{2,3},{3,4},{4,5},{5,6},{6,7},{7,8},{8,9},{9,10},{10,1... | collective-permute-start | bytes 442376 | tf_op jit(solution)/shard_map/ppermute | solution.py:876
  16.9 0.4 %first_edges.1 = (f32[4,32,1024]{2,1,0:T(8,128)S(1)}, f32[8,1024]{1,0:T(8,128)S(1)}, f32[8,128]{1,0:T(8,128)S(1)}) custom-call(f32[2,4,32,1024]{3,2,1,0:T(8,128)S(1)} %bitcast.13, bf16[2,4,32,1024]{3,2,1,0:T(8,128)(2,1)S(1)} %bitcast.20, bf16[5,32,1024]{2,1,0:T(8,128)(2,1)S(1)} %collective-permute-done.y_ref.refs_3_, ...), custom_call_target="tpu_custom_call", output_to_operand_aliasing={{0}: (5, {})} | custom-call | tf_op jit(solution)/shard_map/first_edges/pallas_call | solution.py:771
  17.3 1.4 %first_row.1.row_ref = f32[4,32,1024]{2,1,0:T(8,128)S(1)} custom-call(s32[8]{0:T(128)S(1)} %bitcast.30, f32[2,4,32,1024]{3,2,1,0:T(8,128)S(1)} %bitcast.14, bf16[2,4,32,1024]{3,2,1,0:T(8,128)(2,1)S(1)} %bitcast.21, bf16[5,32,1024]{2,1,0:T(8,128)(2,1)S(1)} %collective-permute-done.y_ref.refs_3_, f32[4,32,1024]{2,1,0:T(8,128)S(1)} %get-tuple-element.42.box_ref, ...), custom_call_target="tpu_custom_call" | custom-call | tf_op jit(solution)/shard_map/first_row/pallas_call | solution.py:771
  18.7 1.8 %rows.1.partial_ref = f32[3,4,32,1024]{3,2,1,0:T(8,128)} custom-call(s32[2]{0:T(128)S(1)} %copy-done.4, f32[4,32,1024]{2,1,0:T(8,128)S(1)} %first_row.1.row_ref, f32[2,32,1024]{2,1,0:T(8,128)S(1)} %get-tuple-element.45.last_a_ref, f32[2,32,1024]{2,1,0:T(8,128)S(1)} %get-tuple-element.46.last_b_ref), custom_call_target="tpu_custom_call" | custom-call | tf_op jit(solution)/shard_map/rows/pallas_call | solution.py:771
  20.5 1.6 %collective-permute-done.3.code_ref.code_a_ref = s16[96,1024]{1,0:T(8,128)(2,1)S(1)} collective-permute-done((s16[96,1024]{1,0:T(8,128)(2,1)S(1)}, s16[96,1024]{1,0:T(8,128)(2,1)S(1)}, u32[]{:S(2)}, u32[]{:S(2)}) %collective-permute-start.3) | collective-permute-done | bytes 196640 | tf_op jit(solution)/shard_map/ppermute | solution.py:866
  22.1 2.5 %finish.1.partial_ref = f32[3,4,32,1024]{3,2,1,0:T(8,128)} custom-call(s32[2]{0:T(128)S(1)} %copy-done.4, s32[8]{0:T(128)S(1)} %bitcast.31, f32[2,4,32,1024]{3,2,1,0:T(8,128)S(1)} %bitcast.15, bf16[2,4,32,1024]{3,2,1,0:T(8,128)(2,1)S(1)} %bitcast.22, bf16[5,32,1024]{2,1,0:T(8,128)(2,1)S(1)} %collective-permute-done.y_ref.refs_3_, ...), custom_call_target="tpu_custom_call", output_to_operand_aliasing={{}: (12, {})} | custom-call | tf_op jit(solution)/shard_map/finish/pallas_call | solution.py:771
  24.6 0.0 collective-permute-done.4.code_ref
  24.6 0.9 %place.1 = f32[3,4,32,1024]{3,2,1,0:T(8,128)} custom-call(s16[96,1024]{1,0:T(8,128)(2,1)S(1)} %collective-permute-done.3.code_ref.code_a_ref, s16[72,1024]{1,0:T(8,128)(2,1)S(1)} %collective-permute-done.4.code_ref, f32[3,4,32,1024]{3,2,1,0:T(8,128)} %finish.1.partial_ref), custom_call_target="tpu_custom_call", output_to_operand_aliasing={{}: (2, {})} | custom-call | tf_op jit(solution)/shard_map/place/pallas_call | solution.py:771
Async XLA Ops:
  1.3 8.8 %copy-start = (f32[2,1,4,32,1024]{4,3,2,1,0:T(8,128)S(1)}, f32[2,1,4,32,1024]{4,3,2,1,0:T(8,128)}, u32[]{:S(2)}) copy-start(f32[2,1,4,32,1024]{4,3,2,1,0:T(8,128)} %param.5) | copy-start | bytes 3145732
  1.3 8.8 %copy-start.2 = (f32[2,1,4,32,1024]{4,3,2,1,0:T(8,128)S(1)}, f32[2,1,4,32,1024]{4,3,2,1,0:T(8,128)}, u32[]{:S(2)}) copy-start(f32[2,1,4,32,1024]{4,3,2,1,0:T(8,128)} %param.6) | copy-start | bytes 3145732
  1.3 11.5 %collective-permute-start = (bf16[5,32,1024]{2,1,0:T(8,128)(2,1)S(1)}, bf16[5,32,1024]{2,1,0:T(8,128)(2,1)S(1)}, u32[]{:S(2)}, u32[]{:S(2)}) collective-permute-start(bf16[5,32,1024]{2,1,0:T(8,128)(2,1)S(1)} %pack_region.1), channel_id=1, source_target_pairs={{0,16},{16,0},{1,17},{17,1},{2,18},{18,2},{3,19},{19,3},{4,20},{20... | collective-permute-start | bytes 983048 | tf_op jit(solution)/shard_map/ppermute | solution.py:823
  5.4 7.0 %collective-permute-start.1 = (bf16[144,128]{1,0:T(8,128)(2,1)S(1)}, bf16[144,128]{1,0:T(8,128)(2,1)S(1)}, u32[]{:S(2)}, u32[]{:S(2)}) collective-permute-start(bf16[144,128]{1,0:T(8,128)(2,1)S(1)} %get-tuple-element.26), channel_id=1, source_target_pairs={{0,15},{1,0},{2,1},{3,2},{4,3},{5,4},{6,5},{7,6},{8,7},{9,8},{10,9... | collective-permute-start | bytes 110600 | tf_op jit(solution)/shard_map/ppermute | solution.py:824
  9.1 3.6 %copy-start.1 = (bf16[1,1,2,4,32,1024]{5,4,3,2,1,0:T(8,128)(2,1)S(1)}, bf16[1,1,2,4,32,1024]{5,4,3,2,1,0:T(8,128)(2,1)}, u32[]{:S(2)}) copy-start(bf16[1,1,2,4,32,1024]{5,4,3,2,1,0:T(8,128)(2,1)} %param.7) | copy-start | bytes 1572868
  9.1 3.6 %copy-start.3 = (s32[1,1,8]{2,1,0:T(1,128)S(1)}, s32[1,1,8]{2,1,0:T(1,128)}, u32[]{:S(2)}) copy-start(s32[1,1,8]{2,1,0:T(1,128)} %param.8) | copy-start | bytes 100
  9.1 3.6 %copy-start.4 = (s32[2]{0:T(128)S(1)}, s32[2]{0:T(128)}, u32[]{:S(2)}) copy-start(s32[2]{0:T(128)} %owner_ref.5) | copy-start | bytes 28
  9.1 3.2 %collective-permute-start.2 = (bf16[64,128]{1,0:T(8,128)(2,1)S(1)}, bf16[64,128]{1,0:T(8,128)(2,1)S(1)}, u32[]{:S(2)}, u32[]{:S(2)}) collective-permute-start(bf16[64,128]{1,0:T(8,128)(2,1)S(1)} %get-tuple-element.27), channel_id=1, source_target_pairs={{0,31},{1,16},{2,17},{3,18},{4,19},{5,20},{6,21},{7,22},{8,23},{9,... | collective-permute-start | bytes 49160 | tf_op jit(solution)/shard_map/ppermute | solution.py:825
  14.2 7.9 %collective-permute-start.3 = (s16[96,1024]{1,0:T(8,128)(2,1)S(1)}, s16[96,1024]{1,0:T(8,128)(2,1)S(1)}, u32[]{:S(2)}, u32[]{:S(2)}) collective-permute-start(s16[96,1024]{1,0:T(8,128)(2,1)S(1)} %get-tuple-element.36), channel_id=1, source_target_pairs={{0,1},{1,2},{2,3},{3,4},{4,5},{5,6},{6,7},{7,8},{8,9},{9,10},{10,1... | collective-permute-start | bytes 589832 | tf_op jit(solution)/shard_map/ppermute | solution.py:866
  15.4 9.2 %collective-permute-start.4 = (s16[72,1024]{1,0:T(8,128)(2,1)S(1)}, s16[72,1024]{1,0:T(8,128)(2,1)S(1)}, u32[]{:S(2)}, u32[]{:S(2)}) collective-permute-start(s16[72,1024]{1,0:T(8,128)(2,1)S(1)} %get-tuple-element.41), channel_id=1, source_target_pairs={{0,1},{1,2},{2,3},{3,4},{4,5},{5,6},{6,7},{7,8},{8,9},{9,10},{10,1... | collective-permute-start | bytes 442376 | tf_op jit(solution)/shard_map/ppermute | solution.py:876

commit v7 on v6

--- a/solution.py
+++ b/solution.py
@@ -448,6 +448,12 @@
     tail_ref[4:8, :] = jnp.zeros((4, LANES), F32)
 
 
+def load_map(map_any, map_ref, sem):
+    copy = pltpu.make_async_copy(map_any, map_ref, sem)
+    copy.start()
+    return copy
+
+
 class Pieces:
     def __init__(self, map_ref, coef_ref, slab_ref):
         self.coef, self.slab = coef_ref, slab_ref
@@ -497,20 +503,26 @@
 
 
 def last_row_a_body(
-    map_ref, owner_ref, u_ref, coef_ref, y_ref, straight_ref, diag_ref, box0_ref, rim_ref, side_lap_ref, side_coef_ref,
-    side_rim_ref, drift_ref, box_in, box_ref, lap_ref, side_ref, sums_ref, row_ref, code_ref, power_ref, extra_ref
+    map_any, owner_any, u_ref, coef_ref, y_ref, straight_ref, diag_ref, box0_ref, rim_ref, side_lap_ref, side_coef_ref,
+    side_rim_ref, drift_ref, box_in, box_ref, lap_ref, side_ref, sums_ref, row_ref, code_ref, power_ref, extra_ref,
+    map_ref, owner_ref, sems
 ):
+    copies = [load_map(map_any, map_ref, sems.at[0]), load_map(owner_any, owner_ref, sems.at[1])]
     tail = last_edges(
         coef_ref, y_ref, straight_ref, diag_ref, box0_ref, rim_ref, side_lap_ref, side_coef_ref, side_rim_ref, box_in,
         box_ref, lap_ref, side_ref, sums_ref
     )
+    for copy in copies:
+        copy.wait()
     more = (owner_ref, tail, extra_ref)
     refs = (map_ref, u_ref, coef_ref, y_ref, box_ref, drift_ref, lap_ref, side_ref, sums_ref, row_ref, code_ref, power_ref)
     last_row(0, *refs, more=more)
 
 
-def last_row_b_body(first, *refs):
-    last_row(first, *refs)
+def last_row_b_body(first, map_any, *refs):
+    map_ref, sem = refs[-2:]
+    load_map(map_any, map_ref, sem).wait()
+    last_row(first, map_ref, *refs[:-2])
 
 
 def last_row(
@@ -525,7 +537,6 @@
     pieces = Pieces(map_ref, coef_ref, y_ref)
     lower = pieces.region == 0
     before = slice(width - LANES, width)
-    base = count * depth
     last_tiles = []
     for f in range(first, first + count):
         coef = pieces.piece(fields + f)
@@ -533,43 +544,51 @@
         middle = [drift_ref[1, f, :, tile_at(t)] + coefs[t] * box_ref[f, :, tile_at(t)] for t in range(main)]
         local = drift_ref[0, f, :, before] + pieces.piece(f)(before) * lap_ref[f]
         sums = nine_sum([local] + middle + [side_ref[f]], lane)
-        at = f - first
         for t in range(main):
             lanes = tile_at(t)
             row = sums_ref[f : f + 1, lanes]
             value = second_step(middle[t], u_ref[1, f, :, lanes], sums[t + 1], coefs[t], row_id, row, lower)
-            row_ref[at, :, lanes] = value
+            row_ref[f - first, :, lanes] = value
             power = power_of(jnp.max(jnp.abs(value), axis=0, keepdims=True))
-            code_ref[at * depth : (at + 1) * depth, lanes] = narrow(coded(value, power))
-            power_ref[at : at + 1, lanes] = power
+            at = (f - first) * main + t
+            code_ref[at * depth : (at + 1) * depth, :] = narrow(coded(value, power))
+            power_ref[at : at + 1, :] = power
         last_tiles.append(middle[main - 1])
-    power_ref[count:8, :] = jnp.zeros((8 - count, width), F32)
-    code_ref[base : base + 8, :] = narrow(power_ref[...])
+    base = count * main * depth
+    code_ref[base : base + count * main, :] = narrow(power_ref[...])
     if more is not None:
         owner_ref, tail, extra_ref = more
-        near = y_ref[4, 0:16, before].astype(F32)
-        extra_ref[2:3, :] = jnp.zeros((1, width), F32) + jnp.where(owner_ref[1] != lax.axis_index("blk"), 1.0, 0.0)
-        extra_ref[3:8, :] = jnp.zeros((5, width), F32)
+        base += count * main
+        both = []
         for f in range(fields):
             if f < count:
                 stepped = last_tiles[f]
             else:
                 stepped = drift_ref[1, f, :, before] + pieces.piece(fields + f)(before) * box_ref[f, :, before]
-            both = jnp.where(lane >= 96, u_ref[1, f, :, before], pltpu.roll(stepped, 96, 1))
-            rows = [near[4 + f : 5 + f], near[12 + f : 13 + f], tail[f : f + 1]]
-            size = jnp.max(jnp.abs(both), axis=0, keepdims=True)
-            for row in rows:
-                size = jnp.maximum(size, jnp.abs(row))
-            power = power_of(size)
-            codes = narrow(coded(both, power))
-            here, there = tile_at(f), tile_at(fields + f)
-            code_ref[base + 8 : base + 8 + depth // 2, here] = codes[0 : depth // 2]
-            code_ref[base + 8 : base + 8 + depth // 2, there] = codes[depth // 2 : depth]
-            extra_ref[0:1, here] = power
-            extra_ref[0:1, there] = coded(rows[0], power)
-            extra_ref[1:2, here] = coded(rows[1], power)
-            extra_ref[1:2, there] = coded(rows[2], power)
-        code_ref[base + 8 + depth // 2 : base + 16 + depth // 2, :] = narrow(extra_ref[...])
+            both.append(jnp.where(lane >= 96, u_ref[1, f, :, before], pltpu.roll(stepped, 96, 1)))
+        for g in range(fields // 2):
+            pair = jnp.where(lane >= 64, both[2 * g], pltpu.roll(both[2 * g + 1], 64, 1))
+            power = power_of(jnp.max(jnp.abs(pair), axis=0, keepdims=True))
+            code_ref[base : base + depth, :] = narrow(coded(pair, power))
+            extra_ref[g : g + 1, :] = power
+            base += depth
+        near = y_ref[4, 0:16, before].astype(F32)
+        kinds = []
+        for rows in (near[4:8], near[12:16], tail):
+            kind = jnp.zeros((1, LANES), F32)
+            for f in range(fields):
+                shift = (32 * f + 32) % LANES
+                row = rows[f : f + 1]
+                kind = jnp.where(lane // 32 == f, pltpu.roll(row, shift, 1) if shift else row, kind)
+            kinds.append(kind)
+        power = power_of(jnp.maximum(jnp.maximum(jnp.abs(kinds[0]), jnp.abs(kinds[1])), jnp.abs(kinds[2])))
+        extra_ref[2:3, :] = power
+        for i, kind in enumerate(kinds):
+            extra_ref[3 + i : 4 + i, :] = coded(kind, power)
+        moves = jnp.where(owner_ref[1] != lax.axis_index("blk"), 1.0, 0.0)
+        extra_ref[6:7, :] = jnp.zeros((1, LANES), F32) + moves
+        extra_ref[7:8, :] = jnp.zeros((1, LANES), F32)
+        code_ref[base : base + 8, :] = narrow(extra_ref[...])
 
 
 def first_row_body(map_ref, u_ref, coef_ref, y_ref, box_ref, box1_ref, drift_ref, sums_ref, row_ref):
@@ -594,10 +613,11 @@
 
 def arrival(code_ref):
     rows = code_ref.shape[0]
-    return jnp.max(wide(code_ref[rows - 8 : rows, 0:LANES])[2:3]) > 0.5
-
-
-def code_copies(first, count, depth, row_ref, out_ref, sems, base):
+    return jnp.max(wide(code_ref[rows - 8 : rows, :])[6:7]) > 0.5
+
+
+def code_copies(first, row_ref, out_ref, sems, base):
+    count, depth, _ = row_ref.shape
     part = depth // 2
     copies = []
     for f in range(count):
@@ -608,13 +628,15 @@
     return copies
 
 
-def place_codes(code_ref, first, count, depth, row_ref, out_ref, sems, base):
-    scale = scale_of(wide(code_ref[count * depth : count * depth + 8, :]))
-    part = depth // 2
-    for i, copy in enumerate(code_copies(first, count, depth, row_ref, out_ref, sems, base)):
-        f, h = divmod(i, 2)
-        row_ref[f, h * part : (h + 1) * part] = wide(code_ref[i * part : (i + 1) * part, :]) * scale[f : f + 1]
-        copy.start()
+def decode(code_ref, row_ref):
+    count, depth, width = row_ref.shape
+    main = width // LANES
+    base = count * main * depth
+    scale = scale_of(wide(code_ref[base : base + count * main, :]))
+    for f in range(count):
+        for t in range(main):
+            at = f * main + t
+            row_ref[f, :, tile_at(t)] = wide(code_ref[at * depth : (at + 1) * depth, :]) * scale[at : at + 1]
 
 
 def first_copies(row_ref, out_ref, at, sems, base):
@@ -663,53 +685,36 @@
 
 
 def finish_body(
-    owner_ref, map_ref, u_ref, coef_ref, y_ref, box_ref, drift_ref, tail_ref, code_ref, row_ref,
-    last_a_ref, last_b_ref, partial_ref, out_ref, tile_ref, arrived_ref, sems
+    owner_any, map_any, u_ref, coef_ref, y_ref, box_ref, drift_ref, tail_ref, code_ref, row_ref,
+    last_a_ref, last_b_ref, partial_ref, out_ref, tile_ref, arrived_ref, map_ref, owner_ref, sems
 ):
     fields, depth, width = u_ref.shape[1:]
+    main = width // LANES
     half = arrived_ref.shape[0]
-    base = half * depth
+    copies = [load_map(map_any, map_ref, sems.at[0]), load_map(owner_any, owner_ref, sems.at[1])]
+    arrives = arrival(code_ref)
     lane = lane_ids()
     row_id = lax.broadcasted_iota(jnp.int32, (depth, 1), 0)
-    arrives = arrival(code_ref)
-    slot = jnp.where(arrives, 1, 0)
-    moves_on = jnp.logical_and(arrives, owner_ref[1] == lax.axis_index("blk"))
-    firsts = first_copies(row_ref, out_ref, 1, sems, 1 + 2 * half)
-    lasts = last_copies(last_a_ref, last_b_ref, out_ref, 2, sems, 1 + 2 * half + fields)
-
-    @pl.when(arrives)
-    def _():
-        for copy in firsts:
-            copy.start()
-
-    @pl.when(moves_on)
-    def _():
-        for copy in lasts:
-            copy.start()
-
-    @pl.when(arrives)
-    def _():
-        place_codes(code_ref, 0, half, depth, arrived_ref, out_ref, sems, 1)
-
+    base = half * main * (depth + 1)
     column = ColumnEdge(coef_ref, y_ref)
-    pieces = Pieces(map_ref, coef_ref, y_ref)
-    extra = wide(code_ref[base + 8 + depth // 2 : base + 16 + depth // 2, :])
+    extra = wide(code_ref[base + depth * fields // 2 : base + depth * fields // 2 + 8, :])
     tile0, tile1 = tile_at(0), tile_at(1)
     near = column.near(0, tile0)
-    corners = [[], [], []]
-    rims, before, stepped, nexts, coefs = [], [], [], [], []
-    for f in range(fields):
-        here, there = tile_at(f), tile_at(fields + f)
-        scale = scale_of(extra[0:1, here])
-        corners[0].append(extra[0:1, there] * scale)
-        corners[1].append(extra[1:2, here] * scale)
-        corners[2].append(extra[1:2, there] * scale)
-        upper = wide(code_ref[base + 8 : base + 8 + depth // 2, here])
-        under = wide(code_ref[base + 8 : base + 8 + depth // 2, there])
-        before.append(jnp.concatenate([upper, under], axis=0) * scale)
-    corners = [jnp.concatenate(rows, axis=0) for rows in corners]
+    before = []
+    for g in range(fields // 2):
+        pair = wide(code_ref[base + g * depth : base + (g + 1) * depth, :]) * scale_of(extra[g : g + 1])
+        before += [pair, pltpu.roll(pair, 64, 1)]
+    corners = []
+    for kind in range(3):
+        row = extra[3 + kind : 4 + kind] * scale_of(extra[2:3])
+        shifts = [(96 - 32 * f) % LANES for f in range(fields)]
+        corners.append(jnp.concatenate([pltpu.roll(row, shift, 1) if shift else row for shift in shifts], axis=0))
     near_sum = nine_sum([corners[0], near, column.near(0, tile1)], lane)[1]
     beyond_sum = nine_sum([corners[1], column.beyond(0, tile0), column.beyond(0, tile1)], lane)[1]
+    for copy in copies:
+        copy.wait()
+    pieces = Pieces(map_ref, coef_ref, y_ref)
+    rims, stepped, nexts, coefs = [], [], [], []
     for f in range(fields):
         now = u_ref[0, f, :, tile0]
         total = nine_sum([before[f], now, u_ref[0, f, :, tile1]], lane)[1]
@@ -727,31 +732,45 @@
         total = nine_sum([pltpu.roll(before[f], 32, 1), stepped[f], nexts[f]], lane)[1]
         row = edge_sum[f : f + 1]
         tile_ref[f] = second_step(stepped[f], u_ref[0, f, :, tile0], total, coefs[f], row_id, row, column.lower)
-    last = pltpu.make_async_copy(tile_ref, out_ref.at[slot, :, :, tile0], sems.at[0])
+    decode(code_ref, arrived_ref)
+
+    slot = jnp.where(arrives, 1, 0)
+    moves_on = jnp.logical_and(arrives, owner_ref[1] == lax.axis_index("blk"))
+    last = pltpu.make_async_copy(tile_ref, out_ref.at[slot, :, :, tile0], sems.at[2])
+    coming = code_copies(0, arrived_ref, out_ref, sems, 3) + first_copies(row_ref, out_ref, 1, sems, 3 + 2 * half)
+    lasts = last_copies(last_a_ref, last_b_ref, out_ref, 2, sems, 3 + 2 * half + fields)
     last.start()
 
     @pl.when(arrives)
     def _():
-        for copy in code_copies(0, half, depth, arrived_ref, out_ref, sems, 1):
-            copy.wait()
-        for copy in firsts:
-            copy.wait()
+        for copy in coming:
+            copy.start()
 
     @pl.when(moves_on)
     def _():
         for copy in lasts:
+            copy.start()
+        for copy in lasts:
             copy.wait()
 
+    @pl.when(arrives)
+    def _():
+        for copy in coming:
+            copy.wait()
+
     last.wait()
 
 
 def place_body(first, code_a_ref, code_ref, partial_ref, out_ref, row_ref, sems):
-    count, depth, _ = row_ref.shape
-
-    @pl.when(arrival(code_a_ref))
+    arrives = arrival(code_a_ref)
+    decode(code_ref, row_ref)
+    copies = code_copies(first, row_ref, out_ref, sems, 0)
+
+    @pl.when(arrives)
     def _():
-        place_codes(code_ref, first, count, depth, row_ref, out_ref, sems, 0)
-        for copy in code_copies(first, count, depth, row_ref, out_ref, sems, 0):
+        for copy in copies:
+            copy.start()
+        for copy in copies:
             copy.wait()
 
 
@@ -850,16 +869,18 @@
     )
     half = fields // 2
     part = jax.ShapeDtypeStruct((half, depth, width), F32)
-    codes = jax.ShapeDtypeStruct((half * depth + 8, width), jnp.int16)
-    more_codes = jax.ShapeDtypeStruct((half * depth + depth // 2 + 16, width), jnp.int16)
-    powers = pltpu.VMEM((8, width), F32)
+    tiled = half * width // LANES
+    codes = jax.ShapeDtypeStruct((tiled * (depth + 1), LANES), jnp.int16)
+    more_codes = jax.ShapeDtypeStruct((tiled * (depth + 1) + half * depth + 8, LANES), jnp.int16)
+    scalars = [pltpu.SMEM(order.shape, jnp.int32), pltpu.SMEM(new_owner.shape, jnp.int32)]
+    powers = pltpu.VMEM((tiled, LANES), F32)
     box1, lap1, side1, sums1, last_a, code_a = call(
         last_row_a_body,
         "last_row",
         (row, tiles, tiles, sums, part, more_codes),
-        [SMEM] * 2 + [VMEM] * 12,
+        [ANY] * 2 + [VMEM] * 12,
         (VMEM,) * 6,
-        [powers, powers],
+        [powers, pltpu.VMEM((8, LANES), F32)] + scalars + [pltpu.SemaphoreType.DMA((2,))],
         (order, new_owner, now, coef, y_in, from_right, from_dright, box0, rim, side_lap, side_coef, side_rim, drift, box1),
         input_output_aliases={13: 0},
     )
@@ -868,9 +889,9 @@
         functools.partial(last_row_b_body, half),
         "last_row",
         (part, codes),
-        [SMEM] + [VMEM] * 8,
+        [ANY] + [VMEM] * 8,
         (VMEM,) * 2,
-        [powers],
+        [powers, scalars[0], pltpu.SemaphoreType.DMA],
         (order, now, coef, y_in, box1, drift, lap1, side1, sums1),
     )
     arrived_b = lax.ppermute(code_b, "blk", forward)
@@ -908,13 +929,11 @@
         finish_body,
         "finish",
         whole,
-        [SMEM] * 2 + [VMEM] * 10 + [ANY],
+        [ANY] * 2 + [VMEM] * 10 + [ANY],
         ANY,
-        [
-            pltpu.VMEM((fields, depth, LANES), F32),
-            arrived_half,
-            pltpu.SemaphoreType.DMA((1 + 2 * half + 2 * fields,)),
-        ],
+        [pltpu.VMEM((fields, depth, LANES), F32), arrived_half]
+        + scalars
+        + [pltpu.SemaphoreType.DMA((3 + 2 * half + 2 * fields,))],
         (new_owner, order, now, coef, y_in, box0, drift, tail0, arrived_a, first, last_a, last_b, placed),
         input_output_aliases={12: 0},
     )

time: 25.7 us -> 25.3 us (0.984)
  waiting for transfers between devices: 2.66 us -> 2.18 us
    ppermute x1, waiting for transfers between devices: 1.62 us -> 1.15 us  [fast_on_device(): arrived_a = lax.ppermute(code_a, 'blk', forward)]
  transfers between devices with their start and end apart: 5 -> 5, of which waited for: 2 -> 2; matrix products, arithmetic and copies ran while one was open for 0% -> 0% of each run, Pallas kernels for 39% -> 41%
where the time goes in v7:
time: 25.3 us; the launch traced here: 25.2 us
  Pallas kernels  13.6 us (54%)
  starting transfers between devices  9.24 us (37%)
  waiting for transfers between devices  2.18 us (9%)
    pallas_call x11, Pallas kernels, call(): pl.pallas_call(body, out_shape=out_shape, in_specs=in_specs, out_specs=ou...  13.6 us
    ppermute x1, starting transfers between devices, fast_on_device(): from_right = lax.ppermute(left, 'blk', backward)  3.74 us
    ppermute x1, starting transfers between devices, fast_on_device(): y_in = lax.ppermute(y_out, 'region', swap)  3.03 us
    ppermute x1, starting transfers between devices, fast_on_device(): arrived_b = lax.ppermute(code_b, 'blk', forward)  1.47 us
    ppermute x1, waiting for transfers between devices, fast_on_device(): arrived_a = lax.ppermute(code_a, 'blk', forward)  1.15 us
    ppermute x1, waiting for transfers between devices, fast_on_device(): from_dright = lax.ppermute(dleft, ('region', 'blk'), crossed)  1.03 us
    ppermute x1, starting transfers between devices, fast_on_device(): from_dright = lax.ppermute(dleft, ('region', 'blk'), crossed)  0.94 us
  transfers between devices with their start and end apart: 5, of which 2 were waited for; matrix products, arithmetic and copies ran while one was open for 0% of the time, Pallas kernels for 41%

profile of v7, /device:TPU:0, one launch (start us, length us, event | category | flops | bytes accessed | tf_op | source)
XLA Modules:
  0.0 25.2 jit_solution(8485552502750309293)
XLA Ops:
  0.0 1.2 %pack_region.1 = bf16[5,32,1024]{2,1,0:T(8,128)(2,1)S(1)} custom-call(s32[8]{0:T(128)} %bitcast.26, f32[2,4,32,1024]{3,2,1,0:T(8,128)} %bitcast.7, f32[2,4,32,1024]{3,2,1,0:T(8,128)} %bitcast.23, bf16[2,4,32,1024]{3,2,1,0:T(8,128)(2,1)} %bitcast.16), custom_call_target="tpu_custom_call" | custom-call | tf_op jit(solution)/shard_map/pack_region/pallas_call | solution.py:790
  1.3 0.0 copy-start
  1.3 0.0 copy-start.2
  1.3 3.0 %collective-permute-start = (bf16[5,32,1024]{2,1,0:T(8,128)(2,1)S(1)}, bf16[5,32,1024]{2,1,0:T(8,128)(2,1)S(1)}, u32[]{:S(2)}, u32[]{:S(2)}) collective-permute-start(bf16[5,32,1024]{2,1,0:T(8,128)(2,1)S(1)} %pack_region.1), channel_id=1, source_target_pairs={{0,16},{16,0},{1,17},{17,1},{2,18},{18,2},{3,19},{19,3},{4,20},{20... | collective-permute-start | bytes 983048 | tf_op jit(solution)/shard_map/ppermute | solution.py:842
  4.3 1.1 %pack_back.1 = (bf16[144,128]{1,0:T(8,128)(2,1)S(1)}, bf16[64,128]{1,0:T(8,128)(2,1)S(1)}) custom-call(s32[8]{0:T(128)} %bitcast.27, f32[2,4,32,1024]{3,2,1,0:T(8,128)} %bitcast.8, f32[2,4,32,1024]{3,2,1,0:T(8,128)} %bitcast.24, bf16[2,4,32,1024]{3,2,1,0:T(8,128)(2,1)} %bitcast.17), custom_call_target="tpu_custom_call" | custom-call | tf_op jit(solution)/shard_map/pack_back/pallas_call | solution.py:790
  5.4 3.7 %collective-permute-start.1 = (bf16[144,128]{1,0:T(8,128)(2,1)S(1)}, bf16[144,128]{1,0:T(8,128)(2,1)S(1)}, u32[]{:S(2)}, u32[]{:S(2)}) collective-permute-start(bf16[144,128]{1,0:T(8,128)(2,1)S(1)} %get-tuple-element.26), channel_id=1, source_target_pairs={{0,15},{1,0},{2,1},{3,2},{4,3},{5,4},{6,5},{7,6},{8,7},{9,8},{10,9... | collective-permute-start | bytes 110600 | tf_op jit(solution)/shard_map/ppermute | solution.py:843
  9.1 0.0 copy-start.1
  9.1 0.0 copy-start.3
  9.1 0.0 copy-start.4
  9.1 0.9 %collective-permute-start.2 = (bf16[64,128]{1,0:T(8,128)(2,1)S(1)}, bf16[64,128]{1,0:T(8,128)(2,1)S(1)}, u32[]{:S(2)}, u32[]{:S(2)}) collective-permute-start(bf16[64,128]{1,0:T(8,128)(2,1)S(1)} %get-tuple-element.27), channel_id=1, source_target_pairs={{0,31},{1,16},{2,17},{3,18},{4,19},{5,20},{6,21},{7,22},{8,23},{9,... | collective-permute-start | bytes 49160 | tf_op jit(solution)/shard_map/ppermute | solution.py:844
  10.1 0.0 copy-done
  10.1 0.0 copy-done.2
  10.1 1.3 %local.1 = (f32[4,32,1024]{2,1,0:T(8,128)S(1)}, f32[4,32,1024]{2,1,0:T(8,128)S(1)}, f32[2,4,32,1024]{3,2,1,0:T(8,128)S(1)}, f32[2,8,1024]{2,1,0:T(8,128)S(1)}) custom-call(f32[2,4,32,1024]{3,2,1,0:T(8,128)S(1)} %bitcast.9, f32[2,4,32,1024]{3,2,1,0:T(8,128)S(1)} %bitcast.25), custom_call_target="tpu_custom_call" | custom-call | tf_op jit(solution)/shard_map/local/pallas_call | solution.py:790
  11.3 1.0 %collective-permute-done.2.diag_ref = bf16[64,128]{1,0:T(8,128)(2,1)S(1)} collective-permute-done((bf16[64,128]{1,0:T(8,128)(2,1)S(1)}, bf16[64,128]{1,0:T(8,128)(2,1)S(1)}, u32[]{:S(2)}, u32[]{:S(2)}) %collective-permute-start.2) | collective-permute-done | bytes 16416 | tf_op jit(solution)/shard_map/ppermute | solution.py:844
  12.4 0.0 collective-permute-done.1.straight_ref
  12.4 0.3 %border.1 = (f32[4,32,1024]{2,1,0:T(8,128)S(1)}, f32[4,32,128]{2,1,0:T(8,128)S(1)}, f32[4,32,128]{2,1,0:T(8,128)S(1)}, f32[2,8,128]{2,1,0:T(8,128)S(1)}) custom-call(f32[2,4,32,1024]{3,2,1,0:T(8,128)S(1)} %bitcast.10, bf16[144,128]{1,0:T(8,128)(2,1)S(1)} %collective-permute-done.1.straight_ref, ...), custom_call_target="tpu_custom_call", output_to_operand_aliasing={{0}: (3, {})} | custom-call | bytes 40000000 | tf_op jit(solution)/shard_map/border/pallas_call | solution.py:790
  12.7 0.0 collective-permute-done.y_ref.refs_2_
  12.7 0.0 copy-done.1
  12.8 0.0 copy-done.3
  12.8 0.0 copy-done.4
  12.8 1.2 %last_row.2 = (f32[4,32,1024]{2,1,0:T(8,128)S(1)}, f32[4,32,128]{2,1,0:T(8,128)S(1)}, f32[4,32,128]{2,1,0:T(8,128)S(1)}, f32[8,1024]{1,0:T(8,128)S(1)}, f32[2,32...) custom-call(s32[8]{0:T(128)S(1)} %bitcast.28, s32[2]{0:T(128)S(1)} %copy-done.4, ...), custom_call_target="tpu_custom_call", output_to_operand_aliasing={{0}: (13, {})} | custom-call | tf_op jit(solution)/shard_map/last_row/pallas_call | solution.py:790
  14.0 0.1 collective-permute-start.3
  14.0 1.2 %last_row.3 = (f32[2,32,1024]{2,1,0:T(8,128)S(1)}, s16[528,128]{1,0:T(8,128)(2,1)S(1)}) custom-call(s32[8]{0:T(128)S(1)} %bitcast.29, f32[2,4,32,1024]{3,2,1,0:T(8,128)S(1)} %bitcast.12, bf16[2,4,32,1024]{3,2,1,0:T(8,128)(2,1)S(1)} %bitcast.19, bf16[5,32,1024]{2,1,0:T(8,128)(2,1)S(1)} %collective-permute-done.y_ref.refs_2_, ...), custom_call_target="tpu_custom_call" | custom-call | tf_op jit(solution)/shard_map/last_row/pallas_call | solution.py:790
  15.2 1.5 %collective-permute-start.4 = (s16[528,128]{1,0:T(8,128)(2,1)S(1)}, s16[528,128]{1,0:T(8,128)(2,1)S(1)}, u32[]{:S(2)}, u32[]{:S(2)}) collective-permute-start(s16[528,128]{1,0:T(8,128)(2,1)S(1)} %get-tuple-element.41), channel_id=1, source_target_pairs={{0,1},{1,2},{2,3},{3,4},{4,5},{5,6},{6,7},{7,8},{8,9},{9,10},{10,1... | collective-permute-start | bytes 405512 | tf_op jit(solution)/shard_map/ppermute | solution.py:897
  16.7 0.4 %first_edges.1 = (f32[4,32,1024]{2,1,0:T(8,128)S(1)}, f32[8,1024]{1,0:T(8,128)S(1)}, f32[8,128]{1,0:T(8,128)S(1)}) custom-call(f32[2,4,32,1024]{3,2,1,0:T(8,128)S(1)} %bitcast.13, bf16[2,4,32,1024]{3,2,1,0:T(8,128)(2,1)S(1)} %bitcast.20, bf16[5,32,1024]{2,1,0:T(8,128)(2,1)S(1)} %collective-permute-done.y_ref.refs_2_, ...), custom_call_target="tpu_custom_call", output_to_operand_aliasing={{0}: (5, {})} | custom-call | tf_op jit(solution)/shard_map/first_edges/pallas_call | solution.py:790
  17.1 1.4 %first_row.1.row_ref = f32[4,32,1024]{2,1,0:T(8,128)S(1)} custom-call(s32[8]{0:T(128)S(1)} %bitcast.30, f32[2,4,32,1024]{3,2,1,0:T(8,128)S(1)} %bitcast.14, bf16[2,4,32,1024]{3,2,1,0:T(8,128)(2,1)S(1)} %bitcast.21, bf16[5,32,1024]{2,1,0:T(8,128)(2,1)S(1)} %collective-permute-done.y_ref.refs_2_, f32[4,32,1024]{2,1,0:T(8,128)S(1)} %get-tuple-element.42.box_ref, ...), custom_call_target="tpu_custom_call" | custom-call | tf_op jit(solution)/shard_map/first_row/pallas_call | solution.py:790
  18.5 1.8 %rows.1.partial_ref = f32[3,4,32,1024]{3,2,1,0:T(8,128)} custom-call(s32[2]{0:T(128)S(1)} %copy-done.4, f32[4,32,1024]{2,1,0:T(8,128)S(1)} %first_row.1.row_ref, f32[2,32,1024]{2,1,0:T(8,128)S(1)} %get-tuple-element.45.last_a_ref, f32[2,32,1024]{2,1,0:T(8,128)S(1)} %get-tuple-element.46.last_b_ref), custom_call_target="tpu_custom_call" | custom-call | tf_op jit(solution)/shard_map/rows/pallas_call | solution.py:790
  20.3 1.1 %collective-permute-done.3.code_ref.code_a_ref = s16[600,128]{1,0:T(8,128)(2,1)S(1)} collective-permute-done((s16[600,128]{1,0:T(8,128)(2,1)S(1)}, s16[600,128]{1,0:T(8,128)(2,1)S(1)}, u32[]{:S(2)}, u32[]{:S(2)}) %collective-permute-start.3) | collective-permute-done | bytes 153632 | tf_op jit(solution)/shard_map/ppermute | solution.py:887
  21.4 2.9 %finish.1.partial_ref = f32[3,4,32,1024]{3,2,1,0:T(8,128)} custom-call(s32[2]{0:T(128)S(1)} %copy-done.4, s32[8]{0:T(128)S(1)} %bitcast.31, f32[2,4,32,1024]{3,2,1,0:T(8,128)S(1)} %bitcast.15, bf16[2,4,32,1024]{3,2,1,0:T(8,128)(2,1)S(1)} %bitcast.22, bf16[5,32,1024]{2,1,0:T(8,128)(2,1)S(1)} %collective-permute-done.y_ref.refs_2_, ...), custom_call_target="tpu_custom_call", output_to_operand_aliasing={{}: (12, {})} | custom-call | tf_op jit(solution)/shard_map/finish/pallas_call | solution.py:790
  24.3 0.0 collective-permute-done.4.code_ref
  24.3 0.9 %place.1 = f32[3,4,32,1024]{3,2,1,0:T(8,128)} custom-call(s16[600,128]{1,0:T(8,128)(2,1)S(1)} %collective-permute-done.3.code_ref.code_a_ref, s16[528,128]{1,0:T(8,128)(2,1)S(1)} %collective-permute-done.4.code_ref, f32[3,4,32,1024]{3,2,1,0:T(8,128)} %finish.1.partial_ref), custom_call_target="tpu_custom_call", output_to_operand_aliasing={{}: (2, {})} | custom-call | tf_op jit(solution)/shard_map/place/pallas_call | solution.py:790
Async XLA Ops:
  1.3 8.8 %copy-start = (f32[2,1,4,32,1024]{4,3,2,1,0:T(8,128)S(1)}, f32[2,1,4,32,1024]{4,3,2,1,0:T(8,128)}, u32[]{:S(2)}) copy-start(f32[2,1,4,32,1024]{4,3,2,1,0:T(8,128)} %param.5) | copy-start | bytes 3145732
  1.3 8.8 %copy-start.2 = (f32[2,1,4,32,1024]{4,3,2,1,0:T(8,128)S(1)}, f32[2,1,4,32,1024]{4,3,2,1,0:T(8,128)}, u32[]{:S(2)}) copy-start(f32[2,1,4,32,1024]{4,3,2,1,0:T(8,128)} %param.6) | copy-start | bytes 3145732
  1.3 11.5 %collective-permute-start = (bf16[5,32,1024]{2,1,0:T(8,128)(2,1)S(1)}, bf16[5,32,1024]{2,1,0:T(8,128)(2,1)S(1)}, u32[]{:S(2)}, u32[]{:S(2)}) collective-permute-start(bf16[5,32,1024]{2,1,0:T(8,128)(2,1)S(1)} %pack_region.1), channel_id=1, source_target_pairs={{0,16},{16,0},{1,17},{17,1},{2,18},{18,2},{3,19},{19,3},{4,20},{20... | collective-permute-start | bytes 983048 | tf_op jit(solution)/shard_map/ppermute | solution.py:842
  5.4 7.0 %collective-permute-start.1 = (bf16[144,128]{1,0:T(8,128)(2,1)S(1)}, bf16[144,128]{1,0:T(8,128)(2,1)S(1)}, u32[]{:S(2)}, u32[]{:S(2)}) collective-permute-start(bf16[144,128]{1,0:T(8,128)(2,1)S(1)} %get-tuple-element.26), channel_id=1, source_target_pairs={{0,15},{1,0},{2,1},{3,2},{4,3},{5,4},{6,5},{7,6},{8,7},{9,8},{10,9... | collective-permute-start | bytes 110600 | tf_op jit(solution)/shard_map/ppermute | solution.py:843
  9.1 3.6 %copy-start.1 = (bf16[1,1,2,4,32,1024]{5,4,3,2,1,0:T(8,128)(2,1)S(1)}, bf16[1,1,2,4,32,1024]{5,4,3,2,1,0:T(8,128)(2,1)}, u32[]{:S(2)}) copy-start(bf16[1,1,2,4,32,1024]{5,4,3,2,1,0:T(8,128)(2,1)} %param.7) | copy-start | bytes 1572868
  9.1 3.6 %copy-start.3 = (s32[1,1,8]{2,1,0:T(1,128)S(1)}, s32[1,1,8]{2,1,0:T(1,128)}, u32[]{:S(2)}) copy-start(s32[1,1,8]{2,1,0:T(1,128)} %param.8) | copy-start | bytes 100
  9.1 3.6 %copy-start.4 = (s32[2]{0:T(128)S(1)}, s32[2]{0:T(128)}, u32[]{:S(2)}) copy-start(s32[2]{0:T(128)} %owner_any.3) | copy-start | bytes 28
  9.1 3.2 %collective-permute-start.2 = (bf16[64,128]{1,0:T(8,128)(2,1)S(1)}, bf16[64,128]{1,0:T(8,128)(2,1)S(1)}, u32[]{:S(2)}, u32[]{:S(2)}) collective-permute-start(bf16[64,128]{1,0:T(8,128)(2,1)S(1)} %get-tuple-element.27), channel_id=1, source_target_pairs={{0,31},{1,16},{2,17},{3,18},{4,19},{5,20},{6,21},{7,22},{8,23},{9,... | collective-permute-start | bytes 49160 | tf_op jit(solution)/shard_map/ppermute | solution.py:844
  14.0 7.4 %collective-permute-start.3 = (s16[600,128]{1,0:T(8,128)(2,1)S(1)}, s16[600,128]{1,0:T(8,128)(2,1)S(1)}, u32[]{:S(2)}, u32[]{:S(2)}) collective-permute-start(s16[600,128]{1,0:T(8,128)(2,1)S(1)} %get-tuple-element.36), channel_id=1, source_target_pairs={{0,1},{1,2},{2,3},{3,4},{4,5},{5,6},{6,7},{7,8},{8,9},{9,10},{10,1... | collective-permute-start | bytes 460808 | tf_op jit(solution)/shard_map/ppermute | solution.py:887
  15.2 9.1 %collective-permute-start.4 = (s16[528,128]{1,0:T(8,128)(2,1)S(1)}, s16[528,128]{1,0:T(8,128)(2,1)S(1)}, u32[]{:S(2)}, u32[]{:S(2)}) collective-permute-start(s16[528,128]{1,0:T(8,128)(2,1)S(1)} %get-tuple-element.41), channel_id=1, source_target_pairs={{0,1},{1,2},{2,3},{3,4},{4,5},{5,6},{6,7},{7,8},{8,9},{9,10},{10,1... | collective-permute-start | bytes 405512 | tf_op jit(solution)/shard_map/ppermute | solution.py:897

commit v8 on v7

--- a/solution.py
+++ b/solution.py
@@ -133,57 +133,65 @@
     return pl.multiple_of(jnp.where(lower, depth - size, 0), size)
 
 
-def tag_values(map_ref, region):
-    numbers = [map_ref[region * 4 + s] for s in range(4)] + [map_ref[(1 - region) * 4 + s] for s in range(4)]
-    return [jnp.zeros((1, LANES), F32) + number.astype(F32) for number in numbers]
-
-
-def edge_copies(u_ref, p_ref, coef_ref, ue_ref, pe_ref, ce_ref, some, region, sems):
-    lower = region == 0
-    depth = u_ref.shape[2]
-    edge8 = edge_start(lower, depth, 8)
-    edge16 = edge_start(lower, depth, 16)
-    rows, lanes = some
-    return [
-        pltpu.make_async_copy(u_ref.at[rows, :, pl.ds(edge8, 8), lanes], ue_ref, sems.at[0]),
-        pltpu.make_async_copy(p_ref.at[rows, :, pl.ds(edge8, 8), lanes], pe_ref, sems.at[1]),
-        pltpu.make_async_copy(coef_ref.at[region, :, pl.ds(edge16, 16), lanes], ce_ref, sems.at[2]),
-    ]
-
-
-def edge_rows(ue_ref, pe_ref, m, f, lower):
-    own_edge = jnp.where(lower, 7, 0)
-    own_next = jnp.where(lower, 6, 1)
-    near = ue_ref[m, f, pl.ds(own_edge, 1), :]
-    return near, ue_ref[m, f, pl.ds(own_next, 1), :], 2.0 * near - pe_ref[m, f, pl.ds(own_edge, 1), :]
-
-
-def edge_piece(ce_ref, s, lower):
-    piece = ce_ref[s].astype(F32)
-    return jnp.where(lower, piece[15:16], piece[0:1])
-
-
-def pack_back_body(
-    map_hbm, u_ref, p_ref, coef_ref, straight_ref, diag_ref, ue_ref, pe_ref, ce_ref, ua_ref, pa_ref, ca_ref, map_ref, sems
+def pack_region_body(
+    map_hbm, u_ref, p_ref, coef_ref, y_ref, edges_ref, ua_ref, pa_ref, ca_ref, ue_ref, pe_ref, ce_ref, map_ref, sems
 ):
-    fields = u_ref.shape[1]
-    depth = u_ref.shape[2]
+    fields, depth, width = u_ref.shape[1:]
     region = lax.axis_index("region")
     lower = region == 0
     other = 1 - region
+    half = depth // 2
     front = slice(0, LANES)
+    edge8 = edge_start(lower, depth, 8)
+    edge16 = edge_start(lower, depth, 16)
+    slab = []
+    for s in range(4):
+        for h in range(2):
+            part = slice(h * half, (h + 1) * half)
+            slab.append(pltpu.make_async_copy(coef_ref.at[other, s, part], y_ref.at[s, part], sems.at[7 + 2 * s + h]))
     copies = [
-        pltpu.make_async_copy(map_hbm, map_ref, sems.at[3]),
+        pltpu.make_async_copy(map_hbm, map_ref, sems.at[0]),
+        pltpu.make_async_copy(u_ref.at[:, :, pl.ds(edge8, 8), :], ue_ref, sems.at[1]),
+        pltpu.make_async_copy(p_ref.at[:, :, pl.ds(edge8, 8), :], pe_ref, sems.at[2]),
+        pltpu.make_async_copy(coef_ref.at[region, :, pl.ds(edge16, 16), :], ce_ref, sems.at[3]),
+    ]
+    beside = [
         pltpu.make_async_copy(u_ref.at[0, :, :, front], ua_ref, sems.at[4]),
         pltpu.make_async_copy(p_ref.at[0, :, :, front], pa_ref, sems.at[5]),
         pltpu.make_async_copy(coef_ref.at[:, :, :, front], ca_ref, sems.at[6]),
-    ] + edge_copies(u_ref, p_ref, coef_ref, ue_ref, pe_ref, ce_ref, (slice(0, 1), front), region, sems)
-    for copy in copies:
+    ]
+    for copy in copies + slab + beside:
         copy.start()
     for copy in copies:
         copy.wait()
+    own_edge = jnp.where(lower, 7, 0)
+    own_next = jnp.where(lower, 6, 1)
+    for m in range(2):
+        for f in range(fields):
+            at = m * fields + f
+            near = ue_ref[m, f, pl.ds(own_edge, 1), :]
+            edges_ref[at : at + 1, :] = near
+            edges_ref[8 + at : 9 + at, :] = ue_ref[m, f, pl.ds(own_next, 1), :]
+            edges_ref[16 + at : 17 + at, :] = 2.0 * near - pe_ref[m, f, pl.ds(own_edge, 1), :]
+    for s in range(4):
+        piece = ce_ref[s].astype(F32)
+        edges_ref[24 + s : 25 + s, :] = jnp.where(lower, piece[15:16], piece[0:1])
+    numbers = [map_ref[region * 4 + s] for s in range(4)] + [map_ref[other * 4 + s] for s in range(4)]
+    for i, number in enumerate(numbers):
+        edges_ref[28:29, tile_at(i)] = jnp.zeros((1, LANES), F32) + number.astype(F32)
+    edges_ref[29:32, :] = jnp.zeros((3, width), F32)
+    y_ref[4] = edges_ref[...].astype(BF16)
+    for copy in slab + beside:
+        copy.wait()
+
+
+def pack_back_body(edges_ref, ua_ref, pa_ref, ca_ref, straight_ref, diag_ref):
+    fields, depth, _ = ua_ref.shape
+    region = lax.axis_index("region")
+    lower = region == 0
+    other = 1 - region
     lane = lane_ids()
-    tag_rows = tag_values(map_ref, region)
+    tag_rows = [edges_ref[28:29, tile_at(i)] for i in range(8)]
     blank = jnp.zeros((1, LANES), F32)
     for f in range(fields):
         now = ua_ref[f]
@@ -201,42 +209,8 @@
         moved = pltpu.roll(far[s], 32 * s, 1) if s else far[s]
         plane = jnp.where((lane >= 32 * s) & (lane < 32 * s + 32), moved, plane)
     diag_ref[0:depth, :] = plane.astype(BF16)
-    rows = [edge_rows(ue_ref, pe_ref, 0, f, lower) for f in range(fields)]
-    extra = [row[kind] for kind in range(3) for row in rows]
-    extra += [edge_piece(ce_ref, s, lower) for s in range(4)] + tag_rows + [blank] * 8
-    diag_ref[depth : depth + 32, :] = jnp.concatenate(extra, axis=0).astype(BF16)
-
-
-def pack_region_body(map_hbm, u_ref, p_ref, coef_ref, y_ref, rows_ref, ue_ref, pe_ref, ce_ref, map_ref, sems):
-    fields, depth, width = u_ref.shape[1:]
-    region = lax.axis_index("region")
-    lower = region == 0
-    other = 1 - region
-    half = depth // 2
-    slab = []
-    for s in range(4):
-        for h in range(2):
-            part = slice(h * half, (h + 1) * half)
-            slab.append(pltpu.make_async_copy(coef_ref.at[other, s, part], y_ref.at[s, part], sems.at[4 + 2 * s + h]))
-    copies = [pltpu.make_async_copy(map_hbm, map_ref, sems.at[3])]
-    copies += edge_copies(u_ref, p_ref, coef_ref, ue_ref, pe_ref, ce_ref, (slice(0, 2), slice(0, width)), region, sems)
-    for copy in copies + slab:
-        copy.start()
-    for copy in copies:
-        copy.wait()
-    for m in range(2):
-        for f in range(fields):
-            for kind, row in enumerate(edge_rows(ue_ref, pe_ref, m, f, lower)):
-                at = 8 * kind + m * fields + f
-                rows_ref[at : at + 1, :] = row
-    for s in range(4):
-        rows_ref[24 + s : 25 + s, :] = edge_piece(ce_ref, s, lower)
-    for i, row in enumerate(tag_values(map_ref, region)):
-        rows_ref[28:29, i * LANES : (i + 1) * LANES] = row
-    rows_ref[29:32, :] = jnp.zeros((3, width), F32)
-    y_ref[4] = rows_ref[...].astype(BF16)
-    for copy in slab:
-        copy.wait()
+    rows = [edges_ref[base : base + 4, 0:LANES] for base in (0, 8, 16, 24)]
+    diag_ref[depth : depth + 32, :] = jnp.concatenate(rows + tag_rows + [blank] * 8, axis=0).astype(BF16)
 
 
 def nine_sum(tiles, lane, first=0):
@@ -639,35 +613,25 @@
             row_ref[f, :, tile_at(t)] = wide(code_ref[at * depth : (at + 1) * depth, :]) * scale[at : at + 1]
 
 
-def first_copies(row_ref, out_ref, at, sems, base):
+def row_copies(owner_ref, row_ref, last_a_ref, last_b_ref, zero_ref, out_ref, at, sems, base):
     fields, _, width = row_ref.shape
+    half = last_a_ref.shape[0]
+    keeps = owner_ref[1] == lax.axis_index("blk")
     rest = slice(LANES, width)
-    return [
+    sources = [last_a_ref.at[f] for f in range(half)] + [last_b_ref.at[f] for f in range(half)]
+
+    def copies(sources, at, base):
+        return [pltpu.make_async_copy(source, out_ref.at[at, f], sems.at[base + f]) for f, source in enumerate(sources)]
+
+    firsts = [
         pltpu.make_async_copy(row_ref.at[f, :, rest], out_ref.at[at, f, :, rest], sems.at[base + f])
         for f in range(fields)
     ]
-
-
-def last_copies(last_a_ref, last_b_ref, out_ref, at, sems, base):
-    half = last_a_ref.shape[0]
-    sources = [last_a_ref.at[f] for f in range(half)] + [last_b_ref.at[f] for f in range(half)]
-    return [pltpu.make_async_copy(source, out_ref.at[at, f], sems.at[base + f]) for f, source in enumerate(sources)]
-
-
-def rows_body(owner_ref, row_ref, last_a_ref, last_b_ref, out_ref, zero_ref, sems):
-    fields = row_ref.shape[0]
-    keeps = owner_ref[1] == lax.axis_index("blk")
-    zero_ref[...] = jnp.zeros(zero_ref.shape, F32)
-
-    def zeros(at, base):
-        return [pltpu.make_async_copy(zero_ref, out_ref.at[at, f], sems.at[base + f]) for f in range(fields)]
-
-    always = first_copies(row_ref, out_ref, 0, sems, 0) + zeros(2, fields)
-    kept = last_copies(last_a_ref, last_b_ref, out_ref, 1, sems, 2 * fields)
-    gone = zeros(1, 2 * fields)
-
-    def all_of(act):
-        for copy in always:
+    kept = copies(sources, at + 1, base + fields)
+    gone = copies([zero_ref] * fields, at + 1, base + fields)
+
+    def apply(act):
+        for copy in firsts:
             act(copy)
 
         @pl.when(keeps)
@@ -680,13 +644,19 @@
             for copy in gone:
                 act(copy)
 
-    all_of(lambda copy: copy.start())
-    all_of(lambda copy: copy.wait())
+    return apply
+
+
+def rows_body(owner_ref, row_ref, last_a_ref, last_b_ref, out_ref, zero_ref, sems):
+    zero_ref[...] = jnp.zeros(zero_ref.shape, F32)
+    apply = row_copies(owner_ref, row_ref, last_a_ref, last_b_ref, zero_ref, out_ref, 1, sems, 0)
+    apply(lambda copy: copy.start())
+    apply(lambda copy: copy.wait())
 
 
 def finish_body(
     owner_any, map_any, u_ref, coef_ref, y_ref, box_ref, drift_ref, tail_ref, code_ref, row_ref,
-    last_a_ref, last_b_ref, partial_ref, out_ref, tile_ref, arrived_ref, map_ref, owner_ref, sems
+    last_a_ref, last_b_ref, partial_ref, out_ref, tile_ref, arrived_ref, zero_ref, map_ref, owner_ref, sems
 ):
     fields, depth, width = u_ref.shape[1:]
     main = width // LANES
@@ -732,31 +702,33 @@
         total = nine_sum([pltpu.roll(before[f], 32, 1), stepped[f], nexts[f]], lane)[1]
         row = edge_sum[f : f + 1]
         tile_ref[f] = second_step(stepped[f], u_ref[0, f, :, tile0], total, coefs[f], row_id, row, column.lower)
-    decode(code_ref, arrived_ref)
 
     slot = jnp.where(arrives, 1, 0)
-    moves_on = jnp.logical_and(arrives, owner_ref[1] == lax.axis_index("blk"))
     last = pltpu.make_async_copy(tile_ref, out_ref.at[slot, :, :, tile0], sems.at[2])
-    coming = code_copies(0, arrived_ref, out_ref, sems, 3) + first_copies(row_ref, out_ref, 1, sems, 3 + 2 * half)
-    lasts = last_copies(last_a_ref, last_b_ref, out_ref, 2, sems, 3 + 2 * half + fields)
     last.start()
 
     @pl.when(arrives)
     def _():
+        decode(code_ref, arrived_ref)
+        coming = code_copies(0, arrived_ref, out_ref, sems, 3)
         for copy in coming:
             copy.start()
-
-    @pl.when(moves_on)
-    def _():
-        for copy in lasts:
-            copy.start()
-        for copy in lasts:
-            copy.wait()
-
-    @pl.when(arrives)
-    def _():
         for copy in coming:
             copy.wait()
+
+    @pl.when(jnp.logical_not(arrives))
+    def _():
+        zero_ref[...] = jnp.zeros(zero_ref.shape, F32)
+        apply = row_copies(owner_ref, row_ref, last_a_ref, last_b_ref, zero_ref, out_ref, 0, sems, 3)
+        blank = [
+            pltpu.make_async_copy(zero_ref, out_ref.at[2, f], sems.at[3 + 2 * fields + f]) for f in range(fields)
+        ]
+        apply(lambda copy: copy.start())
+        for copy in blank:
+            copy.start()
+        for copy in blank:
+            copy.wait()
+        apply(lambda copy: copy.wait())
 
     last.wait()
 
@@ -800,41 +772,32 @@
 
     straight = jax.ShapeDtypeStruct((fields * depth + 16, LANES), BF16)
     diag = jax.ShapeDtypeStruct((depth + 32, LANES), BF16)
-    sources = (order_hbm, now_hbm, prev_hbm, coef_hbm)
-    y_out = call(
+    tiles = jax.ShapeDtypeStruct((fields, depth, LANES), F32)
+    y_out, edges, front, front_prev, front_coef = call(
         pack_region_body,
         "pack_region",
-        jax.ShapeDtypeStruct((5, depth, width), BF16),
+        (
+            jax.ShapeDtypeStruct((5, depth, width), BF16),
+            jax.ShapeDtypeStruct((depth, width), F32),
+            tiles,
+            tiles,
+            jax.ShapeDtypeStruct((2, 4, depth, LANES), BF16),
+        ),
         [HBM] * 4,
-        VMEM,
+        (VMEM,) * 5,
         [
-            pltpu.VMEM((depth, width), F32),
             pltpu.VMEM((blocks, fields, 8, width), F32),
             pltpu.VMEM((blocks, fields, 8, width), F32),
             pltpu.VMEM((4, 16, width), BF16),
             pltpu.SMEM(order.shape, jnp.int32),
-            pltpu.SemaphoreType.DMA((12,)),
+            pltpu.SemaphoreType.DMA((15,)),
         ],
-        sources,
+        (order_hbm, now_hbm, prev_hbm, coef_hbm),
     )
     left, dleft = call(
-        pack_back_body,
-        "pack_back",
-        (straight, diag),
-        [HBM] * 4,
-        (VMEM,) * 2,
-        [
-            pltpu.VMEM((1, fields, 8, LANES), F32),
-            pltpu.VMEM((1, fields, 8, LANES), F32),
-            pltpu.VMEM((4, 16, LANES), BF16),
-            pltpu.VMEM((fields, depth, LANES), F32),
-            pltpu.VMEM((fields, depth, LANES), F32),
-            pltpu.VMEM((2, 4, depth, LANES), BF16),
-            pltpu.SMEM(order.shape, jnp.int32),
-            pltpu.SemaphoreType.DMA((7,)),
-        ],
-        sources,
-    )
+        pack_back_body, "pack_back", (straight, diag), [VMEM] * 4, (VMEM,) * 2, [], (edges, front, front_prev, front_coef)
+    )
+
     swap = [(0, 1), (1, 0)]
     forward = [(i, (i + 1) % count) for i in range(count)]
     backward = [(i, (i - 1) % count) for i in range(count)]
@@ -853,7 +816,6 @@
         [],
         (now, prev),
     )
-    tiles = jax.ShapeDtypeStruct((fields, depth, LANES), F32)
     sums = jax.ShapeDtypeStruct((8, width), F32)
     tail = jax.ShapeDtypeStruct((8, LANES), F32)
     box1, side_lap, side_coef, side_rim = call(
@@ -921,7 +883,7 @@
         whole,
         [SMEM] + [VMEM] * 3,
         ANY,
-        [pltpu.VMEM((depth, width), F32), pltpu.SemaphoreType.DMA((3 * fields,))],
+        [pltpu.VMEM((depth, width), F32), pltpu.SemaphoreType.DMA((2 * fields,))],
         (new_owner, first, last_a, last_b),
     )
     arrived_half = pltpu.VMEM((half, depth, width), F32)
@@ -931,9 +893,9 @@
         whole,
         [ANY] * 2 + [VMEM] * 10 + [ANY],
         ANY,
-        [pltpu.VMEM((fields, depth, LANES), F32), arrived_half]
+        [pltpu.VMEM((fields, depth, LANES), F32), arrived_half, pltpu.VMEM((depth, width), F32)]
         + scalars
-        + [pltpu.SemaphoreType.DMA((3 + 2 * half + 2 * fields,))],
+        + [pltpu.SemaphoreType.DMA((3 + 3 * fields,))],
         (new_owner, order, now, coef, y_in, box0, drift, tail0, arrived_a, first, last_a, last_b, placed),
         input_output_aliases={12: 0},
     )

time: 25.3 us -> 24.7 us (0.976)
  Pallas kernels: 13.6 us -> 12.3 us
  waiting for transfers between devices: 2.18 us -> 2.61 us
  starting transfers between devices: 9.24 us -> 9.59 us
    pallas_call x11, Pallas kernels: 13.6 us -> 12.3 us  [call(): pl.pallas_call(body, out_shape=out_shape, in_specs=in_specs, out_specs=ou...]
    ppermute x1, starting transfers between devices: 1.47 us -> 1.86 us  [fast_on_device(): arrived_b = lax.ppermute(code_b, 'blk', forward)]
    ppermute x1, waiting for transfers between devices: 1.03 us -> 1.38 us  [fast_on_device(): from_dright = lax.ppermute(dleft, ('region', 'blk'), crossed)]
    ppermute x1, waiting for transfers between devices: 0.01 us -> 0.3 us  [fast_on_device(): y_in = lax.ppermute(y_out, 'region', swap)]
  transfers between devices with their start and end apart: 5 -> 5, of which waited for: 2 -> 3; matrix products, arithmetic and copies ran while one was open for 0% -> 0% of each run, Pallas kernels for 41% -> 36%
where the time goes in v8:
time: 24.7 us; the launch traced here: 24.6 us
  Pallas kernels  12.3 us (50%)
  starting transfers between devices  9.59 us (39%)
  waiting for transfers between devices  2.61 us (11%)
    pallas_call x11, Pallas kernels, call(): pl.pallas_call(body, out_shape=out_shape, in_specs=in_specs, out_specs=ou...  12.3 us
    ppermute x1, starting transfers between devices, fast_on_device(): from_right = lax.ppermute(left, 'blk', backward)  3.74 us
    ppermute x1, starting transfers between devices, fast_on_device(): y_in = lax.ppermute(y_out, 'region', swap)  3.03 us
    ppermute x1, starting transfers between devices, fast_on_device(): arrived_b = lax.ppermute(code_b, 'blk', forward)  1.86 us
    ppermute x1, waiting for transfers between devices, fast_on_device(): from_dright = lax.ppermute(dleft, ('region', 'blk'), crossed)  1.38 us
    ppermute x1, waiting for transfers between devices, fast_on_device(): arrived_a = lax.ppermute(code_a, 'blk', forward)  0.92 us
    ppermute x1, starting transfers between devices, fast_on_device(): from_dright = lax.ppermute(dleft, ('region', 'blk'), crossed)  0.9 us
  transfers between devices with their start and end apart: 5, of which 3 were waited for; matrix products, arithmetic and copies ran while one was open for 0% of the time, Pallas kernels for 36%

profile of v8, /device:TPU:0, one launch (start us, length us, event | category | flops | bytes accessed | tf_op | source)
XLA Modules:
  0.0 24.6 jit_solution(10830662950528929961)
XLA Ops:
  0.0 0.0 copy-start.2
  0.0 0.0 copy-start
  0.0 1.5 %pack_region.1 = (bf16[5,32,1024]{2,1,0:T(8,128)(2,1)S(1)}, f32[32,1024]{1,0:T(8,128)S(1)}, f32[4,32,128]{2,1,0:T(8,128)S(1)}, f32[4,32,128]{2,1,0:T(8,128)S(1)}, bf16[2,4,32,128]{3,2,1,0:T(8,128)(2,1)S(1)}) custom-call(s32[8]{0:T(128)} %bitcast.23, f32[2,4,32,1024]{3,2,1,0:T(8,128)} %bitcast.7, f32[2,4,32,1024]{3,2,1,0:T(8,128)} %bitcast.21, ...), custom_call_target="tpu_custom_call" | custom-call | tf_op jit(solution)/shard_map/pack_region/pallas_call | solution.py:762
  1.5 3.0 %collective-permute-start = (bf16[5,32,1024]{2,1,0:T(8,128)(2,1)S(1)}, bf16[5,32,1024]{2,1,0:T(8,128)(2,1)S(1)}, u32[]{:S(2)}, u32[]{:S(2)}) collective-permute-start(bf16[5,32,1024]{2,1,0:T(8,128)(2,1)S(1)} %get-tuple-element.31), channel_id=1, source_target_pairs={{0,16},{16,0},{1,17},{17,1},{2,18},{18,2},{3,19},{19,3},{4,20},{20... | collective-permute-start | bytes 983048 | tf_op jit(solution)/shard_map/ppermute | solution.py:805
  4.5 0.1 pack_back.1
  4.6 3.7 %collective-permute-start.1 = (bf16[144,128]{1,0:T(8,128)(2,1)S(1)}, bf16[144,128]{1,0:T(8,128)(2,1)S(1)}, u32[]{:S(2)}, u32[]{:S(2)}) collective-permute-start(bf16[144,128]{1,0:T(8,128)(2,1)S(1)} %get-tuple-element.36), channel_id=1, source_target_pairs={{0,15},{1,0},{2,1},{3,2},{4,3},{5,4},{6,5},{7,6},{8,7},{9,8},{10,9... | collective-permute-start | bytes 110600 | tf_op jit(solution)/shard_map/ppermute | solution.py:806
  8.3 0.0 copy-start.1
  8.3 0.0 copy-start.3
  8.3 0.0 copy-start.4
  8.4 0.9 %collective-permute-start.2 = (bf16[64,128]{1,0:T(8,128)(2,1)S(1)}, bf16[64,128]{1,0:T(8,128)(2,1)S(1)}, u32[]{:S(2)}, u32[]{:S(2)}) collective-permute-start(bf16[64,128]{1,0:T(8,128)(2,1)S(1)} %get-tuple-element.37), channel_id=1, source_target_pairs={{0,31},{1,16},{2,17},{3,18},{4,19},{5,20},{6,21},{7,22},{8,23},{9,... | collective-permute-start | bytes 49160 | tf_op jit(solution)/shard_map/ppermute | solution.py:807
  9.2 0.0 copy-done.2
  9.3 0.0 copy-done
  9.3 1.3 %local.1 = (f32[4,32,1024]{2,1,0:T(8,128)S(1)}, f32[4,32,1024]{2,1,0:T(8,128)S(1)}, f32[2,4,32,1024]{3,2,1,0:T(8,128)S(1)}, f32[2,8,1024]{2,1,0:T(8,128)S(1)}) custom-call(f32[2,4,32,1024]{3,2,1,0:T(8,128)S(1)} %bitcast.8, f32[2,4,32,1024]{3,2,1,0:T(8,128)S(1)} %bitcast.22), custom_call_target="tpu_custom_call" | custom-call | tf_op jit(solution)/shard_map/local/pallas_call | solution.py:762
  10.5 1.4 %collective-permute-done.2.diag_ref = bf16[64,128]{1,0:T(8,128)(2,1)S(1)} collective-permute-done((bf16[64,128]{1,0:T(8,128)(2,1)S(1)}, bf16[64,128]{1,0:T(8,128)(2,1)S(1)}, u32[]{:S(2)}, u32[]{:S(2)}) %collective-permute-start.2) | collective-permute-done | bytes 16416 | tf_op jit(solution)/shard_map/ppermute | solution.py:807
  11.9 0.0 collective-permute-done.1.straight_ref
  11.9 0.3 %border.1 = (f32[4,32,1024]{2,1,0:T(8,128)S(1)}, f32[4,32,128]{2,1,0:T(8,128)S(1)}, f32[4,32,128]{2,1,0:T(8,128)S(1)}, f32[2,8,128]{2,1,0:T(8,128)S(1)}) custom-call(f32[2,4,32,1024]{3,2,1,0:T(8,128)S(1)} %bitcast.9, bf16[144,128]{1,0:T(8,128)(2,1)S(1)} %collective-permute-done.1.straight_ref, ...), custom_call_target="tpu_custom_call", output_to_operand_aliasing={{0}: (3, {})} | custom-call | bytes 40000000 | tf_op jit(solution)/shard_map/border/pallas_call | solution.py:762
  12.3 0.3 %collective-permute-done.y_ref.refs_2_ = bf16[5,32,1024]{2,1,0:T(8,128)(2,1)S(1)} collective-permute-done((bf16[5,32,1024]{2,1,0:T(8,128)(2,1)S(1)}, bf16[5,32,1024]{2,1,0:T(8,128)(2,1)S(1)}, u32[]{:S(2)}, u32[]{:S(2)}) %collective-permute-start) | collective-permute-done | bytes 327712 | tf_op jit(solution)/shard_map/ppermute | solution.py:805
  12.6 0.0 copy-done.1
  12.6 0.0 copy-done.3
  12.6 0.0 copy-done.4
  12.6 1.2 %last_row.2 = (f32[4,32,1024]{2,1,0:T(8,128)S(1)}, f32[4,32,128]{2,1,0:T(8,128)S(1)}, f32[4,32,128]{2,1,0:T(8,128)S(1)}, f32[8,1024]{1,0:T(8,128)S(1)}, f32[2,32...) custom-call(s32[8]{0:T(128)S(1)} %bitcast.24, s32[2]{0:T(128)S(1)} %copy-done.4, ...), custom_call_target="tpu_custom_call", output_to_operand_aliasing={{0}: (13, {})} | custom-call | tf_op jit(solution)/shard_map/last_row/pallas_call | solution.py:762
  13.8 0.1 collective-permute-start.3
  13.8 1.2 %last_row.3 = (f32[2,32,1024]{2,1,0:T(8,128)S(1)}, s16[528,128]{1,0:T(8,128)(2,1)S(1)}) custom-call(s32[8]{0:T(128)S(1)} %bitcast.25, f32[2,4,32,1024]{3,2,1,0:T(8,128)S(1)} %bitcast.11, bf16[2,4,32,1024]{3,2,1,0:T(8,128)(2,1)S(1)} %bitcast.17, bf16[5,32,1024]{2,1,0:T(8,128)(2,1)S(1)} %collective-permute-done.y_ref.refs_2_, ...), custom_call_target="tpu_custom_call" | custom-call | tf_op jit(solution)/shard_map/last_row/pallas_call | solution.py:762
  15.0 1.9 %collective-permute-start.4 = (s16[528,128]{1,0:T(8,128)(2,1)S(1)}, s16[528,128]{1,0:T(8,128)(2,1)S(1)}, u32[]{:S(2)}, u32[]{:S(2)}) collective-permute-start(s16[528,128]{1,0:T(8,128)(2,1)S(1)} %get-tuple-element.51), channel_id=1, source_target_pairs={{0,1},{1,2},{2,3},{3,4},{4,5},{5,6},{6,7},{7,8},{8,9},{9,10},{10,1... | collective-permute-start | bytes 405512 | tf_op jit(solution)/shard_map/ppermute | solution.py:859
  16.9 0.4 %first_edges.1 = (f32[4,32,1024]{2,1,0:T(8,128)S(1)}, f32[8,1024]{1,0:T(8,128)S(1)}, f32[8,128]{1,0:T(8,128)S(1)}) custom-call(f32[2,4,32,1024]{3,2,1,0:T(8,128)S(1)} %bitcast.12, bf16[2,4,32,1024]{3,2,1,0:T(8,128)(2,1)S(1)} %bitcast.18, bf16[5,32,1024]{2,1,0:T(8,128)(2,1)S(1)} %collective-permute-done.y_ref.refs_2_, ...), custom_call_target="tpu_custom_call", output_to_operand_aliasing={{0}: (5, {})} | custom-call | tf_op jit(solution)/shard_map/first_edges/pallas_call | solution.py:762
  17.3 1.4 %first_row.1.row_ref = f32[4,32,1024]{2,1,0:T(8,128)S(1)} custom-call(s32[8]{0:T(128)S(1)} %bitcast.26, f32[2,4,32,1024]{3,2,1,0:T(8,128)S(1)} %bitcast.13, bf16[2,4,32,1024]{3,2,1,0:T(8,128)(2,1)S(1)} %bitcast.19, bf16[5,32,1024]{2,1,0:T(8,128)(2,1)S(1)} %collective-permute-done.y_ref.refs_2_, f32[4,32,1024]{2,1,0:T(8,128)S(1)} %get-tuple-element.52.box_ref, ...), custom_call_target="tpu_custom_call" | custom-call | tf_op jit(solution)/shard_map/first_row/pallas_call | solution.py:762
  18.7 1.5 %rows.1.partial_ref = f32[3,4,32,1024]{3,2,1,0:T(8,128)} custom-call(s32[2]{0:T(128)S(1)} %copy-done.4, f32[4,32,1024]{2,1,0:T(8,128)S(1)} %first_row.1.row_ref, f32[2,32,1024]{2,1,0:T(8,128)S(1)} %get-tuple-element.55.last_a_ref, f32[2,32,1024]{2,1,0:T(8,128)S(1)} %get-tuple-element.56.last_b_ref), custom_call_target="tpu_custom_call" | custom-call | tf_op jit(solution)/shard_map/rows/pallas_call | solution.py:762
  20.2 0.9 %collective-permute-done.3.code_ref.code_a_ref = s16[600,128]{1,0:T(8,128)(2,1)S(1)} collective-permute-done((s16[600,128]{1,0:T(8,128)(2,1)S(1)}, s16[600,128]{1,0:T(8,128)(2,1)S(1)}, u32[]{:S(2)}, u32[]{:S(2)}) %collective-permute-start.3) | collective-permute-done | bytes 153632 | tf_op jit(solution)/shard_map/ppermute | solution.py:849
  21.2 2.6 %finish.1.partial_ref = f32[3,4,32,1024]{3,2,1,0:T(8,128)} custom-call(s32[2]{0:T(128)S(1)} %copy-done.4, s32[8]{0:T(128)S(1)} %bitcast.27, f32[2,4,32,1024]{3,2,1,0:T(8,128)S(1)} %bitcast.14, bf16[2,4,32,1024]{3,2,1,0:T(8,128)(2,1)S(1)} %bitcast.20, bf16[5,32,1024]{2,1,0:T(8,128)(2,1)S(1)} %collective-permute-done.y_ref.refs_2_, ...), custom_call_target="tpu_custom_call", output_to_operand_aliasing={{}: (12, {})} | custom-call | tf_op jit(solution)/shard_map/finish/pallas_call | solution.py:762
  23.7 0.0 collective-permute-done.4.code_ref
  23.7 0.9 %place.1 = f32[3,4,32,1024]{3,2,1,0:T(8,128)} custom-call(s16[600,128]{1,0:T(8,128)(2,1)S(1)} %collective-permute-done.3.code_ref.code_a_ref, s16[528,128]{1,0:T(8,128)(2,1)S(1)} %collective-permute-done.4.code_ref, f32[3,4,32,1024]{3,2,1,0:T(8,128)} %finish.1.partial_ref), custom_call_target="tpu_custom_call", output_to_operand_aliasing={{}: (2, {})} | custom-call | tf_op jit(solution)/shard_map/place/pallas_call | solution.py:762
Async XLA Ops:
  0.0 9.3 %copy-start.2 = (f32[2,1,4,32,1024]{4,3,2,1,0:T(8,128)S(1)}, f32[2,1,4,32,1024]{4,3,2,1,0:T(8,128)}, u32[]{:S(2)}) copy-start(f32[2,1,4,32,1024]{4,3,2,1,0:T(8,128)} %param.6) | copy-start | bytes 3145732
  0.0 9.3 %copy-start = (f32[2,1,4,32,1024]{4,3,2,1,0:T(8,128)S(1)}, f32[2,1,4,32,1024]{4,3,2,1,0:T(8,128)}, u32[]{:S(2)}) copy-start(f32[2,1,4,32,1024]{4,3,2,1,0:T(8,128)} %param.5) | copy-start | bytes 3145732
  1.5 11.1 %collective-permute-start = (bf16[5,32,1024]{2,1,0:T(8,128)(2,1)S(1)}, bf16[5,32,1024]{2,1,0:T(8,128)(2,1)S(1)}, u32[]{:S(2)}, u32[]{:S(2)}) collective-permute-start(bf16[5,32,1024]{2,1,0:T(8,128)(2,1)S(1)} %get-tuple-element.31), channel_id=1, source_target_pairs={{0,16},{16,0},{1,17},{17,1},{2,18},{18,2},{3,19},{19,3},{4,20},{20... | collective-permute-start | bytes 983048 | tf_op jit(solution)/shard_map/ppermute | solution.py:805
  4.6 7.3 %collective-permute-start.1 = (bf16[144,128]{1,0:T(8,128)(2,1)S(1)}, bf16[144,128]{1,0:T(8,128)(2,1)S(1)}, u32[]{:S(2)}, u32[]{:S(2)}) collective-permute-start(bf16[144,128]{1,0:T(8,128)(2,1)S(1)} %get-tuple-element.36), channel_id=1, source_target_pairs={{0,15},{1,0},{2,1},{3,2},{4,3},{5,4},{6,5},{7,6},{8,7},{9,8},{10,9... | collective-permute-start | bytes 110600 | tf_op jit(solution)/shard_map/ppermute | solution.py:806
  8.3 4.2 %copy-start.1 = (bf16[1,1,2,4,32,1024]{5,4,3,2,1,0:T(8,128)(2,1)S(1)}, bf16[1,1,2,4,32,1024]{5,4,3,2,1,0:T(8,128)(2,1)}, u32[]{:S(2)}) copy-start(bf16[1,1,2,4,32,1024]{5,4,3,2,1,0:T(8,128)(2,1)} %param.7) | copy-start | bytes 1572868
  8.3 4.2 %copy-start.3 = (s32[1,1,8]{2,1,0:T(1,128)S(1)}, s32[1,1,8]{2,1,0:T(1,128)}, u32[]{:S(2)}) copy-start(s32[1,1,8]{2,1,0:T(1,128)} %param.8) | copy-start | bytes 100
  8.3 4.2 %copy-start.4 = (s32[2]{0:T(128)S(1)}, s32[2]{0:T(128)}, u32[]{:S(2)}) copy-start(s32[2]{0:T(128)} %owner_any.3) | copy-start | bytes 28
  8.4 3.6 %collective-permute-start.2 = (bf16[64,128]{1,0:T(8,128)(2,1)S(1)}, bf16[64,128]{1,0:T(8,128)(2,1)S(1)}, u32[]{:S(2)}, u32[]{:S(2)}) collective-permute-start(bf16[64,128]{1,0:T(8,128)(2,1)S(1)} %get-tuple-element.37), channel_id=1, source_target_pairs={{0,31},{1,16},{2,17},{3,18},{4,19},{5,20},{6,21},{7,22},{8,23},{9,... | collective-permute-start | bytes 49160 | tf_op jit(solution)/shard_map/ppermute | solution.py:807
  13.8 7.4 %collective-permute-start.3 = (s16[600,128]{1,0:T(8,128)(2,1)S(1)}, s16[600,128]{1,0:T(8,128)(2,1)S(1)}, u32[]{:S(2)}, u32[]{:S(2)}) collective-permute-start(s16[600,128]{1,0:T(8,128)(2,1)S(1)} %get-tuple-element.46), channel_id=1, source_target_pairs={{0,1},{1,2},{2,3},{3,4},{4,5},{5,6},{6,7},{7,8},{8,9},{9,10},{10,1... | collective-permute-start | bytes 460808 | tf_op jit(solution)/shard_map/ppermute | solution.py:849
  15.0 8.7 %collective-permute-start.4 = (s16[528,128]{1,0:T(8,128)(2,1)S(1)}, s16[528,128]{1,0:T(8,128)(2,1)S(1)}, u32[]{:S(2)}, u32[]{:S(2)}) collective-permute-start(s16[528,128]{1,0:T(8,128)(2,1)S(1)} %get-tuple-element.51), channel_id=1, source_target_pairs={{0,1},{1,2},{2,3},{3,4},{4,5},{5,6},{6,7},{7,8},{8,9},{9,10},{10,1... | collective-permute-start | bytes 405512 | tf_op jit(solution)/shard_map/ppermute | solution.py:859

commit v9 on v8

--- a/solution.py
+++ b/solution.py
@@ -213,24 +213,24 @@
     diag_ref[depth : depth + 32, :] = jnp.concatenate(rows + tag_rows + [blank] * 8, axis=0).astype(BF16)
 
 
-def nine_sum(tiles, lane, first=0):
+def lane_sum(tile, lane):
     inside = lane % 32
-    low = inside != 0
-    high = inside != 31
-    rows = []
-    for tile in tiles:
-        rows.append(
-            tile
-            + jnp.where(low, pltpu.roll(tile, 1, 1), 0.0)
-            + jnp.where(high, pltpu.roll(tile, LANES - 1, 1), 0.0)
-        )
+    return (
+        tile
+        + jnp.where(inside != 0, pltpu.roll(tile, 1, 1), 0.0)
+        + jnp.where(inside != 31, pltpu.roll(tile, LANES - 1, 1), 0.0)
+    )
+
+
+def nine_sum(tiles, lane):
+    rows = [lane_sum(tile, lane) for tile in tiles]
     up = [pltpu.roll(row, 32, 1) for row in rows]
     down = [pltpu.roll(row, LANES - 32, 1) for row in rows]
     count = len(tiles)
     result = []
     for t in range(count):
-        before = up[t] if t == 0 else jnp.where(lane < 32, up[t - 1], up[t])
-        after = down[t] if t == count - 1 else jnp.where(lane >= 96, down[t + 1], down[t])
+        before = jnp.where(lane < 32, up[t - 1] if t else 0.0, up[t])
+        after = jnp.where(lane >= 96, down[t + 1] if t < count - 1 else 0.0, down[t])
         result.append(rows[t] + before + after)
     return result
 
@@ -242,14 +242,27 @@
     return tile + jnp.where(row_id == 0, low_row, above) + jnp.where(row_id == depth - 1, high_row, below)
 
 
-def local_body(u_ref, p_ref, box0_ref, box1_ref, drift_ref, rim_ref):
+def local_body(u_hbm, p_hbm, u_ref, box0_ref, box1_ref, drift_ref, rim_ref, p_ref, sems):
     fields, depth, width = u_ref.shape[1:]
     main = width // LANES
+    copies = []
+    for f in range(fields):
+        copies.append(
+            (
+                pltpu.make_async_copy(u_hbm.at[:, f], u_ref.at[:, f], sems.at[2 * f]),
+                pltpu.make_async_copy(p_hbm.at[:, f], p_ref.at[:, f], sems.at[2 * f + 1]),
+            )
+        )
+    for pair in copies:
+        for copy in pair:
+            copy.start()
     lower = lax.axis_index("region") == 0
     lane = lane_ids()
     row_id = lax.broadcasted_iota(jnp.int32, (depth, 1), 0)
     boxes = (box0_ref, box1_ref)
     for f in range(fields):
+        for copy in copies[f]:
+            copy.wait()
         now = [u_ref[m, f, :, tile_at(t)] for m in range(2) for t in range(main)]
         sums = nine_sum(now, lane)
         for i, (tile, total) in enumerate(zip(now, sums)):
@@ -386,10 +399,8 @@
     return stepped[main]
 
 
-def first_edges_body(
-    u_ref, coef_ref, y_ref, box1_ref, rim_ref, box_in, box_ref, sums_ref, tail_ref
-):
-    fields, depth, width = u_ref.shape[1:]
+def first_edges_body(coef_ref, y_ref, rim_ref, box1_ref, box_in, box_ref, sums_ref, edge_c_ref):
+    fields, depth, width = box_in.shape
     main = width // LANES
     lane = lane_ids()
     column = ColumnEdge(coef_ref, y_ref)
@@ -418,8 +429,8 @@
     for t in range(main):
         sums_ref[0:4, tile_at(t)] = stepped_sum[t]
     sums_ref[4:8, :] = jnp.zeros((4, width), F32)
-    tail_ref[0:4, :] = stepped[1]
-    tail_ref[4:8, :] = jnp.zeros((4, LANES), F32)
+    edge_c_ref[0:4, :] = edge_c[0]
+    edge_c_ref[4:8, :] = jnp.zeros((4, LANES), F32)
 
 
 def load_map(map_any, map_ref, sem):
@@ -565,7 +576,7 @@
         code_ref[base : base + 8, :] = narrow(extra_ref[...])
 
 
-def first_row_body(map_ref, u_ref, coef_ref, y_ref, box_ref, box1_ref, drift_ref, sums_ref, row_ref):
+def first_row_body(map_ref, u_ref, coef_ref, y_ref, box_ref, box1_ref, drift_ref, sums_ref, row_ref, coef0_ref):
     fields, depth, width = u_ref.shape[1:]
     main = width // LANES
     lane = lane_ids()
@@ -579,7 +590,8 @@
         now = [drift_ref[0, f, :, tile_at(t)] + coefs[t] * box_ref[f, :, tile_at(t)] for t in range(main)]
         local = drift_ref[1, f, :, after] + pieces.piece(fields + f)(after) * box1_ref[f, :, after]
         sums = nine_sum(now + [local], lane)
-        for t in range(1, main):
+        coef0_ref[f] = coefs[0]
+        for t in range(main):
             lanes = tile_at(t)
             row = sums_ref[f : f + 1, lanes]
             row_ref[f, :, lanes] = second_step(now[t], u_ref[0, f, :, lanes], sums[t], coefs[t], row_id, row, lower)
@@ -655,62 +667,61 @@
 
 
 def finish_body(
-    owner_any, map_any, u_ref, coef_ref, y_ref, box_ref, drift_ref, tail_ref, code_ref, row_ref,
-    last_a_ref, last_b_ref, partial_ref, out_ref, tile_ref, arrived_ref, zero_ref, map_ref, owner_ref, sems
+    owner_any, coef_ref, edge_c_ref, code_ref, row_ref, last_a_ref, last_b_ref, partial_ref,
+    out_ref, tile_ref, arrived_ref, zero_ref, owner_ref, sems
 ):
-    fields, depth, width = u_ref.shape[1:]
+    fields, depth, width = row_ref.shape
     main = width // LANES
     half = arrived_ref.shape[0]
-    copies = [load_map(map_any, map_ref, sems.at[0]), load_map(owner_any, owner_ref, sems.at[1])]
     arrives = arrival(code_ref)
     lane = lane_ids()
     row_id = lax.broadcasted_iota(jnp.int32, (depth, 1), 0)
+    lower = lax.axis_index("region") == 0
+    first = lane < 32
     base = half * main * (depth + 1)
-    column = ColumnEdge(coef_ref, y_ref)
     extra = wide(code_ref[base + depth * fields // 2 : base + depth * fields // 2 + 8, :])
-    tile0, tile1 = tile_at(0), tile_at(1)
-    near = column.near(0, tile0)
-    before = []
+    tile0 = tile_at(0)
+
+    def beside(total, shift):
+        return jnp.where(first, pltpu.roll(total, shift, 1), 0.0)
+
+    def rows(row):
+        return jnp.where(lower, 0.0, row), jnp.where(lower, row, 0.0)
+
+    corners = []
+    for kind in range(3):
+        row = lane_sum(extra[3 + kind : 4 + kind] * scale_of(extra[2:3]), lane)
+        places = [pltpu.roll(row, LANES - 32 * f, 1) if f else row for f in range(fields)]
+        corners.append(jnp.where(first, jnp.concatenate(places, axis=0), 0.0))
+    planes = []
     for g in range(fields // 2):
         pair = wide(code_ref[base + g * depth : base + (g + 1) * depth, :]) * scale_of(extra[g : g + 1])
-        before += [pair, pltpu.roll(pair, 64, 1)]
-    corners = []
-    for kind in range(3):
-        row = extra[3 + kind : 4 + kind] * scale_of(extra[2:3])
-        shifts = [(96 - 32 * f) % LANES for f in range(fields)]
-        corners.append(jnp.concatenate([pltpu.roll(row, shift, 1) if shift else row for shift in shifts], axis=0))
-    near_sum = nine_sum([corners[0], near, column.near(0, tile1)], lane)[1]
-    beyond_sum = nine_sum([corners[1], column.beyond(0, tile0), column.beyond(0, tile1)], lane)[1]
-    for copy in copies:
-        copy.wait()
-    pieces = Pieces(map_ref, coef_ref, y_ref)
-    rims, stepped, nexts, coefs = [], [], [], []
+        total = lane_sum(pair, lane)
+        planes += [(beside(total, 32), beside(total, 64)), (beside(total, 96), total)]
+    planes = [(now, jnp.where(first, then, 0.0)) for now, then in planes]
+    own = [jnp.where(lower, now[depth - 1 : depth], now[0:1]) for now, _ in planes]
+    edge_change = edge_c_ref[0:4, :] * (corners[0] + corners[1] + jnp.concatenate(own, axis=0))
+    edge_sum = lane_sum(edge_change, lane)
+    edge_sum = edge_sum + corners[2] + pltpu.roll(edge_sum, 32, 1)
     for f in range(fields):
-        now = u_ref[0, f, :, tile0]
-        total = nine_sum([before[f], now, u_ref[0, f, :, tile1]], lane)[1]
-        rims.append(column.own(total))
-        low_row, high_row = column.rows(near_sum[f : f + 1])
-        lap = column_sum(total, row_id, low_row, high_row) - 27.0 * now
-        coef = pieces.piece(f)
-        coefs.append(coef(tile0))
-        stepped.append(drift_ref[0, f, :, tile0] + coefs[f] * lap)
-        nexts.append(drift_ref[0, f, :, tile1] + coef(tile1) * box_ref[f, :, tile1])
-    box = near_sum + beyond_sum + jnp.concatenate(rims, axis=0)
-    edge = column.ahead(0, tile0) + column.coefs(0, tile0) * (box - 27.0 * near)
-    edge_sum = nine_sum([corners[2], edge, tail_ref[0:4, :]], lane)[1]
-    for f in range(fields):
-        total = nine_sum([pltpu.roll(before[f], 32, 1), stepped[f], nexts[f]], lane)[1]
-        row = edge_sum[f : f + 1]
-        tile_ref[f] = second_step(stepped[f], u_ref[0, f, :, tile0], total, coefs[f], row_id, row, column.lower)
+        now, then = planes[f]
+        low_row, high_row = rows(corners[0][f : f + 1])
+        coef = coef_ref[f]
+        change = coef * column_sum(now, row_id, low_row, high_row)
+        total = lane_sum(change, lane)
+        total = total + then + pltpu.roll(total, 32, 1)
+        low_row, high_row = rows(edge_sum[f : f + 1])
+        lap = column_sum(total, row_id, low_row, high_row) - 27.0 * change
+        tile_ref[f] = row_ref[f, :, tile0] + 2.0 * change + coef * lap
 
     slot = jnp.where(arrives, 1, 0)
-    last = pltpu.make_async_copy(tile_ref, out_ref.at[slot, :, :, tile0], sems.at[2])
+    last = pltpu.make_async_copy(tile_ref, out_ref.at[slot, :, :, tile0], sems.at[0])
     last.start()
 
     @pl.when(arrives)
     def _():
         decode(code_ref, arrived_ref)
-        coming = code_copies(0, arrived_ref, out_ref, sems, 3)
+        coming = code_copies(0, arrived_ref, out_ref, sems, 1)
         for copy in coming:
             copy.start()
         for copy in coming:
@@ -718,10 +729,11 @@
 
     @pl.when(jnp.logical_not(arrives))
     def _():
+        load_map(owner_any, owner_ref, sems.at[1]).wait()
         zero_ref[...] = jnp.zeros(zero_ref.shape, F32)
-        apply = row_copies(owner_ref, row_ref, last_a_ref, last_b_ref, zero_ref, out_ref, 0, sems, 3)
+        apply = row_copies(owner_ref, row_ref, last_a_ref, last_b_ref, zero_ref, out_ref, 0, sems, 1)
         blank = [
-            pltpu.make_async_copy(zero_ref, out_ref.at[2, f], sems.at[3 + 2 * fields + f]) for f in range(fields)
+            pltpu.make_async_copy(zero_ref, out_ref.at[2, f], sems.at[1 + 2 * fields + f]) for f in range(fields)
         ]
         apply(lambda copy: copy.start())
         for copy in blank:
@@ -807,17 +819,18 @@
     from_dright = lax.ppermute(dleft, ("region", "blk"), crossed)
 
     row = jax.ShapeDtypeStruct((fields, depth, width), F32)
-    box0, box1, drift, rim = call(
+    both = jax.ShapeDtypeStruct(now.shape, F32)
+    now, box0, box1, drift, rim = call(
         local_body,
         "local",
-        (row, row, jax.ShapeDtypeStruct(now.shape, F32), jax.ShapeDtypeStruct((blocks, 8, width), F32)),
-        [VMEM] * 2,
-        (VMEM,) * 4,
-        [],
-        (now, prev),
+        (both, row, row, both, jax.ShapeDtypeStruct((blocks, 8, width), F32)),
+        [HBM] * 2,
+        (VMEM,) * 5,
+        [pltpu.VMEM(now.shape, F32), pltpu.SemaphoreType.DMA((2 * fields,))],
+        (now_hbm, prev_hbm),
     )
     sums = jax.ShapeDtypeStruct((8, width), F32)
-    tail = jax.ShapeDtypeStruct((8, LANES), F32)
+    edge = jax.ShapeDtypeStruct((8, LANES), F32)
     box1, side_lap, side_coef, side_rim = call(
         border_body,
         "border",
@@ -857,22 +870,22 @@
         (order, now, coef, y_in, box1, drift, lap1, side1, sums1),
     )
     arrived_b = lax.ppermute(code_b, "blk", forward)
-    box0, sums0, tail0 = call(
+    box0, sums0, edge_c0 = call(
         first_edges_body,
         "first_edges",
-        (row, sums, tail),
-        [VMEM] * 6,
+        (row, sums, edge),
+        [VMEM] * 3 + [ANY, VMEM],
         (VMEM,) * 3,
         [],
-        (now, coef, y_in, box1, rim, box0),
-        input_output_aliases={5: 0},
-    )
-    first = call(
+        (coef, y_in, rim, box1, box0),
+        input_output_aliases={4: 0},
+    )
+    first, coef0 = call(
         first_row_body,
         "first_row",
-        row,
+        (row, tiles),
         [SMEM] + [VMEM] * 7,
-        VMEM,
+        (VMEM,) * 2,
         [],
         (order, now, coef, y_in, box0, box1, drift, sums0),
     )
@@ -891,13 +904,17 @@
         finish_body,
         "finish",
         whole,
-        [ANY] * 2 + [VMEM] * 10 + [ANY],
+        [ANY] + [VMEM] * 6 + [ANY],
         ANY,
-        [pltpu.VMEM((fields, depth, LANES), F32), arrived_half, pltpu.VMEM((depth, width), F32)]
-        + scalars
-        + [pltpu.SemaphoreType.DMA((3 + 3 * fields,))],
-        (new_owner, order, now, coef, y_in, box0, drift, tail0, arrived_a, first, last_a, last_b, placed),
-        input_output_aliases={12: 0},
+        [
+            pltpu.VMEM((fields, depth, LANES), F32),
+            arrived_half,
+            pltpu.VMEM((depth, width), F32),
+            scalars[1],
+            pltpu.SemaphoreType.DMA((1 + 3 * fields,)),
+        ],
+        (new_owner, coef0, edge_c0, arrived_a, first, last_a, last_b, placed),
+        input_output_aliases={7: 0},
     )
     placed = call(
         functools.partial(place_body, half),

time: 24.7 us -> 23.6 us (0.955)
  waiting for transfers between devices: 2.61 us -> 1.36 us
    ppermute x1, waiting for transfers between devices: 1.38 us -> 0.01 us  [fast_on_device(): from_dright = lax.ppermute(dleft, ('region', 'blk'), crossed)]
  transfers between devices with their start and end apart: 5 -> 5, of which waited for: 3 -> 3; matrix products, arithmetic and copies ran while one was open for 0% -> 0% of each run, Pallas kernels for 36% -> 38%
where the time goes in v9:
time: 23.6 us; the launch traced here: 23.5 us
  Pallas kernels  12.4 us (53%)
  starting transfers between devices  9.59 us (41%)
  waiting for transfers between devices  1.36 us (6%)
    pallas_call x11, Pallas kernels, call(): pl.pallas_call(body, out_shape=out_shape, in_specs=in_specs, out_specs=ou...  12.4 us
    ppermute x1, starting transfers between devices, fast_on_device(): from_right = lax.ppermute(left, 'blk', backward)  3.74 us
    ppermute x1, starting transfers between devices, fast_on_device(): y_in = lax.ppermute(y_out, 'region', swap)  3.03 us
    ppermute x1, starting transfers between devices, fast_on_device(): arrived_b = lax.ppermute(code_b, 'blk', forward)  1.86 us
    ppermute x1, starting transfers between devices, fast_on_device(): from_dright = lax.ppermute(dleft, ('region', 'blk'), crossed)  0.9 us
    ppermute x1, waiting for transfers between devices, fast_on_device(): arrived_a = lax.ppermute(code_a, 'blk', forward)  0.87 us
  transfers between devices with their start and end apart: 5, of which 3 were waited for; matrix products, arithmetic and copies ran while one was open for 0% of the time, Pallas kernels for 38%

profile of v9, /device:TPU:0, one launch (start us, length us, event | category | flops | bytes accessed | tf_op | source)
XLA Modules:
  0.0 23.5 jit_solution(12016407173247864662)
XLA Ops:
  0.0 1.3 %pack_region.1 = (bf16[5,32,1024]{2,1,0:T(8,128)(2,1)S(1)}, f32[32,1024]{1,0:T(8,128)S(1)}, f32[4,32,128]{2,1,0:T(8,128)S(1)}, f32[4,32,128]{2,1,0:T(8,128)S(1)}, bf16[2,4,32,128]{3,2,1,0:T(8,128)(2,1)S(1)}) custom-call(s32[8]{0:T(128)} %bitcast.12, f32[2,4,32,1024]{3,2,1,0:T(8,128)} %bitcast.16, f32[2,4,32,1024]{3,2,1,0:T(8,128)} %bitcast.18, ...), custom_call_target="tpu_custom_call" | custom-call | tf_op jit(solution)/shard_map/pack_region/pallas_call | solution.py:774
  1.3 3.0 %collective-permute-start = (bf16[5,32,1024]{2,1,0:T(8,128)(2,1)S(1)}, bf16[5,32,1024]{2,1,0:T(8,128)(2,1)S(1)}, u32[]{:S(2)}, u32[]{:S(2)}) collective-permute-start(bf16[5,32,1024]{2,1,0:T(8,128)(2,1)S(1)} %get-tuple-element.35), channel_id=1, source_target_pairs={{0,16},{16,0},{1,17},{17,1},{2,18},{18,2},{3,19},{19,3},{4,20},{20... | collective-permute-start | bytes 983048 | tf_op jit(solution)/shard_map/ppermute | solution.py:817
  4.4 0.1 pack_back.1
  4.5 3.7 %collective-permute-start.1 = (bf16[144,128]{1,0:T(8,128)(2,1)S(1)}, bf16[144,128]{1,0:T(8,128)(2,1)S(1)}, u32[]{:S(2)}, u32[]{:S(2)}) collective-permute-start(bf16[144,128]{1,0:T(8,128)(2,1)S(1)} %get-tuple-element.40), channel_id=1, source_target_pairs={{0,15},{1,0},{2,1},{3,2},{4,3},{5,4},{6,5},{7,6},{8,7},{9,8},{10,9... | collective-permute-start | bytes 110600 | tf_op jit(solution)/shard_map/ppermute | solution.py:818
  8.2 0.0 copy-start
  8.2 0.0 copy-start.1
  8.2 0.0 copy-start.2
  8.2 0.9 %collective-permute-start.2 = (bf16[64,128]{1,0:T(8,128)(2,1)S(1)}, bf16[64,128]{1,0:T(8,128)(2,1)S(1)}, u32[]{:S(2)}, u32[]{:S(2)}) collective-permute-start(bf16[64,128]{1,0:T(8,128)(2,1)S(1)} %get-tuple-element.41), channel_id=1, source_target_pairs={{0,31},{1,16},{2,17},{3,18},{4,19},{5,20},{6,21},{7,22},{8,23},{9,... | collective-permute-start | bytes 49160 | tf_op jit(solution)/shard_map/ppermute | solution.py:819
  9.1 2.7 %local.1 = (f32[2,4,32,1024]{3,2,1,0:T(8,128)S(1)}, f32[4,32,1024]{2,1,0:T(8,128)S(1)}, f32[4,32,1024]{2,1,0:T(8,128)S(1)}, f32[2,4,32,1024]{3,2,1,0:T(8,128)S(1)}, f32[2,8,1024]{2,1,0:T(8,128)S(1)}) custom-call(f32[2,4,32,1024]{3,2,1,0:T(8,128)} %bitcast.17, f32[2,4,32,1024]{3,2,1,0:T(8,128)} %bitcast.19), custom_call_target="tpu_custom_call" | custom-call | tf_op jit(solution)/shard_map/local/pallas_call | solution.py:774
  11.8 0.0 collective-permute-done.2.diag_ref
  11.8 0.0 collective-permute-done.1.straight_ref
  11.8 0.3 %border.1 = (f32[4,32,1024]{2,1,0:T(8,128)S(1)}, f32[4,32,128]{2,1,0:T(8,128)S(1)}, f32[4,32,128]{2,1,0:T(8,128)S(1)}, f32[2,8,128]{2,1,0:T(8,128)S(1)}) custom-call(f32[2,4,32,1024]{3,2,1,0:T(8,128)S(1)} %get-tuple-element.34.u_ref.refs_0_, bf16[144,128]{1,0:T(8,128)(2,1)S(1)} %collective-permute-done.1.straight_ref, ...), custom_call_target="tpu_custom_call", output_to_operand_aliasing={{0}: (3, {})} | custom-call | bytes 40000000 | tf_op jit(solution)/shard_map/border/pallas_call | solution.py:774
  12.2 0.3 %collective-permute-done.y_ref.refs_2_ = bf16[5,32,1024]{2,1,0:T(8,128)(2,1)S(1)} collective-permute-done((bf16[5,32,1024]{2,1,0:T(8,128)(2,1)S(1)}, bf16[5,32,1024]{2,1,0:T(8,128)(2,1)S(1)}, u32[]{:S(2)}, u32[]{:S(2)}) %collective-permute-start) | collective-permute-done | bytes 327712 | tf_op jit(solution)/shard_map/ppermute | solution.py:817
  12.4 0.0 copy-done
  12.4 0.0 copy-done.1
  12.4 0.0 copy-done.2
  12.4 1.3 %last_row.2 = (f32[4,32,1024]{2,1,0:T(8,128)S(1)}, f32[4,32,128]{2,1,0:T(8,128)S(1)}, f32[4,32,128]{2,1,0:T(8,128)S(1)}, f32[8,1024]{1,0:T(8,128)S(1)}, f32[2,32...) custom-call(s32[8]{0:T(128)S(1)} %bitcast.13, s32[2]{0:T(128)S(1)} %copy-done.2, ...), custom_call_target="tpu_custom_call", output_to_operand_aliasing={{0}: (13, {})} | custom-call | tf_op jit(solution)/shard_map/last_row/pallas_call | solution.py:774
  13.8 0.1 collective-permute-start.3
  13.8 1.2 %last_row.3 = (f32[2,32,1024]{2,1,0:T(8,128)S(1)}, s16[528,128]{1,0:T(8,128)(2,1)S(1)}) custom-call(s32[8]{0:T(128)S(1)} %bitcast.14, f32[2,4,32,1024]{3,2,1,0:T(8,128)S(1)} %get-tuple-element.34.u_ref.refs_0_, bf16[2,4,32,1024]{3,2,1,0:T(8,128)(2,1)S(1)} %bitcast.9, bf16[5,32,1024]{2,1,0:T(8,128)(2,1)S(1)} %collective-permute-done.y_ref.refs_2_, ...), custom_call_target="tpu_custom_call" | custom-call | tf_op jit(solution)/shard_map/last_row/pallas_call | solution.py:774
  15.0 1.9 %collective-permute-start.4 = (s16[528,128]{1,0:T(8,128)(2,1)S(1)}, s16[528,128]{1,0:T(8,128)(2,1)S(1)}, u32[]{:S(2)}, u32[]{:S(2)}) collective-permute-start(s16[528,128]{1,0:T(8,128)(2,1)S(1)} %get-tuple-element.55), channel_id=1, source_target_pairs={{0,1},{1,2},{2,3},{3,4},{4,5},{5,6},{6,7},{7,8},{8,9},{9,10},{10,1... | collective-permute-start | bytes 405512 | tf_op jit(solution)/shard_map/ppermute | solution.py:872
  16.9 0.4 %first_edges.1 = (f32[4,32,1024]{2,1,0:T(8,128)S(1)}, f32[8,1024]{1,0:T(8,128)S(1)}, f32[8,128]{1,0:T(8,128)S(1)}) custom-call(bf16[2,4,32,1024]{3,2,1,0:T(8,128)(2,1)S(1)} %bitcast.10, bf16[5,32,1024]{2,1,0:T(8,128)(2,1)S(1)} %collective-permute-done.y_ref.refs_2_, f32[2,8,1024]{2,1,0:T(8,128)S(1)} %get-tuple-element.43.rim_ref, ...), custom_call_target="tpu_custom_call", output_to_operand_aliasing={{0}: (4, {})} | custom-call | tf_op jit(solution)/shard_map/first_edges/pallas_call | solution.py:774
  17.3 1.5 %first_row.1 = (f32[4,32,1024]{2,1,0:T(8,128)S(1)}, f32[4,32,128]{2,1,0:T(8,128)S(1)}) custom-call(s32[8]{0:T(128)S(1)} %bitcast.15, f32[2,4,32,1024]{3,2,1,0:T(8,128)S(1)} %get-tuple-element.34.u_ref.refs_0_, bf16[2,4,32,1024]{3,2,1,0:T(8,128)(2,1)S(1)} %bitcast.11, bf16[5,32,1024]{2,1,0:T(8,128)(2,1)S(1)} %collective-permute-done.y_ref.refs_2_, ...), custom_call_target="tpu_custom_call" | custom-call | tf_op jit(solution)/shard_map/first_row/pallas_call | solution.py:774
  18.7 1.5 %rows.1.partial_ref = f32[3,4,32,1024]{3,2,1,0:T(8,128)} custom-call(s32[2]{0:T(128)S(1)} %copy-done.2, f32[4,32,1024]{2,1,0:T(8,128)S(1)} %get-tuple-element.60.row_ref, f32[2,32,1024]{2,1,0:T(8,128)S(1)} %get-tuple-element.61.last_a_ref, f32[2,32,1024]{2,1,0:T(8,128)S(1)} %get-tuple-element.62.last_b_ref), custom_call_target="tpu_custom_call" | custom-call | tf_op jit(solution)/shard_map/rows/pallas_call | solution.py:774
  20.3 0.9 %collective-permute-done.3.code_ref.code_a_ref = s16[600,128]{1,0:T(8,128)(2,1)S(1)} collective-permute-done((s16[600,128]{1,0:T(8,128)(2,1)S(1)}, s16[600,128]{1,0:T(8,128)(2,1)S(1)}, u32[]{:S(2)}, u32[]{:S(2)}) %collective-permute-start.3) | collective-permute-done | bytes 153632 | tf_op jit(solution)/shard_map/ppermute | solution.py:862
  21.2 1.2 %finish.1.partial_ref = f32[3,4,32,1024]{3,2,1,0:T(8,128)} custom-call(s32[2]{0:T(128)S(1)} %copy-done.2, f32[4,32,128]{2,1,0:T(8,128)S(1)} %get-tuple-element.58.coef_ref, f32[8,128]{1,0:T(8,128)S(1)} %get-tuple-element.59.edge_c_ref, s16[600,128]{1,0:T(8,128)(2,1)S(1)} %collective-permute-done.3.code_ref.code_a_ref, ...), custom_call_target="tpu_custom_call", output_to_operand_aliasing={{}: (7, {})} | custom-call | tf_op jit(solution)/shard_map/finish/pallas_call | solution.py:774
  22.4 0.2 collective-permute-done.4.code_ref
  22.6 0.8 %place.1 = f32[3,4,32,1024]{3,2,1,0:T(8,128)} custom-call(s16[600,128]{1,0:T(8,128)(2,1)S(1)} %collective-permute-done.3.code_ref.code_a_ref, s16[528,128]{1,0:T(8,128)(2,1)S(1)} %collective-permute-done.4.code_ref, f32[3,4,32,1024]{3,2,1,0:T(8,128)} %finish.1.partial_ref), custom_call_target="tpu_custom_call", output_to_operand_aliasing={{}: (2, {})} | custom-call | tf_op jit(solution)/shard_map/place/pallas_call | solution.py:774
Async XLA Ops:
  1.3 11.1 %collective-permute-start = (bf16[5,32,1024]{2,1,0:T(8,128)(2,1)S(1)}, bf16[5,32,1024]{2,1,0:T(8,128)(2,1)S(1)}, u32[]{:S(2)}, u32[]{:S(2)}) collective-permute-start(bf16[5,32,1024]{2,1,0:T(8,128)(2,1)S(1)} %get-tuple-element.35), channel_id=1, source_target_pairs={{0,16},{16,0},{1,17},{17,1},{2,18},{18,2},{3,19},{19,3},{4,20},{20... | collective-permute-start | bytes 983048 | tf_op jit(solution)/shard_map/ppermute | solution.py:817
  4.5 7.3 %collective-permute-start.1 = (bf16[144,128]{1,0:T(8,128)(2,1)S(1)}, bf16[144,128]{1,0:T(8,128)(2,1)S(1)}, u32[]{:S(2)}, u32[]{:S(2)}) collective-permute-start(bf16[144,128]{1,0:T(8,128)(2,1)S(1)} %get-tuple-element.40), channel_id=1, source_target_pairs={{0,15},{1,0},{2,1},{3,2},{4,3},{5,4},{6,5},{7,6},{8,7},{9,8},{10,9... | collective-permute-start | bytes 110600 | tf_op jit(solution)/shard_map/ppermute | solution.py:818
  8.2 4.2 %copy-start = (bf16[1,1,2,4,32,1024]{5,4,3,2,1,0:T(8,128)(2,1)S(1)}, bf16[1,1,2,4,32,1024]{5,4,3,2,1,0:T(8,128)(2,1)}, u32[]{:S(2)}) copy-start(bf16[1,1,2,4,32,1024]{5,4,3,2,1,0:T(8,128)(2,1)} %param.7) | copy-start | bytes 1572868
  8.2 4.2 %copy-start.1 = (s32[1,1,8]{2,1,0:T(1,128)S(1)}, s32[1,1,8]{2,1,0:T(1,128)}, u32[]{:S(2)}) copy-start(s32[1,1,8]{2,1,0:T(1,128)} %param.8) | copy-start | bytes 100
  8.2 4.2 %copy-start.2 = (s32[2]{0:T(128)S(1)}, s32[2]{0:T(128)}, u32[]{:S(2)}) copy-start(s32[2]{0:T(128)} %owner_any.3) | copy-start | bytes 28
  8.2 3.6 %collective-permute-start.2 = (bf16[64,128]{1,0:T(8,128)(2,1)S(1)}, bf16[64,128]{1,0:T(8,128)(2,1)S(1)}, u32[]{:S(2)}, u32[]{:S(2)}) collective-permute-start(bf16[64,128]{1,0:T(8,128)(2,1)S(1)} %get-tuple-element.41), channel_id=1, source_target_pairs={{0,31},{1,16},{2,17},{3,18},{4,19},{5,20},{6,21},{7,22},{8,23},{9,... | collective-permute-start | bytes 49160 | tf_op jit(solution)/shard_map/ppermute | solution.py:819
  13.8 7.4 %collective-permute-start.3 = (s16[600,128]{1,0:T(8,128)(2,1)S(1)}, s16[600,128]{1,0:T(8,128)(2,1)S(1)}, u32[]{:S(2)}, u32[]{:S(2)}) collective-permute-start(s16[600,128]{1,0:T(8,128)(2,1)S(1)} %get-tuple-element.50), channel_id=1, source_target_pairs={{0,1},{1,2},{2,3},{3,4},{4,5},{5,6},{6,7},{7,8},{8,9},{9,10},{10,1... | collective-permute-start | bytes 460808 | tf_op jit(solution)/shard_map/ppermute | solution.py:862
  15.0 7.6 %collective-permute-start.4 = (s16[528,128]{1,0:T(8,128)(2,1)S(1)}, s16[528,128]{1,0:T(8,128)(2,1)S(1)}, u32[]{:S(2)}, u32[]{:S(2)}) collective-permute-start(s16[528,128]{1,0:T(8,128)(2,1)S(1)} %get-tuple-element.55), channel_id=1, source_target_pairs={{0,1},{1,2},{2,3},{3,4},{4,5},{5,6},{6,7},{7,8},{8,9},{9,10},{10,1... | collective-permute-start | bytes 405512 | tf_op jit(solution)/shard_map/ppermute | solution.py:872

commit v10 on v9

--- a/solution.py
+++ b/solution.py
@@ -134,7 +134,8 @@
 
 
 def pack_region_body(
-    map_hbm, u_ref, p_ref, coef_ref, y_ref, edges_ref, ua_ref, pa_ref, ca_ref, ue_ref, pe_ref, ce_ref, map_ref, sems
+    map_hbm, owner_hbm, u_ref, p_ref, coef_ref, y_ref, edges_ref, ua_ref, pa_ref, ca_ref, ue_ref, pe_ref, ce_ref,
+    map_ref, owner_ref, sems
 ):
     fields, depth, width = u_ref.shape[1:]
     region = lax.axis_index("region")
@@ -143,7 +144,7 @@
     half = depth // 2
     front = slice(0, LANES)
     edge8 = edge_start(lower, depth, 8)
-    edge16 = edge_start(lower, depth, 16)
+    pair = jnp.where(lower, depth - 2, 0)
     slab = []
     for s in range(4):
         for h in range(2):
@@ -151,9 +152,10 @@
             slab.append(pltpu.make_async_copy(coef_ref.at[other, s, part], y_ref.at[s, part], sems.at[7 + 2 * s + h]))
     copies = [
         pltpu.make_async_copy(map_hbm, map_ref, sems.at[0]),
-        pltpu.make_async_copy(u_ref.at[:, :, pl.ds(edge8, 8), :], ue_ref, sems.at[1]),
-        pltpu.make_async_copy(p_ref.at[:, :, pl.ds(edge8, 8), :], pe_ref, sems.at[2]),
-        pltpu.make_async_copy(coef_ref.at[region, :, pl.ds(edge16, 16), :], ce_ref, sems.at[3]),
+        pltpu.make_async_copy(owner_hbm, owner_ref, sems.at[15]),
+        pltpu.make_async_copy(u_ref.at[:, :, pl.ds(pair, 2), :], ue_ref, sems.at[1]),
+        pltpu.make_async_copy(p_ref.at[:, :, pl.ds(pair, 2), :], pe_ref, sems.at[2]),
+        pltpu.make_async_copy(coef_ref.at[region, :, pl.ds(edge8, 8), :], ce_ref, sems.at[3]),
     ]
     beside = [
         pltpu.make_async_copy(u_ref.at[0, :, :, front], ua_ref, sems.at[4]),
@@ -164,8 +166,8 @@
         copy.start()
     for copy in copies:
         copy.wait()
-    own_edge = jnp.where(lower, 7, 0)
-    own_next = jnp.where(lower, 6, 1)
+    own_edge = jnp.where(lower, 1, 0)
+    own_next = 1 - own_edge
     for m in range(2):
         for f in range(fields):
             at = m * fields + f
@@ -175,11 +177,12 @@
             edges_ref[16 + at : 17 + at, :] = 2.0 * near - pe_ref[m, f, pl.ds(own_edge, 1), :]
     for s in range(4):
         piece = ce_ref[s].astype(F32)
-        edges_ref[24 + s : 25 + s, :] = jnp.where(lower, piece[15:16], piece[0:1])
+        edges_ref[24 + s : 25 + s, :] = jnp.where(lower, piece[7:8], piece[0:1])
     numbers = [map_ref[region * 4 + s] for s in range(4)] + [map_ref[other * 4 + s] for s in range(4)]
     for i, number in enumerate(numbers):
         edges_ref[28:29, tile_at(i)] = jnp.zeros((1, LANES), F32) + number.astype(F32)
-    edges_ref[29:32, :] = jnp.zeros((3, width), F32)
+    edges_ref[29:30, :] = jnp.zeros((1, width), F32) + jnp.where(owner_ref[1] != lax.axis_index("blk"), 1.0, 0.0)
+    edges_ref[30:32, :] = jnp.zeros((2, width), F32)
     y_ref[4] = edges_ref[...].astype(BF16)
     for copy in slab + beside:
         copy.wait()
@@ -214,16 +217,25 @@
 
 
 def lane_sum(tile, lane):
-    inside = lane % 32
+    return sum_along_c(tile, *c_masks(lane))
+
+
+def c_masks(lane):
+    inside = lane & 31
+    return inside != 0, inside != 31
+
+
+def sum_along_c(tile, low, high):
     return (
         tile
-        + jnp.where(inside != 0, pltpu.roll(tile, 1, 1), 0.0)
-        + jnp.where(inside != 31, pltpu.roll(tile, LANES - 1, 1), 0.0)
+        + jnp.where(low, pltpu.roll(tile, 1, 1), 0.0)
+        + jnp.where(high, pltpu.roll(tile, LANES - 1, 1), 0.0)
     )
 
 
 def nine_sum(tiles, lane):
-    rows = [lane_sum(tile, lane) for tile in tiles]
+    low, high = c_masks(lane)
+    rows = [sum_along_c(tile, low, high) for tile in tiles]
     up = [pltpu.roll(row, 32, 1) for row in rows]
     down = [pltpu.roll(row, LANES - 32, 1) for row in rows]
     count = len(tiles)
@@ -242,7 +254,9 @@
     return tile + jnp.where(row_id == 0, low_row, above) + jnp.where(row_id == depth - 1, high_row, below)
 
 
-def local_body(u_hbm, p_hbm, u_ref, box0_ref, box1_ref, drift_ref, rim_ref, p_ref, sems):
+def local_body(
+    map_hbm, u_hbm, p_hbm, coef_ref, u_ref, box0_ref, box1_ref, drift_ref, rim_ref, held_ref, p_ref, map_ref, sems
+):
     fields, depth, width = u_ref.shape[1:]
     main = width // LANES
     copies = []
@@ -253,9 +267,15 @@
                 pltpu.make_async_copy(p_hbm.at[:, f], p_ref.at[:, f], sems.at[2 * f + 1]),
             )
         )
+    numbers = load_map(map_hbm, map_ref, sems.at[2 * fields])
     for pair in copies:
         for copy in pair:
             copy.start()
+    held_ref[...] = jnp.zeros(held_ref.shape, held_ref.dtype)
+    numbers.wait()
+    region = lax.axis_index("region")
+    for s in range(4):
+        held_ref[map_ref[region * 4 + s]] = coef_ref[region, s]
     lower = lax.axis_index("region") == 0
     lane = lane_ids()
     row_id = lax.broadcasted_iota(jnp.int32, (depth, 1), 0)
@@ -440,20 +460,18 @@
 
 
 class Pieces:
-    def __init__(self, map_ref, coef_ref, slab_ref):
-        self.coef, self.slab = coef_ref, slab_ref
-        self.region = lax.axis_index("region")
-        self.numbers = [map_ref[q] for q in range(8)]
+    def __init__(self, edges_ref, held_ref, slab_ref):
+        self.held, self.slab = held_ref, slab_ref
+        self.tags = [edges_ref[28:29, tile_at(4 + s)] for s in range(4)]
 
     def piece(self, number):
-        place = jnp.int32(0)
-        for q in range(8):
-            place = jnp.where(self.numbers[q] == number, q, place)
-        slot = place & 3
-        held = (place >> 2) == self.region
+        here = [tag == F32(number) for tag in self.tags]
 
         def tile(lanes):
-            return jnp.where(held, self.coef[self.region, slot, :, lanes], self.slab[slot, :, lanes]).astype(F32)
+            total = self.held[number, :, lanes].astype(F32)
+            for s, mask in enumerate(here):
+                total = jnp.where(mask, self.slab[s, :, lanes].astype(F32), total)
+            return total
 
         return tile
 
@@ -488,30 +506,23 @@
 
 
 def last_row_a_body(
-    map_any, owner_any, u_ref, coef_ref, y_ref, straight_ref, diag_ref, box0_ref, rim_ref, side_lap_ref, side_coef_ref,
-    side_rim_ref, drift_ref, box_in, box_ref, lap_ref, side_ref, sums_ref, row_ref, code_ref, power_ref, extra_ref,
-    map_ref, owner_ref, sems
+    edges_ref, u_ref, coef_ref, held_ref, y_ref, straight_ref, diag_ref, box0_ref, rim_ref, side_lap_ref, side_coef_ref,
+    side_rim_ref, drift_ref, box_in, box_ref, lap_ref, side_ref, sums_ref, row_ref, code_ref, power_ref, extra_ref
 ):
-    copies = [load_map(map_any, map_ref, sems.at[0]), load_map(owner_any, owner_ref, sems.at[1])]
     tail = last_edges(
         coef_ref, y_ref, straight_ref, diag_ref, box0_ref, rim_ref, side_lap_ref, side_coef_ref, side_rim_ref, box_in,
         box_ref, lap_ref, side_ref, sums_ref
     )
-    for copy in copies:
-        copy.wait()
-    more = (owner_ref, tail, extra_ref)
-    refs = (map_ref, u_ref, coef_ref, y_ref, box_ref, drift_ref, lap_ref, side_ref, sums_ref, row_ref, code_ref, power_ref)
-    last_row(0, *refs, more=more)
-
-
-def last_row_b_body(first, map_any, *refs):
-    map_ref, sem = refs[-2:]
-    load_map(map_any, map_ref, sem).wait()
-    last_row(first, map_ref, *refs[:-2])
+    refs = (edges_ref, u_ref, held_ref, y_ref, box_ref, drift_ref, lap_ref, side_ref, sums_ref, row_ref, code_ref, power_ref)
+    last_row(0, *refs, more=(tail, extra_ref))
+
+
+def last_row_b_body(first, *refs):
+    last_row(first, *refs)
 
 
 def last_row(
-    first, map_ref, u_ref, coef_ref, y_ref, box_ref, drift_ref, lap_ref, side_ref, sums_ref, row_ref, code_ref, power_ref,
+    first, edges_ref, u_ref, held_ref, y_ref, box_ref, drift_ref, lap_ref, side_ref, sums_ref, row_ref, code_ref, power_ref,
     more=None
 ):
     count, depth, width = row_ref.shape
@@ -519,8 +530,8 @@
     main = width // LANES
     lane = lane_ids()
     row_id = lax.broadcasted_iota(jnp.int32, (depth, 1), 0)
-    pieces = Pieces(map_ref, coef_ref, y_ref)
-    lower = pieces.region == 0
+    pieces = Pieces(edges_ref, held_ref, y_ref)
+    lower = lax.axis_index("region") == 0
     before = slice(width - LANES, width)
     last_tiles = []
     for f in range(first, first + count):
@@ -542,7 +553,7 @@
     base = count * main * depth
     code_ref[base : base + count * main, :] = narrow(power_ref[...])
     if more is not None:
-        owner_ref, tail, extra_ref = more
+        tail, extra_ref = more
         base += count * main
         both = []
         for f in range(fields):
@@ -570,19 +581,18 @@
         extra_ref[2:3, :] = power
         for i, kind in enumerate(kinds):
             extra_ref[3 + i : 4 + i, :] = coded(kind, power)
-        moves = jnp.where(owner_ref[1] != lax.axis_index("blk"), 1.0, 0.0)
-        extra_ref[6:7, :] = jnp.zeros((1, LANES), F32) + moves
+        extra_ref[6:7, :] = edges_ref[29:30, 0:LANES]
         extra_ref[7:8, :] = jnp.zeros((1, LANES), F32)
         code_ref[base : base + 8, :] = narrow(extra_ref[...])
 
 
-def first_row_body(map_ref, u_ref, coef_ref, y_ref, box_ref, box1_ref, drift_ref, sums_ref, row_ref, coef0_ref):
+def first_row_body(edges_ref, u_ref, held_ref, y_ref, box_ref, box1_ref, drift_ref, sums_ref, row_ref, coef0_ref):
     fields, depth, width = u_ref.shape[1:]
     main = width // LANES
     lane = lane_ids()
     row_id = lax.broadcasted_iota(jnp.int32, (depth, 1), 0)
-    pieces = Pieces(map_ref, coef_ref, y_ref)
-    lower = pieces.region == 0
+    pieces = Pieces(edges_ref, held_ref, y_ref)
+    lower = lax.axis_index("region") == 0
     after = slice(0, LANES)
     for f in range(fields):
         coef = pieces.piece(f)
@@ -599,7 +609,7 @@
 
 def arrival(code_ref):
     rows = code_ref.shape[0]
-    return jnp.max(wide(code_ref[rows - 8 : rows, :])[6:7]) > 0.5
+    return wide(code_ref[rows - 8 : rows, :])[6, 0] > 0.5
 
 
 def code_copies(first, row_ref, out_ref, sems, base):
@@ -765,8 +775,8 @@
     coef = coef_store[0, 0]
     count = lax.axis_size("blk")
     order = store_map.reshape(-1)
-    order_hbm, now_hbm, prev_hbm, coef_hbm = (
-        pltpu.with_memory_space_constraint(array, pltpu.HBM) for array in (order, now, prev, coef)
+    order_hbm, owner_hbm, now_hbm, prev_hbm, coef_hbm = (
+        pltpu.with_memory_space_constraint(array, pltpu.HBM) for array in (order, new_owner, now, prev, coef)
     )
     params = pltpu.CompilerParams(vmem_limit_bytes=48 * 1024 * 1024)
 
@@ -795,16 +805,17 @@
             tiles,
             jax.ShapeDtypeStruct((2, 4, depth, LANES), BF16),
         ),
-        [HBM] * 4,
+        [HBM] * 5,
         (VMEM,) * 5,
         [
-            pltpu.VMEM((blocks, fields, 8, width), F32),
-            pltpu.VMEM((blocks, fields, 8, width), F32),
-            pltpu.VMEM((4, 16, width), BF16),
+            pltpu.VMEM((blocks, fields, 2, width), F32),
+            pltpu.VMEM((blocks, fields, 2, width), F32),
+            pltpu.VMEM((4, 8, width), BF16),
             pltpu.SMEM(order.shape, jnp.int32),
-            pltpu.SemaphoreType.DMA((15,)),
+            pltpu.SMEM(new_owner.shape, jnp.int32),
+            pltpu.SemaphoreType.DMA((16,)),
         ],
-        (order_hbm, now_hbm, prev_hbm, coef_hbm),
+        (order_hbm, owner_hbm, now_hbm, prev_hbm, coef_hbm),
     )
     left, dleft = call(
         pack_back_body, "pack_back", (straight, diag), [VMEM] * 4, (VMEM,) * 2, [], (edges, front, front_prev, front_coef)
@@ -820,14 +831,25 @@
 
     row = jax.ShapeDtypeStruct((fields, depth, width), F32)
     both = jax.ShapeDtypeStruct(now.shape, F32)
-    now, box0, box1, drift, rim = call(
+    now, box0, box1, drift, rim, held = call(
         local_body,
         "local",
-        (both, row, row, both, jax.ShapeDtypeStruct((blocks, 8, width), F32)),
-        [HBM] * 2,
-        (VMEM,) * 5,
-        [pltpu.VMEM(now.shape, F32), pltpu.SemaphoreType.DMA((2 * fields,))],
-        (now_hbm, prev_hbm),
+        (
+            both,
+            row,
+            row,
+            both,
+            jax.ShapeDtypeStruct((blocks, 8, width), F32),
+            jax.ShapeDtypeStruct((blocks * fields, depth, width), BF16),
+        ),
+        [HBM] * 3 + [VMEM],
+        (VMEM,) * 6,
+        [
+            pltpu.VMEM(now.shape, F32),
+            pltpu.SMEM(order.shape, jnp.int32),
+            pltpu.SemaphoreType.DMA((2 * fields + 1,)),
+        ],
+        (order_hbm, now_hbm, prev_hbm, coef),
     )
     sums = jax.ShapeDtypeStruct((8, width), F32)
     edge = jax.ShapeDtypeStruct((8, LANES), F32)
@@ -847,16 +869,15 @@
     tiled = half * width // LANES
     codes = jax.ShapeDtypeStruct((tiled * (depth + 1), LANES), jnp.int16)
     more_codes = jax.ShapeDtypeStruct((tiled * (depth + 1) + half * depth + 8, LANES), jnp.int16)
-    scalars = [pltpu.SMEM(order.shape, jnp.int32), pltpu.SMEM(new_owner.shape, jnp.int32)]
     powers = pltpu.VMEM((tiled, LANES), F32)
     box1, lap1, side1, sums1, last_a, code_a = call(
         last_row_a_body,
         "last_row",
         (row, tiles, tiles, sums, part, more_codes),
-        [ANY] * 2 + [VMEM] * 12,
+        [VMEM] * 14,
         (VMEM,) * 6,
-        [powers, pltpu.VMEM((8, LANES), F32)] + scalars + [pltpu.SemaphoreType.DMA((2,))],
-        (order, new_owner, now, coef, y_in, from_right, from_dright, box0, rim, side_lap, side_coef, side_rim, drift, box1),
+        [powers, pltpu.VMEM((8, LANES), F32)],
+        (edges, now, coef, held, y_in, from_right, from_dright, box0, rim, side_lap, side_coef, side_rim, drift, box1),
         input_output_aliases={13: 0},
     )
     arrived_a = lax.ppermute(code_a, "blk", forward)
@@ -864,10 +885,10 @@
         functools.partial(last_row_b_body, half),
         "last_row",
         (part, codes),
-        [ANY] + [VMEM] * 8,
+        [VMEM] * 9,
         (VMEM,) * 2,
-        [powers, scalars[0], pltpu.SemaphoreType.DMA],
-        (order, now, coef, y_in, box1, drift, lap1, side1, sums1),
+        [powers],
+        (edges, now, held, y_in, box1, drift, lap1, side1, sums1),
     )
     arrived_b = lax.ppermute(code_b, "blk", forward)
     box0, sums0, edge_c0 = call(
@@ -884,10 +905,10 @@
         first_row_body,
         "first_row",
         (row, tiles),
-        [SMEM] + [VMEM] * 7,
+        [VMEM] * 8,
         (VMEM,) * 2,
         [],
-        (order, now, coef, y_in, box0, box1, drift, sums0),
+        (edges, now, held, y_in, box0, box1, drift, sums0),
     )
     whole = jax.ShapeDtypeStruct((blocks + 1, fields, depth, width), F32)
     placed = call(
@@ -910,7 +931,7 @@
             pltpu.VMEM((fields, depth, LANES), F32),
             arrived_half,
             pltpu.VMEM((depth, width), F32),
-            scalars[1],
+            pltpu.SMEM(new_owner.shape, jnp.int32),
             pltpu.SemaphoreType.DMA((1 + 3 * fields,)),
         ],
         (new_owner, coef0, edge_c0, arrived_a, first, last_a, last_b, placed),

time: 23.6 us -> 23.1 us (0.979)
  Pallas kernels: 12.4 us -> 10.7 us
  waiting for transfers between devices: 1.36 us -> 2.46 us
    pallas_call x11, Pallas kernels: 12.4 us -> 10.7 us  [call(): pl.pallas_call(body, out_shape=out_shape, in_specs=in_specs, out_specs=ou...]
    ppermute x1, waiting for transfers between devices: 0.87 us -> 2 us  [fast_on_device(): arrived_a = lax.ppermute(code_a, 'blk', forward)]
  transfers between devices with their start and end apart: 5 -> 5, of which waited for: 3 -> 3; matrix products, arithmetic and copies ran while one was open for 0% -> 0% of each run, Pallas kernels for 38% -> 34%
where the time goes in v10:
time: 23.1 us; the launch traced here: 22.9 us
  Pallas kernels  10.7 us (46%)
  starting transfers between devices  9.59 us (42%)
  waiting for transfers between devices  2.46 us (11%)
    pallas_call x11, Pallas kernels, call(): pl.pallas_call(body, out_shape=out_shape, in_specs=in_specs, out_specs=ou...  10.7 us
    ppermute x1, starting transfers between devices, fast_on_device(): from_right = lax.ppermute(left, 'blk', backward)  3.74 us
    ppermute x1, starting transfers between devices, fast_on_device(): y_in = lax.ppermute(y_out, 'region', swap)  3.03 us
    ppermute x1, waiting for transfers between devices, fast_on_device(): arrived_a = lax.ppermute(code_a, 'blk', forward)  2 us
    ppermute x1, starting transfers between devices, fast_on_device(): arrived_b = lax.ppermute(code_b, 'blk', forward)  1.86 us
    ppermute x1, starting transfers between devices, fast_on_device(): from_dright = lax.ppermute(dleft, ('region', 'blk'), crossed)  0.9 us
  transfers between devices with their start and end apart: 5, of which 3 were waited for; matrix products, arithmetic and copies ran while one was open for 0% of the time, Pallas kernels for 34%

profile of v10, /device:TPU:0, one launch (start us, length us, event | category | flops | bytes accessed | tf_op | source)
XLA Modules:
  0.0 22.9 jit_solution(5908358447100368973)
XLA Ops:
  0.0 0.0 copy-start
  0.0 1.3 %pack_region.1 = (bf16[5,32,1024]{2,1,0:T(8,128)(2,1)S(1)}, f32[32,1024]{1,0:T(8,128)S(1)}, f32[4,32,128]{2,1,0:T(8,128)S(1)}, f32[4,32,128]{2,1,0:T(8,128)S(1)}, bf16[2,4,32,128]{3,2,1,0:T(8,128)(2,1)S(1)}) custom-call(s32[8]{0:T(128)} %bitcast.15, s32[2]{0:T(128)} %owner_any.1, f32[2,4,32,1024]{3,2,1,0:T(8,128)} %bitcast.11, f32[2,4,32,1024]{3,2,1,0:T(8,128)} %bitcast.13, ...), custom_call_target="tpu_custom_call" | custom-call | tf_op jit(solution)/shard_map/pack_region/pallas_call | solution.py:784
  1.3 3.0 %collective-permute-start = (bf16[5,32,1024]{2,1,0:T(8,128)(2,1)S(1)}, bf16[5,32,1024]{2,1,0:T(8,128)(2,1)S(1)}, u32[]{:S(2)}, u32[]{:S(2)}) collective-permute-start(bf16[5,32,1024]{2,1,0:T(8,128)(2,1)S(1)} %get-tuple-element.38), channel_id=1, source_target_pairs={{0,16},{16,0},{1,17},{17,1},{2,18},{18,2},{3,19},{19,3},{4,20},{20... | collective-permute-start | bytes 983048 | tf_op jit(solution)/shard_map/ppermute | solution.py:828
  4.4 0.1 pack_back.1
  4.5 3.7 %collective-permute-start.1 = (bf16[144,128]{1,0:T(8,128)(2,1)S(1)}, bf16[144,128]{1,0:T(8,128)(2,1)S(1)}, u32[]{:S(2)}, u32[]{:S(2)}) collective-permute-start(bf16[144,128]{1,0:T(8,128)(2,1)S(1)} %get-tuple-element.42), channel_id=1, source_target_pairs={{0,15},{1,0},{2,1},{3,2},{4,3},{5,4},{6,5},{7,6},{8,7},{9,8},{10,9... | collective-permute-start | bytes 110600 | tf_op jit(solution)/shard_map/ppermute | solution.py:829
  8.2 0.9 %collective-permute-start.2 = (bf16[64,128]{1,0:T(8,128)(2,1)S(1)}, bf16[64,128]{1,0:T(8,128)(2,1)S(1)}, u32[]{:S(2)}, u32[]{:S(2)}) collective-permute-start(bf16[64,128]{1,0:T(8,128)(2,1)S(1)} %get-tuple-element.43), channel_id=1, source_target_pairs={{0,31},{1,16},{2,17},{3,18},{4,19},{5,20},{6,21},{7,22},{8,23},{9,... | collective-permute-start | bytes 49160 | tf_op jit(solution)/shard_map/ppermute | solution.py:830
  9.1 0.0 copy-done
  9.1 2.7 %local.1 = (f32[2,4,32,1024]{3,2,1,0:T(8,128)S(1)}, f32[4,32,1024]{2,1,0:T(8,128)S(1)}, f32[4,32,1024]{2,1,0:T(8,128)S(1)}, f32[2,4,32,1024]{3,2,1,0:T(8,128)S(1...) custom-call(s32[8]{0:T(128)} %bitcast.16, f32[2,4,32,1024]{3,2,1,0:T(8,128)} %bitcast.12, ...), custom_call_target="tpu_custom_call" | custom-call | tf_op jit(solution)/shard_map/local/pallas_call | solution.py:784
  11.8 0.0 collective-permute-done.2.diag_ref
  11.8 0.0 collective-permute-done.1.straight_ref
  11.8 0.3 %border.1 = (f32[4,32,1024]{2,1,0:T(8,128)S(1)}, f32[4,32,128]{2,1,0:T(8,128)S(1)}, f32[4,32,128]{2,1,0:T(8,128)S(1)}, f32[2,8,128]{2,1,0:T(8,128)S(1)}) custom-call(f32[2,4,32,1024]{3,2,1,0:T(8,128)S(1)} %get-tuple-element.36.u_ref.refs_1_, bf16[144,128]{1,0:T(8,128)(2,1)S(1)} %collective-permute-done.1.straight_ref, ...), custom_call_target="tpu_custom_call", output_to_operand_aliasing={{0}: (3, {})} | custom-call | bytes 40000000 | tf_op jit(solution)/shard_map/border/pallas_call | solution.py:784
  12.2 0.2 collective-permute-done.y_ref.refs_3_
  12.4 0.9 %last_row.2 = (f32[4,32,1024]{2,1,0:T(8,128)S(1)}, f32[4,32,128]{2,1,0:T(8,128)S(1)}, f32[4,32,128]{2,1,0:T(8,128)S(1)}, f32[8,1024]{1,0:T(8,128)S(1)}, f32[2,32...) custom-call(f32[32,1024]{1,0:T(8,128)S(1)} %get-tuple-element.35.edges_ref.refs_0_, ...), custom_call_target="tpu_custom_call", output_to_operand_aliasing={{0}: (13, {})} | custom-call | tf_op jit(solution)/shard_map/last_row/pallas_call | solution.py:784
  13.3 0.1 collective-permute-start.3
  13.4 0.6 %last_row.3 = (f32[2,32,1024]{2,1,0:T(8,128)S(1)}, s16[528,128]{1,0:T(8,128)(2,1)S(1)}) custom-call(f32[32,1024]{1,0:T(8,128)S(1)} %get-tuple-element.35.edges_ref.refs_0_, f32[2,4,32,1024]{3,2,1,0:T(8,128)S(1)} %get-tuple-element.36.u_ref.refs_1_, bf16[8,32,1024]{2,1,0:T(8,128)(2,1)S(1)} %get-tuple-element.37.held_ref.refs_2_, ...), custom_call_target="tpu_custom_call" | custom-call | tf_op jit(solution)/shard_map/last_row/pallas_call | solution.py:784
  14.0 1.9 %collective-permute-start.4 = (s16[528,128]{1,0:T(8,128)(2,1)S(1)}, s16[528,128]{1,0:T(8,128)(2,1)S(1)}, u32[]{:S(2)}, u32[]{:S(2)}) collective-permute-start(s16[528,128]{1,0:T(8,128)(2,1)S(1)} %get-tuple-element.57), channel_id=1, source_target_pairs={{0,1},{1,2},{2,3},{3,4},{4,5},{5,6},{6,7},{7,8},{8,9},{9,10},{10,1... | collective-permute-start | bytes 405512 | tf_op jit(solution)/shard_map/ppermute | solution.py:893
  15.8 0.4 %first_edges.1 = (f32[4,32,1024]{2,1,0:T(8,128)S(1)}, f32[8,1024]{1,0:T(8,128)S(1)}, f32[8,128]{1,0:T(8,128)S(1)}) custom-call(bf16[2,4,32,1024]{3,2,1,0:T(8,128)(2,1)S(1)} %bitcast.10, bf16[5,32,1024]{2,1,0:T(8,128)(2,1)S(1)} %collective-permute-done.y_ref.refs_3_, f32[2,8,1024]{2,1,0:T(8,128)S(1)} %get-tuple-element.45.rim_ref, ...), custom_call_target="tpu_custom_call", output_to_operand_aliasing={{0}: (4, {})} | custom-call | tf_op jit(solution)/shard_map/first_edges/pallas_call | solution.py:784
  16.2 0.0 copy-start.1
  16.2 0.9 %first_row.1 = (f32[4,32,1024]{2,1,0:T(8,128)S(1)}, f32[4,32,128]{2,1,0:T(8,128)S(1)}) custom-call(f32[32,1024]{1,0:T(8,128)S(1)} %get-tuple-element.35.edges_ref.refs_0_, f32[2,4,32,1024]{3,2,1,0:T(8,128)S(1)} %get-tuple-element.36.u_ref.refs_1_, bf16[8,32,1024]{2,1,0:T(8,128)(2,1)S(1)} %get-tuple-element.37.held_ref.refs_2_, ...), custom_call_target="tpu_custom_call" | custom-call | tf_op jit(solution)/shard_map/first_row/pallas_call | solution.py:784
  17.1 0.0 copy-done.1
  17.1 1.5 %rows.1.partial_ref = f32[3,4,32,1024]{3,2,1,0:T(8,128)} custom-call(s32[2]{0:T(128)S(1)} %copy-done.1, f32[4,32,1024]{2,1,0:T(8,128)S(1)} %get-tuple-element.62.row_ref, f32[2,32,1024]{2,1,0:T(8,128)S(1)} %get-tuple-element.63.last_a_ref, f32[2,32,1024]{2,1,0:T(8,128)S(1)} %get-tuple-element.64.last_b_ref), custom_call_target="tpu_custom_call" | custom-call | tf_op jit(solution)/shard_map/rows/pallas_call | solution.py:784
  18.7 2.0 %collective-permute-done.3.code_ref.code_a_ref = s16[600,128]{1,0:T(8,128)(2,1)S(1)} collective-permute-done((s16[600,128]{1,0:T(8,128)(2,1)S(1)}, s16[600,128]{1,0:T(8,128)(2,1)S(1)}, u32[]{:S(2)}, u32[]{:S(2)}) %collective-permute-start.3) | collective-permute-done | bytes 153632 | tf_op jit(solution)/shard_map/ppermute | solution.py:883
  20.7 1.2 %finish.1.partial_ref = f32[3,4,32,1024]{3,2,1,0:T(8,128)} custom-call(s32[2]{0:T(128)S(1)} %copy-done.1, f32[4,32,128]{2,1,0:T(8,128)S(1)} %get-tuple-element.60.coef_ref, f32[8,128]{1,0:T(8,128)S(1)} %get-tuple-element.61.edge_c_ref, s16[600,128]{1,0:T(8,128)(2,1)S(1)} %collective-permute-done.3.code_ref.code_a_ref, ...), custom_call_target="tpu_custom_call", output_to_operand_aliasing={{}: (7, {})} | custom-call | tf_op jit(solution)/shard_map/finish/pallas_call | solution.py:784
  21.9 0.2 %collective-permute-done.4.code_ref = s16[528,128]{1,0:T(8,128)(2,1)S(1)} collective-permute-done((s16[528,128]{1,0:T(8,128)(2,1)S(1)}, s16[528,128]{1,0:T(8,128)(2,1)S(1)}, u32[]{:S(2)}, u32[]{:S(2)}) %collective-permute-start.4) | collective-permute-done | bytes 135200 | tf_op jit(solution)/shard_map/ppermute | solution.py:893
  22.1 0.8 %place.1 = f32[3,4,32,1024]{3,2,1,0:T(8,128)} custom-call(s16[600,128]{1,0:T(8,128)(2,1)S(1)} %collective-permute-done.3.code_ref.code_a_ref, s16[528,128]{1,0:T(8,128)(2,1)S(1)} %collective-permute-done.4.code_ref, f32[3,4,32,1024]{3,2,1,0:T(8,128)} %finish.1.partial_ref), custom_call_target="tpu_custom_call", output_to_operand_aliasing={{}: (2, {})} | custom-call | tf_op jit(solution)/shard_map/place/pallas_call | solution.py:784
Async XLA Ops:
  0.0 9.1 %copy-start = (bf16[1,1,2,4,32,1024]{5,4,3,2,1,0:T(8,128)(2,1)S(1)}, bf16[1,1,2,4,32,1024]{5,4,3,2,1,0:T(8,128)(2,1)}, u32[]{:S(2)}) copy-start(bf16[1,1,2,4,32,1024]{5,4,3,2,1,0:T(8,128)(2,1)} %param.7) | copy-start | bytes 1572868
  1.3 11.1 %collective-permute-start = (bf16[5,32,1024]{2,1,0:T(8,128)(2,1)S(1)}, bf16[5,32,1024]{2,1,0:T(8,128)(2,1)S(1)}, u32[]{:S(2)}, u32[]{:S(2)}) collective-permute-start(bf16[5,32,1024]{2,1,0:T(8,128)(2,1)S(1)} %get-tuple-element.38), channel_id=1, source_target_pairs={{0,16},{16,0},{1,17},{17,1},{2,18},{18,2},{3,19},{19,3},{4,20},{20... | collective-permute-start | bytes 983048 | tf_op jit(solution)/shard_map/ppermute | solution.py:828
  4.5 7.4 %collective-permute-start.1 = (bf16[144,128]{1,0:T(8,128)(2,1)S(1)}, bf16[144,128]{1,0:T(8,128)(2,1)S(1)}, u32[]{:S(2)}, u32[]{:S(2)}) collective-permute-start(bf16[144,128]{1,0:T(8,128)(2,1)S(1)} %get-tuple-element.42), channel_id=1, source_target_pairs={{0,15},{1,0},{2,1},{3,2},{4,3},{5,4},{6,5},{7,6},{8,7},{9,8},{10,9... | collective-permute-start | bytes 110600 | tf_op jit(solution)/shard_map/ppermute | solution.py:829
  8.2 3.6 %collective-permute-start.2 = (bf16[64,128]{1,0:T(8,128)(2,1)S(1)}, bf16[64,128]{1,0:T(8,128)(2,1)S(1)}, u32[]{:S(2)}, u32[]{:S(2)}) collective-permute-start(bf16[64,128]{1,0:T(8,128)(2,1)S(1)} %get-tuple-element.43), channel_id=1, source_target_pairs={{0,31},{1,16},{2,17},{3,18},{4,19},{5,20},{6,21},{7,22},{8,23},{9,... | collective-permute-start | bytes 49160 | tf_op jit(solution)/shard_map/ppermute | solution.py:830
  13.3 7.4 %collective-permute-start.3 = (s16[600,128]{1,0:T(8,128)(2,1)S(1)}, s16[600,128]{1,0:T(8,128)(2,1)S(1)}, u32[]{:S(2)}, u32[]{:S(2)}) collective-permute-start(s16[600,128]{1,0:T(8,128)(2,1)S(1)} %get-tuple-element.52), channel_id=1, source_target_pairs={{0,1},{1,2},{2,3},{3,4},{4,5},{5,6},{6,7},{7,8},{8,9},{9,10},{10,1... | collective-permute-start | bytes 460808 | tf_op jit(solution)/shard_map/ppermute | solution.py:883
  14.0 8.2 %collective-permute-start.4 = (s16[528,128]{1,0:T(8,128)(2,1)S(1)}, s16[528,128]{1,0:T(8,128)(2,1)S(1)}, u32[]{:S(2)}, u32[]{:S(2)}) collective-permute-start(s16[528,128]{1,0:T(8,128)(2,1)S(1)} %get-tuple-element.57), channel_id=1, source_target_pairs={{0,1},{1,2},{2,3},{3,4},{4,5},{5,6},{6,7},{7,8},{8,9},{9,10},{10,1... | collective-permute-start | bytes 405512 | tf_op jit(solution)/shard_map/ppermute | solution.py:893
  16.2 0.9 %copy-start.1 = (s32[2]{0:T(128)S(1)}, s32[2]{0:T(128)}, u32[]{:S(2)}) copy-start(s32[2]{0:T(128)} %owner_any.1) | copy-start | bytes 28

commit v11 on v10

--- a/solution.py
+++ b/solution.py
@@ -141,20 +141,15 @@
     region = lax.axis_index("region")
     lower = region == 0
     other = 1 - region
-    half = depth // 2
     front = slice(0, LANES)
     edge8 = edge_start(lower, depth, 8)
     pair = jnp.where(lower, depth - 2, 0)
-    slab = []
-    for s in range(4):
-        for h in range(2):
-            part = slice(h * half, (h + 1) * half)
-            slab.append(pltpu.make_async_copy(coef_ref.at[other, s, part], y_ref.at[s, part], sems.at[7 + 2 * s + h]))
+    slab = [pltpu.make_async_copy(coef_ref.at[other], y_ref.at[0:4], sems.at[7])]
     copies = [
         pltpu.make_async_copy(map_hbm, map_ref, sems.at[0]),
-        pltpu.make_async_copy(owner_hbm, owner_ref, sems.at[15]),
+        pltpu.make_async_copy(owner_hbm, owner_ref, sems.at[8]),
         pltpu.make_async_copy(u_ref.at[:, :, pl.ds(pair, 2), :], ue_ref, sems.at[1]),
-        pltpu.make_async_copy(p_ref.at[:, :, pl.ds(pair, 2), :], pe_ref, sems.at[2]),
+        pltpu.make_async_copy(p_ref.at[:, :, pl.ds(jnp.where(lower, depth - 1, 0), 1), :], pe_ref, sems.at[2]),
         pltpu.make_async_copy(coef_ref.at[region, :, pl.ds(edge8, 8), :], ce_ref, sems.at[3]),
     ]
     beside = [
@@ -172,9 +167,10 @@
         for f in range(fields):
             at = m * fields + f
             near = ue_ref[m, f, pl.ds(own_edge, 1), :]
-            edges_ref[at : at + 1, :] = near
-            edges_ref[8 + at : 9 + at, :] = ue_ref[m, f, pl.ds(own_next, 1), :]
-            edges_ref[16 + at : 17 + at, :] = 2.0 * near - pe_ref[m, f, pl.ds(own_edge, 1), :]
+            pair_at = 8 * m + f
+            edges_ref[pair_at : pair_at + 1, :] = near
+            edges_ref[pair_at + 4 : pair_at + 5, :] = ue_ref[m, f, pl.ds(own_next, 1), :]
+            edges_ref[16 + at : 17 + at, :] = 2.0 * near - pe_ref[m, f]
     for s in range(4):
         piece = ce_ref[s].astype(F32)
         edges_ref[24 + s : 25 + s, :] = jnp.where(lower, piece[7:8], piece[0:1])
@@ -212,7 +208,7 @@
         moved = pltpu.roll(far[s], 32 * s, 1) if s else far[s]
         plane = jnp.where((lane >= 32 * s) & (lane < 32 * s + 32), moved, plane)
     diag_ref[0:depth, :] = plane.astype(BF16)
-    rows = [edges_ref[base : base + 4, 0:LANES] for base in (0, 8, 16, 24)]
+    rows = [edges_ref[base : base + 4, 0:LANES] for base in (0, 4, 16, 24)]
     diag_ref[depth : depth + 32, :] = jnp.concatenate(rows + tag_rows + [blank] * 8, axis=0).astype(BF16)
 
 
@@ -308,11 +304,8 @@
         self.tags = [self.extra[28:29, i * LANES : (i + 1) * LANES] for i in range(8)]
         self.field_id = lax.broadcasted_iota(jnp.int32, (4, LANES), 0).astype(F32)
 
-    def near(self, m, lanes):
-        return self.extra[4 * m : 4 * m + 4, lanes]
-
-    def beyond(self, m, lanes):
-        return self.extra[8 + 4 * m : 12 + 4 * m, lanes]
+    def pair(self, m, lanes):
+        return self.extra[8 * m : 8 * m + 8, lanes]
 
     def ahead(self, m, lanes):
         return self.extra[16 + 4 * m : 20 + 4 * m, lanes]
@@ -376,19 +369,20 @@
     extra_d = diag_ref[depth : depth + 32, :].astype(F32)
     tags_d = [extra_d[16 + i : 17 + i] for i in range(8)]
 
-    def edge_tiles(of, base):
-        return [of(0, before)] + [of(1, tile_at(t)) for t in range(main)] + [extra_d[base : base + 4]]
-
-    near = edge_tiles(column.near, 0)
-    beyond = edge_tiles(column.beyond, 4)
-    ahead = edge_tiles(column.ahead, 8)
+    def edge_tiles(of, remote):
+        return [of(0, before)] + [of(1, tile_at(t)) for t in range(main)] + [remote]
+
+    pairs = edge_tiles(column.pair, extra_d[0:8])
+    near = [pair[0:4] for pair in pairs]
+    ahead = edge_tiles(column.ahead, extra_d[8:12])
     corner = jnp.zeros((4, LANES), F32)
     for s in range(4):
         corner = corner + jnp.where(tags_d[s] == column.field_id, extra_d[12 + s : 13 + s], 0.0)
         corner = corner + jnp.where(tags_d[4 + s] == column.field_id, extra_s[s : s + 1], 0.0)
     edge_c = [column.coefs(0, before)] + [column.coefs(1, tile_at(t)) for t in range(main)] + [corner]
-    near_sum = nine_sum(near, lane)
-    beyond_sum = nine_sum(beyond, lane)
+    pair_sum = nine_sum(pairs, lane)
+    near_sum = [total[0:4] for total in pair_sum]
+    both_sum = [total[0:4] + total[4:8] for total in pair_sum]
     top = slice(0, 1)
     bottom = slice(depth - 1, depth)
     for f in range(fields):
@@ -410,13 +404,13 @@
     rims[main] = jnp.where(lane >= 96, side_rim_ref[0, 0:4, :], rims[main])
     stepped = []
     for t in range(main + 2):
-        box = near_sum[t] + beyond_sum[t] + rims[t]
+        box = both_sum[t] + rims[t]
         stepped.append(ahead[t] + edge_c[t] * (box - 27.0 * near[t]))
     stepped_sum = nine_sum(stepped, lane)
     for t in range(main):
         sums_ref[0:4, tile_at(t)] = stepped_sum[t + 1]
     sums_ref[4:8, :] = jnp.zeros((4, width), F32)
-    return stepped[main]
+    return stepped[main], stepped_sum[1 : main + 1]
 
 
 def first_edges_body(coef_ref, y_ref, rim_ref, box1_ref, box_in, box_ref, sums_ref, edge_c_ref):
@@ -429,9 +423,11 @@
     def edge_tiles(of):
         return [of(0, tile_at(t)) for t in range(main)] + [of(1, after)]
 
-    near = edge_tiles(column.near)
-    near_sum = nine_sum(near, lane)
-    beyond_sum = nine_sum(edge_tiles(column.beyond), lane)
+    pairs = edge_tiles(column.pair)
+    near = [pair[0:4] for pair in pairs]
+    pair_sum = nine_sum(pairs, lane)
+    near_sum = [total[0:4] for total in pair_sum]
+    both_sum = [total[0:4] + total[4:8] for total in pair_sum]
     ahead = edge_tiles(column.ahead)
     edge_c = edge_tiles(column.coefs)
     for f in range(fields):
@@ -443,7 +439,7 @@
     rims = [rim_ref[0, 0:4, tile_at(t)] for t in range(main)] + [rim_ref[1, 0:4, after]]
     stepped = []
     for t in range(main + 1):
-        box = near_sum[t] + beyond_sum[t] + rims[t]
+        box = both_sum[t] + rims[t]
         stepped.append(ahead[t] + edge_c[t] * (box - 27.0 * near[t]))
     stepped_sum = nine_sum(stepped, lane)
     for t in range(main):
@@ -509,12 +505,12 @@
     edges_ref, u_ref, coef_ref, held_ref, y_ref, straight_ref, diag_ref, box0_ref, rim_ref, side_lap_ref, side_coef_ref,
     side_rim_ref, drift_ref, box_in, box_ref, lap_ref, side_ref, sums_ref, row_ref, code_ref, power_ref, extra_ref
 ):
-    tail = last_edges(
+    tail, edge_sums = last_edges(
         coef_ref, y_ref, straight_ref, diag_ref, box0_ref, rim_ref, side_lap_ref, side_coef_ref, side_rim_ref, box_in,
         box_ref, lap_ref, side_ref, sums_ref
     )
     refs = (edges_ref, u_ref, held_ref, y_ref, box_ref, drift_ref, lap_ref, side_ref, sums_ref, row_ref, code_ref, power_ref)
-    last_row(0, *refs, more=(tail, extra_ref))
+    last_row(0, *refs, more=(tail, edge_sums, extra_ref))
 
 
 def last_row_b_body(first, *refs):
@@ -542,7 +538,7 @@
         sums = nine_sum([local] + middle + [side_ref[f]], lane)
         for t in range(main):
             lanes = tile_at(t)
-            row = sums_ref[f : f + 1, lanes]
+            row = sums_ref[f : f + 1, lanes] if more is None else more[1][t][f : f + 1]
             value = second_step(middle[t], u_ref[1, f, :, lanes], sums[t + 1], coefs[t], row_id, row, lower)
             row_ref[f - first, :, lanes] = value
             power = power_of(jnp.max(jnp.abs(value), axis=0, keepdims=True))
@@ -553,7 +549,7 @@
     base = count * main * depth
     code_ref[base : base + count * main, :] = narrow(power_ref[...])
     if more is not None:
-        tail, extra_ref = more
+        tail, _, extra_ref = more
         base += count * main
         both = []
         for f in range(fields):
@@ -570,7 +566,7 @@
             base += depth
         near = y_ref[4, 0:16, before].astype(F32)
         kinds = []
-        for rows in (near[4:8], near[12:16], tail):
+        for rows in (near[8:12], near[12:16], tail):
             kind = jnp.zeros((1, LANES), F32)
             for f in range(fields):
                 shift = (32 * f + 32) % LANES
@@ -613,15 +609,8 @@
 
 
 def code_copies(first, row_ref, out_ref, sems, base):
-    count, depth, _ = row_ref.shape
-    part = depth // 2
-    copies = []
-    for f in range(count):
-        for h in range(2):
-            rows = slice(h * part, (h + 1) * part)
-            sem = sems.at[base + 2 * f + h]
-            copies.append(pltpu.make_async_copy(row_ref.at[f, rows], out_ref.at[0, first + f, rows], sem))
-    return copies
+    count = row_ref.shape[0]
+    return [pltpu.make_async_copy(row_ref, out_ref.at[0, first : first + count], sems.at[base])]
 
 
 def decode(code_ref, row_ref):
@@ -635,12 +624,11 @@
             row_ref[f, :, tile_at(t)] = wide(code_ref[at * depth : (at + 1) * depth, :]) * scale[at : at + 1]
 
 
-def row_copies(owner_ref, row_ref, last_a_ref, last_b_ref, zero_ref, out_ref, at, sems, base):
+def row_copies(owner_ref, row_ref, last_refs, zero_ref, out_ref, at, sems, base):
     fields, _, width = row_ref.shape
-    half = last_a_ref.shape[0]
     keeps = owner_ref[1] == lax.axis_index("blk")
     rest = slice(LANES, width)
-    sources = [last_a_ref.at[f] for f in range(half)] + [last_b_ref.at[f] for f in range(half)]
+    sources = [ref.at[f] for ref in last_refs for f in range(ref.shape[0])]
 
     def copies(sources, at, base):
         return [pltpu.make_async_copy(source, out_ref.at[at, f], sems.at[base + f]) for f, source in enumerate(sources)]
@@ -669,26 +657,24 @@
     return apply
 
 
-def rows_body(owner_ref, row_ref, last_a_ref, last_b_ref, out_ref, zero_ref, sems):
+def rows_body(owner_ref, row_ref, *refs):
+    last_refs, (out_ref, zero_ref, sems) = refs[:-3], refs[-3:]
     zero_ref[...] = jnp.zeros(zero_ref.shape, F32)
-    apply = row_copies(owner_ref, row_ref, last_a_ref, last_b_ref, zero_ref, out_ref, 1, sems, 0)
+    apply = row_copies(owner_ref, row_ref, last_refs, zero_ref, out_ref, 1, sems, 0)
     apply(lambda copy: copy.start())
     apply(lambda copy: copy.wait())
 
 
-def finish_body(
-    owner_any, coef_ref, edge_c_ref, code_ref, row_ref, last_a_ref, last_b_ref, partial_ref,
-    out_ref, tile_ref, arrived_ref, zero_ref, owner_ref, sems
-):
+def finish_body(owner_any, coef_ref, edge_c_ref, code_ref, row_ref, *refs):
+    last_refs, (partial_ref, out_ref, tile_ref, arrived_ref, zero_ref, owner_ref, sems) = refs[:-7], refs[-7:]
     fields, depth, width = row_ref.shape
     main = width // LANES
-    half = arrived_ref.shape[0]
     arrives = arrival(code_ref)
     lane = lane_ids()
     row_id = lax.broadcasted_iota(jnp.int32, (depth, 1), 0)
     lower = lax.axis_index("region") == 0
     first = lane < 32
-    base = half * main * (depth + 1)
+    base = arrived_ref.shape[0] * main * (depth + 1)
     extra = wide(code_ref[base + depth * fields // 2 : base + depth * fields // 2 + 8, :])
     tile0 = tile_at(0)
 
@@ -741,7 +727,7 @@
     def _():
         load_map(owner_any, owner_ref, sems.at[1]).wait()
         zero_ref[...] = jnp.zeros(zero_ref.shape, F32)
-        apply = row_copies(owner_ref, row_ref, last_a_ref, last_b_ref, zero_ref, out_ref, 0, sems, 1)
+        apply = row_copies(owner_ref, row_ref, last_refs, zero_ref, out_ref, 0, sems, 1)
         blank = [
             pltpu.make_async_copy(zero_ref, out_ref.at[2, f], sems.at[1 + 2 * fields + f]) for f in range(fields)
         ]
@@ -809,11 +795,11 @@
         (VMEM,) * 5,
         [
             pltpu.VMEM((blocks, fields, 2, width), F32),
-            pltpu.VMEM((blocks, fields, 2, width), F32),
+            pltpu.VMEM((blocks, fields, 1, width), F32),
             pltpu.VMEM((4, 8, width), BF16),
             pltpu.SMEM(order.shape, jnp.int32),
             pltpu.SMEM(new_owner.shape, jnp.int32),
-            pltpu.SemaphoreType.DMA((16,)),
+            pltpu.SemaphoreType.DMA((9,)),
         ],
         (order_hbm, owner_hbm, now_hbm, prev_hbm, coef_hbm),
     )
@@ -864,33 +850,41 @@
         input_output_aliases={3: 0},
         cost_estimate=pl.CostEstimate(flops=0, transcendentals=0, bytes_accessed=40_000_000),
     )
-    half = fields // 2
-    part = jax.ShapeDtypeStruct((half, depth, width), F32)
-    tiled = half * width // LANES
-    codes = jax.ShapeDtypeStruct((tiled * (depth + 1), LANES), jnp.int16)
-    more_codes = jax.ShapeDtypeStruct((tiled * (depth + 1) + half * depth + 8, LANES), jnp.int16)
-    powers = pltpu.VMEM((tiled, LANES), F32)
-    box1, lap1, side1, sums1, last_a, code_a = call(
+    bounds = sorted({0, fields // 2, fields})
+    parts = [(first, end - first) for first, end in zip(bounds, bounds[1:])]
+
+    def part_shapes(size, more):
+        tiled = size * width // LANES
+        codes = tiled * (depth + 1) + more
+        shapes = (jax.ShapeDtypeStruct((size, depth, width), F32), jax.ShapeDtypeStruct((codes, LANES), jnp.int16))
+        return shapes, pltpu.VMEM((tiled, LANES), F32)
+
+    shapes, powers = part_shapes(parts[0][1], fields // 2 * depth + 8)
+    box1, lap1, side1, sums1, last, code = call(
         last_row_a_body,
         "last_row",
-        (row, tiles, tiles, sums, part, more_codes),
+        (row, tiles, tiles, sums) + shapes,
         [VMEM] * 14,
         (VMEM,) * 6,
         [powers, pltpu.VMEM((8, LANES), F32)],
         (edges, now, coef, held, y_in, from_right, from_dright, box0, rim, side_lap, side_coef, side_rim, drift, box1),
         input_output_aliases={13: 0},
     )
-    arrived_a = lax.ppermute(code_a, "blk", forward)
-    last_b, code_b = call(
-        functools.partial(last_row_b_body, half),
-        "last_row",
-        (part, codes),
-        [VMEM] * 9,
-        (VMEM,) * 2,
-        [powers],
-        (edges, now, held, y_in, box1, drift, lap1, side1, sums1),
-    )
-    arrived_b = lax.ppermute(code_b, "blk", forward)
+    lasts = [last]
+    arrived = [lax.ppermute(code, "blk", forward)]
+    for first, size in parts[1:]:
+        shapes, powers = part_shapes(size, 0)
+        last, code = call(
+            functools.partial(last_row_b_body, first),
+            "last_row",
+            shapes,
+            [VMEM] * 9,
+            (VMEM,) * 2,
+            [powers],
+            (edges, now, held, y_in, box1, drift, lap1, side1, sums1),
+        )
+        lasts.append(last)
+        arrived.append(lax.ppermute(code, "blk", forward))
     box0, sums0, edge_c0 = call(
         first_edges_body,
         "first_edges",
@@ -901,7 +895,7 @@
         (coef, y_in, rim, box1, box0),
         input_output_aliases={4: 0},
     )
-    first, coef0 = call(
+    first_row, coef0 = call(
         first_row_body,
         "first_row",
         (row, tiles),
@@ -915,38 +909,38 @@
         rows_body,
         "rows",
         whole,
-        [SMEM] + [VMEM] * 3,
+        [SMEM] + [VMEM] * (1 + len(lasts)),
         ANY,
         [pltpu.VMEM((depth, width), F32), pltpu.SemaphoreType.DMA((2 * fields,))],
-        (new_owner, first, last_a, last_b),
-    )
-    arrived_half = pltpu.VMEM((half, depth, width), F32)
+        (new_owner, first_row, *lasts),
+    )
     placed = call(
         finish_body,
         "finish",
         whole,
-        [ANY] + [VMEM] * 6 + [ANY],
+        [ANY] + [VMEM] * (4 + len(lasts)) + [ANY],
         ANY,
         [
             pltpu.VMEM((fields, depth, LANES), F32),
-            arrived_half,
+            pltpu.VMEM((parts[0][1], depth, width), F32),
             pltpu.VMEM((depth, width), F32),
             pltpu.SMEM(new_owner.shape, jnp.int32),
             pltpu.SemaphoreType.DMA((1 + 3 * fields,)),
         ],
-        (new_owner, coef0, edge_c0, arrived_a, first, last_a, last_b, placed),
-        input_output_aliases={7: 0},
-    )
-    placed = call(
-        functools.partial(place_body, half),
-        "place",
-        whole,
-        [VMEM, VMEM, ANY],
-        ANY,
-        [arrived_half, pltpu.SemaphoreType.DMA((2 * half,))],
-        (arrived_a, arrived_b, placed),
-        input_output_aliases={2: 0},
-    )
+        (new_owner, coef0, edge_c0, arrived[0], first_row, *lasts, placed),
+        input_output_aliases={5 + len(lasts): 0},
+    )
+    for (first, size), codes in zip(parts[1:], arrived[1:]):
+        placed = call(
+            functools.partial(place_body, first),
+            "place",
+            whole,
+            [VMEM, VMEM, ANY],
+            ANY,
+            [pltpu.VMEM((size, depth, width), F32), pltpu.SemaphoreType.DMA((2 * size,))],
+            (arrived[0], codes, placed),
+            input_output_aliases={2: 0},
+        )
     return placed[:, None]
 
 

time: 23.1 us -> 22.9 us (level)
  no operation moved by 1% of the time
where the time goes in v11:
time: 22.9 us; the launch traced here: 22.7 us
  Pallas kernels  10.5 us (46%)
  starting transfers between devices  9.59 us (42%)
  waiting for transfers between devices  2.47 us (11%)
    pallas_call x11, Pallas kernels, call(): pl.pallas_call(body, out_shape=out_shape, in_specs=in_specs, out_specs=ou...  10.5 us
    ppermute x1, starting transfers between devices, fast_on_device(): from_right = lax.ppermute(left, 'blk', backward)  3.74 us
    ppermute x1, starting transfers between devices, fast_on_device(): y_in = lax.ppermute(y_out, 'region', swap)  3.03 us
    ppermute x1, waiting for transfers between devices, fast_on_device(): arrived = [lax.ppermute(code, 'blk', forward)]  2.02 us
    ppermute x1, starting transfers between devices, fast_on_device(): arrived.append(lax.ppermute(code, 'blk', forward))  1.86 us
    ppermute x1, starting transfers between devices, fast_on_device(): from_dright = lax.ppermute(dleft, ('region', 'blk'), crossed)  0.9 us
  transfers between devices with their start and end apart: 5, of which 3 were waited for; matrix products, arithmetic and copies ran while one was open for 0% of the time, Pallas kernels for 34%

profile of v11, /device:TPU:0, one launch (start us, length us, event | category | flops | bytes accessed | tf_op | source)
XLA Modules:
  0.0 22.7 jit_solution(11354588819792555580)
XLA Ops:
  0.0 0.0 copy-start
  0.0 1.2 %pack_region.1 = (bf16[5,32,1024]{2,1,0:T(8,128)(2,1)S(1)}, f32[32,1024]{1,0:T(8,128)S(1)}, f32[4,32,128]{2,1,0:T(8,128)S(1)}, f32[4,32,128]{2,1,0:T(8,128)S(1)}, bf16[2,4,32,128]{3,2,1,0:T(8,128)(2,1)S(1)}) custom-call(s32[8]{0:T(128)} %bitcast.15, s32[2]{0:T(128)} %owner_any.1, f32[2,4,32,1024]{3,2,1,0:T(8,128)} %bitcast.11, f32[2,4,32,1024]{3,2,1,0:T(8,128)} %bitcast.13, ...), custom_call_target="tpu_custom_call" | custom-call | tf_op jit(solution)/shard_map/pack_region/pallas_call | solution.py:770
  1.2 3.0 %collective-permute-start = (bf16[5,32,1024]{2,1,0:T(8,128)(2,1)S(1)}, bf16[5,32,1024]{2,1,0:T(8,128)(2,1)S(1)}, u32[]{:S(2)}, u32[]{:S(2)}) collective-permute-start(bf16[5,32,1024]{2,1,0:T(8,128)(2,1)S(1)} %get-tuple-element.38), channel_id=1, source_target_pairs={{0,16},{16,0},{1,17},{17,1},{2,18},{18,2},{3,19},{19,3},{4,20},{20... | collective-permute-start | bytes 983048 | tf_op jit(solution)/shard_map/ppermute | solution.py:814
  4.2 0.1 pack_back.1
  4.3 3.7 %collective-permute-start.1 = (bf16[144,128]{1,0:T(8,128)(2,1)S(1)}, bf16[144,128]{1,0:T(8,128)(2,1)S(1)}, u32[]{:S(2)}, u32[]{:S(2)}) collective-permute-start(bf16[144,128]{1,0:T(8,128)(2,1)S(1)} %get-tuple-element.42), channel_id=1, source_target_pairs={{0,15},{1,0},{2,1},{3,2},{4,3},{5,4},{6,5},{7,6},{8,7},{9,8},{10,9... | collective-permute-start | bytes 110600 | tf_op jit(solution)/shard_map/ppermute | solution.py:815
  8.1 0.9 %collective-permute-start.2 = (bf16[64,128]{1,0:T(8,128)(2,1)S(1)}, bf16[64,128]{1,0:T(8,128)(2,1)S(1)}, u32[]{:S(2)}, u32[]{:S(2)}) collective-permute-start(bf16[64,128]{1,0:T(8,128)(2,1)S(1)} %get-tuple-element.43), channel_id=1, source_target_pairs={{0,31},{1,16},{2,17},{3,18},{4,19},{5,20},{6,21},{7,22},{8,23},{9,... | collective-permute-start | bytes 49160 | tf_op jit(solution)/shard_map/ppermute | solution.py:816
  9.0 0.0 copy-done
  9.0 2.7 %local.1 = (f32[2,4,32,1024]{3,2,1,0:T(8,128)S(1)}, f32[4,32,1024]{2,1,0:T(8,128)S(1)}, f32[4,32,1024]{2,1,0:T(8,128)S(1)}, f32[2,4,32,1024]{3,2,1,0:T(8,128)S(1...) custom-call(s32[8]{0:T(128)} %bitcast.16, f32[2,4,32,1024]{3,2,1,0:T(8,128)} %bitcast.12, ...), custom_call_target="tpu_custom_call" | custom-call | tf_op jit(solution)/shard_map/local/pallas_call | solution.py:770
  11.7 0.0 collective-permute-done.2.diag_ref
  11.7 0.0 collective-permute-done.1.straight_ref
  11.7 0.3 %border.1 = (f32[4,32,1024]{2,1,0:T(8,128)S(1)}, f32[4,32,128]{2,1,0:T(8,128)S(1)}, f32[4,32,128]{2,1,0:T(8,128)S(1)}, f32[2,8,128]{2,1,0:T(8,128)S(1)}) custom-call(f32[2,4,32,1024]{3,2,1,0:T(8,128)S(1)} %get-tuple-element.36.u_ref.refs_1_, bf16[144,128]{1,0:T(8,128)(2,1)S(1)} %collective-permute-done.1.straight_ref, ...), custom_call_target="tpu_custom_call", output_to_operand_aliasing={{0}: (3, {})} | custom-call | bytes 40000000 | tf_op jit(solution)/shard_map/border/pallas_call | solution.py:770
  12.1 0.2 collective-permute-done.y_ref.refs_3_
  12.3 0.8 %last_row.2 = (f32[4,32,1024]{2,1,0:T(8,128)S(1)}, f32[4,32,128]{2,1,0:T(8,128)S(1)}, f32[4,32,128]{2,1,0:T(8,128)S(1)}, f32[8,1024]{1,0:T(8,128)S(1)}, f32[2,32...) custom-call(f32[32,1024]{1,0:T(8,128)S(1)} %get-tuple-element.35.edges_ref.refs_0_, ...), custom_call_target="tpu_custom_call", output_to_operand_aliasing={{0}: (13, {})} | custom-call | tf_op jit(solution)/shard_map/last_row/pallas_call | solution.py:770
  13.1 0.1 collective-permute-start.3
  13.2 0.6 %last_row.3 = (f32[2,32,1024]{2,1,0:T(8,128)S(1)}, s16[528,128]{1,0:T(8,128)(2,1)S(1)}) custom-call(f32[32,1024]{1,0:T(8,128)S(1)} %get-tuple-element.35.edges_ref.refs_0_, f32[2,4,32,1024]{3,2,1,0:T(8,128)S(1)} %get-tuple-element.36.u_ref.refs_1_, bf16[8,32,1024]{2,1,0:T(8,128)(2,1)S(1)} %get-tuple-element.37.held_ref.refs_2_, ...), custom_call_target="tpu_custom_call" | custom-call | tf_op jit(solution)/shard_map/last_row/pallas_call | solution.py:770
  13.8 1.9 %collective-permute-start.4 = (s16[528,128]{1,0:T(8,128)(2,1)S(1)}, s16[528,128]{1,0:T(8,128)(2,1)S(1)}, u32[]{:S(2)}, u32[]{:S(2)}) collective-permute-start(s16[528,128]{1,0:T(8,128)(2,1)S(1)} %get-tuple-element.57), channel_id=1, source_target_pairs={{0,1},{1,2},{2,3},{3,4},{4,5},{5,6},{6,7},{7,8},{8,9},{9,10},{10,1... | collective-permute-start | bytes 405512 | tf_op jit(solution)/shard_map/ppermute | solution.py:887
  15.6 0.4 %first_edges.1 = (f32[4,32,1024]{2,1,0:T(8,128)S(1)}, f32[8,1024]{1,0:T(8,128)S(1)}, f32[8,128]{1,0:T(8,128)S(1)}) custom-call(bf16[2,4,32,1024]{3,2,1,0:T(8,128)(2,1)S(1)} %bitcast.10, bf16[5,32,1024]{2,1,0:T(8,128)(2,1)S(1)} %collective-permute-done.y_ref.refs_3_, f32[2,8,1024]{2,1,0:T(8,128)S(1)} %get-tuple-element.45.rim_ref, ...), custom_call_target="tpu_custom_call", output_to_operand_aliasing={{0}: (4, {})} | custom-call | tf_op jit(solution)/shard_map/first_edges/pallas_call | solution.py:770
  16.0 0.0 copy-start.1
  16.0 0.9 %first_row.1 = (f32[4,32,1024]{2,1,0:T(8,128)S(1)}, f32[4,32,128]{2,1,0:T(8,128)S(1)}) custom-call(f32[32,1024]{1,0:T(8,128)S(1)} %get-tuple-element.35.edges_ref.refs_0_, f32[2,4,32,1024]{3,2,1,0:T(8,128)S(1)} %get-tuple-element.36.u_ref.refs_1_, bf16[8,32,1024]{2,1,0:T(8,128)(2,1)S(1)} %get-tuple-element.37.held_ref.refs_2_, ...), custom_call_target="tpu_custom_call" | custom-call | tf_op jit(solution)/shard_map/first_row/pallas_call | solution.py:770
  16.9 0.0 copy-done.1
  16.9 1.5 %rows.1.refs_2_ = f32[3,4,32,1024]{3,2,1,0:T(8,128)} custom-call(s32[2]{0:T(128)S(1)} %copy-done.1, f32[4,32,1024]{2,1,0:T(8,128)S(1)} %get-tuple-element.62.row_ref, f32[2,32,1024]{2,1,0:T(8,128)S(1)} %get-tuple-element.63.refs_0_, f32[2,32,1024]{2,1,0:T(8,128)S(1)} %get-tuple-element.64.refs_1_), custom_call_target="tpu_custom_call" | custom-call | tf_op jit(solution)/shard_map/rows/pallas_call | solution.py:770
  18.5 2.0 %collective-permute-done.3.code_ref.code_a_ref = s16[600,128]{1,0:T(8,128)(2,1)S(1)} collective-permute-done((s16[600,128]{1,0:T(8,128)(2,1)S(1)}, s16[600,128]{1,0:T(8,128)(2,1)S(1)}, u32[]{:S(2)}, u32[]{:S(2)}) %collective-permute-start.3) | collective-permute-done | bytes 153632 | tf_op jit(solution)/shard_map/ppermute | solution.py:874
  20.5 1.2 %finish.1.partial_ref = f32[3,4,32,1024]{3,2,1,0:T(8,128)} custom-call(s32[2]{0:T(128)S(1)} %copy-done.1, f32[4,32,128]{2,1,0:T(8,128)S(1)} %get-tuple-element.60.coef_ref, f32[8,128]{1,0:T(8,128)S(1)} %get-tuple-element.61.edge_c_ref, s16[600,128]{1,0:T(8,128)(2,1)S(1)} %collective-permute-done.3.code_ref.code_a_ref, ...), custom_call_target="tpu_custom_call", output_to_operand_aliasing={{}: (7, {})} | custom-call | tf_op jit(solution)/shard_map/finish/pallas_call | solution.py:770
  21.7 0.2 collective-permute-done.4.code_ref
  22.0 0.8 %place.1 = f32[3,4,32,1024]{3,2,1,0:T(8,128)} custom-call(s16[600,128]{1,0:T(8,128)(2,1)S(1)} %collective-permute-done.3.code_ref.code_a_ref, s16[528,128]{1,0:T(8,128)(2,1)S(1)} %collective-permute-done.4.code_ref, f32[3,4,32,1024]{3,2,1,0:T(8,128)} %finish.1.partial_ref), custom_call_target="tpu_custom_call", output_to_operand_aliasing={{}: (2, {})} | custom-call | tf_op jit(solution)/shard_map/place/pallas_call | solution.py:770
Async XLA Ops:
  0.0 9.0 %copy-start = (bf16[1,1,2,4,32,1024]{5,4,3,2,1,0:T(8,128)(2,1)S(1)}, bf16[1,1,2,4,32,1024]{5,4,3,2,1,0:T(8,128)(2,1)}, u32[]{:S(2)}) copy-start(bf16[1,1,2,4,32,1024]{5,4,3,2,1,0:T(8,128)(2,1)} %param.7) | copy-start | bytes 1572868
  1.2 11.1 %collective-permute-start = (bf16[5,32,1024]{2,1,0:T(8,128)(2,1)S(1)}, bf16[5,32,1024]{2,1,0:T(8,128)(2,1)S(1)}, u32[]{:S(2)}, u32[]{:S(2)}) collective-permute-start(bf16[5,32,1024]{2,1,0:T(8,128)(2,1)S(1)} %get-tuple-element.38), channel_id=1, source_target_pairs={{0,16},{16,0},{1,17},{17,1},{2,18},{18,2},{3,19},{19,3},{4,20},{20... | collective-permute-start | bytes 983048 | tf_op jit(solution)/shard_map/ppermute | solution.py:814
  4.3 7.4 %collective-permute-start.1 = (bf16[144,128]{1,0:T(8,128)(2,1)S(1)}, bf16[144,128]{1,0:T(8,128)(2,1)S(1)}, u32[]{:S(2)}, u32[]{:S(2)}) collective-permute-start(bf16[144,128]{1,0:T(8,128)(2,1)S(1)} %get-tuple-element.42), channel_id=1, source_target_pairs={{0,15},{1,0},{2,1},{3,2},{4,3},{5,4},{6,5},{7,6},{8,7},{9,8},{10,9... | collective-permute-start | bytes 110600 | tf_op jit(solution)/shard_map/ppermute | solution.py:815
  8.1 3.6 %collective-permute-start.2 = (bf16[64,128]{1,0:T(8,128)(2,1)S(1)}, bf16[64,128]{1,0:T(8,128)(2,1)S(1)}, u32[]{:S(2)}, u32[]{:S(2)}) collective-permute-start(bf16[64,128]{1,0:T(8,128)(2,1)S(1)} %get-tuple-element.43), channel_id=1, source_target_pairs={{0,31},{1,16},{2,17},{3,18},{4,19},{5,20},{6,21},{7,22},{8,23},{9,... | collective-permute-start | bytes 49160 | tf_op jit(solution)/shard_map/ppermute | solution.py:816
  13.1 7.4 %collective-permute-start.3 = (s16[600,128]{1,0:T(8,128)(2,1)S(1)}, s16[600,128]{1,0:T(8,128)(2,1)S(1)}, u32[]{:S(2)}, u32[]{:S(2)}) collective-permute-start(s16[600,128]{1,0:T(8,128)(2,1)S(1)} %get-tuple-element.52), channel_id=1, source_target_pairs={{0,1},{1,2},{2,3},{3,4},{4,5},{5,6},{6,7},{7,8},{8,9},{9,10},{10,1... | collective-permute-start | bytes 460808 | tf_op jit(solution)/shard_map/ppermute | solution.py:874
  13.8 8.2 %collective-permute-start.4 = (s16[528,128]{1,0:T(8,128)(2,1)S(1)}, s16[528,128]{1,0:T(8,128)(2,1)S(1)}, u32[]{:S(2)}, u32[]{:S(2)}) collective-permute-start(s16[528,128]{1,0:T(8,128)(2,1)S(1)} %get-tuple-element.57), channel_id=1, source_target_pairs={{0,1},{1,2},{2,3},{3,4},{4,5},{5,6},{6,7},{7,8},{8,9},{9,10},{10,1... | collective-permute-start | bytes 405512 | tf_op jit(solution)/shard_map/ppermute | solution.py:887
  16.0 0.9 %copy-start.1 = (s32[2]{0:T(128)S(1)}, s32[2]{0:T(128)}, u32[]{:S(2)}) copy-start(s32[2]{0:T(128)} %owner_any.1) | copy-start | bytes 28

commit v12 on v11

--- a/solution.py
+++ b/solution.py
@@ -134,8 +134,8 @@
 
 
 def pack_region_body(
-    map_hbm, owner_hbm, u_ref, p_ref, coef_ref, y_ref, edges_ref, ua_ref, pa_ref, ca_ref, ue_ref, pe_ref, ce_ref,
-    map_ref, owner_ref, sems
+    map_hbm, u_ref, p_ref, coef_ref, y_ref, edges_ref, ua_ref, pa_ref, ca_ref, ue_ref, pe_ref, ce_ref,
+    map_ref, sems
 ):
     fields, depth, width = u_ref.shape[1:]
     region = lax.axis_index("region")
@@ -147,7 +147,6 @@
     slab = [pltpu.make_async_copy(coef_ref.at[other], y_ref.at[0:4], sems.at[7])]
     copies = [
         pltpu.make_async_copy(map_hbm, map_ref, sems.at[0]),
-        pltpu.make_async_copy(owner_hbm, owner_ref, sems.at[8]),
         pltpu.make_async_copy(u_ref.at[:, :, pl.ds(pair, 2), :], ue_ref, sems.at[1]),
         pltpu.make_async_copy(p_ref.at[:, :, pl.ds(jnp.where(lower, depth - 1, 0), 1), :], pe_ref, sems.at[2]),
         pltpu.make_async_copy(coef_ref.at[region, :, pl.ds(edge8, 8), :], ce_ref, sems.at[3]),
@@ -177,8 +176,7 @@
     numbers = [map_ref[region * 4 + s] for s in range(4)] + [map_ref[other * 4 + s] for s in range(4)]
     for i, number in enumerate(numbers):
         edges_ref[28:29, tile_at(i)] = jnp.zeros((1, LANES), F32) + number.astype(F32)
-    edges_ref[29:30, :] = jnp.zeros((1, width), F32) + jnp.where(owner_ref[1] != lax.axis_index("blk"), 1.0, 0.0)
-    edges_ref[30:32, :] = jnp.zeros((2, width), F32)
+    edges_ref[29:32, :] = jnp.zeros((3, width), F32)
     y_ref[4] = edges_ref[...].astype(BF16)
     for copy in slab + beside:
         copy.wait()
@@ -209,7 +207,7 @@
         plane = jnp.where((lane >= 32 * s) & (lane < 32 * s + 32), moved, plane)
     diag_ref[0:depth, :] = plane.astype(BF16)
     rows = [edges_ref[base : base + 4, 0:LANES] for base in (0, 4, 16, 24)]
-    diag_ref[depth : depth + 32, :] = jnp.concatenate(rows + tag_rows + [blank] * 8, axis=0).astype(BF16)
+    diag_ref[depth : depth + 24, :] = jnp.concatenate(rows + tag_rows, axis=0).astype(BF16)
 
 
 def lane_sum(tile, lane):
@@ -251,7 +249,8 @@
 
 
 def local_body(
-    map_hbm, u_hbm, p_hbm, coef_ref, u_ref, box0_ref, box1_ref, drift_ref, rim_ref, held_ref, p_ref, map_ref, sems
+    map_hbm, owner_hbm, u_hbm, p_hbm, coef_ref, u_ref, box0_ref, box1_ref, drift_ref, rim_ref, held_ref, p_ref,
+    map_ref, owner_ref, sems
 ):
     fields, depth, width = u_ref.shape[1:]
     main = width // LANES
@@ -264,6 +263,7 @@
             )
         )
     numbers = load_map(map_hbm, map_ref, sems.at[2 * fields])
+    owners = load_map(owner_hbm, owner_ref, sems.at[2 * fields + 1])
     for pair in copies:
         for copy in pair:
             copy.start()
@@ -288,6 +288,9 @@
             boxes[m][f, :, lanes] = column_sum(total, row_id, 0.0, 0.0) - 27.0 * tile
             drift_ref[m, f, :, lanes] = 2.0 * tile - p_ref[m, f, :, lanes]
     rim_ref[:, 4:8, :] = jnp.zeros((2, 4, width), F32)
+    owners.wait()
+    moves = jnp.where(owner_ref[1] != lax.axis_index("blk"), 1.0, 0.0)
+    rim_ref[0, 4:5, :] = jnp.zeros((1, width), F32) + moves
 
 
 def tile_at(t):
@@ -366,7 +369,7 @@
     column = ColumnEdge(coef_ref, y_ref)
     before = slice(width - LANES, width)
     extra_s = straight_ref[fields * depth : fields * depth + 16, :].astype(F32)
-    extra_d = diag_ref[depth : depth + 32, :].astype(F32)
+    extra_d = diag_ref[depth : depth + 24, :].astype(F32)
     tags_d = [extra_d[16 + i : 17 + i] for i in range(8)]
 
     def edge_tiles(of, remote):
@@ -383,6 +386,8 @@
     pair_sum = nine_sum(pairs, lane)
     near_sum = [total[0:4] for total in pair_sum]
     both_sum = [total[0:4] + total[4:8] for total in pair_sum]
+    laps, sides = [], []
+    row_id = lax.broadcasted_iota(jnp.int32, (depth, 1), 0)
     top = slice(0, 1)
     bottom = slice(depth - 1, depth)
     for f in range(fields):
@@ -392,14 +397,14 @@
             box_ref[f, top, lanes] = box_in[f, top, lanes] + low_row
             box_ref[f, bottom, lanes] = box_in[f, bottom, lanes] + high_row
         remote = straight_ref[f * depth : (f + 1) * depth, :].astype(F32)
-        side_ref[f] = pltpu.roll(remote, 64, 1) + side_coef_ref[f] * side_lap_ref[f]
         low_row, high_row = column.rows(near_sum[main + 1][f : f + 1])
-        side_ref[f, top] += side_coef_ref[f, top] * low_row
-        side_ref[f, bottom] += side_coef_ref[f, bottom] * high_row
+        lap = side_lap_ref[f] + jnp.where(row_id == 0, low_row, 0.0) + jnp.where(row_id == depth - 1, high_row, 0.0)
+        sides.append(pltpu.roll(remote, 64, 1) + side_coef_ref[f] * lap)
+        side_ref[f] = sides[f]
         low_row, high_row = column.rows(near_sum[0][f : f + 1])
-        lap_ref[f] = box0_ref[f, :, before]
-        lap_ref[f, top] += low_row
-        lap_ref[f, bottom] += high_row
+        lap = box0_ref[f, :, before]
+        laps.append(lap + jnp.where(row_id == 0, low_row, 0.0) + jnp.where(row_id == depth - 1, high_row, 0.0))
+        lap_ref[f] = laps[f]
     rims = [rim_ref[0, 0:4, before]] + [rim_ref[1, 0:4, tile_at(t)] for t in range(main)] + [side_rim_ref[1, 0:4, :]]
     rims[main] = jnp.where(lane >= 96, side_rim_ref[0, 0:4, :], rims[main])
     stepped = []
@@ -410,7 +415,7 @@
     for t in range(main):
         sums_ref[0:4, tile_at(t)] = stepped_sum[t + 1]
     sums_ref[4:8, :] = jnp.zeros((4, width), F32)
-    return stepped[main], stepped_sum[1 : main + 1]
+    return stepped[main], stepped_sum[1 : main + 1], laps, sides
 
 
 def first_edges_body(coef_ref, y_ref, rim_ref, box1_ref, box_in, box_ref, sums_ref, edge_c_ref):
@@ -505,12 +510,12 @@
     edges_ref, u_ref, coef_ref, held_ref, y_ref, straight_ref, diag_ref, box0_ref, rim_ref, side_lap_ref, side_coef_ref,
     side_rim_ref, drift_ref, box_in, box_ref, lap_ref, side_ref, sums_ref, row_ref, code_ref, power_ref, extra_ref
 ):
-    tail, edge_sums = last_edges(
+    tail, edge_sums, laps, sides = last_edges(
         coef_ref, y_ref, straight_ref, diag_ref, box0_ref, rim_ref, side_lap_ref, side_coef_ref, side_rim_ref, box_in,
         box_ref, lap_ref, side_ref, sums_ref
     )
     refs = (edges_ref, u_ref, held_ref, y_ref, box_ref, drift_ref, lap_ref, side_ref, sums_ref, row_ref, code_ref, power_ref)
-    last_row(0, *refs, more=(tail, edge_sums, extra_ref))
+    last_row(0, *refs, more=(tail, edge_sums, laps, sides, rim_ref[0, 4:5, 0:LANES], extra_ref))
 
 
 def last_row_b_body(first, *refs):
@@ -534,8 +539,9 @@
         coef = pieces.piece(fields + f)
         coefs = [coef(tile_at(t)) for t in range(main)]
         middle = [drift_ref[1, f, :, tile_at(t)] + coefs[t] * box_ref[f, :, tile_at(t)] for t in range(main)]
-        local = drift_ref[0, f, :, before] + pieces.piece(f)(before) * lap_ref[f]
-        sums = nine_sum([local] + middle + [side_ref[f]], lane)
+        lap, side = (lap_ref[f], side_ref[f]) if more is None else (more[2][f], more[3][f])
+        local = drift_ref[0, f, :, before] + pieces.piece(f)(before) * lap
+        sums = nine_sum([local] + middle + [side], lane)
         for t in range(main):
             lanes = tile_at(t)
             row = sums_ref[f : f + 1, lanes] if more is None else more[1][t][f : f + 1]
@@ -549,7 +555,7 @@
     base = count * main * depth
     code_ref[base : base + count * main, :] = narrow(power_ref[...])
     if more is not None:
-        tail, _, extra_ref = more
+        tail, _, _, _, flag, extra_ref = more
         base += count * main
         both = []
         for f in range(fields):
@@ -577,7 +583,7 @@
         extra_ref[2:3, :] = power
         for i, kind in enumerate(kinds):
             extra_ref[3 + i : 4 + i, :] = coded(kind, power)
-        extra_ref[6:7, :] = edges_ref[29:30, 0:LANES]
+        extra_ref[6:7, :] = flag
         extra_ref[7:8, :] = jnp.zeros((1, LANES), F32)
         code_ref[base : base + 8, :] = narrow(extra_ref[...])
 
@@ -779,7 +785,7 @@
         )(*args)
 
     straight = jax.ShapeDtypeStruct((fields * depth + 16, LANES), BF16)
-    diag = jax.ShapeDtypeStruct((depth + 32, LANES), BF16)
+    diag = jax.ShapeDtypeStruct((depth + 24, LANES), BF16)
     tiles = jax.ShapeDtypeStruct((fields, depth, LANES), F32)
     y_out, edges, front, front_prev, front_coef = call(
         pack_region_body,
@@ -791,17 +797,16 @@
             tiles,
             jax.ShapeDtypeStruct((2, 4, depth, LANES), BF16),
         ),
-        [HBM] * 5,
+        [HBM] * 4,
         (VMEM,) * 5,
         [
             pltpu.VMEM((blocks, fields, 2, width), F32),
             pltpu.VMEM((blocks, fields, 1, width), F32),
             pltpu.VMEM((4, 8, width), BF16),
             pltpu.SMEM(order.shape, jnp.int32),
-            pltpu.SMEM(new_owner.shape, jnp.int32),
-            pltpu.SemaphoreType.DMA((9,)),
+            pltpu.SemaphoreType.DMA((8,)),
         ],
-        (order_hbm, owner_hbm, now_hbm, prev_hbm, coef_hbm),
+        (order_hbm, now_hbm, prev_hbm, coef_hbm),
     )
     left, dleft = call(
         pack_back_body, "pack_back", (straight, diag), [VMEM] * 4, (VMEM,) * 2, [], (edges, front, front_prev, front_coef)
@@ -828,14 +833,15 @@
             jax.ShapeDtypeStruct((blocks, 8, width), F32),
             jax.ShapeDtypeStruct((blocks * fields, depth, width), BF16),
         ),
-        [HBM] * 3 + [VMEM],
+        [HBM] * 4 + [VMEM],
         (VMEM,) * 6,
         [
             pltpu.VMEM(now.shape, F32),
             pltpu.SMEM(order.shape, jnp.int32),
-            pltpu.SemaphoreType.DMA((2 * fields + 1,)),
+            pltpu.SMEM(new_owner.shape, jnp.int32),
+            pltpu.SemaphoreType.DMA((2 * fields + 2,)),
         ],
-        (order_hbm, now_hbm, prev_hbm, coef),
+        (order_hbm, owner_hbm, now_hbm, prev_hbm, coef),
     )
     sums = jax.ShapeDtypeStruct((8, width), F32)
     edge = jax.ShapeDtypeStruct((8, LANES), F32)

time: 22.9 us -> 22.8 us (level)
  no operation moved by 1% of the time
where the time goes in v12:
time: 22.8 us; the launch traced here: 22.7 us
  Pallas kernels  10.5 us (46%)
  starting transfers between devices  9.59 us (42%)
  waiting for transfers between devices  2.4 us (11%)
    pallas_call x11, Pallas kernels, call(): pl.pallas_call(body, out_shape=out_shape, in_specs=in_specs, out_specs=ou...  10.5 us
    ppermute x1, starting transfers between devices, fast_on_device(): from_right = lax.ppermute(left, 'blk', backward)  3.74 us
    ppermute x1, starting transfers between devices, fast_on_device(): y_in = lax.ppermute(y_out, 'region', swap)  3.03 us
    ppermute x1, waiting for transfers between devices, fast_on_device(): arrived = [lax.ppermute(code, 'blk', forward)]  2.02 us
    ppermute x1, starting transfers between devices, fast_on_device(): arrived.append(lax.ppermute(code, 'blk', forward))  1.86 us
    ppermute x1, starting transfers between devices, fast_on_device(): from_dright = lax.ppermute(dleft, ('region', 'blk'), crossed)  0.9 us
  transfers between devices with their start and end apart: 5, of which 3 were waited for; matrix products, arithmetic and copies ran while one was open for 0% of the time, Pallas kernels for 34%

profile of v12, /device:TPU:0, one launch (start us, length us, event | category | flops | bytes accessed | tf_op | source)
XLA Modules:
  0.0 22.7 jit_solution(6172833296545884834)
XLA Ops:
  0.0 0.0 copy-start
  0.0 1.2 %pack_region.1 = (bf16[5,32,1024]{2,1,0:T(8,128)(2,1)S(1)}, f32[32,1024]{1,0:T(8,128)S(1)}, f32[4,32,128]{2,1,0:T(8,128)S(1)}, f32[4,32,128]{2,1,0:T(8,128)S(1)}, bf16[2,4,32,128]{3,2,1,0:T(8,128)(2,1)S(1)}) custom-call(s32[8]{0:T(128)} %bitcast.15, f32[2,4,32,1024]{3,2,1,0:T(8,128)} %bitcast.11, f32[2,4,32,1024]{3,2,1,0:T(8,128)} %bitcast.13, ...), custom_call_target="tpu_custom_call" | custom-call | tf_op jit(solution)/shard_map/pack_region/pallas_call | solution.py:776
  1.2 3.0 %collective-permute-start = (bf16[5,32,1024]{2,1,0:T(8,128)(2,1)S(1)}, bf16[5,32,1024]{2,1,0:T(8,128)(2,1)S(1)}, u32[]{:S(2)}, u32[]{:S(2)}) collective-permute-start(bf16[5,32,1024]{2,1,0:T(8,128)(2,1)S(1)} %get-tuple-element.38), channel_id=1, source_target_pairs={{0,16},{16,0},{1,17},{17,1},{2,18},{18,2},{3,19},{19,3},{4,20},{20... | collective-permute-start | bytes 983048 | tf_op jit(solution)/shard_map/ppermute | solution.py:819
  4.2 0.1 pack_back.1
  4.3 3.7 %collective-permute-start.1 = (bf16[144,128]{1,0:T(8,128)(2,1)S(1)}, bf16[144,128]{1,0:T(8,128)(2,1)S(1)}, u32[]{:S(2)}, u32[]{:S(2)}) collective-permute-start(bf16[144,128]{1,0:T(8,128)(2,1)S(1)} %get-tuple-element.42), channel_id=1, source_target_pairs={{0,15},{1,0},{2,1},{3,2},{4,3},{5,4},{6,5},{7,6},{8,7},{9,8},{10,9... | collective-permute-start | bytes 110600 | tf_op jit(solution)/shard_map/ppermute | solution.py:820
  8.1 0.9 %collective-permute-start.2 = (bf16[56,128]{1,0:T(8,128)(2,1)S(1)}, bf16[56,128]{1,0:T(8,128)(2,1)S(1)}, u32[]{:S(2)}, u32[]{:S(2)}) collective-permute-start(bf16[56,128]{1,0:T(8,128)(2,1)S(1)} %get-tuple-element.43), channel_id=1, source_target_pairs={{0,31},{1,16},{2,17},{3,18},{4,19},{5,20},{6,21},{7,22},{8,23},{9,... | collective-permute-start | bytes 43016 | tf_op jit(solution)/shard_map/ppermute | solution.py:821
  9.0 0.0 copy-done
  9.0 2.7 %local.1 = (f32[2,4,32,1024]{3,2,1,0:T(8,128)S(1)}, f32[4,32,1024]{2,1,0:T(8,128)S(1)}, f32[4,32,1024]{2,1,0:T(8,128)S(1)}, f32[2,4,32,1024]{3,2,1,0:T(8,128)S(1...) custom-call(s32[8]{0:T(128)} %bitcast.16, s32[2]{0:T(128)} %owner_any.1, f32[2,4,32,1024]{3,2,1,0:T(8,128)} %bitcast.12, ...), custom_call_target="tpu_custom_call" | custom-call | tf_op jit(solution)/shard_map/local/pallas_call | solution.py:776
  11.7 0.0 collective-permute-done.2.diag_ref
  11.7 0.0 collective-permute-done.1.straight_ref
  11.7 0.3 %border.1 = (f32[4,32,1024]{2,1,0:T(8,128)S(1)}, f32[4,32,128]{2,1,0:T(8,128)S(1)}, f32[4,32,128]{2,1,0:T(8,128)S(1)}, f32[2,8,128]{2,1,0:T(8,128)S(1)}) custom-call(f32[2,4,32,1024]{3,2,1,0:T(8,128)S(1)} %get-tuple-element.36.u_ref.refs_1_, bf16[144,128]{1,0:T(8,128)(2,1)S(1)} %collective-permute-done.1.straight_ref, ...), custom_call_target="tpu_custom_call", output_to_operand_aliasing={{0}: (3, {})} | custom-call | bytes 40000000 | tf_op jit(solution)/shard_map/border/pallas_call | solution.py:776
  12.1 0.2 collective-permute-done.y_ref.refs_3_
  12.3 0.8 %last_row.2 = (f32[4,32,1024]{2,1,0:T(8,128)S(1)}, f32[4,32,128]{2,1,0:T(8,128)S(1)}, f32[4,32,128]{2,1,0:T(8,128)S(1)}, f32[8,1024]{1,0:T(8,128)S(1)}, f32[2,32...) custom-call(f32[32,1024]{1,0:T(8,128)S(1)} %get-tuple-element.35.edges_ref.refs_0_, ...), custom_call_target="tpu_custom_call", output_to_operand_aliasing={{0}: (13, {})} | custom-call | tf_op jit(solution)/shard_map/last_row/pallas_call | solution.py:776
  13.1 0.1 collective-permute-start.3
  13.1 0.6 %last_row.3 = (f32[2,32,1024]{2,1,0:T(8,128)S(1)}, s16[528,128]{1,0:T(8,128)(2,1)S(1)}) custom-call(f32[32,1024]{1,0:T(8,128)S(1)} %get-tuple-element.35.edges_ref.refs_0_, f32[2,4,32,1024]{3,2,1,0:T(8,128)S(1)} %get-tuple-element.36.u_ref.refs_1_, bf16[8,32,1024]{2,1,0:T(8,128)(2,1)S(1)} %get-tuple-element.37.held_ref.refs_2_, ...), custom_call_target="tpu_custom_call" | custom-call | tf_op jit(solution)/shard_map/last_row/pallas_call | solution.py:776
  13.7 1.9 %collective-permute-start.4 = (s16[528,128]{1,0:T(8,128)(2,1)S(1)}, s16[528,128]{1,0:T(8,128)(2,1)S(1)}, u32[]{:S(2)}, u32[]{:S(2)}) collective-permute-start(s16[528,128]{1,0:T(8,128)(2,1)S(1)} %get-tuple-element.57), channel_id=1, source_target_pairs={{0,1},{1,2},{2,3},{3,4},{4,5},{5,6},{6,7},{7,8},{8,9},{9,10},{10,1... | collective-permute-start | bytes 405512 | tf_op jit(solution)/shard_map/ppermute | solution.py:893
  15.6 0.4 %first_edges.1 = (f32[4,32,1024]{2,1,0:T(8,128)S(1)}, f32[8,1024]{1,0:T(8,128)S(1)}, f32[8,128]{1,0:T(8,128)S(1)}) custom-call(bf16[2,4,32,1024]{3,2,1,0:T(8,128)(2,1)S(1)} %bitcast.10, bf16[5,32,1024]{2,1,0:T(8,128)(2,1)S(1)} %collective-permute-done.y_ref.refs_3_, f32[2,8,1024]{2,1,0:T(8,128)S(1)} %get-tuple-element.45.rim_ref, ...), custom_call_target="tpu_custom_call", output_to_operand_aliasing={{0}: (4, {})} | custom-call | tf_op jit(solution)/shard_map/first_edges/pallas_call | solution.py:776
  16.0 0.0 copy-start.1
  16.0 0.9 %first_row.1 = (f32[4,32,1024]{2,1,0:T(8,128)S(1)}, f32[4,32,128]{2,1,0:T(8,128)S(1)}) custom-call(f32[32,1024]{1,0:T(8,128)S(1)} %get-tuple-element.35.edges_ref.refs_0_, f32[2,4,32,1024]{3,2,1,0:T(8,128)S(1)} %get-tuple-element.36.u_ref.refs_1_, bf16[8,32,1024]{2,1,0:T(8,128)(2,1)S(1)} %get-tuple-element.37.held_ref.refs_2_, ...), custom_call_target="tpu_custom_call" | custom-call | tf_op jit(solution)/shard_map/first_row/pallas_call | solution.py:776
  16.9 0.0 copy-done.1
  16.9 1.5 %rows.1.refs_2_ = f32[3,4,32,1024]{3,2,1,0:T(8,128)} custom-call(s32[2]{0:T(128)S(1)} %copy-done.1, f32[4,32,1024]{2,1,0:T(8,128)S(1)} %get-tuple-element.62.row_ref, f32[2,32,1024]{2,1,0:T(8,128)S(1)} %get-tuple-element.63.refs_0_, f32[2,32,1024]{2,1,0:T(8,128)S(1)} %get-tuple-element.64.refs_1_), custom_call_target="tpu_custom_call" | custom-call | tf_op jit(solution)/shard_map/rows/pallas_call | solution.py:776
  18.4 2.0 %collective-permute-done.3.code_ref.code_a_ref = s16[600,128]{1,0:T(8,128)(2,1)S(1)} collective-permute-done((s16[600,128]{1,0:T(8,128)(2,1)S(1)}, s16[600,128]{1,0:T(8,128)(2,1)S(1)}, u32[]{:S(2)}, u32[]{:S(2)}) %collective-permute-start.3) | collective-permute-done | bytes 153632 | tf_op jit(solution)/shard_map/ppermute | solution.py:880
  20.4 1.2 %finish.1.partial_ref = f32[3,4,32,1024]{3,2,1,0:T(8,128)} custom-call(s32[2]{0:T(128)S(1)} %copy-done.1, f32[4,32,128]{2,1,0:T(8,128)S(1)} %get-tuple-element.60.coef_ref, f32[8,128]{1,0:T(8,128)S(1)} %get-tuple-element.61.edge_c_ref, s16[600,128]{1,0:T(8,128)(2,1)S(1)} %collective-permute-done.3.code_ref.code_a_ref, ...), custom_call_target="tpu_custom_call", output_to_operand_aliasing={{}: (7, {})} | custom-call | tf_op jit(solution)/shard_map/finish/pallas_call | solution.py:776
  21.7 0.2 collective-permute-done.4.code_ref
  21.9 0.8 %place.1 = f32[3,4,32,1024]{3,2,1,0:T(8,128)} custom-call(s16[600,128]{1,0:T(8,128)(2,1)S(1)} %collective-permute-done.3.code_ref.code_a_ref, s16[528,128]{1,0:T(8,128)(2,1)S(1)} %collective-permute-done.4.code_ref, f32[3,4,32,1024]{3,2,1,0:T(8,128)} %finish.1.partial_ref), custom_call_target="tpu_custom_call", output_to_operand_aliasing={{}: (2, {})} | custom-call | tf_op jit(solution)/shard_map/place/pallas_call | solution.py:776
Async XLA Ops:
  0.0 9.0 %copy-start = (bf16[1,1,2,4,32,1024]{5,4,3,2,1,0:T(8,128)(2,1)S(1)}, bf16[1,1,2,4,32,1024]{5,4,3,2,1,0:T(8,128)(2,1)}, u32[]{:S(2)}) copy-start(bf16[1,1,2,4,32,1024]{5,4,3,2,1,0:T(8,128)(2,1)} %param.7) | copy-start | bytes 1572868
  1.2 11.0 %collective-permute-start = (bf16[5,32,1024]{2,1,0:T(8,128)(2,1)S(1)}, bf16[5,32,1024]{2,1,0:T(8,128)(2,1)S(1)}, u32[]{:S(2)}, u32[]{:S(2)}) collective-permute-start(bf16[5,32,1024]{2,1,0:T(8,128)(2,1)S(1)} %get-tuple-element.38), channel_id=1, source_target_pairs={{0,16},{16,0},{1,17},{17,1},{2,18},{18,2},{3,19},{19,3},{4,20},{20... | collective-permute-start | bytes 983048 | tf_op jit(solution)/shard_map/ppermute | solution.py:819
  4.3 7.4 %collective-permute-start.1 = (bf16[144,128]{1,0:T(8,128)(2,1)S(1)}, bf16[144,128]{1,0:T(8,128)(2,1)S(1)}, u32[]{:S(2)}, u32[]{:S(2)}) collective-permute-start(bf16[144,128]{1,0:T(8,128)(2,1)S(1)} %get-tuple-element.42), channel_id=1, source_target_pairs={{0,15},{1,0},{2,1},{3,2},{4,3},{5,4},{6,5},{7,6},{8,7},{9,8},{10,9... | collective-permute-start | bytes 110600 | tf_op jit(solution)/shard_map/ppermute | solution.py:820
  8.1 3.6 %collective-permute-start.2 = (bf16[56,128]{1,0:T(8,128)(2,1)S(1)}, bf16[56,128]{1,0:T(8,128)(2,1)S(1)}, u32[]{:S(2)}, u32[]{:S(2)}) collective-permute-start(bf16[56,128]{1,0:T(8,128)(2,1)S(1)} %get-tuple-element.43), channel_id=1, source_target_pairs={{0,31},{1,16},{2,17},{3,18},{4,19},{5,20},{6,21},{7,22},{8,23},{9,... | collective-permute-start | bytes 43016 | tf_op jit(solution)/shard_map/ppermute | solution.py:821
  13.1 7.4 %collective-permute-start.3 = (s16[600,128]{1,0:T(8,128)(2,1)S(1)}, s16[600,128]{1,0:T(8,128)(2,1)S(1)}, u32[]{:S(2)}, u32[]{:S(2)}) collective-permute-start(s16[600,128]{1,0:T(8,128)(2,1)S(1)} %get-tuple-element.52), channel_id=1, source_target_pairs={{0,1},{1,2},{2,3},{3,4},{4,5},{5,6},{6,7},{7,8},{8,9},{9,10},{10,1... | collective-permute-start | bytes 460808 | tf_op jit(solution)/shard_map/ppermute | solution.py:880
  13.7 8.2 %collective-permute-start.4 = (s16[528,128]{1,0:T(8,128)(2,1)S(1)}, s16[528,128]{1,0:T(8,128)(2,1)S(1)}, u32[]{:S(2)}, u32[]{:S(2)}) collective-permute-start(s16[528,128]{1,0:T(8,128)(2,1)S(1)} %get-tuple-element.57), channel_id=1, source_target_pairs={{0,1},{1,2},{2,3},{3,4},{4,5},{5,6},{6,7},{7,8},{8,9},{9,10},{10,1... | collective-permute-start | bytes 405512 | tf_op jit(solution)/shard_map/ppermute | solution.py:893
  16.0 0.9 %copy-start.1 = (s32[2]{0:T(128)S(1)}, s32[2]{0:T(128)}, u32[]{:S(2)}) copy-start(s32[2]{0:T(128)} %owner_any.1) | copy-start | bytes 28

commit v13 on v11

--- a/solution.py
+++ b/solution.py
@@ -850,7 +850,7 @@
         input_output_aliases={3: 0},
         cost_estimate=pl.CostEstimate(flops=0, transcendentals=0, bytes_accessed=40_000_000),
     )
-    bounds = sorted({0, fields // 2, fields})
+    bounds = sorted({0, 1, fields})
     parts = [(first, end - first) for first, end in zip(bounds, bounds[1:])]
 
     def part_shapes(size, more):
@@ -929,6 +929,7 @@
         ],
         (new_owner, coef0, edge_c0, arrived[0], first_row, *lasts, placed),
         input_output_aliases={5 + len(lasts): 0},
+        cost_estimate=pl.CostEstimate(flops=10**10, transcendentals=0, bytes_accessed=10**6),
     )
     for (first, size), codes in zip(parts[1:], arrived[1:]):
         placed = call(

time: 22.9 us -> 22.7 us (level)
    ppermute x1, waiting for transfers between devices: 2.02 us -> 1.12 us  [fast_on_device(): arrived = [lax.ppermute(code, 'blk', forward)]]
    ppermute x1, waiting for transfers between devices: 0.22 us -> 1 us  [fast_on_device(): arrived.append(lax.ppermute(code, 'blk', forward))]
  transfers between devices with their start and end apart: 5 -> 5, of which waited for: 3 -> 3; matrix products, arithmetic and copies ran while one was open for 0% -> 0% of each run, Pallas kernels for 34% -> 35%
where the time goes in v13:
time: 22.7 us; the launch traced here: 22.6 us
  Pallas kernels  10.5 us (46%)
  starting transfers between devices  9.59 us (42%)
  waiting for transfers between devices  2.38 us (10%)
    pallas_call x11, Pallas kernels, call(): pl.pallas_call(body, out_shape=out_shape, in_specs=in_specs, out_specs=ou...  10.5 us
    ppermute x1, starting transfers between devices, fast_on_device(): from_right = lax.ppermute(left, 'blk', backward)  3.74 us
    ppermute x1, starting transfers between devices, fast_on_device(): y_in = lax.ppermute(y_out, 'region', swap)  3.03 us
    ppermute x1, starting transfers between devices, fast_on_device(): arrived.append(lax.ppermute(code, 'blk', forward))  1.86 us
    ppermute x1, waiting for transfers between devices, fast_on_device(): arrived = [lax.ppermute(code, 'blk', forward)]  1.12 us
    ppermute x1, waiting for transfers between devices, fast_on_device(): arrived.append(lax.ppermute(code, 'blk', forward))  1 us
    ppermute x1, starting transfers between devices, fast_on_device(): from_dright = lax.ppermute(dleft, ('region', 'blk'), crossed)  0.9 us
  transfers between devices with their start and end apart: 5, of which 3 were waited for; matrix products, arithmetic and copies ran while one was open for 0% of the time, Pallas kernels for 35%

profile of v13, /device:TPU:0, one launch (start us, length us, event | category | flops | bytes accessed | tf_op | source)
XLA Modules:
  0.0 22.6 jit_solution(10085052057904968626)
XLA Ops:
  0.0 0.0 copy-start
  0.0 1.2 %pack_region.1 = (bf16[5,32,1024]{2,1,0:T(8,128)(2,1)S(1)}, f32[32,1024]{1,0:T(8,128)S(1)}, f32[4,32,128]{2,1,0:T(8,128)S(1)}, f32[4,32,128]{2,1,0:T(8,128)S(1)}, bf16[2,4,32,128]{3,2,1,0:T(8,128)(2,1)S(1)}) custom-call(s32[8]{0:T(128)} %bitcast.15, s32[2]{0:T(128)} %owner_any.1, f32[2,4,32,1024]{3,2,1,0:T(8,128)} %bitcast.11, f32[2,4,32,1024]{3,2,1,0:T(8,128)} %bitcast.13, ...), custom_call_target="tpu_custom_call" | custom-call | tf_op jit(solution)/shard_map/pack_region/pallas_call | solution.py:770
  1.2 3.0 %collective-permute-start = (bf16[5,32,1024]{2,1,0:T(8,128)(2,1)S(1)}, bf16[5,32,1024]{2,1,0:T(8,128)(2,1)S(1)}, u32[]{:S(2)}, u32[]{:S(2)}) collective-permute-start(bf16[5,32,1024]{2,1,0:T(8,128)(2,1)S(1)} %get-tuple-element.38), channel_id=1, source_target_pairs={{0,16},{16,0},{1,17},{17,1},{2,18},{18,2},{3,19},{19,3},{4,20},{20... | collective-permute-start | bytes 983048 | tf_op jit(solution)/shard_map/ppermute | solution.py:814
  4.2 0.1 pack_back.1
  4.3 3.7 %collective-permute-start.1 = (bf16[144,128]{1,0:T(8,128)(2,1)S(1)}, bf16[144,128]{1,0:T(8,128)(2,1)S(1)}, u32[]{:S(2)}, u32[]{:S(2)}) collective-permute-start(bf16[144,128]{1,0:T(8,128)(2,1)S(1)} %get-tuple-element.42), channel_id=1, source_target_pairs={{0,15},{1,0},{2,1},{3,2},{4,3},{5,4},{6,5},{7,6},{8,7},{9,8},{10,9... | collective-permute-start | bytes 110600 | tf_op jit(solution)/shard_map/ppermute | solution.py:815
  8.1 0.9 %collective-permute-start.2 = (bf16[64,128]{1,0:T(8,128)(2,1)S(1)}, bf16[64,128]{1,0:T(8,128)(2,1)S(1)}, u32[]{:S(2)}, u32[]{:S(2)}) collective-permute-start(bf16[64,128]{1,0:T(8,128)(2,1)S(1)} %get-tuple-element.43), channel_id=1, source_target_pairs={{0,31},{1,16},{2,17},{3,18},{4,19},{5,20},{6,21},{7,22},{8,23},{9,... | collective-permute-start | bytes 49160 | tf_op jit(solution)/shard_map/ppermute | solution.py:816
  9.0 0.0 copy-done
  9.0 2.7 %local.1 = (f32[2,4,32,1024]{3,2,1,0:T(8,128)S(1)}, f32[4,32,1024]{2,1,0:T(8,128)S(1)}, f32[4,32,1024]{2,1,0:T(8,128)S(1)}, f32[2,4,32,1024]{3,2,1,0:T(8,128)S(1...) custom-call(s32[8]{0:T(128)} %bitcast.16, f32[2,4,32,1024]{3,2,1,0:T(8,128)} %bitcast.12, ...), custom_call_target="tpu_custom_call" | custom-call | tf_op jit(solution)/shard_map/local/pallas_call | solution.py:770
  11.7 0.0 collective-permute-done.2.diag_ref
  11.7 0.0 collective-permute-done.1.straight_ref
  11.7 0.3 %border.1 = (f32[4,32,1024]{2,1,0:T(8,128)S(1)}, f32[4,32,128]{2,1,0:T(8,128)S(1)}, f32[4,32,128]{2,1,0:T(8,128)S(1)}, f32[2,8,128]{2,1,0:T(8,128)S(1)}) custom-call(f32[2,4,32,1024]{3,2,1,0:T(8,128)S(1)} %get-tuple-element.36.u_ref.refs_1_, bf16[144,128]{1,0:T(8,128)(2,1)S(1)} %collective-permute-done.1.straight_ref, ...), custom_call_target="tpu_custom_call", output_to_operand_aliasing={{0}: (3, {})} | custom-call | bytes 40000000 | tf_op jit(solution)/shard_map/border/pallas_call | solution.py:770
  12.1 0.3 %collective-permute-done.y_ref.refs_3_ = bf16[5,32,1024]{2,1,0:T(8,128)(2,1)S(1)} collective-permute-done((bf16[5,32,1024]{2,1,0:T(8,128)(2,1)S(1)}, bf16[5,32,1024]{2,1,0:T(8,128)(2,1)S(1)}, u32[]{:S(2)}, u32[]{:S(2)}) %collective-permute-start) | collective-permute-done | bytes 327712 | tf_op jit(solution)/shard_map/ppermute | solution.py:814
  12.3 0.6 %last_row.2 = (f32[4,32,1024]{2,1,0:T(8,128)S(1)}, f32[4,32,128]{2,1,0:T(8,128)S(1)}, f32[4,32,128]{2,1,0:T(8,128)S(1)}, f32[8,1024]{1,0:T(8,128)S(1)}, f32[1,32...) custom-call(f32[32,1024]{1,0:T(8,128)S(1)} %get-tuple-element.35.edges_ref.refs_0_, ...), custom_call_target="tpu_custom_call", output_to_operand_aliasing={{0}: (13, {})} | custom-call | tf_op jit(solution)/shard_map/last_row/pallas_call | solution.py:770
  12.9 0.1 collective-permute-start.3
  12.9 0.8 %last_row.3 = (f32[3,32,1024]{2,1,0:T(8,128)S(1)}, s16[792,128]{1,0:T(8,128)(2,1)S(1)}) custom-call(f32[32,1024]{1,0:T(8,128)S(1)} %get-tuple-element.35.edges_ref.refs_0_, f32[2,4,32,1024]{3,2,1,0:T(8,128)S(1)} %get-tuple-element.36.u_ref.refs_1_, bf16[8,32,1024]{2,1,0:T(8,128)(2,1)S(1)} %get-tuple-element.37.held_ref.refs_2_, ...), custom_call_target="tpu_custom_call" | custom-call | tf_op jit(solution)/shard_map/last_row/pallas_call | solution.py:770
  13.8 1.9 %collective-permute-start.4 = (s16[792,128]{1,0:T(8,128)(2,1)S(1)}, s16[792,128]{1,0:T(8,128)(2,1)S(1)}, u32[]{:S(2)}, u32[]{:S(2)}) collective-permute-start(s16[792,128]{1,0:T(8,128)(2,1)S(1)} %get-tuple-element.57), channel_id=1, source_target_pairs={{0,1},{1,2},{2,3},{3,4},{4,5},{5,6},{6,7},{7,8},{8,9},{9,10},{10,1... | collective-permute-start | bytes 608264 | tf_op jit(solution)/shard_map/ppermute | solution.py:887
  15.6 0.4 %first_edges.1 = (f32[4,32,1024]{2,1,0:T(8,128)S(1)}, f32[8,1024]{1,0:T(8,128)S(1)}, f32[8,128]{1,0:T(8,128)S(1)}) custom-call(bf16[2,4,32,1024]{3,2,1,0:T(8,128)(2,1)S(1)} %bitcast.10, bf16[5,32,1024]{2,1,0:T(8,128)(2,1)S(1)} %collective-permute-done.y_ref.refs_3_, f32[2,8,1024]{2,1,0:T(8,128)S(1)} %get-tuple-element.45.rim_ref, ...), custom_call_target="tpu_custom_call", output_to_operand_aliasing={{0}: (4, {})} | custom-call | tf_op jit(solution)/shard_map/first_edges/pallas_call | solution.py:770
  16.0 0.0 copy-start.1
  16.0 0.8 %first_row.1 = (f32[4,32,1024]{2,1,0:T(8,128)S(1)}, f32[4,32,128]{2,1,0:T(8,128)S(1)}) custom-call(f32[32,1024]{1,0:T(8,128)S(1)} %get-tuple-element.35.edges_ref.refs_0_, f32[2,4,32,1024]{3,2,1,0:T(8,128)S(1)} %get-tuple-element.36.u_ref.refs_1_, bf16[8,32,1024]{2,1,0:T(8,128)(2,1)S(1)} %get-tuple-element.37.held_ref.refs_2_, ...), custom_call_target="tpu_custom_call" | custom-call | tf_op jit(solution)/shard_map/first_row/pallas_call | solution.py:770
  16.9 0.0 copy-done.1
  16.9 1.5 %rows.1.refs_2_ = f32[3,4,32,1024]{3,2,1,0:T(8,128)} custom-call(s32[2]{0:T(128)S(1)} %copy-done.1, f32[4,32,1024]{2,1,0:T(8,128)S(1)} %get-tuple-element.62.row_ref, f32[1,32,1024]{2,1,0:T(8,128)S(1)} %get-tuple-element.63.refs_0_, f32[3,32,1024]{2,1,0:T(8,128)S(1)} %get-tuple-element.64.refs_1_), custom_call_target="tpu_custom_call" | custom-call | tf_op jit(solution)/shard_map/rows/pallas_call | solution.py:770
  18.4 1.1 %collective-permute-done.3.code_ref.code_a_ref = s16[336,128]{1,0:T(8,128)(2,1)S(1)} collective-permute-done((s16[336,128]{1,0:T(8,128)(2,1)S(1)}, s16[336,128]{1,0:T(8,128)(2,1)S(1)}, u32[]{:S(2)}, u32[]{:S(2)}) %collective-permute-start.3) | collective-permute-done | bytes 86048 | tf_op jit(solution)/shard_map/ppermute | solution.py:874
  19.5 1.2 %finish.1.partial_ref = f32[3,4,32,1024]{3,2,1,0:T(8,128)} custom-call(s32[2]{0:T(128)S(1)} %copy-done.1, f32[4,32,128]{2,1,0:T(8,128)S(1)} %get-tuple-element.60.coef_ref, f32[8,128]{1,0:T(8,128)S(1)} %get-tuple-element.61.edge_c_ref, s16[336,128]{1,0:T(8,128)(2,1)S(1)} %collective-permute-done.3.code_ref.code_a_ref, ...), custom_call_target="tpu_custom_call", output_to_operand_aliasing={{}: (7, {})} | custom-call | flops 10000000000 | bytes 1000000 | tf_op jit(solution)/shard_map/finish/pallas_call | solution.py:770
  20.7 1.0 %collective-permute-done.4.code_ref = s16[792,128]{1,0:T(8,128)(2,1)S(1)} collective-permute-done((s16[792,128]{1,0:T(8,128)(2,1)S(1)}, s16[792,128]{1,0:T(8,128)(2,1)S(1)}, u32[]{:S(2)}, u32[]{:S(2)}) %collective-permute-start.4) | collective-permute-done | bytes 202784 | tf_op jit(solution)/shard_map/ppermute | solution.py:887
  21.7 0.9 %place.1 = f32[3,4,32,1024]{3,2,1,0:T(8,128)} custom-call(s16[336,128]{1,0:T(8,128)(2,1)S(1)} %collective-permute-done.3.code_ref.code_a_ref, s16[792,128]{1,0:T(8,128)(2,1)S(1)} %collective-permute-done.4.code_ref, f32[3,4,32,1024]{3,2,1,0:T(8,128)} %finish.1.partial_ref), custom_call_target="tpu_custom_call", output_to_operand_aliasing={{}: (2, {})} | custom-call | tf_op jit(solution)/shard_map/place/pallas_call | solution.py:770
Async XLA Ops:
  0.0 9.0 %copy-start = (bf16[1,1,2,4,32,1024]{5,4,3,2,1,0:T(8,128)(2,1)S(1)}, bf16[1,1,2,4,32,1024]{5,4,3,2,1,0:T(8,128)(2,1)}, u32[]{:S(2)}) copy-start(bf16[1,1,2,4,32,1024]{5,4,3,2,1,0:T(8,128)(2,1)} %param.7) | copy-start | bytes 1572868
  1.2 11.1 %collective-permute-start = (bf16[5,32,1024]{2,1,0:T(8,128)(2,1)S(1)}, bf16[5,32,1024]{2,1,0:T(8,128)(2,1)S(1)}, u32[]{:S(2)}, u32[]{:S(2)}) collective-permute-start(bf16[5,32,1024]{2,1,0:T(8,128)(2,1)S(1)} %get-tuple-element.38), channel_id=1, source_target_pairs={{0,16},{16,0},{1,17},{17,1},{2,18},{18,2},{3,19},{19,3},{4,20},{20... | collective-permute-start | bytes 983048 | tf_op jit(solution)/shard_map/ppermute | solution.py:814
  4.3 7.3 %collective-permute-start.1 = (bf16[144,128]{1,0:T(8,128)(2,1)S(1)}, bf16[144,128]{1,0:T(8,128)(2,1)S(1)}, u32[]{:S(2)}, u32[]{:S(2)}) collective-permute-start(bf16[144,128]{1,0:T(8,128)(2,1)S(1)} %get-tuple-element.42), channel_id=1, source_target_pairs={{0,15},{1,0},{2,1},{3,2},{4,3},{5,4},{6,5},{7,6},{8,7},{9,8},{10,9... | collective-permute-start | bytes 110600 | tf_op jit(solution)/shard_map/ppermute | solution.py:815
  8.1 3.6 %collective-permute-start.2 = (bf16[64,128]{1,0:T(8,128)(2,1)S(1)}, bf16[64,128]{1,0:T(8,128)(2,1)S(1)}, u32[]{:S(2)}, u32[]{:S(2)}) collective-permute-start(bf16[64,128]{1,0:T(8,128)(2,1)S(1)} %get-tuple-element.43), channel_id=1, source_target_pairs={{0,31},{1,16},{2,17},{3,18},{4,19},{5,20},{6,21},{7,22},{8,23},{9,... | collective-permute-start | bytes 49160 | tf_op jit(solution)/shard_map/ppermute | solution.py:816
  12.9 6.7 %collective-permute-start.3 = (s16[336,128]{1,0:T(8,128)(2,1)S(1)}, s16[336,128]{1,0:T(8,128)(2,1)S(1)}, u32[]{:S(2)}, u32[]{:S(2)}) collective-permute-start(s16[336,128]{1,0:T(8,128)(2,1)S(1)} %get-tuple-element.52), channel_id=1, source_target_pairs={{0,1},{1,2},{2,3},{3,4},{4,5},{5,6},{6,7},{7,8},{8,9},{9,10},{10,1... | collective-permute-start | bytes 258056 | tf_op jit(solution)/shard_map/ppermute | solution.py:874
  13.8 8.0 %collective-permute-start.4 = (s16[792,128]{1,0:T(8,128)(2,1)S(1)}, s16[792,128]{1,0:T(8,128)(2,1)S(1)}, u32[]{:S(2)}, u32[]{:S(2)}) collective-permute-start(s16[792,128]{1,0:T(8,128)(2,1)S(1)} %get-tuple-element.57), channel_id=1, source_target_pairs={{0,1},{1,2},{2,3},{3,4},{4,5},{5,6},{6,7},{7,8},{8,9},{9,10},{10,1... | collective-permute-start | bytes 608264 | tf_op jit(solution)/shard_map/ppermute | solution.py:887
  16.0 0.9 %copy-start.1 = (s32[2]{0:T(128)S(1)}, s32[2]{0:T(128)}, u32[]{:S(2)}) copy-start(s32[2]{0:T(128)} %owner_any.1) | copy-start | bytes 28
